TPU v7x, 32 devices: a whole 2x2x4 slice. The times are simulated.
32 devices in a mesh: dp: 8 (over y, x, core), fsdp: 4 (over z).
Axes of the slice: x: 2, y: 2, z: 4, core: 2. Of those that a mesh axis runs over, the one named last changes fastest.
Arguments:
- tokens: bfloat16 [32768, 1024], P(('dp', 'fsdp')), may hold values from -6 to 6
- prefix_len: int32 [32], P(('dp', 'fsdp')), may hold values from 64 to 256
- padding_len: int32 [32], P(('dp', 'fsdp')), may hold values from 0 to 384
- first_gain: bfloat16 [1024], P(('dp', 'fsdp')), may hold values from 0.5 to 1.5
- first_shift: bfloat16 [1024], P(('dp', 'fsdp')), may hold values from -4 to 4
- inproj_weight: bfloat16 [1024, 3072], P(('dp', 'fsdp')), may hold values from -0.1875 to 0.1875
- query_bias: bfloat16 [1024], P(('dp', 'fsdp')), may hold values from -4 to 4
- value_bias: bfloat16 [1024], P(('dp', 'fsdp')), may hold values from -4 to 4
- outproj_weight: bfloat16 [1024, 1024], P(('dp', 'fsdp')), may hold values from -1.5 to 1.5
- outproj_bias: bfloat16 [1024], P(('dp', 'fsdp')), may hold values from -4 to 4
- second_gain: bfloat16 [1024], P(('dp', 'fsdp')), may hold values from 0.5 to 1.5
- second_shift: bfloat16 [1024], P(('dp', 'fsdp')), may hold values from -4 to 4
- up_weight: bfloat16 [1024, 4096], P(('dp', 'fsdp')), may hold values from -0.1875 to 0.1875
- up_bias: bfloat16 [4096], P(('dp', 'fsdp')), may hold values from -4 to 4
- down_weight: bfloat16 [4096, 1024], P(('dp', 'fsdp')), may hold values from -0.09375 to 0.09375
- down_bias: bfloat16 [1024], P(('dp', 'fsdp')), may hold values from -4 to 4
- grad_out: bfloat16 [32768, 1024], P(('dp', 'fsdp')), may hold values from -6 to 6
Outputs:
- out_tokens: bfloat16 [32768, 1024], P(('dp', 'fsdp'))
- tokens_grad: bfloat16 [32768, 1024], P(('dp', 'fsdp'))
- first_gain_grad: float32 [1024], P(('dp', 'fsdp'))
- first_shift_grad: float32 [1024], P(('dp', 'fsdp'))
- inproj_grad: float32 [1024, 3072], P(('dp', 'fsdp'))
- query_bias_grad: float32 [1024], P(('dp', 'fsdp'))
- value_bias_grad: float32 [1024], P(('dp', 'fsdp'))
- outproj_grad: float32 [1024, 1024], P(('dp', 'fsdp'))
- outbias_grad: float32 [1024], P(('dp', 'fsdp'))
- second_gain_grad: float32 [1024], P(('dp', 'fsdp'))
- second_shift_grad: float32 [1024], P(('dp', 'fsdp'))
- up_grad: float32 [1024, 4096], P(('dp', 'fsdp'))
- upbias_grad: float32 [4096], P(('dp', 'fsdp'))
- down_grad: float32 [4096, 1024], P(('dp', 'fsdp'))
- downbias_grad: float32 [1024], P(('dp', 'fsdp'))
All inputs are finite; a program needn't handle non-finite values.
Results may differ from a plain program's by a relative error of at most 0.013.
Values may be sent and summed in bfloat16 or wider, within the bound.
No kernel may reach another device: no remote copies, remote signals or barrier semaphores. Data moves between devices by JAX's collectives and lax.ppermute only.
A program may use at most 320 MiB of HBM per device.

v0:
```python
import math

import jax
import jax.numpy as jnp
from jax import lax
from jax.sharding import PartitionSpec as P

HEADS = 16


EPSILON = 1e-05
NEGATIVE = -1000000000.0


def layer_norm(values, gain, shift):
    center = values - jnp.mean(values, axis=-1, keepdims=True)
    spread = jnp.mean(center * center, axis=-1, keepdims=True)
    return center * lax.rsqrt(spread + EPSILON) * gain + shift


def gelu_exact(values):
    return jax.nn.gelu(values, approximate=False)


def allowed_keys(start, block, stop, prefix, padding, seq_length):
    query_place = start + lax.broadcasted_iota(jnp.int32, (block, stop), 0)
    key_place = lax.broadcasted_iota(jnp.int32, (block, stop), 1)
    return ((key_place < prefix) | (key_place <= query_place)) & (key_place < seq_length - padding)


def block_scores(query_low, key_low, start, stop, prefix, padding):
    seq_length, heads, head_dim = query_low.shape
    block = stop - start
    scores = jnp.einsum(
        "qhd,khd->hqk", query_low[start:stop], key_low[:stop], preferred_element_type=jnp.float32
    ) * (1.0 / math.sqrt(head_dim))
    allowed = allowed_keys(start, block, stop, prefix, padding, seq_length)
    return jnp.where(allowed[None], scores, NEGATIVE)


def attend_forward(query_low, key_low, value_low, prefix, padding):
    seq_length = query_low.shape[0]
    block = min(512, seq_length)
    pieces = []
    totals = []
    for start in range(0, seq_length, block):
        stop = start + block
        scores = block_scores(query_low, key_low, start, stop, prefix, padding)
        highest = jnp.max(scores, axis=-1, keepdims=True)
        exponent = jnp.exp(scores - highest)
        total = jnp.sum(exponent, axis=-1, keepdims=True)
        probability = (exponent / total).astype(jnp.bfloat16)
        context = jnp.einsum(
            "hqk,khd->qhd", probability, value_low[:stop], preferred_element_type=jnp.float32
        )
        pieces.append(context.astype(jnp.bfloat16))
        totals.append((highest + jnp.log(total))[..., 0])
    return (jnp.concatenate(pieces, axis=0), jnp.concatenate(totals, axis=1))


def attend_backward(query_low, key_low, value_low, dctx_low, log_total, prefix, padding):
    seq_length, heads, head_dim = query_low.shape
    block = min(512, seq_length)
    scale = 1.0 / math.sqrt(head_dim)
    query_parts = []
    d_key = jnp.zeros((seq_length, heads, head_dim), jnp.float32)
    d_value = jnp.zeros((seq_length, heads, head_dim), jnp.float32)
    for start in range(0, seq_length, block):
        stop = start + block
        scores = block_scores(query_low, key_low, start, stop, prefix, padding)
        probability = jnp.exp(scores - log_total[:, start:stop, None])
        d_probs = jnp.einsum(
            "qhd,khd->hqk",
            dctx_low[start:stop],
            value_low[:stop],
            preferred_element_type=jnp.float32,
        )
        inner = jnp.sum(probability * d_probs, axis=-1, keepdims=True)
        d_scores = (probability * (d_probs - inner)).astype(jnp.bfloat16)
        query_parts.append(
            jnp.einsum("hqk,khd->qhd", d_scores, key_low[:stop], preferred_element_type=jnp.float32)
            * scale
        )
        d_key = d_key.at[:stop].add(
            jnp.einsum(
                "hqk,qhd->khd", d_scores, query_low[start:stop], preferred_element_type=jnp.float32
            )
            * scale
        )
        d_value = d_value.at[:stop].add(
            jnp.einsum(
                "hqk,qhd->khd",
                probability.astype(jnp.bfloat16),
                dctx_low[start:stop],
                preferred_element_type=jnp.float32,
            )
        )
    return (jnp.concatenate(query_parts, axis=0), d_key, d_value)


def left_product(first, second):
    return lax.dot_general(
        first, second, (((0,), (0,)), ((), ())), preferred_element_type=jnp.float32
    )


def right_product(first, second):
    return lax.dot_general(
        first, second, (((1,), (1,)), ((), ())), preferred_element_type=jnp.float32
    )


def body(
    tokens,
    prefix_len,
    padding_len,
    first_gain,
    first_shift,
    inproj_weight,
    query_bias,
    value_bias,
    outproj_weight,
    outproj_bias,
    second_gain,
    second_shift,
    up_weight,
    up_bias,
    down_weight,
    down_bias,
    grad_out,
):
    f32 = jnp.float32
    bf16 = jnp.bfloat16
    gathered = (
        lax.all_gather(first_gain, ("dp", "fsdp"), axis=0, tiled=True),
        lax.all_gather(first_shift, ("dp", "fsdp"), axis=0, tiled=True),
        lax.all_gather(inproj_weight, ("dp", "fsdp"), axis=0, tiled=True),
        lax.all_gather(query_bias, ("dp", "fsdp"), axis=0, tiled=True),
        lax.all_gather(value_bias, ("dp", "fsdp"), axis=0, tiled=True),
        lax.all_gather(outproj_weight, ("dp", "fsdp"), axis=0, tiled=True),
        lax.all_gather(outproj_bias, ("dp", "fsdp"), axis=0, tiled=True),
        lax.all_gather(second_gain, ("dp", "fsdp"), axis=0, tiled=True),
        lax.all_gather(second_shift, ("dp", "fsdp"), axis=0, tiled=True),
        lax.all_gather(up_weight, ("dp", "fsdp"), axis=0, tiled=True),
        lax.all_gather(up_bias, ("dp", "fsdp"), axis=0, tiled=True),
        lax.all_gather(down_weight, ("dp", "fsdp"), axis=0, tiled=True),
        lax.all_gather(down_bias, ("dp", "fsdp"), axis=0, tiled=True),
    )
    (
        gain_first,
        shift_first,
        inproj_full,
        query_full,
        value_full,
        outproj_full,
        outbias_full,
        gain_second,
        shift_second,
        upproj_full,
        upbias_full,
        downproj_full,
        downbias_full,
    ) = gathered
    seq_count = prefix_len.shape[0]
    row_count = tokens.shape[0]
    feature_count = tokens.shape[1]
    seq_length = row_count // seq_count
    head_dim = feature_count // HEADS
    shape4 = (seq_count, seq_length, HEADS, head_dim)
    xfloat = tokens.astype(f32)
    gain_one = gain_first.astype(f32)
    shift_one = shift_first.astype(f32)
    normed_one = layer_norm(xfloat, gain_one, shift_one).astype(bf16)
    projected = jnp.dot(normed_one, inproj_full, preferred_element_type=f32)
    query_low = (projected[:, :feature_count] + query_full.astype(f32)).astype(bf16).reshape(shape4)
    key_low = projected[:, feature_count : 2 * feature_count].astype(bf16).reshape(shape4)
    value_low = (
        (projected[:, 2 * feature_count :] + value_full.astype(f32)).astype(bf16).reshape(shape4)
    )
    context, log_total = lax.map(
        lambda item: attend_forward(*item), (query_low, key_low, value_low, prefix_len, padding_len)
    )
    context_low = context.reshape(row_count, feature_count)
    branch = jnp.dot(context_low, outproj_full, preferred_element_type=f32) + outbias_full.astype(
        f32
    )
    resid = xfloat + branch
    gain_two = gain_second.astype(f32)
    shift_two = shift_second.astype(f32)
    normed_two = layer_norm(resid, gain_two, shift_two).astype(bf16)
    upper = jnp.dot(normed_two, upproj_full, preferred_element_type=f32) + upbias_full.astype(f32)
    active = gelu_exact(upper).astype(bf16)
    out_tokens = (
        resid
        + jnp.dot(active, downproj_full, preferred_element_type=f32)
        + downbias_full.astype(f32)
    ).astype(bf16)
    again = (
        lax.all_gather(first_gain, ("dp", "fsdp"), axis=0, tiled=True),
        lax.all_gather(first_shift, ("dp", "fsdp"), axis=0, tiled=True),
        lax.all_gather(inproj_weight, ("dp", "fsdp"), axis=0, tiled=True),
        lax.all_gather(query_bias, ("dp", "fsdp"), axis=0, tiled=True),
        lax.all_gather(value_bias, ("dp", "fsdp"), axis=0, tiled=True),
        lax.all_gather(outproj_weight, ("dp", "fsdp"), axis=0, tiled=True),
        lax.all_gather(outproj_bias, ("dp", "fsdp"), axis=0, tiled=True),
        lax.all_gather(second_gain, ("dp", "fsdp"), axis=0, tiled=True),
        lax.all_gather(second_shift, ("dp", "fsdp"), axis=0, tiled=True),
        lax.all_gather(up_weight, ("dp", "fsdp"), axis=0, tiled=True),
        lax.all_gather(up_bias, ("dp", "fsdp"), axis=0, tiled=True),
        lax.all_gather(down_weight, ("dp", "fsdp"), axis=0, tiled=True),
        lax.all_gather(down_bias, ("dp", "fsdp"), axis=0, tiled=True),
    )
    inproj_back = again[2]
    outproj_back = again[5]
    upproj_back = again[9]
    downproj_back = again[11]
    cotangent = grad_out.astype(f32)
    down_grad = left_product(active, grad_out)
    downbias_grad = jnp.sum(cotangent, axis=0)
    d_active = right_product(grad_out, downproj_back)
    _, gelu_back = jax.vjp(gelu_exact, upper)
    d_upper = gelu_back(d_active)[0].astype(bf16)
    up_grad = left_product(normed_two, d_upper)
    upbias_grad = jnp.sum(d_upper.astype(f32), axis=0)
    d_normed_two = right_product(d_upper, upproj_back)
    _, second_back = jax.vjp(layer_norm, resid, gain_two, shift_two)
    resid_part, gain_two_grad, shift_two_grad = second_back(d_normed_two)
    d_resid = cotangent + resid_part
    d_branch = d_resid.astype(bf16)
    outproj_grad = left_product(context_low, d_branch)
    outbias_grad = jnp.sum(d_branch.astype(f32), axis=0)
    d_context = right_product(d_branch, outproj_back).astype(bf16).reshape(shape4)
    d_query, d_key, d_value = lax.map(
        lambda item: attend_backward(*item),
        (query_low, key_low, value_low, d_context, log_total, prefix_len, padding_len),
    )
    dquery_low = d_query.reshape(row_count, feature_count).astype(bf16)
    dvalue_low = d_value.reshape(row_count, feature_count).astype(bf16)
    d_projected = jnp.concatenate(
        [dquery_low, d_key.reshape(row_count, feature_count).astype(bf16), dvalue_low], axis=1
    )
    inproj_grad = left_product(normed_one, d_projected)
    query_bias_grad = jnp.sum(dquery_low.astype(f32), axis=0)
    value_bias_grad = jnp.sum(dvalue_low.astype(f32), axis=0)
    d_normed_one = right_product(d_projected, inproj_back)
    _, first_back = jax.vjp(layer_norm, xfloat, gain_one, shift_one)
    tokens_part, gain_one_grad, shift_one_grad = first_back(d_normed_one)
    tokens_grad = (d_resid + tokens_part).astype(bf16)
    summed = (
        lax.psum_scatter(gain_one_grad, ("dp", "fsdp"), scatter_dimension=0, tiled=True),
        lax.psum_scatter(shift_one_grad, ("dp", "fsdp"), scatter_dimension=0, tiled=True),
        lax.psum_scatter(inproj_grad, ("dp", "fsdp"), scatter_dimension=0, tiled=True),
        lax.psum_scatter(query_bias_grad, ("dp", "fsdp"), scatter_dimension=0, tiled=True),
        lax.psum_scatter(value_bias_grad, ("dp", "fsdp"), scatter_dimension=0, tiled=True),
        lax.psum_scatter(outproj_grad, ("dp", "fsdp"), scatter_dimension=0, tiled=True),
        lax.psum_scatter(outbias_grad, ("dp", "fsdp"), scatter_dimension=0, tiled=True),
        lax.psum_scatter(gain_two_grad, ("dp", "fsdp"), scatter_dimension=0, tiled=True),
        lax.psum_scatter(shift_two_grad, ("dp", "fsdp"), scatter_dimension=0, tiled=True),
        lax.psum_scatter(up_grad, ("dp", "fsdp"), scatter_dimension=0, tiled=True),
        lax.psum_scatter(upbias_grad, ("dp", "fsdp"), scatter_dimension=0, tiled=True),
        lax.psum_scatter(down_grad, ("dp", "fsdp"), scatter_dimension=0, tiled=True),
        lax.psum_scatter(downbias_grad, ("dp", "fsdp"), scatter_dimension=0, tiled=True),
    )
    return (out_tokens, tokens_grad) + tuple(summed)


def solution(mesh):
    placed = (
        P(("dp", "fsdp"), None),
        P(("dp", "fsdp")),
        P(("dp", "fsdp")),
        P(("dp", "fsdp")),
        P(("dp", "fsdp")),
        P(("dp", "fsdp"), None),
        P(("dp", "fsdp")),
        P(("dp", "fsdp")),
        P(("dp", "fsdp"), None),
        P(("dp", "fsdp")),
        P(("dp", "fsdp")),
        P(("dp", "fsdp")),
        P(("dp", "fsdp"), None),
        P(("dp", "fsdp")),
        P(("dp", "fsdp"), None),
        P(("dp", "fsdp")),
        P(("dp", "fsdp"), None),
    )
    return jax.shard_map(
        body,
        mesh=mesh,
        in_specs=placed,
        out_specs=(
            P(("dp", "fsdp"), None),
            P(("dp", "fsdp"), None),
            P(("dp", "fsdp")),
            P(("dp", "fsdp")),
            P(("dp", "fsdp"), None),
            P(("dp", "fsdp")),
            P(("dp", "fsdp")),
            P(("dp", "fsdp"), None),
            P(("dp", "fsdp")),
            P(("dp", "fsdp")),
            P(("dp", "fsdp")),
            P(("dp", "fsdp"), None),
            P(("dp", "fsdp")),
            P(("dp", "fsdp"), None),
            P(("dp", "fsdp")),
        ),
        check_vma=False,
    )
```

profile of v0, /device:TPU:0, one launch (start us, length us, event | category | flops | bytes accessed | tf_op | source)
XLA Modules:
  0.0 1433.0 jit_solution(3069517388561070427)
XLA Ops:
  18.1 42.3 %all-reduce.20 = (bf16[1024]{0:T(1024)(128)(2,1)S(1)}, bf16[1024]{0:T(1024)(128)(2,1)S(1)}, bf16[1024]{0:T(1024)(128)(2,1)S(1)}, bf16[1024]{0:T(1024)(128)(2,1)S...) all-reduce(bf16[1024]{0:T(1024)(128)(2,1)S(1)} %dynamic-update-slic, ...), channel_id=1, replica_groups=mesh['dp'=8,'fsdp'=4] {'dp','fsdp'}, use_global_device_ids=true, to_apply=%add.6 | all-reduce | flops 8192 | bytes 32768
  60.5 66.7 %all-gather = bf16[32,1,128]{2,1,0:T(2,128)(2,1)S(1)} all-gather(bf16[1,1,128]{2,1,0:T(2,128)(2,1)} %bitcast.104), channel_id=1, replica_groups=mesh['dp'=8,'fsdp'=4] {'dp','fsdp'}, dimensions={0}, use_global_device_ids=true | all-gather | bytes 8448 | tf_op jit(solution)/shard_map/all_gather | solution.py:145
  137.2 11.0 fusion.64
  175.8 9.9 fusion.66
  185.7 8.9 fusion.12
  194.6 15.7 %fusion.65 = (f32[16,512]{1,0:T(8,128)S(1)}, f32[16,512,1024]{2,1,0:T(8,128)}) fusion(bf16[512,16,64]{0,2,1:T(8,128)(2,1)S(1)} %bitcast.80, bf16[1024,16,64]{0,2,1:T(8,128)(2,1)} %bitcast.78, pred[512,1024]{1,0:T(8,128)(4,1)S(1)} %copy-done.23), kind=kOutput, calls=%fused_computation.123 | convolution fusion | flops 1098899456 | bytes 37257216 | tf_op jit(solution)/shard_map/while/body/eval_jaxpr/qhd,khd->hqk/dot_general | solution.py:34
  210.4 14.7 %fusion = f32[16,512]{1,0:T(8,128)S(1)} fusion(f32[16,512,1024]{2,1,0:T(8,128)} %get-tuple-element.242, f32[16,512]{1,0:T(8,128)S(1)} %get-tuple-element.241), kind=kLoop, calls=%fused_computation.6 | loop fusion | flops 16769024 | bytes 33619968 | tf_op jit(solution)/shard_map/while/body/eval_jaxpr/reduce_sum | solution.py:51
  225.1 7.8 fusion.46
  233.0 13.3 fusion.45
  257.0 17.0 %fusion.58 = f32[1024,4096]{1,0:T(8,128)} fusion(bf16[1024,4096]{1,0:T(8,128)(2,1)} %all-gather.10.cloned.1.call-done, f32[1024,1024]{0,1:T(8,128)} %copy-done.6, f32[1024]{0:T(1024)S(1)} %convert_element_type.152, f32[1024]{0:T(1024)S(1)} %convert_element_type.151, f32[1024]{0:T(1024)S(1)} %fusion.51, f32[1024]{0:T(1024)S(1)} %broadcast_multiply_fusion), kind=kOutput, calls=%fused_computation.118 | convolution fusion | flops 8595177472 | bytes 29376512 | tf_op jit(solution)/shard_map/dot_general | solution.py:191
  274.0 25.5 %all-gather.12.cloned.1.call-done = bf16[4096,1024]{1,0:T(8,128)(2,1)} async-done(((bf16[128,1024]{1,0:T(8,128)(2,1)}), bf16[4096,1024]{1,0:T(8,128)(2,1)}) %all-gather.12.cloned.1.call-update) | async-done | bytes 8388624 | tf_op jit(solution)/shard_map/all_gather | solution.py:146
  299.6 51.7 %convert_reduce_fusion = (f32[4096]{0:T(1024)}, bf16[1024,4096]{1,0:T(8,128)(2,1)S(1)}, f32[1024,4096]{1,0:T(8,128)}) fusion(f32[1024,4096]{1,0:T(8,128)} %fusion.58, f32[4096]{0:T(1024)S(1)} %bitcast.102, bf16[1024,1024]{1,0:T(8,128)(2,1)S(1)} %copy-done.26, bf16[4096,1024]{1,0:T(8,128)(2,1)} %all-gather.12.cloned.1.call-done), kind=kOutput, calls=%fused_computation.11 | convolution fusion | flops 8904503296 | bytes 52461568 | tf_op jit(solution)/shard_map/dot_general | solution.py:108
  351.3 11.1 fusion.69
  387.8 11.2 multiply_reduce_fusion.1
  399.0 22.4 %multiply_reduce_fusion = (f32[16,512]{1,0:T(8,128)S(1)}, f32[16,512,1024]{2,1,0:T(8,128)}) fusion(f32[16,512,1024]{2,1,0:T(8,128)} %get-tuple-element.242, f32[16,512]{1,0:T(8,128)S(1)} %copy-done.29, bf16[512,16,64]{0,2,1:T(8,128)(2,1)S(1)} %bitcast.86, bf16[1024,16,64]{0,2,1:T(8,128)(2,1)S(1)} %bitcast.85), kind=kOutput, calls=%fused_computation.1 | convolution fusion | flops 1098899456 | bytes 70320128 | tf_op jit(solution)/shard_map/while/body/eval_jaxpr/qhd,khd->hqk/dot_general | solution.py:72
  421.4 27.9 %multiply_convert_fusion = bf16[16,512,1024]{2,1,0:T(8,128)(2,1)} fusion(f32[16,512,1024]{2,1,0:T(8,128)} %get-tuple-element.250, f32[16,512,1024]{2,1,0:T(8,128)} %get-tuple-element.242, f32[16,512]{1,0:T(8,128)S(1)} %get-tuple-element.249, f32[16,512]{1,0:T(8,128)S(1)} %copy-done.29), kind=kLoop, calls=%fused_computation | loop fusion | flops 33554432 | bytes 83951616 | tf_op jit(solution)/shard_map/while/body/eval_jaxpr/convert_element_type | solution.py:79
  449.3 12.3 multiply_convert_fusion.1
  466.5 12.0 multiply_bitcast_fusion.1
  482.1 7.5 multiply_bitcast_fusion
  489.6 10.2 fusion.40
  499.8 6.0 fusion.32
  505.9 15.9 %convert_reduce_fusion.4 = (f32[16,64]{1,0:T(8,128)S(1)}, bf16[1024,16,64]{0,2,1:T(8,128)(2,1)}) fusion(bf16[512,16,64]{0,2,1:T(8,128)(2,1)} %bitcast.87, f32[16,512,1024]{2,1,0:T(8,128)} %get-tuple-element.242, f32[16,512]{1,0:T(8,128)} %log_add_fusion, f32[512,16,64]{0,2,1:T(8,128)} %fusion.40), kind=kOutput, calls=%fused_computation.70 | convolution fusion | flops 1094712320 | bytes 38834176 | tf_op jit(solution)/shard_map/while/body/eval_jaxpr/hqk,qhd->khd/dot_general | solution.py:91
  521.8 14.2 fusion.34
  536.7 16.7 %fusion.57 = f32[1024,4096]{1,0:T(8,128)} fusion(bf16[1024,4096]{1,0:T(8,128)(2,1)} %copy-done.62, f32[1024,1024]{0,1:T(8,128)} %copy-done.6, f32[1024]{0:T(1024)S(1)} %copy-done.59, f32[1024]{0:T(1024)S(1)} %copy-done.46, f32[1024]{0:T(1024)S(1)} %copy-done.48, f32[1024]{0:T(1024)S(1)} %copy-done.42), kind=kOutput, calls=%fused_computation.117 | convolution fusion | flops 8595177472 | bytes 29376512 | tf_op jit(solution)/shard_map/dot_general | solution.py:102
  554.1 14.3 multiply_convert_fusion.2
  571.7 11.5 fusion.71
  584.0 15.4 %add_convert_fusion.2 = bf16[1024,1024]{0,1:T(8,128)(2,1)} fusion(f32[1024,1024]{0,1:T(8,128)} %copy-done.6, f32[1024]{0:T(1024)S(1)} %convert_element_type.156, bf16[1024,4096]{1,0:T(8,128)(2,1)} %copy-done.21, bf16[4096,1024]{1,0:T(8,128)(2,1)} %all-gather.12.cloned.1.call-done), kind=kOutput, calls=%fused_computation.74 | convolution fusion | flops 8593080320 | bytes 23072768 | tf_op jit(solution)/shard_map/dot_general | solution.py:195
  603.5 12.1 fusion.68
  630.7 40.8 %all-reduce.19 = (f32[1024]{0:T(1024)S(1)}, f32[1024]{0:T(1024)S(1)}, f32[1024]{0:T(1024)S(1)}, f32[1024]{0:T(1024)S(1)}, f32[1024]{0:T(1024)S(1)}, /*index=5*/f...) all-reduce(f32[1024]{0:T(1024)S(1)} %get-tuple-element.203, ...), channel_id=2, replica_groups=mesh['dp'=8,'fsdp'=4] {'dp','fsdp'}, use_global_device_ids=true, to_apply=%region_15.16.clone | all-reduce | flops 12288 | bytes 98304
  680.7 13.7 reduce-scatter.5.cloned.1.call-done
  694.4 366.3 %reduce-scatter.9.cloned.1.call-done = f32[32,4096]{1,0:T(8,128)} async-done(((f32[1024,4096]{1,0:T(8,128)}), f32[32,4096]{1,0:T(8,128)}) %reduce-scatter.9.cloned.1.call-update) | async-done | bytes 524304 | tf_op jit(solution)/shard_map/reduce_scatter | solution.py:259
  1060.7 365.2 %reduce-scatter.11.cloned.1.call-done = f32[128,1024]{1,0:T(8,128)} async-done(((f32[4096,1024]{1,0:T(8,128)}), f32[128,1024]{1,0:T(8,128)}) %reduce-scatter.11.cloned.1.call-update) | async-done | bytes 524304 | tf_op jit(solution)/shard_map/reduce_scatter | solution.py:261
  (239 shorter events, 125.0 us)
Async XLA Ops:
  7.2 130.0 %all-gather.6.cloned.1.call-start = ((), (), s32[]{:S(2)}) async-start(), calls=%async_computation.4 | async-start | bytes 6488064 | tf_op jit(solution)/shard_map/all_gather | solution.py:137
  7.9 240.0 %all-gather.8.cloned.1.call-start = ((), (), s32[]{:S(2)}) async-start(), calls=%async_computation.5 | async-start | bytes 2162688 | tf_op jit(solution)/shard_map/all_gather | solution.py:140
  8.7 248.3 %all-gather.10.cloned.1.call-start = ((), (), s32[]{:S(2)}) async-start(), calls=%async_computation.6 | async-start | bytes 8650752 | tf_op jit(solution)/shard_map/all_gather | solution.py:144
  9.4 290.2 %all-gather.12.cloned.1.call-start = ((), (), s32[]{:S(2)}) async-start(), calls=%async_computation.7 | async-start | bytes 8650752 | tf_op jit(solution)/shard_map/all_gather | solution.py:146
  10.0 670.8 %reduce-scatter.7.cloned.1.call-start = ((), (), s32[]{:S(2)}) async-start(), calls=%async_computation.9 | async-start | bytes 4325376 | tf_op jit(solution)/shard_map/reduce_scatter | solution.py:255
  60.4 76.7 %copy-start.32 = (f32[1024]{0:T(1024)}, f32[1024]{0:T(1024)S(1)}, u32[]{:S(2)}) copy-start(f32[1024]{0:T(1024)S(1)} %convert_element_type.137) | copy-start | bytes 12292
  60.4 196.5 %copy-start.45 = (f32[1024]{0:T(1024)}, f32[1024]{0:T(1024)S(1)}, u32[]{:S(2)}) copy-start(f32[1024]{0:T(1024)S(1)} %convert_element_type.151) | copy-start | bytes 12292
  60.5 76.7 %copy-start.37 = (f32[1024]{0:T(1024)}, f32[1024]{0:T(1024)S(1)}, u32[]{:S(2)}) copy-start(f32[1024]{0:T(1024)S(1)} %convert_element_type.138) | copy-start | bytes 12292
  60.5 196.5 %copy-start.58 = (f32[1024]{0:T(1024)}, f32[1024]{0:T(1024)S(1)}, u32[]{:S(2)}) copy-start(f32[1024]{0:T(1024)S(1)} %convert_element_type.152) | copy-start | bytes 12292
  130.7 117.2 %copy-start.1 = (bf16[1024,1024]{0,1:T(8,128)(2,1)}, bf16[1024,1024]{0,1:T(8,128)(2,1)S(1)}, u32[]{:S(2)}) copy-start(bf16[1024,1024]{0,1:T(8,128)(2,1)S(1)} %copy.76) | copy-start | bytes 6291460
  131.1 17.1 %copy-start.30 = (f32[1024]{0:T(1024)}, f32[1024]{0:T(1024)S(1)}, u32[]{:S(2)}) copy-start(f32[1024]{0:T(1024)S(1)} %broadcast_multiply_fusion.1) | copy-start | bytes 12292
  131.7 16.5 %copy-start.49 = (f32[1024]{0:T(1024)}, f32[1024]{0:T(1024)S(1)}, u32[]{:S(2)}) copy-start(f32[1024]{0:T(1024)S(1)} %fusion.27) | copy-start | bytes 12292
  131.7 16.5 %copy-start.35 = (f32[1024]{0:T(1024)}, f32[1024]{0:T(1024)S(1)}, u32[]{:S(2)}) copy-start(f32[1024]{0:T(1024)S(1)} %fusion.50) | copy-start | bytes 12292
  166.7 27.9 %copy-start.10 = (bf16[512,1024]{0,1:T(8,128)(2,1)}, bf16[512,1024]{0,1:T(8,128)(2,1)S(1)}, u32[]{:S(2)}) copy-start(bf16[512,1024]{0,1:T(8,128)(2,1)S(1)} %copy.82) | copy-start | bytes 3145732
  253.1 20.9 %copy-start.41 = (f32[1024]{0:T(1024)}, f32[1024]{0:T(1024)S(1)}, u32[]{:S(2)}) copy-start(f32[1024]{0:T(1024)S(1)} %broadcast_multiply_fusion) | copy-start | bytes 12292
  255.7 18.4 %copy-start.51 = (f32[1024]{0:T(1024)}, f32[1024]{0:T(1024)S(1)}, u32[]{:S(2)}) copy-start(f32[1024]{0:T(1024)S(1)} %multiply_reduce_fusion.4) | copy-start | bytes 12292
  255.7 18.3 %copy-start.47 = (f32[1024]{0:T(1024)}, f32[1024]{0:T(1024)S(1)}, u32[]{:S(2)}) copy-start(f32[1024]{0:T(1024)S(1)} %fusion.51) | copy-start | bytes 12292
  256.9 42.6 %copy-start.26 = (bf16[1024,1024]{1,0:T(8,128)(2,1)S(1)}, bf16[1024,1024]{1,0:T(8,128)(2,1)}, u32[]{:S(2)}) copy-start(bf16[1024,1024]{1,0:T(8,128)(2,1)} %param.45) | copy-start | bytes 6291460
  256.9 42.6 %copy-start.39 = (f32[32,1,128]{2,1,0:T(1,128)S(1)}, f32[32,1,128]{2,1,0:T(1,128)}, u32[]{:S(2)}) copy-start(f32[32,1,128]{2,1,0:T(1,128)} %convert_element_type.177) | copy-start | bytes 49156
  299.6 51.7 %copy-start.61 = (bf16[1024,4096]{1,0:T(8,128)(2,1)S(1)}, bf16[1024,4096]{1,0:T(8,128)(2,1)}, u32[]{:S(2)}) copy-start(bf16[1024,4096]{1,0:T(8,128)(2,1)} %all-gather.10.cloned.1.call-done) | copy-start | bytes 25165828
  386.5 307.8 %reduce-scatter.5.cloned.1.call-start = ((), (), s32[]{:S(2)}) async-start(), calls=%async_computation.8 | async-start | bytes 12976128 | tf_op jit(solution)/shard_map/reduce_scatter | solution.py:252
  449.3 15.6 %copy-start.14 = (bf16[512,1024]{0,1:T(8,128)(2,1)S(1)}, bf16[512,1024]{0,1:T(8,128)(2,1)}, u32[]{:S(2)}) copy-start(bf16[512,1024]{0,1:T(8,128)(2,1)} %copy.79) | copy-start | bytes 3145732
  482.1 17.7 %slice-start = ((s8[16777216]{0:T(1024)(128)(4,1)}), s8[4194304]{0:T(1024)(128)(4,1)S(1)}, s32[]{:S(2)}) async-start(s8[16777216]{0:T(1024)(128)(4,1)} %bitcast.76), calls=%async_computation.12 | async-start | bytes 8388608
  482.1 17.7 %slice-start.1 = ((s8[16777216]{0:T(1024)(128)(4,1)}), s8[4194304]{0:T(1024)(128)(4,1)S(1)}, s32[]{:S(2)}) async-start(s8[16777216]{0:T(1024)(128)(4,1)} %bitcast.76), calls=%async_computation.13 | async-start | bytes 8388608
  505.9 15.9 %copy-start.2 = (bf16[1024,1024]{0,1:T(8,128)(2,1)S(1)}, bf16[1024,1024]{0,1:T(8,128)(2,1)}, u32[]{:S(2)}) copy-start(bf16[1024,1024]{0,1:T(8,128)(2,1)} %copy-done.1) | copy-start | bytes 6291460
  505.9 15.9 %copy-start.31 = (f32[1024]{0:T(1024)S(1)}, f32[1024]{0:T(1024)}, u32[]{:S(2)}) copy-start(f32[1024]{0:T(1024)} %copy-done.30) | copy-start | bytes 12292
  505.9 15.9 %copy-start.33 = (f32[1024]{0:T(1024)S(1)}, f32[1024]{0:T(1024)}, u32[]{:S(2)}) copy-start(f32[1024]{0:T(1024)} %copy-done.32) | copy-start | bytes 12292
  505.9 16.0 %copy-start.36 = (f32[1024]{0:T(1024)S(1)}, f32[1024]{0:T(1024)}, u32[]{:S(2)}) copy-start(f32[1024]{0:T(1024)} %copy-done.35) | copy-start | bytes 12292
  505.9 16.0 %copy-start.38 = (f32[1024]{0:T(1024)S(1)}, f32[1024]{0:T(1024)}, u32[]{:S(2)}) copy-start(f32[1024]{0:T(1024)} %copy-done.37) | copy-start | bytes 12292
  536.1 524.6 %reduce-scatter.9.cloned.1.call-start = ((), (), s32[]{:S(2)}) async-start(), calls=%async_computation.10 | async-start | bytes 17301504 | tf_op jit(solution)/shard_map/reduce_scatter | solution.py:259
  553.5 872.4 %reduce-scatter.11.cloned.1.call-start = ((), (), s32[]{:S(2)}) async-start(), calls=%async_computation.11 | async-start | bytes 17301504 | tf_op jit(solution)/shard_map/reduce_scatter | solution.py:261
  554.1 17.6 %copy-start.27 = (bf16[1024,1024]{1,0:T(8,128)(2,1)S(1)}, bf16[1024,1024]{1,0:T(8,128)(2,1)}, u32[]{:S(2)}) copy-start(bf16[1024,1024]{1,0:T(8,128)(2,1)} %param.45) | copy-start | bytes 6291460
  (43 other events, 221.0 us)
Sparse Core Ops, SparseCore 0:
  10.9 72.2 all-gather.5
  86.1 55.2 all-gather.7
  144.3 76.2 all-gather.9
  223.4 76.0 all-gather.11
  386.7 146.5 reduce-scatter.6
  539.7 154.6 reduce-scatter.4
  697.3 363.2 reduce-scatter.8
  1063.6 362.1 reduce-scatter.10
where the time goes:
time: 1440 us; the launch traced here: 1430 us
  waiting for transfers between devices  773 us (54%)
  matrix products  308 us (21%)
  blocking collectives  150 us (10%)
  other arithmetic  107 us (7%)
  local copies, waits for them, and re-layouts  78.1 us (5%)
  between operations  16.5 us (1%)
    reduce_scatter x1, waiting for transfers between devices, body(): lax.psum_scatter(up_grad, ('dp', 'fsdp'), scatter_dimension=0, tiled=True)  366 us
    reduce_scatter x1, waiting for transfers between devices, body(): lax.psum_scatter(down_grad, ('dp', 'fsdp'), scatter_dimension=0, tiled=True)  365 us
    unnamed x2, blocking collectives  83.2 us
    dot_general x4, matrix products, right_product(): lax.dot_general(first, second, (((1,), (1,)), ((), ())), preferred_elemen...  78.8 us
    all_gather x1, blocking collectives, body(): lax.all_gather(up_bias, ('dp', 'fsdp'), axis=0, tiled=True)  66.7 us
    dot_general x4, matrix products, left_product(): lax.dot_general(first, second, (((0,), (0,)), ((), ())), preferred_elemen...  46.8 us
    unnamed x163, local copies, waits for them, and re-layouts  43 us
    convert_element_type x2, other arithmetic, attend_backward(): d_scores = (probability * (d_probs - inner)).astype(jnp.bfloat16)  40.2 us
  transfers between devices with their start and end apart: 8, of which 4 were waited for; matrix products, arithmetic and copies ran while one was open for 27% of the time, Pallas kernels for 0%

commit v1 on v0

v1 whole, which is shorter than its diff:
```python
import functools, math
import jax, jax.numpy as jnp
from jax import lax
from jax.sharding import PartitionSpec as P
from jax.experimental import pallas as pl
from jax.experimental.pallas import tpu as pltpu
HEADS=16
EPSILON = 1e-05
NEGATIVE = -1000000000.0
bf16=jnp.bfloat16; f32=jnp.float32
VMEM_LIMIT=60*1024*1024
def cp(n=1): return pltpu.CompilerParams(dimension_semantics=("arbitrary",)*n, vmem_limit_bytes=VMEM_LIMIT)
def dot(a,b): return lax.dot_general(a,b,(((1,),(0,)),((),())),preferred_element_type=f32)
def dot_nt(a,b): return lax.dot_general(a,b,(((1,),(1,)),((),())),preferred_element_type=f32)
def dot_tn(a,b): return lax.dot_general(a,b,(((0,),(0,)),((),())),preferred_element_type=f32)

def project_kernel(tokens_ref, gain_ref, shift_ref, weight_ref, bias_ref, normed_ref, out_ref, low_ref):
    step = pl.program_id(0)
    @pl.when(step == 0)
    def _():
        x = tokens_ref[...].astype(f32)
        center = x - jnp.mean(x, axis=-1, keepdims=True)
        spread = jnp.mean(center * center, axis=-1, keepdims=True)
        normed = center * lax.rsqrt(spread + EPSILON) * gain_ref[...].astype(f32) + shift_ref[...].astype(f32)
        low_ref[...] = normed.astype(bf16)
        normed_ref[...] = normed.astype(bf16)
    tn = out_ref.shape[1]
    third = pl.num_programs(0) // 3
    factor = jnp.where(step < third, 0.125, 1.0)
    out = dot(low_ref[...], weight_ref[...]) + bias_ref[...].astype(f32)
    out_ref[...] = (out * factor).astype(bf16)

def project(tokens, gain, shift, weight, bias, tn=512):
    R, D = tokens.shape
    N = weight.shape[1]
    full = pl.BlockSpec((R, D), lambda j: (0, 0))
    row = pl.BlockSpec((1, D), lambda j: (0, 0))
    return pl.pallas_call(
        project_kernel, grid=(N // tn,),
        in_specs=[full, row, row, pl.BlockSpec((D, tn), lambda j: (0, j)), pl.BlockSpec((1, tn), lambda j: (0, j))],
        out_specs=[full, pl.BlockSpec((R, tn), lambda j: (0, j))],
        out_shape=[jax.ShapeDtypeStruct((R, D), bf16), jax.ShapeDtypeStruct((R, N), bf16)],
        scratch_shapes=[pltpu.VMEM((R, D), bf16)],
        compiler_params=cp(), name="project",
        cost_estimate=pl.CostEstimate(flops=2*R*D*N, bytes_accessed=2*(D*N+R*N+2*R*D), transcendentals=0),
    )(tokens, gain, shift, weight, bias)

def mask_rows(start, bq, lo, hi, prefix, limit):
    q = start + lax.broadcasted_iota(jnp.int32, (bq, hi - lo), 0)
    k = lo + lax.broadcasted_iota(jnp.int32, (bq, hi - lo), 1)
    return ((k < prefix) | (k <= q)) & (k < limit)

def attend_kernel(prefix_ref, padding_ref, q_ref, k_ref, v_ref, out_ref, lse_ref, stat_ref, *, bq):
    L = q_ref.shape[0]
    step = pl.program_id(0)
    prefix = prefix_ref[0]
    limit = L - padding_ref[0]
    lane = lax.broadcasted_iota(jnp.int32, (1, 128), 1)
    stat_lane = lax.broadcasted_iota(jnp.int32, (bq, 128), 1)
    @pl.when(step == 0)
    def _():
        stat_ref[...] = jnp.zeros_like(stat_ref)
    for start in range(0, L, bq):
        stop = start + bq
        parts = []
        stat = stat_ref[start:stop, :]
        for half in range(2):
            mine = (lane < 64) if half == 0 else (lane >= 64)
            q = jnp.where(mine, q_ref[start:stop, :], 0).astype(bf16)
            s = dot_nt(q, k_ref[:stop, :])
            s = jnp.where(mask_rows(start, bq, 0, stop, prefix, limit), s, NEGATIVE)
            m = jnp.max(s, axis=-1, keepdims=True)
            e = jnp.exp(s - m)
            t = jnp.sum(e, axis=-1, keepdims=True)
            p = (e * (1.0 / t)).astype(bf16)
            parts.append(dot(p, v_ref[:stop, :]))
            stat = jnp.where(stat_lane == 2 * step + half, m + jnp.log(t), stat)
        stat_ref[start:stop, :] = stat
        out_ref[start:stop, :] = jnp.where(lane < 64, parts[0], parts[1]).astype(bf16)
    @pl.when(step == pl.num_programs(0) - 1)
    def _():
        lse_ref[...] = jnp.transpose(stat_ref[...])

def attend(prefix, padding, qkv, bq=256):
    L = qkv.shape[0]
    D = qkv.shape[1] // 3
    n = D // 128
    smem = pl.BlockSpec(memory_space=pltpu.SMEM)
    col = lambda off: pl.BlockSpec((L, 128), lambda j: (0, j + off))
    return pl.pallas_call(
        functools.partial(attend_kernel, bq=bq), grid=(n,),
        in_specs=[smem, smem, col(0), col(n), col(2 * n)],
        out_specs=[col(0), pl.BlockSpec((128, L), lambda j: (0, 0))],
        out_shape=[jax.ShapeDtypeStruct((L, D), bf16), jax.ShapeDtypeStruct((128, L), f32)],
        scratch_shapes=[pltpu.VMEM((L, 128), f32)],
        compiler_params=cp(), name="attend",
        cost_estimate=pl.CostEstimate(flops=4*L*L*D, bytes_accessed=8*L*D, transcendentals=L*L*n),
    )(prefix, padding, qkv, qkv, qkv)

def branch_kernel(ctx_ref, weight_ref, tokens_ref, bias_ref, gain_ref, shift_ref, resid_ref, normed_ref):
    resid = tokens_ref[...].astype(f32) + (dot(ctx_ref[...], weight_ref[...]) + bias_ref[...].astype(f32))
    center = resid - jnp.mean(resid, axis=-1, keepdims=True)
    spread = jnp.mean(center * center, axis=-1, keepdims=True)
    normed = center * lax.rsqrt(spread + EPSILON) * gain_ref[...].astype(f32) + shift_ref[...].astype(f32)
    resid_ref[...] = resid
    normed_ref[...] = normed.astype(bf16)

def branch(ctx, weight, tokens, bias, gain, shift, tm=256):
    R, D = ctx.shape
    rows = pl.BlockSpec((tm, D), lambda i: (i, 0))
    vec = pl.BlockSpec((1, D), lambda i: (0, 0))
    return pl.pallas_call(
        branch_kernel, grid=(R // tm,),
        in_specs=[rows, pl.BlockSpec((D, D), lambda i: (0, 0)), rows, vec, vec, vec],
        out_specs=[rows, rows],
        out_shape=[jax.ShapeDtypeStruct((R, D), f32), jax.ShapeDtypeStruct((R, D), bf16)],
        compiler_params=cp(), name="branch",
        cost_estimate=pl.CostEstimate(flops=2*R*D*D, bytes_accessed=2*D*D+10*R*D, transcendentals=0),
    )(ctx, weight, tokens, bias, gain, shift)

def ffn_kernel(normed_ref, grad_ref, up_ref, bias_ref, down_ref, out_ref, dn_ref, upg_ref, downg_ref, biasg_ref, *, tr):
    step = pl.program_id(0)
    R = normed_ref.shape[0]
    n2 = normed_ref[...]
    go = grad_ref[...]
    up = up_ref[...]
    down = down_ref[...]
    u = dot(n2, up) + bias_ref[...].astype(f32)
    cdf = 0.5 * (1.0 + lax.erf(u * math.sqrt(0.5)))
    a = (u * cdf).astype(bf16)
    slope = cdf + u * (jnp.exp(-0.5 * u * u) * (1.0 / math.sqrt(2 * math.pi)))
    da = dot_nt(go, down)
    du32 = da * slope
    du = du32.astype(bf16)
    @pl.when(step == 0)
    def _():
        out_ref[...] = jnp.zeros_like(out_ref)
        dn_ref[...] = jnp.zeros_like(dn_ref)
    out_ref[...] += dot(a, down)
    dn_ref[...] += dot_nt(du, up)
    upg_ref[...] = dot_tn(n2, du).astype(bf16)
    downg_ref[...] = dot_tn(a, go).astype(bf16)
    biasg_ref[...] = jnp.sum(du.astype(f32), axis=0, keepdims=True)

def ffn(normed, grad, up, bias, down, tf=512):
    R, D = normed.shape
    F = up.shape[1]
    full = pl.BlockSpec((R, D), lambda j: (0, 0))
    return pl.pallas_call(
        functools.partial(ffn_kernel, tr=R), grid=(F // tf,),
        in_specs=[full, full, pl.BlockSpec((D, tf), lambda j: (0, j)), pl.BlockSpec((1, tf), lambda j: (0, j)), pl.BlockSpec((tf, D), lambda j: (j, 0))],
        out_specs=[full, full, pl.BlockSpec((D, tf), lambda j: (0, j)), pl.BlockSpec((tf, D), lambda j: (j, 0)), pl.BlockSpec((1, tf), lambda j: (0, j))],
        out_shape=[jax.ShapeDtypeStruct((R, D), f32), jax.ShapeDtypeStruct((R, D), f32), jax.ShapeDtypeStruct((D, F), bf16), jax.ShapeDtypeStruct((F, D), bf16), jax.ShapeDtypeStruct((1, F), f32)],
        compiler_params=cp(), name="ffn",
        cost_estimate=pl.CostEstimate(flops=12*R*D*F, bytes_accessed=8*D*F+12*R*D, transcendentals=2*R*F),
    )(normed, grad, up, bias, down)

def middle_kernel(resid_ref, outacc_ref, dn_ref, go_ref, gain_ref, dbias_ref, weight_ref, ctx_ref,
                  out_ref, dres_ref, dctx_ref, wg_ref, small_ref, low_ref):
    i = pl.program_id(0)
    tm = resid_ref.shape[0]
    resid = resid_ref[...]
    out_ref[...] = (resid + outacc_ref[...] + dbias_ref[...].astype(f32)).astype(bf16)
    center = resid - jnp.mean(resid, axis=-1, keepdims=True)
    spread = jnp.mean(center * center, axis=-1, keepdims=True)
    r = lax.rsqrt(spread + EPSILON)
    nhat = center * r
    dn = dn_ref[...]
    go = go_ref[...].astype(f32)
    e = dn * gain_ref[...].astype(f32)
    d_res = go + r * (e - jnp.mean(e, axis=-1, keepdims=True) - nhat * jnp.mean(e * nhat, axis=-1, keepdims=True))
    dres_ref[...] = d_res
    low = d_res.astype(bf16)
    low_ref[pl.ds(i * tm, tm), :] = low
    dctx_ref[...] = dot_nt(low, weight_ref[...]).astype(bf16)
    @pl.when(i == 0)
    def _():
        small_ref[...] = jnp.zeros_like(small_ref)
    small_ref[0:1, :] += jnp.sum(dn * nhat, axis=0, keepdims=True)
    small_ref[1:2, :] += jnp.sum(dn, axis=0, keepdims=True)
    small_ref[2:3, :] += jnp.sum(low.astype(f32), axis=0, keepdims=True)
    small_ref[3:4, :] += jnp.sum(go, axis=0, keepdims=True)
    @pl.when(i == pl.num_programs(0) - 1)
    def _():
        wg_ref[...] = dot_tn(ctx_ref[...], low_ref[...]).astype(bf16)

def middle(resid, outacc, dn, go, gain, dbias, weight, ctx, tm=256):
    R, D = resid.shape
    rows = pl.BlockSpec((tm, D), lambda i: (i, 0))
    vec = pl.BlockSpec((1, D), lambda i: (0, 0))
    sq = pl.BlockSpec((D, D), lambda i: (0, 0))
    full = pl.BlockSpec((R, D), lambda i: (0, 0))
    return pl.pallas_call(
        middle_kernel, grid=(R // tm,),
        in_specs=[rows, rows, rows, rows, vec, vec, sq, full],
        out_specs=[rows, rows, rows, sq, pl.BlockSpec((8, D), lambda i: (0, 0))],
        out_shape=[jax.ShapeDtypeStruct((R, D), bf16), jax.ShapeDtypeStruct((R, D), f32), jax.ShapeDtypeStruct((R, D), bf16),
                   jax.ShapeDtypeStruct((D, D), bf16), jax.ShapeDtypeStruct((8, D), f32)],
        scratch_shapes=[pltpu.VMEM((R, D), bf16)],
        compiler_params=cp(), name="middle",
        cost_estimate=pl.CostEstimate(flops=4*R*D*D, bytes_accessed=4*D*D+26*R*D, transcendentals=0),
    )(resid, outacc, dn, go, gain, dbias, weight, ctx)

def attend_back_kernel(prefix_ref, padding_ref, q_ref, k_ref, v_ref, do_ref, lse_ref, dq_ref, dk_ref, dv_ref, small_ref, dka_ref, dva_ref, *, bq):
    L = q_ref.shape[0]
    step = pl.program_id(0)
    prefix = prefix_ref[0]
    limit = L - padding_ref[0]
    lane = lax.broadcasted_iota(jnp.int32, (1, 128), 1)
    dka_ref[...] = jnp.zeros_like(dka_ref)
    dva_ref[...] = jnp.zeros_like(dva_ref)
    kT = jnp.transpose(k_ref[...])
    for start in range(0, L, bq):
        stop = start + bq
        dqT = []
        for half in range(2):
            mine = (lane < 64) if half == 0 else (lane >= 64)
            q = jnp.where(mine, q_ref[start:stop, :], 0).astype(bf16)
            do = jnp.where(mine, do_ref[start:stop, :], 0).astype(bf16)
            s = dot_nt(k_ref[:stop, :], q)
            kk = lax.broadcasted_iota(jnp.int32, (stop, bq), 0)
            qq = start + lax.broadcasted_iota(jnp.int32, (stop, bq), 1)
            ok = ((kk < prefix) | (kk <= qq)) & (kk < limit)
            lse = lse_ref[pl.ds(2 * step + half, 1), start:stop]
            p = jnp.where(ok, jnp.exp(s - lse), 0.0)
            dp = dot_nt(v_ref[:stop, :], do)
            inner = jnp.sum(p * dp, axis=0, keepdims=True)
            ds = (p * (dp - inner)).astype(bf16)
            dva_ref[:stop, :] += dot(p.astype(bf16), do)
            dka_ref[:stop, :] += dot(ds, q)
            dqT.append(dot(kT[64 * half:64 * half + 64, :stop], ds))
        dq = jnp.transpose(jnp.concatenate(dqT, axis=0)) * 0.125
        dq_ref[start:stop, :] = dq.astype(bf16)
    dk_ref[...] = dka_ref[...].astype(bf16)
    dv_ref[...] = dva_ref[...].astype(bf16)
    small_ref[0:1, :] = jnp.sum(dq_ref[...].astype(f32), axis=0, keepdims=True)
    small_ref[1:2, :] = jnp.sum(dv_ref[...].astype(f32), axis=0, keepdims=True)

def attend_back(prefix, padding, qkv, dctx, lse, bq=256):
    L = qkv.shape[0]
    D = dctx.shape[1]
    n = D // 128
    smem = pl.BlockSpec(memory_space=pltpu.SMEM)
    col = lambda off: pl.BlockSpec((L, 128), lambda j: (0, j + off))
    o = jax.ShapeDtypeStruct((L, D), bf16)
    return pl.pallas_call(
        functools.partial(attend_back_kernel, bq=bq), grid=(n,),
        in_specs=[smem, smem, col(0), col(n), col(2 * n), col(0), pl.BlockSpec((128, L), lambda j: (0, 0))],
        out_specs=[col(0), col(0), col(0), pl.BlockSpec((8, 128), lambda j: (0, j))],
        out_shape=[o, o, o, jax.ShapeDtypeStruct((8, D), f32)],
        scratch_shapes=[pltpu.VMEM((L, 128), f32), pltpu.VMEM((L, 128), f32)],
        compiler_params=cp(), name="attend_back",
        cost_estimate=pl.CostEstimate(flops=10*L*L*D, bytes_accessed=14*L*D, transcendentals=L*L*n),
    )(prefix, padding, qkv, qkv, qkv, dctx, lse)

def inproj_grad_kernel(n_ref, d_ref, o_ref):
    o_ref[...] = dot_tn(n_ref[...], d_ref[...]).astype(bf16)

def inproj_grad(n1, d, tn=256):
    R, D = n1.shape
    N = d.shape[1]
    return pl.pallas_call(
        inproj_grad_kernel, grid=(N // tn,),
        in_specs=[pl.BlockSpec((R, D), lambda j: (0, 0)), pl.BlockSpec((R, tn), lambda j: (0, j))],
        out_specs=pl.BlockSpec((D, tn), lambda j: (0, j)),
        out_shape=jax.ShapeDtypeStruct((D, N), bf16),
        compiler_params=cp(), name="inproj_grad",
        cost_estimate=pl.CostEstimate(flops=2*R*D*N, bytes_accessed=2*(D*N+R*N+R*D), transcendentals=0),
    )(n1, d)

def last_kernel(dq_ref, dk_ref, dv_ref, w_ref, tokens_ref, dres_ref, gain_ref, out_ref, small_ref):
    i = pl.program_id(0)
    D = tokens_ref.shape[1]
    dn = dot_nt(dq_ref[...], w_ref[:, :D]) + dot_nt(dk_ref[...], w_ref[:, D:2*D]) + dot_nt(dv_ref[...], w_ref[:, 2*D:])
    x = tokens_ref[...].astype(f32)
    center = x - jnp.mean(x, axis=-1, keepdims=True)
    spread = jnp.mean(center * center, axis=-1, keepdims=True)
    r = lax.rsqrt(spread + EPSILON)
    nhat = center * r
    e = dn * gain_ref[...].astype(f32)
    d = dres_ref[...] + r * (e - jnp.mean(e, axis=-1, keepdims=True) - nhat * jnp.mean(e * nhat, axis=-1, keepdims=True))
    out_ref[...] = d.astype(bf16)
    @pl.when(i == 0)
    def _():
        small_ref[...] = jnp.zeros_like(small_ref)
    small_ref[0:1, :] += jnp.sum(dn * nhat, axis=0, keepdims=True)
    small_ref[1:2, :] += jnp.sum(dn, axis=0, keepdims=True)

def last(dq, dk, dv, w, tokens, dres, gain, tm=256):
    R, D = tokens.shape
    rows = pl.BlockSpec((tm, D), lambda i: (i, 0))
    return pl.pallas_call(
        last_kernel, grid=(R // tm,),
        in_specs=[rows, rows, rows, pl.BlockSpec((D, 3 * D), lambda i: (0, 0)), rows, rows, pl.BlockSpec((1, D), lambda i: (0, 0))],
        out_specs=[rows, pl.BlockSpec((8, D), lambda i: (0, 0))],
        out_shape=[jax.ShapeDtypeStruct((R, D), bf16), jax.ShapeDtypeStruct((8, D), f32)],
        compiler_params=cp(), name="last",
        cost_estimate=pl.CostEstimate(flops=6*R*D*D, bytes_accessed=6*D*D+14*R*D, transcendentals=0),
    )(dq, dk, dv, w, tokens, dres, gain)


def own_index(axes):
    return lax.axis_index(axes)

def swap_stages(sizes):
    total = math.prod(sizes)
    return [total >> (b + 1) for b in range(total.bit_length() - 1)]

def gather_small(buf, axes, total):
    me = lax.axis_index(axes)
    stride = 1
    while stride < total:
        pairs = [(i, i ^ stride) for i in range(total)]
        other = lax.ppermute(buf, axes, pairs)
        low = (me & stride) == 0
        buf = jnp.where(low, jnp.concatenate([buf, other]), jnp.concatenate([other, buf]))
        stride *= 2
    return buf

def scatter_small(buf, axes, total):
    me = lax.axis_index(axes)
    stride = total // 2
    while stride:
        pairs = [(i, i ^ stride) for i in range(total)]
        low = (me & stride) == 0
        lower, upper = buf[:stride], buf[stride:]
        other = lax.ppermute(jnp.where(low, upper, lower), axes, pairs)
        buf = jnp.where(low, lower, upper) + other
        stride //= 2
    return buf

def body(plan, tokens, prefix_len, padding_len, first_gain, first_shift, inproj_weight, query_bias, value_bias,
         outproj_weight, outproj_bias, second_gain, second_shift, up_weight, up_bias, down_weight, down_bias, grad_out):
    axes, sizes, core, yx, z = plan
    total = math.prod(sizes)
    R, D = tokens.shape
    gather = lambda w: lax.all_gather(w, axes, axis=0, tiled=True)
    small = jnp.concatenate([first_gain, first_shift, query_bias, value_bias, outproj_bias, second_gain, second_shift, down_bias, up_bias])
    n = first_gain.shape[0]
    small = gather_small(small[None], axes, total)
    vec = lambda i: small[:, i * n:(i + 1) * n].reshape(1, D)
    gain1, shift1, qbias, vbias, obias, gain2, shift2, dbias = [vec(i) for i in range(8)]
    ubias = small[:, 8 * n:].reshape(1, -1)
    w_in = gather(inproj_weight)
    w_out = gather(outproj_weight)
    w_up = gather(up_weight)
    w_down = gather(down_weight)
    bias = jnp.concatenate([qbias, jnp.zeros_like(qbias), vbias], axis=1)
    n1, qkv = project(tokens, gain1, shift1, w_in, bias)
    ctx, lse = attend(prefix_len, padding_len, qkv)
    resid, n2 = branch(ctx, w_out, tokens, obias, gain2, shift2)
    acc, dn2, up_g, down_g, ubias_g = ffn(n2, grad_out, w_up, ubias, w_down)
    out, dres, dctx, out_g, mid = middle(resid, acc, dn2, grad_out, gain2, dbias, w_out, ctx)
    dq, dk, dv, att = attend_back(prefix_len, padding_len, qkv, dctx, lse)
    in_g = jnp.concatenate([inproj_grad(n1, d) for d in (dq, dk, dv)], axis=1)
    tokens_grad, end = last(dq, dk, dv, w_in, tokens, dres, gain1)

    def scatter(g):
        rows = g.shape[0] // total
        cols = g.shape[1]
        if core:
            outer = math.prod(sizes[:sizes_index(axes, core)])
            inner = total // 2 // outer
            g = g.reshape(outer, 2, inner * rows * cols // 1024, 1024).transpose(1, 0, 2, 3)
            g = lax.psum_scatter(g, core, scatter_dimension=0, tiled=True)
            g = g.reshape(total // 2 * rows, cols)
            g = lax.psum_scatter(g, yx, scatter_dimension=0, tiled=True)
            g = lax.psum_scatter(g, z, scatter_dimension=0, tiled=True)
        else:
            g = lax.psum_scatter(g, axes, scatter_dimension=0, tiled=True)
        return g.astype(f32)
    down_grad, up_grad, out_grad, in_grad = scatter(down_g), scatter(up_g), scatter(out_g), scatter(in_g)
    rows8 = lambda *v: jnp.concatenate([a.reshape(total, -1) for a in v], axis=1)
    early = scatter_small(rows8(att[0], att[1], mid[2], mid[0], mid[1], mid[3], ubias_g[0]), axes, total)[0]
    late = scatter_small(rows8(end[0], end[1]), axes, total)[0]
    e = [early[i * n:(i + 1) * n] for i in range(6)]
    return (out, tokens_grad, late[:n], late[n:], in_grad, e[0], e[1], out_grad, e[2], e[3], e[4], up_grad, early[6 * n:], down_grad, e[5])

def sizes_index(axes, name):
    return axes.index(name)

def solution(mesh):
    shape = dict(mesh.shape)
    if shape == {"dp": 8, "fsdp": 4}:
        mesh = jax.sharding.Mesh(mesh.devices.reshape(2, 2, 2, 4), ("y", "x", "core", "fsdp"))
        plan = (("y", "x", "core", "fsdp"), (2, 2, 2, 4), "core", ("y", "x"), "fsdp")
    else:
        plan = (("dp", "fsdp"), tuple(mesh.shape[a] for a in ("dp", "fsdp")), None, None, None)
    axes = plan[0]
    rows, flat = P(axes, None), P(axes)
    ins = (rows, flat, flat, flat, flat, rows, flat, flat, rows, flat, flat, flat, rows, flat, rows, flat, rows)
    outs = (rows, rows, flat, flat, rows, flat, flat, rows, flat, flat, flat, rows, flat, rows, flat)
    return jax.shard_map(functools.partial(body, plan), mesh=mesh, in_specs=ins, out_specs=outs, check_vma=False)
```

time: 1440 us -> 851 us (0.59)
  matrix products: 308 us -> 0 us
  waiting for transfers between devices: 773 us -> 522 us
  Pallas kernels: 0 us -> 209 us
  blocking collectives: 150 us -> 0 us
  other arithmetic: 107 us -> 13.1 us
  starting transfers between devices: 0.32 us -> 23.4 us
    reduce_scatter x4 -> x8, waiting for transfers between devices: 745 us -> 221 us  [the longest x4 134 us: scatter(): g = lax.psum_scatter(g, yx, scatter_dimension=0, tiled=True)]
    dot_general x24 -> x0, matrix products: 308 us -> none  [the longest x4 78.8 us: right_product(): lax.dot_general(first, second, (((1,), (1,)), ((), ())), preferred_elemen...]
    pallas_call x0 -> x10, Pallas kernels: none -> 209 us  [the longest x1 59.6 us: ffn(): pl.pallas_call(functools.partial(ffn_kernel, tr=R), grid=(F // tf,), in_s...]
    all_gather x4, waiting for transfers between devices: 25.5 us -> 203 us  [body(): gather = lambda w: lax.all_gather(w, axes, axis=0, tiled=True)]
    unnamed x2 -> x0, blocking collectives: 83.2 us -> none
    unnamed x8 -> x14, waiting for transfers between devices: 2.65 us -> 81.8 us
    all_gather x1 -> x0, blocking collectives: 66.7 us -> none  [body(): lax.all_gather(up_bias, ('dp', 'fsdp'), axis=0, tiled=True)]
    convert_element_type x13 -> x4, other arithmetic: 57.7 us -> 6.77 us  [scatter(): return g.astype(f32)]
  transfers between devices with their start and end apart: 8 -> 28, of which waited for: 4 -> 23; matrix products, arithmetic and copies ran while one was open for 27% -> 5% of each run, Pallas kernels for 0% -> 8%
where the time goes in v1:
time: 851 us; the launch traced here: 850 us
  waiting for transfers between devices  522 us (61%)
  Pallas kernels  209 us (25%)
  local copies, waits for them, and re-layouts  67 us (8%)
  starting transfers between devices  23.4 us (3%)
  between operations  15.5 us (2%)
  other arithmetic  13.1 us (2%)
    all_gather x4, waiting for transfers between devices, body(): gather = lambda w: lax.all_gather(w, axes, axis=0, tiled=True)  203 us
    reduce_scatter x4, waiting for transfers between devices, scatter(): g = lax.psum_scatter(g, yx, scatter_dimension=0, tiled=True)  134 us
    reduce_scatter x4, waiting for transfers between devices, scatter(): g = lax.psum_scatter(g, z, scatter_dimension=0, tiled=True)  86.5 us
    unnamed x14, waiting for transfers between devices  81.8 us
    pallas_call x1, Pallas kernels, ffn(): pl.pallas_call(functools.partial(ffn_kernel, tr=R), grid=(F // tf,), in_s...  59.6 us
    pallas_call x1, Pallas kernels, attend_back(): pl.pallas_call(functools.partial(attend_back_kernel, bq=bq), grid=(n,), i...  43 us
    pallas_call x1, Pallas kernels, attend(): pl.pallas_call(functools.partial(attend_kernel, bq=bq), grid=(n,), in_spe...  36 us
    reshape x2, local copies, waits for them, and re-layouts, scatter(): g.reshape(outer, 2, inner * rows * cols // 1024, 1024).transpose(1, 0, 2, 3)  24.4 us
  transfers between devices with their start and end apart: 28, of which 23 were waited for; matrix products, arithmetic and copies ran while one was open for 5% of the time, Pallas kernels for 8%

profile of v1, /device:TPU:0, one launch (start us, length us, event | category | flops | bytes accessed | tf_op | source)
XLA Modules:
  0.0 849.6 jit_solution(17252438114577320936)
XLA Ops:
  10.0 6.1 concatenate.45
  16.1 3.1 collective-permute-start
  20.8 3.1 collective-permute-start.1
  39.7 43.5 %all-gather.5.cloned.1.call-done.weight_ref.w_ref = bf16[1024,3072]{1,0:T(8,128)(2,1)} async-done(((bf16[32,3072]{1,0:T(8,128)(2,1)}), bf16[1024,3072]{1,0:T(8,128)(2,1)}) %all-gather.5.cloned.1.call-update) | async-done | bytes 6291472 | tf_op jit(solution)/shard_map/all_gather | solution.py:337
  83.2 13.0 %project.1 = (bf16[1024,1024]{1,0:T(8,128)(2,1)}, bf16[1024,3072]{1,0:T(8,128)(2,1)}) custom-call(bf16[1024,1024]{1,0:T(8,128)(2,1)} %tokens_ref.5, bf16[1,1024]{1,0:T(2,128)(2,1)} %reshape.90.gain_ref, bf16[1,1024]{1,0:T(2,128)(2,1)} %reshape.91.shift_ref, bf16[1024,3072]{1,0:T(8,128)(2,1)} %all-gather.5.cloned.1.call-done.weight_ref.w_ref, ...), custom_call_target="tpu_custom_call" | custom-call | flops 6442450944 | bytes 16777216 | tf_op jit(solution)/shard_map/project/pallas_call | solution.py:38
  96.2 36.0 %attend.1 = (bf16[1024,1024]{1,0:T(8,128)(2,1)}, f32[128,1024]{1,0:T(8,128)}) custom-call(s32[1]{0:T(128)S(6)} %copy.47.prefix_ref, s32[1]{0:T(128)S(6)} %copy.48.padding_ref, bf16[1024,3072]{1,0:T(8,128)(2,1)} %get-tuple-element.37.q_ref.k_ref.v_ref, bf16[1024,3072]{1,0:T(8,128)(2,1)} %get-tuple-element.37.q_ref.k_ref.v_ref, ...), custom_call_target="tpu_custom_call" | custom-call | flops 4294967296 | bytes 8388608 | tf_op jit(solution)/shard_map/attend/pallas_call | solution.py:90
  132.2 9.0 %all-gather.7.cloned.1.call-done.weight_ref = bf16[1024,1024]{1,0:T(8,128)(2,1)} async-done(((bf16[32,1024]{1,0:T(8,128)(2,1)}), bf16[1024,1024]{1,0:T(8,128)(2,1)}) %all-gather.7.cloned.1.call-update) | async-done | bytes 2097168 | tf_op jit(solution)/shard_map/all_gather | solution.py:337
  141.2 7.4 branch.1
  148.6 71.8 %all-gather.9.cloned.1.call-done.up_ref = bf16[1024,4096]{1,0:T(8,128)(2,1)} async-done(((bf16[32,4096]{1,0:T(8,128)(2,1)}), bf16[1024,4096]{1,0:T(8,128)(2,1)}) %all-gather.9.cloned.1.call-update) | async-done | bytes 8388624 | tf_op jit(solution)/shard_map/all_gather | solution.py:337
  220.4 78.8 %all-gather.11.cloned.1.call-done.down_ref = bf16[4096,1024]{1,0:T(8,128)(2,1)} async-done(((bf16[128,1024]{1,0:T(8,128)(2,1)}), bf16[4096,1024]{1,0:T(8,128)(2,1)}) %all-gather.11.cloned.1.call-update) | async-done | bytes 8388624 | tf_op jit(solution)/shard_map/all_gather | solution.py:337
  299.2 59.6 %ffn.1 = (f32[1024,1024]{1,0:T(8,128)}, f32[1024,1024]{1,0:T(8,128)}, bf16[1024,4096]{1,0:T(8,128)(2,1)}, bf16[4096,1024]{1,0:T(8,128)(2,1)}, f32[1,4096]{1,0:T(1,128)}) custom-call(bf16[1024,1024]{1,0:T(8,128)(2,1)} %get-tuple-element.40.normed_ref, bf16[1024,1024]{1,0:T(8,128)(2,1)} %go_ref.1, bf16[1024,4096]{1,0:T(8,128)(2,1)} %all-gather.9.cloned.1.call-done.up_ref, ...), custom_call_target="tpu_custom_call" | custom-call | flops 51539607552 | bytes 46137344 | tf_op jit(solution)/shard_map/ffn/pallas_call | solution.py:149
  358.8 16.3 %middle.1 = (bf16[1024,1024]{1,0:T(8,128)(2,1)}, f32[1024,1024]{1,0:T(8,128)}, bf16[1024,1024]{1,0:T(8,128)(2,1)}, bf16[1024,1024]{1,0:T(8,128)(2,1)}, f32[8,1024]{1,0:T(8,128)}) custom-call(f32[1024,1024]{1,0:T(8,128)} %get-tuple-element.39.resid_ref, f32[1024,1024]{1,0:T(8,128)} %get-tuple-element.41.outacc_ref, f32[1024,1024]{1,0:T(8,128)} %get-tuple-element.42.dn_ref, ...), custom_call_target="tpu_custom_call" | custom-call | flops 4294967296 | bytes 31457280 | tf_op jit(solution)/shard_map/middle/pallas_call | solution.py:193
  375.2 43.0 %attend_back.1 = (bf16[1024,1024]{1,0:T(8,128)(2,1)}, bf16[1024,1024]{1,0:T(8,128)(2,1)}, bf16[1024,1024]{1,0:T(8,128)(2,1)}, f32[8,1024]{1,0:T(8,128)}) custom-call(s32[1]{0:T(128)S(6)} %copy.47.prefix_ref, s32[1]{0:T(128)S(6)} %copy.48.padding_ref, bf16[1024,3072]{1,0:T(8,128)(2,1)} %get-tuple-element.37.q_ref.k_ref.v_ref, ...), custom_call_target="tpu_custom_call" | custom-call | flops 10737418240 | bytes 14680064 | tf_op jit(solution)/shard_map/attend_back/pallas_call | solution.py:246
  418.2 6.3 inproj_grad.3
  424.5 6.3 inproj_grad.4
  430.8 6.4 inproj_grad.5
  437.3 5.4 pad_maximum_fusion
  442.7 10.4 %reshape.99 = bf16[4,2,384,1024]{3,2,1,0:T(8,128)(2,1)} reshape(bf16[1024,3072]{1,0:T(8,128)(2,1)} %pad_maximum_fusion) | data formatting | bytes 12582912 | tf_op jit(solution)/shard_map/reshape | solution.py:364
  453.1 14.0 %reshape.103 = bf16[4,2,512,1024]{3,2,1,0:T(8,128)(2,1)} reshape(bf16[1024,4096]{1,0:T(8,128)(2,1)} %get-tuple-element.57) | data formatting | bytes 16777216 | tf_op jit(solution)/shard_map/reshape | solution.py:364
  468.3 79.0 %all-reduce.7.cloned.1.call-done = (bf16[2,4,384,1024]{3,2,0,1:T(8,128)(2,1)}, bf16[2,4,128,1024]{3,2,0,1:T(8,128)(2,1)}, bf16[2,4,512,1024]{3,2,0,1:T(8,128)(2,1)}, bf16[2,4,512,1024]{3,2,0,1:T(8,128)(2,1)}) async-done(((bf16[2,4,384,1024]{3,2,0,1:T(8,128)(2,1)}, bf16[2,4,128,1024]{3,2,0,1:T(8,128)(2,1)}, bf16[2,4,512,1024]{3,2,0,1:T(8,128)(2,1)}, bf16[2,4,512,1024]{3,2,0,1:T(8,128)(2,1)}), ...) | async-done | bytes 25165840
  556.2 5.4 constant_dynamic-slice_fusion
  561.7 5.4 constant_dynamic-slice_fusion.1
  567.1 7.6 reshape.104
  574.8 5.0 reduce-scatter.25.cloned.1.call-done
  579.8 47.2 %reduce-scatter.21.cloned.1.call-done = bf16[128,3072]{1,0:T(8,128)(2,1)} async-done(((bf16[512,3072]{1,0:T(8,128)(2,1)}), bf16[128,3072]{1,0:T(8,128)(2,1)}) %reduce-scatter.21.cloned.1.call-update) | async-done | bytes 786448 | tf_op jit(solution)/shard_map/reduce_scatter | solution.py:367
  627.1 14.7 %last.1 = (bf16[1024,1024]{1,0:T(8,128)(2,1)}, f32[8,1024]{1,0:T(8,128)}) custom-call(bf16[1024,1024]{1,0:T(8,128)(2,1)} %get-tuple-element.46.dq_ref.d_ref, bf16[1024,1024]{1,0:T(8,128)(2,1)} %get-tuple-element.47.dk_ref.d_ref, bf16[1024,1024]{1,0:T(8,128)(2,1)} %get-tuple-element.48.dv_ref.d_ref, ...), custom_call_target="tpu_custom_call" | custom-call | flops 6442450944 | bytes 20971520 | tf_op jit(solution)/shard_map/last/pallas_call | solution.py:292
  648.8 34.2 %reduce-scatter.33.cloned.1.call-done = bf16[512,1024]{1,0:T(8,128)(2,1)} async-done(((bf16[2048,1024]{1,0:T(8,128)(2,1)}), bf16[512,1024]{1,0:T(8,128)(2,1)}) %reduce-scatter.33.cloned.1.call-update) | async-done | bytes 1048592 | tf_op jit(solution)/shard_map/reduce_scatter | solution.py:367
  691.0 47.7 %reduce-scatter.29.cloned.1.call-done = bf16[128,4096]{1,0:T(8,128)(2,1)} async-done(((bf16[512,4096]{1,0:T(8,128)(2,1)}), bf16[128,4096]{1,0:T(8,128)(2,1)}) %reduce-scatter.29.cloned.1.call-update) | async-done | bytes 1048592 | tf_op jit(solution)/shard_map/reduce_scatter | solution.py:367
  749.7 10.8 %reduce-scatter.27.cloned.1.call-done = bf16[32,1024]{1,0:T(8,128)(2,1)} async-done(((bf16[128,1024]{1,0:T(8,128)(2,1)}), bf16[32,1024]{1,0:T(8,128)(2,1)}) %reduce-scatter.27.cloned.1.call-update) | async-done | bytes 65552 | tf_op jit(solution)/shard_map/reduce_scatter | solution.py:368
  762.0 22.5 %reduce-scatter.23.cloned.1.call-done = bf16[32,3072]{1,0:T(8,128)(2,1)} async-done(((bf16[128,3072]{1,0:T(8,128)(2,1)}), bf16[32,3072]{1,0:T(8,128)(2,1)}) %reduce-scatter.23.cloned.1.call-update) | async-done | bytes 196624 | tf_op jit(solution)/shard_map/reduce_scatter | solution.py:368
  786.2 26.8 %reduce-scatter.35.cloned.1.call-done = bf16[128,1024]{1,0:T(8,128)(2,1)} async-done(((bf16[512,1024]{1,0:T(8,128)(2,1)}), bf16[128,1024]{1,0:T(8,128)(2,1)}) %reduce-scatter.35.cloned.1.call-update) | async-done | bytes 262160 | tf_op jit(solution)/shard_map/reduce_scatter | solution.py:368
  814.9 26.4 %reduce-scatter.31.cloned.1.call-done = bf16[32,4096]{1,0:T(8,128)(2,1)} async-done(((bf16[128,4096]{1,0:T(8,128)(2,1)}), bf16[32,4096]{1,0:T(8,128)(2,1)}) %reduce-scatter.31.cloned.1.call-update) | async-done | bytes 262160 | tf_op jit(solution)/shard_map/reduce_scatter | solution.py:368
  (124 shorter events, 61.9 us)
Async XLA Ops:
  7.2 76.0 %all-gather.5.cloned.1.call-start = ((), (), s32[]{:S(2)}) async-start(), calls=%async_computation.8 | async-start | bytes 6488064 | tf_op jit(solution)/shard_map/all_gather | solution.py:337
  7.9 133.3 %all-gather.7.cloned.1.call-start = ((), (), s32[]{:S(2)}) async-start(), calls=%async_computation.9 | async-start | bytes 2162688 | tf_op jit(solution)/shard_map/all_gather | solution.py:337
  8.7 211.7 %all-gather.9.cloned.1.call-start = ((), (), s32[]{:S(2)}) async-start(), calls=%async_computation.10 | async-start | bytes 8650752 | tf_op jit(solution)/shard_map/all_gather | solution.py:337
  9.4 289.8 %all-gather.11.cloned.1.call-start = ((), (), s32[]{:S(2)}) async-start(), calls=%async_computation.11 | async-start | bytes 8650752 | tf_op jit(solution)/shard_map/all_gather | solution.py:337
  10.0 537.4 %all-reduce.7.cloned.1.call-start = ((), (), s32[]{:S(2)}) async-start(), calls=%async_computation.20 | async-start | bytes 50331648
  16.1 4.6 collective-permute-start
  20.8 4.8 collective-permute-start.1
  25.6 1.2 collective-permute-start.2
  26.8 3.7 collective-permute-start.3
  30.5 3.7 collective-permute-start.4
  430.8 6.5 copy-start
  467.1 0.7 copy-start.3
  467.1 112.6 %reduce-scatter.25.cloned.1.call-start = ((), (), s32[]{:S(2)}) async-start(), calls=%async_computation.14 | async-start | bytes 1310720 | tf_op jit(solution)/shard_map/reduce_scatter | solution.py:367
  550.3 76.7 %reduce-scatter.21.cloned.1.call-start = ((), (), s32[]{:S(2)}) async-start(), calls=%async_computation.12 | async-start | bytes 3932160 | tf_op jit(solution)/shard_map/reduce_scatter | solution.py:367
  556.2 126.8 %reduce-scatter.33.cloned.1.call-start = ((), (), s32[]{:S(2)}) async-start(), calls=%async_computation.18 | async-start | bytes 5242880 | tf_op jit(solution)/shard_map/reduce_scatter | solution.py:367
  561.6 177.1 %reduce-scatter.29.cloned.1.call-start = ((), (), s32[]{:S(2)}) async-start(), calls=%async_computation.16 | async-start | bytes 5242880 | tf_op jit(solution)/shard_map/reduce_scatter | solution.py:367
  574.7 185.8 %reduce-scatter.27.cloned.1.call-start = ((), (), s32[]{:S(2)}) async-start(), calls=%async_computation.15 | async-start | bytes 327680 | tf_op jit(solution)/shard_map/reduce_scatter | solution.py:368
  579.8 204.8 %reduce-scatter.23.cloned.1.call-start = ((), (), s32[]{:S(2)}) async-start(), calls=%async_computation.13 | async-start | bytes 983040 | tf_op jit(solution)/shard_map/reduce_scatter | solution.py:368
  627.0 186.1 %reduce-scatter.35.cloned.1.call-start = ((), (), s32[]{:S(2)}) async-start(), calls=%async_computation.19 | async-start | bytes 1310720 | tf_op jit(solution)/shard_map/reduce_scatter | solution.py:368
  627.0 21.2 %copy-start.2 = (f32[8,1024]{1,0:T(8,128)S(1)}, f32[8,1024]{1,0:T(8,128)}, u32[]{:S(2)}) copy-start(f32[8,1024]{1,0:T(8,128)} %get-tuple-element.54) | copy-start | bytes 98308
  627.0 21.6 %copy-start.1 = (f32[1,4096]{1,0:T(1,128)S(1)}, f32[1,4096]{1,0:T(1,128)}, u32[]{:S(2)}) copy-start(f32[1,4096]{1,0:T(1,128)} %get-tuple-element.55) | copy-start | bytes 49156
  642.8 3.8 collective-permute-start.5
  646.7 36.4 %collective-permute-start.6 = (f32[8,64]{1,0:T(8,128)S(1)}, f32[8,64]{1,0:T(8,128)S(1)}, u32[]{:S(2)}, u32[]{:S(2)}) collective-permute-start(f32[8,64]{1,0:T(8,128)S(1)} %slice_select_fusion.3), channel_id=1, source_target_pairs={{0,8},{1,9},{2,10},{3,11},{4,12},{5,13},{6,14},{7,15},{8,0},{9,1},... | collective-permute-start | bytes 6152 | tf_op jit(solution)/shard_map/ppermute | solution.py:327
  683.0 158.2 %reduce-scatter.31.cloned.1.call-start = ((), (), s32[]{:S(2)}) async-start(), calls=%async_computation.17 | async-start | bytes 1310720 | tf_op jit(solution)/shard_map/reduce_scatter | solution.py:368
  683.1 1.5 collective-permute-start.7
  683.2 3.9 collective-permute-start.10
  684.7 4.5 collective-permute-start.8
  687.2 3.8 collective-permute-start.11
  691.0 49.4 %collective-permute-start.12 = (f32[4,320]{1,0:T(4,128)S(1)}, f32[4,320]{1,0:T(4,128)S(1)}, u32[]{:S(2)}, u32[]{:S(2)}) collective-permute-start(f32[4,320]{1,0:T(4,128)S(1)} %slice_select_fusion.2), channel_id=1, source_target_pairs={{0,4},{1,5},{2,6},{3,7},{4,0},{5,1},{6,2},{7,3},{8,12},{9,13},{10,... | collective-permute-start | bytes 15368 | tf_op jit(solution)/shard_map/ppermute | solution.py:327
  738.7 4.1 collective-permute-start.9
  740.3 4.6 collective-permute-start.13
  744.9 3.6 collective-permute-start.14
Sparse Core Ops, SparseCore 0:
  10.9 72.2 all-gather.4
  86.2 54.9 all-gather.6
  144.1 76.2 all-gather.8
  223.2 75.9 all-gather.10
  467.2 80.0 all-reduce.6
  550.7 29.0 reduce-scatter.24
  583.0 43.9 reduce-scatter.20
  630.2 52.7 reduce-scatter.32
  686.0 52.6 reduce-scatter.28
  740.9 19.5 reduce-scatter.26
  762.8 21.6 reduce-scatter.22
  786.7 26.3 reduce-scatter.34
  815.5 25.7 reduce-scatter.30

commit v2 on v1

v2 whole, which is shorter than its diff:
```python
import functools, math
import jax, jax.numpy as jnp
from jax import lax
from jax.sharding import PartitionSpec as P
from jax.experimental import pallas as pl
from jax.experimental.pallas import tpu as pltpu
HEADS=16
EPSILON = 1e-05
NEGATIVE = -1000000000.0
bf16=jnp.bfloat16; f32=jnp.float32
VMEM_LIMIT=60*1024*1024
HINT=pl.CostEstimate(flops=1000, bytes_accessed=1000, transcendentals=0)
def cp(n=1): return pltpu.CompilerParams(dimension_semantics=("arbitrary",)*n, vmem_limit_bytes=VMEM_LIMIT)
def dot(a,b): return lax.dot_general(a,b,(((1,),(0,)),((),())),preferred_element_type=f32)
def dot_nt(a,b): return lax.dot_general(a,b,(((1,),(1,)),((),())),preferred_element_type=f32)
def dot_tn(a,b): return lax.dot_general(a,b,(((0,),(0,)),((),())),preferred_element_type=f32)

def project_kernel(order_ref, tokens_ref, gain_ref, shift_ref, bias_ref, *refs):
    *pieces, normed_ref, out_ref, weight_ref = refs
    step = pl.program_id(0)
    @pl.when(step == 0)
    def _():
        x = tokens_ref[...].astype(f32)
        center = x - jnp.mean(x, axis=-1, keepdims=True)
        spread = jnp.mean(center * center, axis=-1, keepdims=True)
        normed = center * lax.rsqrt(spread + EPSILON) * gain_ref[...].astype(f32) + shift_ref[...].astype(f32)
        normed_ref[...] = normed.astype(bf16)
    n, rows, tn = pieces[0].shape
    for p, piece in enumerate(pieces):
        for i in range(n):
            weight_ref[pl.ds(pl.multiple_of(order_ref[p * n + i] * rows, rows), rows), :] = piece[i]
    third = pl.num_programs(0) // 3
    factor = jnp.where(step < third, 0.125, 1.0)
    out = dot(normed_ref[...], weight_ref[...]) + bias_ref[...].astype(f32)
    out_ref[...] = (out * factor).astype(bf16)

def project(order, tokens, gain, shift, bias, pieces, tn=512):
    R, D = tokens.shape
    n, rows, N = pieces[0].shape
    full = pl.BlockSpec((R, D), lambda j: (0, 0))
    row = pl.BlockSpec((1, D), lambda j: (0, 0))
    cols = pl.BlockSpec((R, tn), lambda j: (0, j))
    return pl.pallas_call(
        project_kernel, grid=(N // tn,),
        in_specs=[pl.BlockSpec(memory_space=pltpu.SMEM), full, row, row, pl.BlockSpec((1, tn), lambda j: (0, j))]
        + [pl.BlockSpec((n, rows, tn), lambda j: (0, 0, j))] * len(pieces),
        out_specs=[full, cols, pl.BlockSpec((D, tn), lambda j: (0, j))],
        out_shape=[jax.ShapeDtypeStruct((R, D), bf16), jax.ShapeDtypeStruct((R, N), bf16), jax.ShapeDtypeStruct((D, N), bf16)],
        compiler_params=cp(), name="project",
        cost_estimate=HINT,
    )(order, tokens, gain, shift, bias, *pieces)

def mask_rows(start, bq, lo, hi, prefix, limit):
    q = start + lax.broadcasted_iota(jnp.int32, (bq, hi - lo), 0)
    k = lo + lax.broadcasted_iota(jnp.int32, (bq, hi - lo), 1)
    return ((k < prefix) | (k <= q)) & (k < limit)

def attend_kernel(prefix_ref, padding_ref, q_ref, k_ref, v_ref, out_ref, lse_ref, stat_ref, *, bq):
    L = q_ref.shape[0]
    step = pl.program_id(0)
    prefix = prefix_ref[0]
    limit = L - padding_ref[0]
    lane = lax.broadcasted_iota(jnp.int32, (1, 128), 1)
    stat_lane = lax.broadcasted_iota(jnp.int32, (bq, 128), 1)
    @pl.when(step == 0)
    def _():
        stat_ref[...] = jnp.zeros_like(stat_ref)
    for start in range(0, L, bq):
        stop = start + bq
        parts = []
        stat = stat_ref[start:stop, :]
        for half in range(2):
            mine = (lane < 64) if half == 0 else (lane >= 64)
            q = jnp.where(mine, q_ref[start:stop, :], 0).astype(bf16)
            s = dot_nt(q, k_ref[:stop, :])
            s = jnp.where(mask_rows(start, bq, 0, stop, prefix, limit), s, NEGATIVE)
            m = jnp.max(s, axis=-1, keepdims=True)
            e = jnp.exp(s - m)
            t = jnp.sum(e, axis=-1, keepdims=True)
            p = (e * (1.0 / t)).astype(bf16)
            parts.append(dot(p, v_ref[:stop, :]))
            stat = jnp.where(stat_lane == 2 * step + half, m + jnp.log(t), stat)
        stat_ref[start:stop, :] = stat
        out_ref[start:stop, :] = jnp.where(lane < 64, parts[0], parts[1]).astype(bf16)
    @pl.when(step == pl.num_programs(0) - 1)
    def _():
        lse_ref[...] = jnp.transpose(stat_ref[...])

def attend(prefix, padding, qkv, bq=256):
    L = qkv.shape[0]
    D = qkv.shape[1] // 3
    n = D // 128
    smem = pl.BlockSpec(memory_space=pltpu.SMEM)
    col = lambda off: pl.BlockSpec((L, 128), lambda j: (0, j + off))
    return pl.pallas_call(
        functools.partial(attend_kernel, bq=bq), grid=(n,),
        in_specs=[smem, smem, col(0), col(n), col(2 * n)],
        out_specs=[col(0), pl.BlockSpec((128, L), lambda j: (0, 0))],
        out_shape=[jax.ShapeDtypeStruct((L, D), bf16), jax.ShapeDtypeStruct((128, L), f32)],
        scratch_shapes=[pltpu.VMEM((L, 128), f32)],
        compiler_params=cp(), name="attend",
        cost_estimate=HINT,
    )(prefix, padding, qkv, qkv, qkv)

def branch_kernel(ctx_ref, weight_ref, tokens_ref, bias_ref, gain_ref, shift_ref, resid_ref, normed_ref):
    resid = tokens_ref[...].astype(f32) + (dot(ctx_ref[...], weight_ref[...]) + bias_ref[...].astype(f32))
    center = resid - jnp.mean(resid, axis=-1, keepdims=True)
    spread = jnp.mean(center * center, axis=-1, keepdims=True)
    normed = center * lax.rsqrt(spread + EPSILON) * gain_ref[...].astype(f32) + shift_ref[...].astype(f32)
    resid_ref[...] = resid
    normed_ref[...] = normed.astype(bf16)

def branch(ctx, weight, tokens, bias, gain, shift, tm=256):
    R, D = ctx.shape
    rows = pl.BlockSpec((tm, D), lambda i: (i, 0))
    vec = pl.BlockSpec((1, D), lambda i: (0, 0))
    return pl.pallas_call(
        branch_kernel, grid=(R // tm,),
        in_specs=[rows, pl.BlockSpec((D, D), lambda i: (0, 0)), rows, vec, vec, vec],
        out_specs=[rows, rows],
        out_shape=[jax.ShapeDtypeStruct((R, D), f32), jax.ShapeDtypeStruct((R, D), bf16)],
        compiler_params=cp(), name="branch",
        cost_estimate=HINT,
    )(ctx, weight, tokens, bias, gain, shift)

def ffn_kernel(pos_ref, normed_ref, grad_ref, up_ref, bias_ref, down_ref, *refs, shards, per, F, chained):
    out_in, dn_in = refs[:2] if chained else (None, None)
    out_ref, dn_ref, keep_ref, send_ref, biasg_ref, ups_ref, dns_ref, up_sem, dn_sem, acc_sem = refs[2 if chained else 0:]
    step = pl.program_id(0)
    last = pl.num_programs(0) - 1
    D = normed_ref.shape[1]
    tf = up_ref.shape[1]
    half = shards // 2
    rows = D // shards
    slot = lax.rem(step, 2)
    block = lax.div(step, per)
    bslot = lax.rem(block, 2)

    def up_copies(slot, step):
        cols = pl.ds(pl.multiple_of(step * tf, tf), tf)
        return [pltpu.make_async_copy(ups_ref.at[slot, pl.ds(0, half)], keep_ref.at[:, :, cols], up_sem.at[slot, 0]),
                pltpu.make_async_copy(ups_ref.at[slot, pl.ds(half, half)], send_ref.at[:, :, cols], up_sem.at[slot, 1])]

    def down_copies(bslot, block):
        cols = pl.ds(pl.multiple_of(F + block * D, D), D)
        return [pltpu.make_async_copy(dns_ref.at[bslot, pl.ds(0, half)], keep_ref.at[:, :, cols], dn_sem.at[bslot, 0]),
                pltpu.make_async_copy(dns_ref.at[bslot, pl.ds(half, half)], send_ref.at[:, :, cols], dn_sem.at[bslot, 1])]

    earlier = [pltpu.make_async_copy(out_in, out_ref, acc_sem.at[0]), pltpu.make_async_copy(dn_in, dn_ref, acc_sem.at[1])] if chained else []

    @pl.when(step == 0)
    def _():
        if chained:
            for c in earlier:
                c.start()
        else:
            out_ref[...] = jnp.zeros_like(out_ref)
            dn_ref[...] = jnp.zeros_like(dn_ref)
    n2 = normed_ref[...]
    go = grad_ref[...]
    up = up_ref[...]
    down = down_ref[...]
    u = dot(n2, up) + bias_ref[...].astype(f32)
    cdf = 0.5 * (1.0 + lax.erf(u * math.sqrt(0.5)))
    a = (u * cdf).astype(bf16)
    slope = cdf + u * (jnp.exp(-0.5 * u * u) * (1.0 / math.sqrt(2 * math.pi)))
    du = (dot_nt(go, down) * slope).astype(bf16)
    if chained:
        @pl.when(step == 0)
        def _():
            for c in earlier:
                c.wait()
    out_ref[...] += dot(a, down)
    dn_ref[...] += dot_nt(du, up)
    biasg_ref[...] = jnp.sum(du.astype(f32), axis=0, keepdims=True)
    upg = dot_tn(n2, du).astype(bf16)
    downg = dot_tn(a, go).astype(bf16)

    @pl.when(step >= 2)
    def _():
        for c in up_copies(slot, step - 2):
            c.wait()
    for i in range(shards):
        ups_ref[slot, pos_ref[i]] = upg[i * rows:(i + 1) * rows]
    for c in up_copies(slot, step):
        c.start()

    @pl.when((step >= 2 * per) & (lax.rem(step, per) == 0))
    def _():
        for c in down_copies(bslot, block - 2):
            c.wait()
    here = tf // rows
    first = lax.rem(step, per) * here
    for i in range(here):
        dns_ref[bslot, pos_ref[first + i]] = downg[i * rows:(i + 1) * rows]

    @pl.when(lax.rem(step, per) == per - 1)
    def _():
        for c in down_copies(bslot, block):
            c.start()

    @pl.when(step == last)
    def _():
        for c in up_copies(1 - slot, step - 1) + up_copies(slot, step) + down_copies(1 - bslot, block - 1) + down_copies(bslot, block):
            c.wait()

def ffn(pos, normed, grad, wide, bias, first, blocks, extra=0, earlier=(), tf=512):
    R, D = normed.shape
    F = blocks * D
    shards = pos.shape[0]
    rows = D // shards
    per = D // tf
    every = (wide.shape[1] // D - 1) // 2
    full = pl.BlockSpec((R, D), lambda j: (0, 0))
    hbm = pl.BlockSpec(memory_space=pl.ANY)
    part = jax.ShapeDtypeStruct((shards // 2, rows, 2 * F + extra), bf16)
    return pl.pallas_call(
        functools.partial(ffn_kernel, shards=shards, per=per, F=F, chained=bool(earlier)), grid=(F // tf,),
        in_specs=[pl.BlockSpec(memory_space=pltpu.SMEM), full, full,
                  pl.BlockSpec((D, tf), lambda j: (0, j + (1 + first) * per)), pl.BlockSpec((1, tf), lambda j: (0, j + first * per)),
                  pl.BlockSpec((tf, D), lambda j: (lax.rem(j, per), 1 + every + first + lax.div(j, per)))] + [hbm] * len(earlier),
        out_specs=[full, full, hbm, hbm, pl.BlockSpec((1, tf), lambda j: (0, j))],
        out_shape=[jax.ShapeDtypeStruct((R, D), f32), jax.ShapeDtypeStruct((R, D), f32), part, part, jax.ShapeDtypeStruct((1, F), f32)],
        scratch_shapes=[pltpu.VMEM((2, shards, rows, tf), bf16), pltpu.VMEM((2, shards, rows, D), bf16),
                        pltpu.SemaphoreType.DMA((2, 2)), pltpu.SemaphoreType.DMA((2, 2)), pltpu.SemaphoreType.DMA((2,))],
        compiler_params=cp(), name="ffn",
        cost_estimate=HINT,
    )(pos, normed, grad, wide, bias, wide, *earlier)

def middle_kernel(resid_ref, outacc_ref, dn_ref, go_ref, gain_ref, dbias_ref, weight_ref,
                  out_ref, dres_ref, low_ref, dctx_ref, small_ref):
    i = pl.program_id(0)
    resid = resid_ref[...]
    out_ref[...] = (resid + outacc_ref[...] + dbias_ref[...].astype(f32)).astype(bf16)
    center = resid - jnp.mean(resid, axis=-1, keepdims=True)
    spread = jnp.mean(center * center, axis=-1, keepdims=True)
    r = lax.rsqrt(spread + EPSILON)
    nhat = center * r
    dn = dn_ref[...]
    go = go_ref[...].astype(f32)
    e = dn * gain_ref[...].astype(f32)
    d_res = go + r * (e - jnp.mean(e, axis=-1, keepdims=True) - nhat * jnp.mean(e * nhat, axis=-1, keepdims=True))
    dres_ref[...] = d_res
    low = d_res.astype(bf16)
    low_ref[...] = low
    dctx_ref[...] = dot_nt(low, weight_ref[...]).astype(bf16)
    @pl.when(i == 0)
    def _():
        small_ref[...] = jnp.zeros_like(small_ref)
    small_ref[0:1, :] += jnp.sum(dn * nhat, axis=0, keepdims=True)
    small_ref[1:2, :] += jnp.sum(dn, axis=0, keepdims=True)
    small_ref[2:3, :] += jnp.sum(low.astype(f32), axis=0, keepdims=True)
    small_ref[3:4, :] += jnp.sum(go, axis=0, keepdims=True)

def middle(resid, outacc, dn, go, gain, dbias, weight, tm=256):
    R, D = resid.shape
    rows = pl.BlockSpec((tm, D), lambda i: (i, 0))
    vec = pl.BlockSpec((1, D), lambda i: (0, 0))
    low = jax.ShapeDtypeStruct((R, D), bf16)
    return pl.pallas_call(
        middle_kernel, grid=(R // tm,),
        in_specs=[rows, rows, rows, rows, vec, vec, pl.BlockSpec((D, D), lambda i: (0, 0))],
        out_specs=[rows, rows, rows, rows, pl.BlockSpec((8, D), lambda i: (0, 0))],
        out_shape=[low, jax.ShapeDtypeStruct((R, D), f32), low, low, jax.ShapeDtypeStruct((8, D), f32)],
        compiler_params=cp(), name="middle",
        cost_estimate=HINT,
    )(resid, outacc, dn, go, gain, dbias, weight)

def attend_back_kernel(prefix_ref, padding_ref, q_ref, k_ref, v_ref, do_ref, lse_ref, *refs, bq, first):
    dq_ref, dk_ref, dv_ref, small_ref, dka_ref, dva_ref = refs[-6:]
    L = q_ref.shape[0]
    step = pl.program_id(0) + first
    prefix = prefix_ref[0]
    limit = L - padding_ref[0]
    lane = lax.broadcasted_iota(jnp.int32, (1, 128), 1)
    dka_ref[...] = jnp.zeros_like(dka_ref)
    dva_ref[...] = jnp.zeros_like(dva_ref)
    kT = jnp.transpose(k_ref[...])
    for start in range(0, L, bq):
        stop = start + bq
        dqT = []
        for half in range(2):
            mine = (lane < 64) if half == 0 else (lane >= 64)
            q = jnp.where(mine, q_ref[start:stop, :], 0).astype(bf16)
            do = jnp.where(mine, do_ref[start:stop, :], 0).astype(bf16)
            s = dot_nt(k_ref[:stop, :], q)
            kk = lax.broadcasted_iota(jnp.int32, (stop, bq), 0)
            qq = start + lax.broadcasted_iota(jnp.int32, (stop, bq), 1)
            ok = ((kk < prefix) | (kk <= qq)) & (kk < limit)
            lse = lse_ref[pl.ds(2 * step + half, 1), start:stop]
            p = jnp.where(ok, jnp.exp(s - lse), 0.0)
            dp = dot_nt(v_ref[:stop, :], do)
            inner = jnp.sum(p * dp, axis=0, keepdims=True)
            ds = (p * (dp - inner)).astype(bf16)
            dva_ref[:stop, :] += dot(p.astype(bf16), do)
            dka_ref[:stop, :] += dot(ds, q)
            dqT.append(dot(kT[64 * half:64 * half + 64, :stop], ds))
        dq = jnp.transpose(jnp.concatenate(dqT, axis=0)) * 0.125
        dq_ref[start:stop, :] = dq.astype(bf16)
    dk_ref[...] = dka_ref[...].astype(bf16)
    dv_ref[...] = dva_ref[...].astype(bf16)
    small_ref[0:1, :] = jnp.sum(dq_ref[...].astype(f32), axis=0, keepdims=True)
    small_ref[1:2, :] = jnp.sum(dv_ref[...].astype(f32), axis=0, keepdims=True)

def attend_back(prefix, padding, qkv, dctx, lse, first, count, width, earlier=(), bq=256):
    L = qkv.shape[0]
    D = dctx.shape[1]
    n = D // 128
    at = first % (width // 128)
    smem = pl.BlockSpec(memory_space=pltpu.SMEM)
    col = lambda off: pl.BlockSpec((L, 128), lambda j: (0, j + off))
    o = jax.ShapeDtypeStruct((L, width), bf16)
    return pl.pallas_call(
        functools.partial(attend_back_kernel, bq=bq, first=first), grid=(count,),
        in_specs=[smem, smem, col(first), col(n + first), col(2 * n + first), col(first), pl.BlockSpec((128, L), lambda j: (0, 0))]
        + [pl.BlockSpec(memory_space=pl.ANY)] * len(earlier),
        out_specs=[col(at), col(at), col(at), pl.BlockSpec((8, 128), lambda j: (0, j + at))],
        out_shape=[o, o, o, jax.ShapeDtypeStruct((8, width), f32)],
        scratch_shapes=[pltpu.VMEM((L, 128), f32), pltpu.VMEM((L, 128), f32)],
        input_output_aliases={7 + i: i for i in range(len(earlier))},
        compiler_params=cp(), name="attend_back",
        cost_estimate=HINT,
    )(prefix, padding, qkv, qkv, qkv, dctx, lse, *earlier)

def weight_grad_kernel(pos_ref, *refs, sources, extra):
    left = refs[:max(sources) + 1]
    refs = refs[len(left):]
    right = refs[:len(sources)]
    refs = refs[len(right):]
    small_ref = refs[0] if extra else None
    keep_ref, send_ref, wide_ref = refs[1 if extra else 0:]
    shards = wide_ref.shape[0]
    half = shards // 2
    rows = left[0].shape[1] // shards
    for g, (source, d_ref) in enumerate(zip(sources, right)):
        value = dot_tn(left[source][...], d_ref[...]).astype(bf16)
        for i in range(shards):
            wide_ref[pos_ref[i], g * rows:(g + 1) * rows, :] = value[i * rows:(i + 1) * rows]
    if extra:
        for i in range(shards):
            wide_ref[pos_ref[i], len(sources) * rows:, :] = jnp.broadcast_to(small_ref[i:i + 1, :], (extra, small_ref.shape[1])).astype(bf16)
    keep_ref[...] = wide_ref[:half]
    send_ref[...] = wide_ref[half:]

def weight_grad(pos, left, right, sources, small=None, width=512, tn=256):
    R, D = left[0].shape
    shards = pos.shape[0]
    rows = D // shards
    extra = min(rows, 16) if small is not None else 0
    high = len(right) * rows + extra
    part = pl.BlockSpec((shards // 2, high, tn), lambda j: (0, 0, j))
    half = jax.ShapeDtypeStruct((shards // 2, high, width), bf16)
    more = [small] if extra else []
    cols = lambda first: pl.BlockSpec((R, tn), lambda j: (0, j + first))
    return pl.pallas_call(
        functools.partial(weight_grad_kernel, sources=sources, extra=extra), grid=(width // tn,),
        in_specs=[pl.BlockSpec(memory_space=pltpu.SMEM)] + [pl.BlockSpec((R, D), lambda j: (0, 0))] * len(left)
        + [cols(first) for _, first in right] + [pl.BlockSpec((shards, tn), lambda j: (0, j))] * len(more),
        out_specs=[part, part], out_shape=[half, half],
        scratch_shapes=[pltpu.VMEM((shards, high, tn), bf16)],
        compiler_params=cp(), name="weight_grad",
        cost_estimate=HINT,
    )(pos, *left, *[r for r, _ in right], *more)

def last_kernel(w_ref, tokens_ref, dres_ref, gain_ref, *refs, count):
    parts = refs[:count]
    out_ref, small_ref = refs[-2:]
    i = pl.program_id(0)
    D = tokens_ref.shape[1]
    count = len(parts) // 3
    dn = None
    for p, part in enumerate(parts):
        width = part.shape[1]
        at = (p // count) * D + (p % count) * width
        term = dot_nt(part[...], w_ref[:, at:at + width])
        dn = term if dn is None else dn + term
    x = tokens_ref[...].astype(f32)
    center = x - jnp.mean(x, axis=-1, keepdims=True)
    spread = jnp.mean(center * center, axis=-1, keepdims=True)
    r = lax.rsqrt(spread + EPSILON)
    nhat = center * r
    e = dn * gain_ref[...].astype(f32)
    d = dres_ref[...] + r * (e - jnp.mean(e, axis=-1, keepdims=True) - nhat * jnp.mean(e * nhat, axis=-1, keepdims=True))
    out_ref[...] = d.astype(bf16)
    @pl.when(i == 0)
    def _():
        small_ref[...] = jnp.zeros_like(small_ref)
    small_ref[0:1, :] += jnp.sum(dn * nhat, axis=0, keepdims=True)
    small_ref[1:2, :] += jnp.sum(dn, axis=0, keepdims=True)

def last(parts, w, tokens, dres, gain, first, steps, earlier=(), tm=256):
    R, D = tokens.shape
    rows = lambda width: pl.BlockSpec((tm, width), lambda i: (i + first, 0))
    return pl.pallas_call(
        functools.partial(last_kernel, count=len(parts)), grid=(steps,),
        in_specs=[pl.BlockSpec((D, 3 * D), lambda i: (0, 0)), rows(D), rows(D), pl.BlockSpec((1, D), lambda i: (0, 0))]
        + [rows(p.shape[1]) for p in parts] + [pl.BlockSpec(memory_space=pl.ANY)] * len(earlier),
        out_specs=[rows(D), pl.BlockSpec((8, D), lambda i: (0, 0))],
        out_shape=[jax.ShapeDtypeStruct((R, D), bf16), jax.ShapeDtypeStruct((8, D), f32)],
        input_output_aliases={4 + len(parts): 0} if earlier else {},
        compiler_params=cp(), name="last",
        cost_estimate=HINT,
    )(w, tokens, dres, gain, *parts, *earlier)


class Plan:
    def __init__(self, dp, fsdp):
        self.total = dp * fsdp
        bits = self.total.bit_length() - 1
        low = fsdp.bit_length() - 1
        if fsdp == 4:
            self.core, z, rest = low, list(range(low)), list(range(low + 1, bits))
        else:
            self.core, z, rest = 0, list(range(1, low)), list(range(low, bits))
        a, b = rest[:len(rest) // 2], rest[len(rest) // 2:]
        self.stages = [(a, b), (b, a), (z, z)]
        self.third = len(z) == low

    def masks(self, stage, core):
        bits = self.stages[stage][core]
        return [sum(1 << b for k, b in enumerate(bits) if j >> k & 1) for j in range(1 << len(bits))]

    def pairs(self, stage, j):
        return [(i, i ^ self.masks(stage, i >> self.core & 1)[j]) for i in range(self.total)]

    def size(self, stage):
        return 1 << len(self.stages[stage][0])

    def places(self, me, fixed=False):
        shard = lax.iota(jnp.int32, self.total)
        rel = shard ^ me
        core = (shard >> self.core) & 1
        pos = (rel >> self.core) & 1
        for k, (a, b) in enumerate(self.stages):
            pick = lambda bits, v: sum((((v >> bit) & 1) << k) for k, bit in enumerate(bits))
            own = pick(a, shard) if fixed and k == 2 else jnp.where(core == 0, pick(a, rel), pick(b, rel))
            pos = (pos << len(a)) + own
        return pos

AXES = ("dp", "fsdp")

def swap_core(plan, x):
    return lax.ppermute(x, AXES, [(i, i ^ (1 << plan.core)) for i in range(plan.total)])

def exchange(plan, x, stage, j):
    return lax.ppermute(x, AXES, plan.pairs(stage, j))

def gather_pieces(plan, shard, beside):
    arrived = tie(beside, *[exchange(plan, shard, 2, j) for j in range(1, plan.size(2))])[1:]
    column = jnp.stack([shard] + arrived)
    pieces = [column] + [exchange(plan, column, 1, j) for j in range(1, plan.size(1))]
    pieces = pieces + [exchange(plan, p, 0, j) for j in range(1, plan.size(0)) for p in pieces]
    return pieces + [swap_core(plan, p) for p in pieces]

def step(x, after, *reductions):
    x, _ = tie(x, after, *reductions)
    reductions = [r for r in reductions if r.stage < 3]
    if reductions:
        for r in reductions:
            r.add()
        x, = tie(x, *reductions)
        for r in reductions:
            r.go()
    return x

class Reduction:
    def __init__(self, plan, keep, send):
        self.plan, self.stage, self.size = plan, 0, keep.shape[0]
        self.terms = [keep, swap_core(plan, send)]
        self.sent = []

    def cut(self, j):
        part = self.size // self.plan.size(self.stage)
        return sum(t[j * part:(j + 1) * part].astype(f32) for t in self.terms).astype(bf16)

    def add(self):
        self.sent = [self.cut(j) for j in range(1, self.plan.size(self.stage))]

    def go(self):
        self.terms = self.terms + [exchange(self.plan, s, self.stage, j + 1) for j, s in enumerate(self.sent)]
        self.sent = []
        self.size //= self.plan.size(self.stage)
        self.stage += 1

    def finish(self):
        while self.stage < 3:
            self.add()
            self.go()
        return sum(t[0].astype(f32) for t in self.terms)

    def scatter(self):
        if not self.plan.third:
            return self.finish()
        whole = sum(t[:self.size].astype(f32) for t in self.terms).astype(bf16)
        return lax.psum_scatter(whole, "fsdp", scatter_dimension=0, tiled=False).astype(f32)

def tie(*trees):
    flat = []
    for t in trees:
        flat += t.terms + t.sent if isinstance(t, Reduction) else [t]
    flat = list(lax.optimization_barrier(tuple(flat)))
    out = []
    for t in trees:
        if isinstance(t, Reduction):
            t.terms = [flat.pop(0) for _ in t.terms]
            t.sent = [flat.pop(0) for _ in t.sent]
        else:
            out.append(flat.pop(0))
    return out

def gather_small(plan, buf):
    me = lax.axis_index(AXES)
    stride = 1
    while stride < plan.total:
        other = lax.ppermute(buf, AXES, [(i, i ^ stride) for i in range(plan.total)])
        low = (me & stride) == 0
        buf = jnp.where(low, jnp.concatenate([buf, other]), jnp.concatenate([other, buf]))
        stride *= 2
    return buf

def scatter_small(plan, buf):
    me = lax.axis_index(AXES)
    stride = plan.total // 2
    while stride:
        low = (me & stride) == 0
        lower, upper = buf[:stride], buf[stride:]
        other = lax.ppermute(jnp.where(low, upper, lower), AXES, [(i, i ^ stride) for i in range(plan.total)])
        buf = jnp.where(low, lower, upper) + other
        stride //= 2
    return buf[0]

def body(plan, tokens, prefix_len, padding_len, first_gain, first_shift, inproj_weight, query_bias, value_bias,
         outproj_weight, outproj_bias, second_gain, second_shift, up_weight, up_bias, down_weight, down_bias, grad_out):
    total = plan.total
    R, D = tokens.shape
    F = up_weight.shape[1]
    rows = D // total
    blocks = F // D
    me = lax.axis_index(AXES)
    pos = plan.places(me)
    shard = lax.iota(jnp.int32, total)
    order = jnp.sum(jnp.where(pos[None, :] == shard[:, None], shard[None, :], 0), axis=1)
    small = jnp.concatenate([first_gain, first_shift, query_bias, value_bias, outproj_bias, second_gain, second_shift, down_bias, up_bias])
    n = first_gain.shape[0]
    small = gather_small(plan, small[None])
    vec = lambda i: small[:, i * n:(i + 1) * n].reshape(1, D)
    gain1, shift1, qbias, vbias, obias, gain2, shift2, dbias = [vec(i) for i in range(8)]
    ubias = small[:, 8 * n:].reshape(total, blocks, rows).transpose(1, 0, 2).reshape(1, F)
    pieces = gather_pieces(plan, inproj_weight, small)
    up_local = up_weight.reshape(rows, total, blocks, rows).transpose(0, 2, 1, 3).reshape(rows, F)
    down_local = [down_weight[b * rows:(b + 1) * rows] for b in range(blocks)]
    wide = lax.all_gather(jnp.concatenate([outproj_weight, up_local] + down_local, axis=1), AXES, axis=0, tiled=True)
    bias = jnp.concatenate([qbias, jnp.zeros_like(qbias), vbias], axis=1)
    n1, qkv, w_in = project(order, tokens, gain1, shift1, bias, pieces)
    ctx, lse = attend(prefix_len, padding_len, qkv)
    resid, n2 = branch(ctx, wide, tokens, obias, gain2, shift2)
    half = blocks // 2
    cut = D // 2
    n_pairs = D // 128
    def back(first, x, earlier=()):
        return attend_back(prefix_len, padding_len, qkv, x, lse, first, n_pairs // 4, cut, earlier)
    acc, dn2, keep, send, ub1 = ffn(pos, n2, grad_out, wide, ubias, 0, half)
    g1 = Reduction(plan, keep, send)
    acc, dn2, keep, send, ub2 = ffn(pos, n2, grad_out, wide, ubias, half, half, 0, (acc, dn2))
    g2 = Reduction(plan, keep, send)
    acc = step(acc, dn2, g1)
    out, dres, low, dctx, mid = middle(resid, acc, dn2, grad_out, gain2, dbias, wide)
    dctx = step(dctx, dres, g2)
    d1 = back(0, dctx)
    dctx = step(dctx, d1[0], g1)
    d1 = back(n_pairs // 4, dctx, d1)
    n1a, _ = tie(n1, d1[0])
    g3 = Reduction(plan, *weight_grad(pos, (n1a, ctx), ((d1[0], 0), (d1[1], 0), (d1[2], 0), (low, 0), (low, cut // 256)), (0, 0, 0, 1, 1), width=cut))
    dctx, _ = tie(dctx, g3.terms[0])
    dctx = step(dctx, dctx, g1, g2)
    d2 = back(n_pairs // 2, dctx)
    dctx = step(dctx, d2[0], g3)
    d2 = back(n_pairs * 3 // 4, dctx, d2)
    n1b = step(n1, d2[0], g2, g1)
    per = lambda v: v.reshape(total, -1)
    att = jnp.concatenate([d1[3], d2[3]], axis=1)
    ubg = jnp.concatenate([ub1, ub2], axis=1).reshape(blocks, total, rows).transpose(1, 0, 2).reshape(total, -1)
    early = jnp.concatenate([per(att[0]), per(att[1]), per(mid[2]), per(mid[0]), per(mid[1]), per(mid[3]), ubg], axis=1)
    early = jnp.pad(early, ((0, 0), (0, cut - early.shape[1])))
    g4 = Reduction(plan, *weight_grad(pos, (n1b,), ((d2[0], 0), (d2[1], 0), (d2[2], 0)), (0, 0, 0), early, width=cut))
    dres, _ = tie(dres, g4.terms[0])
    dres = step(dres, dres, g3)
    parts = [d1[0], d2[0], d1[1], d2[1], d1[2], d2[2]]
    tokens_grad, end1 = last(parts, w_in, tokens, dres, gain1, 0, R // 512)
    dres = step(dres, end1, g4)
    tokens_grad, end2 = last(parts, w_in, tokens, dres, gain1, R // 512, R // 512, (tokens_grad,))
    end = step(end1 + end2, end2, g3, g4, g2)
    end = step(end, end, g4)
    in2, in1, ffn2, ffn1 = g4.finish(), g3.finish(), g2.finish(), g1.finish()
    late = scatter_small(plan, jnp.concatenate([per(end[0]), per(end[1])], axis=1))
    up_grad = jnp.concatenate([ffn1[:, :F // 2], ffn2[:, :F // 2]], axis=1).reshape(rows, blocks, total, rows).transpose(0, 2, 1, 3).reshape(rows, F)
    down_grad = jnp.concatenate([g[:, F // 2 + b * D:F // 2 + (b + 1) * D] for g in (ffn1, ffn2) for b in range(half)], axis=0)
    out_grad = jnp.concatenate([in1[3 * rows:4 * rows], in1[4 * rows:]], axis=1)
    in_grad = jnp.concatenate([g[k * rows:(k + 1) * rows] for k in range(3) for g in (in1, in2)], axis=1)
    early = in2[3 * rows]
    e = [early[i * n:(i + 1) * n] for i in range(6)]
    return (out, tokens_grad, late[:n], late[n:], in_grad, e[0], e[1], out_grad, e[2], e[3], e[4], up_grad, early[6 * n:6 * n + F // total], down_grad, e[5])

def solution(mesh):
    plan = Plan(mesh.shape["dp"], mesh.shape["fsdp"])
    rows, flat = P(AXES, None), P(AXES)
    ins = (rows, flat, flat, flat, flat, rows, flat, flat, rows, flat, flat, flat, rows, flat, rows, flat, rows)
    outs = (rows, rows, flat, flat, rows, flat, flat, rows, flat, flat, flat, rows, flat, rows, flat)
    return jax.shard_map(functools.partial(body, plan), mesh=mesh, in_specs=ins, out_specs=outs, check_vma=False)
```

time: 851 us -> 488 us (0.57)
  waiting for transfers between devices: 522 us -> 107 us
  local copies, waits for them, and re-layouts: 67 us -> 25.8 us
  other arithmetic: 13.1 us -> 43.8 us
  Pallas kernels: 209 us -> 236 us
  starting transfers between devices: 23.4 us -> 50 us
    reduce_scatter x8 -> x0, waiting for transfers between devices: 221 us -> none  [the longest x4 134 us: scatter(): g = lax.psum_scatter(g, yx, scatter_dimension=0, tiled=True)]
    all_gather x4 -> x1, waiting for transfers between devices: 203 us -> 10.1 us  [body(): lax.all_gather(jnp.concatenate([outproj_weight, up_local] + down_local, a...]
    unnamed x14 -> x1, waiting for transfers between devices: 81.8 us -> 0.02 us
    ppermute x15 -> x44, waiting for transfers between devices: 16.1 us -> 97.2 us  [the longest x26 81.4 us: exchange(): return lax.ppermute(x, AXES, plan.pairs(stage, j))]
    pallas_call x7 -> x11, Pallas kernels: 149 us -> 180 us  [the longest x2 76.4 us: ffn(): pl.pallas_call(functools.partial(ffn_kernel, shards=shards, per=per, F=F,...]
    convert_element_type x4 -> x12, other arithmetic: 6.77 us -> 34.2 us  [cut(): sum((t[j * part:(j + 1) * part].astype(f32) for t in self.terms))]
    ppermute x15 -> x44, starting transfers between devices: 22.9 us -> 49.9 us  [the longest x26 34.5 us: exchange(): return lax.ppermute(x, AXES, plan.pairs(stage, j))]
    reshape x4 -> x11, local copies, waits for them, and re-layouts: 34.9 us -> 9.18 us  [the longest x2 5.14 us: body(): jnp.concatenate([ffn1[:, :F // 2], ffn2[:, :F // 2]], axis=1)]
  transfers between devices with their start and end apart: 28 -> 45, of which waited for: 23 -> 19; matrix products, arithmetic and copies ran while one was open for 5% -> 11% of each run, Pallas kernels for 8% -> 38%
where the time goes in v2:
time: 488 us; the launch traced here: 479 us
  Pallas kernels  236 us (48%)
  waiting for transfers between devices  107 us (22%)
  starting transfers between devices  50 us (10%)
  other arithmetic  43.8 us (9%)
  local copies, waits for them, and re-layouts  25.8 us (5%)
  between operations  16.7 us (3%)
    ppermute x26, waiting for transfers between devices, exchange(): return lax.ppermute(x, AXES, plan.pairs(stage, j))  81.4 us
    pallas_call x2, Pallas kernels, ffn(): pl.pallas_call(functools.partial(ffn_kernel, shards=shards, per=per, F=F,...  76.4 us
    pallas_call x4, Pallas kernels, attend_back(): pl.pallas_call(functools.partial(attend_back_kernel, bq=bq, first=first),...  49.7 us
    pallas_call x1, Pallas kernels, attend(): pl.pallas_call(functools.partial(attend_kernel, bq=bq), grid=(n,), in_spe...  36 us
    ppermute x26, starting transfers between devices, exchange(): return lax.ppermute(x, AXES, plan.pairs(stage, j))  34.5 us
    convert_element_type x12, other arithmetic, cut(): sum((t[j * part:(j + 1) * part].astype(f32) for t in self.terms))  34.2 us
    pallas_call x2, Pallas kernels, last(): pl.pallas_call(functools.partial(last_kernel, count=len(parts)), grid=(st...  19.8 us
    pallas_call x2, Pallas kernels, weight_grad(): pl.pallas_call(functools.partial(weight_grad_kernel, sources=sources, ext...  19.3 us
  transfers between devices with their start and end apart: 45, of which 19 were waited for; matrix products, arithmetic and copies ran while one was open for 11% of the time, Pallas kernels for 38%

profile of v2, /device:TPU:0, one launch (start us, length us, event | category | flops | bytes accessed | tf_op | source)
XLA Modules:
  0.0 479.4 jit_solution(6451172172063231388)
XLA Ops:
  12.4 3.1 collective-permute-start
  17.1 3.1 collective-permute-start.1
  32.8 10.2 %collective-permute-done.5 = bf16[32,3072]{1,0:T(8,128)(2,1)S(1)} collective-permute-done((bf16[32,3072]{1,0:T(8,128)(2,1)S(1)}, bf16[32,3072]{1,0:T(8,128)(2,1)S(1)}, u32[]{:S(2)}, u32[]{:S(2)}) %collective-permute-start.5) | collective-permute-done | bytes 196640 | tf_op jit(solution)/shard_map/ppermute | solution.py:446
  43.0 4.2 collective-permute-done.7
  47.2 10.2 %collective-permute-done.6 = bf16[32,3072]{1,0:T(8,128)(2,1)S(1)} collective-permute-done((bf16[32,3072]{1,0:T(8,128)(2,1)S(1)}, bf16[32,3072]{1,0:T(8,128)(2,1)S(1)}, u32[]{:S(2)}, u32[]{:S(2)}) %collective-permute-start.6) | collective-permute-done | bytes 196640 | tf_op jit(solution)/shard_map/ppermute | solution.py:446
  60.5 25.8 %collective-permute-done.8.refs_1_ = bf16[4,32,3072]{2,1,0:T(8,128)(2,1)S(1)} collective-permute-done((bf16[4,32,3072]{2,1,0:T(8,128)(2,1)S(1)}, bf16[4,32,3072]{2,1,0:T(8,128)(2,1)S(1)}, u32[]{:S(2)}, u32[]{:S(2)}) %collective-permute-start.8) | collective-permute-done | bytes 786464 | tf_op jit(solution)/shard_map/ppermute | solution.py:446
  88.3 3.3 collective-permute-start.11
  93.6 8.4 %collective-permute-done.10.refs_3_ = bf16[4,32,3072]{2,1,0:T(8,128)(2,1)S(1)} collective-permute-done((bf16[4,32,3072]{2,1,0:T(8,128)(2,1)S(1)}, bf16[4,32,3072]{2,1,0:T(8,128)(2,1)S(1)}, u32[]{:S(2)}, u32[]{:S(2)}) %collective-permute-start.10) | collective-permute-done | bytes 786464 | tf_op jit(solution)/shard_map/ppermute | solution.py:446
  108.0 14.5 %project.1 = (bf16[1024,1024]{1,0:T(8,128)(2,1)}, bf16[1024,3072]{1,0:T(8,128)(2,1)}, bf16[1024,3072]{1,0:T(8,128)(2,1)}) custom-call(s32[32]{0:T(128)} %select_reduce_fusion.order_ref, bf16[1024,1024]{1,0:T(8,128)(2,1)} %tokens_ref.7, bf16[1,1024]{1,0:T(2,128)(2,1)} %reshape.170.gain_ref, bf16[1,1024]{1,0:T(2,128)(2,1)} %reshape.171.shift_ref, ...), custom_call_target="tpu_custom_call" | custom-call | flops 1000 | bytes 1000 | tf_op jit(solution)/shard_map/project/pallas_call | solution.py:43
  122.5 36.0 %attend.1 = (bf16[1024,1024]{1,0:T(8,128)(2,1)}, f32[128,1024]{1,0:T(8,128)}) custom-call(s32[1]{0:T(128)S(6)} %copy.75.prefix_ref, s32[1]{0:T(128)S(6)} %copy.76.padding_ref, bf16[1024,3072]{1,0:T(8,128)(2,1)} %get-tuple-element.196.q_ref.k_ref.v_ref, bf16[1024,3072]{1,0:T(8,128)(2,1)} %get-tuple-element.196.q_ref.k_ref.v_ref, ...), custom_call_target="tpu_custom_call" | custom-call | flops 1000 | bytes 1000 | tf_op jit(solution)/shard_map/attend/pallas_call | solution.py:95
  158.6 10.1 %all-gather.2.cloned.1.call-done.weight_ref.up_ref.down_ref = bf16[1024,9216]{1,0:T(8,128)(2,1)} async-done(((bf16[32,9216]{1,0:T(8,128)(2,1)}), bf16[1024,9216]{1,0:T(8,128)(2,1)}) %all-gather.2.cloned.1.call-update) | async-done | bytes 18874384 | tf_op jit(solution)/shard_map/all_gather | solution.py:552
  168.7 7.4 %branch.1 = (f32[1024,1024]{1,0:T(8,128)}, bf16[1024,1024]{1,0:T(8,128)(2,1)}) custom-call(bf16[1024,1024]{1,0:T(8,128)(2,1)} %get-tuple-element.197.ctx_ref.refs_1_, bf16[1024,9216]{1,0:T(8,128)(2,1)} %all-gather.2.cloned.1.call-done.weight_ref.up_ref.down_ref, bf16[1024,1024]{1,0:T(8,128)(2,1)} %tokens_ref.7, bf16[1,1024]{1,0:T(2,128)(2,1)} %reshape.176.bias_ref, ...), custom_call_target="tpu_custom_call" | custom-call | flops 1000 | bytes 1000 | tf_op jit(solution)/shard_map/branch/pallas_call | solution.py:117
  176.1 37.5 %ffn.2 = (f32[1024,1024]{1,0:T(8,128)}, f32[1024,1024]{1,0:T(8,128)}, bf16[16,32,4096]{2,1,0:T(8,128)(2,1)}, bf16[16,32,4096]{2,1,0:T(8,128)(2,1)}, f32[1,2048]{1,0:T(1,128)}) custom-call(s32[32]{0:T(128)} %copy-done.19, bf16[1024,1024]{1,0:T(8,128)(2,1)} %get-tuple-element.199.normed_ref, bf16[1024,1024]{1,0:T(8,128)(2,1)} %go_ref.1, ...), custom_call_target="tpu_custom_call" | custom-call | flops 1000 | bytes 1000 | tf_op jit(solution)/shard_map/ffn/pallas_call | solution.py:217
  213.9 38.9 %ffn.3 = (f32[1024,1024]{1,0:T(8,128)}, f32[1024,1024]{1,0:T(8,128)}, bf16[16,32,4096]{2,1,0:T(8,128)(2,1)}, bf16[16,32,4096]{2,1,0:T(8,128)(2,1)}, f32[1,2048]{1,0:T(1,128)}) custom-call(s32[32]{0:T(128)} %copy-done.19, bf16[1024,1024]{1,0:T(8,128)(2,1)} %get-tuple-element.199.normed_ref, bf16[1024,1024]{1,0:T(8,128)(2,1)} %go_ref.1, ...), custom_call_target="tpu_custom_call" | custom-call | flops 1000 | bytes 1000 | tf_op jit(solution)/shard_map/ffn/pallas_call | solution.py:217
  253.2 4.5 add_convert_fusion.1
  259.8 12.6 %middle.1 = (bf16[1024,1024]{1,0:T(8,128)(2,1)}, f32[1024,1024]{1,0:T(8,128)}, bf16[1024,1024]{1,0:T(8,128)(2,1)}, bf16[1024,1024]{1,0:T(8,128)(2,1)}, f32[8,1024]{1,0:T(8,128)}) custom-call(f32[1024,1024]{1,0:T(8,128)} %get-tuple-element.198.resid_ref, f32[1024,1024]{1,0:T(8,128)} %get-tuple-element.209.outacc_ref, f32[1024,1024]{1,0:T(8,128)} %get-tuple-element.203.dn_ref, ...), custom_call_target="tpu_custom_call" | custom-call | flops 1000 | bytes 1000 | tf_op jit(solution)/shard_map/middle/pallas_call | solution.py:260
  276.1 12.3 %attend_back.4 = (bf16[1024,512]{1,0:T(8,128)(2,1)}, bf16[1024,512]{1,0:T(8,128)(2,1)}, bf16[1024,512]{1,0:T(8,128)(2,1)}, f32[8,512]{1,0:T(8,128)}) custom-call(s32[1]{0:T(128)S(6)} %copy.75.prefix_ref, s32[1]{0:T(128)S(6)} %copy.76.padding_ref, bf16[1024,3072]{1,0:T(8,128)(2,1)} %get-tuple-element.196.q_ref.k_ref.v_ref, ...), custom_call_target="tpu_custom_call" | custom-call | flops 1000 | bytes 1000 | tf_op jit(solution)/shard_map/attend_back/pallas_call | solution.py:313
  288.5 3.3 add_convert_fusion.4
  293.2 12.5 %attend_back.5 = (bf16[1024,512]{1,0:T(8,128)(2,1)}, bf16[1024,512]{1,0:T(8,128)(2,1)}, bf16[1024,512]{1,0:T(8,128)(2,1)}, f32[8,512]{1,0:T(8,128)}) custom-call(s32[1]{0:T(128)S(6)} %copy.75.prefix_ref, s32[1]{0:T(128)S(6)} %copy.76.padding_ref, ...), custom_call_target="tpu_custom_call", output_to_operand_aliasing={{0}: (7, {}), {1}: (8, {}), {2}: (9, {}), {3}: (10, {})} | custom-call | flops 1000 | bytes 1000 | tf_op jit(solution)/shard_map/attend_back/pallas_call | solution.py:313
  305.7 11.3 %weight_grad.2 = (bf16[16,160,512]{2,1,0:T(8,128)(2,1)}, bf16[16,160,512]{2,1,0:T(8,128)(2,1)}) custom-call(s32[32]{0:T(128)} %copy-done.19, bf16[1024,1024]{1,0:T(8,128)(2,1)} %get-tuple-element.283.refs_0_, bf16[1024,1024]{1,0:T(8,128)(2,1)} %get-tuple-element.197.ctx_ref.refs_1_, bf16[1024,512]{1,0:T(8,128)(2,1)} %get-tuple-element.234.refs_2_.refs_0_, ...), custom_call_target="tpu_custom_call" | custom-call | flops 1000 | bytes 1000 | tf_op jit(solution)/shard_map/weight_grad/pallas_call | solution.py:355
  317.7 3.1 add_convert_fusion.11
  320.9 3.4 add_convert_fusion.3
  330.8 12.5 %attend_back.6 = (bf16[1024,512]{1,0:T(8,128)(2,1)}, bf16[1024,512]{1,0:T(8,128)(2,1)}, bf16[1024,512]{1,0:T(8,128)(2,1)}, f32[8,512]{1,0:T(8,128)}) custom-call(s32[1]{0:T(128)S(6)} %copy.75.prefix_ref, s32[1]{0:T(128)S(6)} %copy.76.padding_ref, bf16[1024,3072]{1,0:T(8,128)(2,1)} %get-tuple-element.196.q_ref.k_ref.v_ref, ...), custom_call_target="tpu_custom_call" | custom-call | flops 1000 | bytes 1000 | tf_op jit(solution)/shard_map/attend_back/pallas_call | solution.py:313
  346.1 12.3 %attend_back.7 = (bf16[1024,512]{1,0:T(8,128)(2,1)}, bf16[1024,512]{1,0:T(8,128)(2,1)}, bf16[1024,512]{1,0:T(8,128)(2,1)}, f32[8,512]{1,0:T(8,128)}) custom-call(s32[1]{0:T(128)S(6)} %copy.75.prefix_ref, s32[1]{0:T(128)S(6)} %copy.76.padding_ref, ...), custom_call_target="tpu_custom_call", output_to_operand_aliasing={{0}: (7, {}), {1}: (8, {}), {2}: (9, {}), {3}: (10, {})} | custom-call | flops 1000 | bytes 1000 | tf_op jit(solution)/shard_map/attend_back/pallas_call | solution.py:313
  364.5 8.0 %weight_grad.3 = (bf16[16,112,512]{2,1,0:T(8,128)(2,1)}, bf16[16,112,512]{2,1,0:T(8,128)(2,1)}) custom-call(s32[32]{0:T(128)} %copy-done.19, bf16[1024,1024]{1,0:T(8,128)(2,1)} %get-tuple-element.283.refs_0_, bf16[1024,512]{1,0:T(8,128)(2,1)} %get-tuple-element.266.refs_1_, bf16[1024,512]{1,0:T(8,128)(2,1)} %get-tuple-element.284.refs_2_.refs_3_, ...), custom_call_target="tpu_custom_call" | custom-call | flops 1000 | bytes 1000 | tf_op jit(solution)/shard_map/weight_grad/pallas_call | solution.py:355
  377.5 12.8 %collective-permute-done.25 = bf16[8,160,512]{2,1,0:T(8,128)(2,1)S(1)} collective-permute-done((bf16[8,160,512]{2,1,0:T(8,128)(2,1)}, bf16[8,160,512]{2,1,0:T(8,128)(2,1)S(1)}, u32[]{:S(2)}, u32[]{:S(2)}) %collective-permute-start.25) | collective-permute-done | bytes 1310752 | tf_op jit(solution)/shard_map/ppermute | solution.py:446
  394.2 9.7 %last.2 = (bf16[1024,1024]{1,0:T(8,128)(2,1)}, f32[8,1024]{1,0:T(8,128)}) custom-call(bf16[1024,3072]{1,0:T(8,128)(2,1)} %get-tuple-element.211.w_ref, bf16[1024,1024]{1,0:T(8,128)(2,1)} %tokens_ref.7, f32[1024,1024]{1,0:T(8,128)} %get-tuple-element.306.dres_ref, bf16[1,1024]{1,0:T(2,128)(2,1)} %reshape.170.gain_ref, ...), custom_call_target="tpu_custom_call" | custom-call | flops 1000 | bytes 1000 | tf_op jit(solution)/shard_map/last/pallas_call | solution.py:394
  409.4 10.1 %last.3 = (bf16[1024,1024]{1,0:T(8,128)(2,1)}, f32[8,1024]{1,0:T(8,128)}) custom-call(bf16[1024,3072]{1,0:T(8,128)(2,1)} %get-tuple-element.211.w_ref, bf16[1024,1024]{1,0:T(8,128)(2,1)} %tokens_ref.7, f32[1024,1024]{1,0:T(8,128)} %get-tuple-element.306.dres_ref, bf16[1,1024]{1,0:T(2,128)(2,1)} %reshape.170.gain_ref, ...), custom_call_target="tpu_custom_call", output_to_operand_aliasing={{0}: (10, {})} | custom-call | flops 1000 | bytes 1000 | tf_op jit(solution)/shard_map/last/pallas_call | solution.py:394
  433.1 3.1 copy.48
  436.3 4.5 reshape.185
  452.8 3.8 collective-permute-done.36
  462.3 6.5 %collective-permute-done.42 = bf16[1,112,512]{2,1,0:T(8,128)(2,1)S(1)} collective-permute-done((bf16[1,112,512]{2,1,0:T(8,128)(2,1)S(1)}, bf16[1,112,512]{2,1,0:T(8,128)(2,1)S(1)}, u32[]{:S(2)}, u32[]{:S(2)}) %collective-permute-start.42) | collective-permute-done | bytes 114720 | tf_op jit(solution)/shard_map/ppermute | solution.py:446
  (238 shorter events, 103.4 us)
Async XLA Ops:
  7.2 161.5 %all-gather.2.cloned.1.call-start = ((), (), s32[]{:S(2)}) async-start(), calls=%async_computation | async-start | bytes 19464192 | tf_op jit(solution)/shard_map/all_gather | solution.py:552
  24.9 18.1 %collective-permute-start.5 = (bf16[32,3072]{1,0:T(8,128)(2,1)S(1)}, bf16[32,3072]{1,0:T(8,128)(2,1)S(1)}, u32[]{:S(2)}, u32[]{:S(2)}) collective-permute-start(bf16[32,3072]{1,0:T(8,128)(2,1)S(1)} %copy-done.15), channel_id=1, source_target_pairs={{0,1},{1,0},{2,3},{3,2},{4,5},{5,4},{6,7},{7,6},{8,9},{9,8},{10,11... | collective-permute-start | bytes 589832 | tf_op jit(solution)/shard_map/ppermute | solution.py:446
  26.4 20.7 %collective-permute-start.7 = (bf16[32,3072]{1,0:T(8,128)(2,1)S(1)}, bf16[32,3072]{1,0:T(8,128)(2,1)S(1)}, u32[]{:S(2)}, u32[]{:S(2)}) collective-permute-start(bf16[32,3072]{1,0:T(8,128)(2,1)S(1)} %copy-done.15), channel_id=1, source_target_pairs={{0,3},{1,2},{2,1},{3,0},{4,7},{5,6},{6,5},{7,4},{8,11},{9,10},{10,... | collective-permute-start | bytes 589832 | tf_op jit(solution)/shard_map/ppermute | solution.py:446
  28.9 28.4 %collective-permute-start.6 = (bf16[32,3072]{1,0:T(8,128)(2,1)S(1)}, bf16[32,3072]{1,0:T(8,128)(2,1)S(1)}, u32[]{:S(2)}, u32[]{:S(2)}) collective-permute-start(bf16[32,3072]{1,0:T(8,128)(2,1)S(1)} %copy-done.15), channel_id=1, source_target_pairs={{0,2},{1,3},{2,0},{3,1},{4,6},{5,7},{6,4},{7,5},{8,10},{9,11},{10,... | collective-permute-start | bytes 589832 | tf_op jit(solution)/shard_map/ppermute | solution.py:446
  57.5 28.8 %collective-permute-start.8 = (bf16[4,32,3072]{2,1,0:T(8,128)(2,1)S(1)}, bf16[4,32,3072]{2,1,0:T(8,128)(2,1)S(1)}, u32[]{:S(2)}, u32[]{:S(2)}) collective-permute-start(bf16[4,32,3072]{2,1,0:T(8,128)(2,1)S(1)} %pad_maximum_fusion.refs_0_), channel_id=1, source_target_pairs={{0,16},{1,17},{2,18},{3,19},{4,12},{5,13},{6,14},{7,15},{8,24},{9,... | collective-permute-start | bytes 2359304 | tf_op jit(solution)/shard_map/ppermute | solution.py:446
  59.0 34.6 %collective-permute-start.9 = (bf16[4,32,3072]{2,1,0:T(8,128)(2,1)S(1)}, bf16[4,32,3072]{2,1,0:T(8,128)(2,1)S(1)}, u32[]{:S(2)}, u32[]{:S(2)}) collective-permute-start(bf16[4,32,3072]{2,1,0:T(8,128)(2,1)S(1)} %pad_maximum_fusion.refs_0_), channel_id=1, source_target_pairs={{0,8},{1,9},{2,10},{3,11},{4,20},{5,21},{6,22},{7,23},{8,0},{9,1},... | collective-permute-start | bytes 2359304 | tf_op jit(solution)/shard_map/ppermute | solution.py:446
  86.3 15.8 %collective-permute-start.10 = (bf16[4,32,3072]{2,1,0:T(8,128)(2,1)S(1)}, bf16[4,32,3072]{2,1,0:T(8,128)(2,1)S(1)}, u32[]{:S(2)}, u32[]{:S(2)}) collective-permute-start(bf16[4,32,3072]{2,1,0:T(8,128)(2,1)S(1)} %collective-permute-done.8.refs_1_), channel_id=1, source_target_pairs={{0,8},{1,9},{2,10},{3,11},{4,20},{5,21},{6,22},{7,23},{8,0},{9,1},... | collective-permute-start | bytes 2359304 | tf_op jit(solution)/shard_map/ppermute | solution.py:446
  88.3 19.6 %collective-permute-start.11 = (bf16[4,32,3072]{2,1,0:T(8,128)(2,1)S(1)}, bf16[4,32,3072]{2,1,0:T(8,128)(2,1)}, u32[]{:S(2)}, u32[]{:S(2)}) collective-permute-start(bf16[4,32,3072]{2,1,0:T(8,128)(2,1)S(1)} %pad_maximum_fusion.refs_0_), channel_id=1, source_target_pairs={{0,4},{1,5},{2,6},{3,7},{4,0},{5,1},{6,2},{7,3},{8,12},{9,13},{10,... | collective-permute-start | bytes 2359304 | tf_op jit(solution)/shard_map/ppermute | solution.py:443
  91.6 16.3 %collective-permute-start.12 = (bf16[4,32,3072]{2,1,0:T(8,128)(2,1)S(1)}, bf16[4,32,3072]{2,1,0:T(8,128)(2,1)}, u32[]{:S(2)}, u32[]{:S(2)}) collective-permute-start(bf16[4,32,3072]{2,1,0:T(8,128)(2,1)S(1)} %collective-permute-done.8.refs_1_), channel_id=1, source_target_pairs={{0,4},{1,5},{2,6},{3,7},{4,0},{5,1},{6,2},{7,3},{8,12},{9,13},{10,... | collective-permute-start | bytes 2359304 | tf_op jit(solution)/shard_map/ppermute | solution.py:443
  93.6 14.3 %collective-permute-start.13 = (bf16[4,32,3072]{2,1,0:T(8,128)(2,1)S(1)}, bf16[4,32,3072]{2,1,0:T(8,128)(2,1)}, u32[]{:S(2)}, u32[]{:S(2)}) collective-permute-start(bf16[4,32,3072]{2,1,0:T(8,128)(2,1)S(1)} %collective-permute-done.9.refs_2_), channel_id=1, source_target_pairs={{0,4},{1,5},{2,6},{3,7},{4,0},{5,1},{6,2},{7,3},{8,12},{9,13},{10,... | collective-permute-start | bytes 2359304 | tf_op jit(solution)/shard_map/ppermute | solution.py:443
  213.6 39.6 %collective-permute-start.15 = (bf16[16,32,4096]{2,1,0:T(8,128)(2,1)}, bf16[16,32,4096]{2,1,0:T(8,128)(2,1)}, u32[]{:S(2)}, u32[]{:S(2)}) collective-permute-start(bf16[16,32,4096]{2,1,0:T(8,128)(2,1)} %get-tuple-element.205), channel_id=1, source_target_pairs={{0,4},{1,5},{2,6},{3,7},{4,0},{5,1},{6,2},{7,3},{8,12},{9,13},{10,... | collective-permute-start | bytes 12582920 | tf_op jit(solution)/shard_map/ppermute | solution.py:443
  252.8 19.6 %collective-permute-start.16 = (bf16[16,32,4096]{2,1,0:T(8,128)(2,1)}, bf16[16,32,4096]{2,1,0:T(8,128)(2,1)}, u32[]{:S(2)}, u32[]{:S(2)}) collective-permute-start(bf16[16,32,4096]{2,1,0:T(8,128)(2,1)} %get-tuple-element.216), channel_id=1, source_target_pairs={{0,4},{1,5},{2,6},{3,7},{4,0},{5,1},{6,2},{7,3},{8,12},{9,13},{10,... | collective-permute-start | bytes 12582920 | tf_op jit(solution)/shard_map/ppermute | solution.py:443
  257.7 30.8 %collective-permute-start.17 = (bf16[8,32,4096]{2,1,0:T(8,128)(2,1)}, bf16[8,32,4096]{2,1,0:T(8,128)(2,1)}, u32[]{:S(2)}, u32[]{:S(2)}) collective-permute-start(bf16[8,32,4096]{2,1,0:T(8,128)(2,1)} %add_convert_fusion.1), channel_id=1, source_target_pairs={{0,8},{1,9},{2,10},{3,11},{4,20},{5,21},{6,22},{7,23},{8,0},{9,1},... | collective-permute-start | bytes 6291464 | tf_op jit(solution)/shard_map/ppermute | solution.py:446
  275.4 42.3 %collective-permute-start.19 = (bf16[8,32,4096]{2,1,0:T(8,128)(2,1)S(1)}, bf16[8,32,4096]{2,1,0:T(8,128)(2,1)}, u32[]{:S(2)}, u32[]{:S(2)}) collective-permute-start(bf16[8,32,4096]{2,1,0:T(8,128)(2,1)S(1)} %add_convert_fusion), channel_id=1, source_target_pairs={{0,8},{1,9},{2,10},{3,11},{4,20},{5,21},{6,22},{7,23},{8,0},{9,1},... | collective-permute-start | bytes 6291464 | tf_op jit(solution)/shard_map/ppermute | solution.py:446
  291.8 26.0 %collective-permute-start.18 = (bf16[4,32,4096]{2,1,0:T(8,128)(2,1)}, bf16[4,32,4096]{2,1,0:T(8,128)(2,1)S(1)}, u32[]{:S(2)}, u32[]{:S(2)}) collective-permute-start(bf16[4,32,4096]{2,1,0:T(8,128)(2,1)} %add_convert_fusion.4), channel_id=1, source_target_pairs={{0,16},{1,17},{2,18},{3,19},{4,12},{5,13},{6,14},{7,15},{8,24},{9,... | collective-permute-start | bytes 3145736 | tf_op jit(solution)/shard_map/ppermute | solution.py:446
  317.1 26.3 %collective-permute-start.20 = (bf16[16,160,512]{2,1,0:T(8,128)(2,1)}, bf16[16,160,512]{2,1,0:T(8,128)(2,1)}, u32[]{:S(2)}, u32[]{:S(2)}) collective-permute-start(bf16[16,160,512]{2,1,0:T(8,128)(2,1)} %get-tuple-element.258), channel_id=1, source_target_pairs={{0,4},{1,5},{2,6},{3,7},{4,0},{5,1},{6,2},{7,3},{8,12},{9,13},{10,... | collective-permute-start | bytes 7864328 | tf_op jit(solution)/shard_map/ppermute | solution.py:443
  324.3 35.0 %collective-permute-start.21 = (bf16[4,32,4096]{2,1,0:T(8,128)(2,1)}, bf16[4,32,4096]{2,1,0:T(8,128)(2,1)}, u32[]{:S(2)}, u32[]{:S(2)}) collective-permute-start(bf16[4,32,4096]{2,1,0:T(8,128)(2,1)} %add_convert_fusion.3), channel_id=1, source_target_pairs={{0,16},{1,17},{2,18},{3,19},{4,12},{5,13},{6,14},{7,15},{8,24},{9,... | collective-permute-start | bytes 3145736 | tf_op jit(solution)/shard_map/ppermute | solution.py:446
  326.4 32.8 %collective-permute-start.22 = (bf16[1,32,4096]{2,1,0:T(8,128)(2,1)}, bf16[1,32,4096]{2,1,0:T(8,128)(2,1)S(1)}, u32[]{:S(2)}, u32[]{:S(2)}) collective-permute-start(bf16[1,32,4096]{2,1,0:T(8,128)(2,1)} %get-tuple-element.275), channel_id=1, source_target_pairs={{0,1},{1,0},{2,3},{3,2},{4,5},{5,4},{6,7},{7,6},{8,9},{9,8},{10,11... | collective-permute-start | bytes 786440 | tf_op jit(solution)/shard_map/ppermute | solution.py:446
  326.6 32.6 %collective-permute-start.23 = (bf16[1,32,4096]{2,1,0:T(8,128)(2,1)}, bf16[1,32,4096]{2,1,0:T(8,128)(2,1)S(1)}, u32[]{:S(2)}, u32[]{:S(2)}) collective-permute-start(bf16[1,32,4096]{2,1,0:T(8,128)(2,1)} %get-tuple-element.276), channel_id=1, source_target_pairs={{0,2},{1,3},{2,0},{3,1},{4,6},{5,7},{6,4},{7,5},{8,10},{9,11},{10,... | collective-permute-start | bytes 786440 | tf_op jit(solution)/shard_map/ppermute | solution.py:446
  328.4 30.8 %collective-permute-start.24 = (bf16[1,32,4096]{2,1,0:T(8,128)(2,1)}, bf16[1,32,4096]{2,1,0:T(8,128)(2,1)S(1)}, u32[]{:S(2)}, u32[]{:S(2)}) collective-permute-start(bf16[1,32,4096]{2,1,0:T(8,128)(2,1)} %get-tuple-element.277), channel_id=1, source_target_pairs={{0,3},{1,2},{2,1},{3,0},{4,7},{5,6},{6,5},{7,4},{8,11},{9,10},{10,... | collective-permute-start | bytes 786440 | tf_op jit(solution)/shard_map/ppermute | solution.py:446
  372.5 31.4 %collective-permute-start.26 = (bf16[16,112,512]{2,1,0:T(8,128)(2,1)}, bf16[16,112,512]{2,1,0:T(8,128)(2,1)}, u32[]{:S(2)}, u32[]{:S(2)}) collective-permute-start(bf16[16,112,512]{2,1,0:T(8,128)(2,1)} %get-tuple-element.302), channel_id=1, source_target_pairs={{0,4},{1,5},{2,6},{3,7},{4,0},{5,1},{6,2},{7,3},{8,12},{9,13},{10,... | collective-permute-start | bytes 5505032 | tf_op jit(solution)/shard_map/ppermute | solution.py:443
  372.5 17.9 %collective-permute-start.25 = (bf16[8,160,512]{2,1,0:T(8,128)(2,1)}, bf16[8,160,512]{2,1,0:T(8,128)(2,1)S(1)}, u32[]{:S(2)}, u32[]{:S(2)}) collective-permute-start(bf16[8,160,512]{2,1,0:T(8,128)(2,1)} %add_convert_fusion.2), channel_id=1, source_target_pairs={{0,8},{1,9},{2,10},{3,11},{4,20},{5,21},{6,22},{7,23},{8,0},{9,1},... | collective-permute-start | bytes 3932168 | tf_op jit(solution)/shard_map/ppermute | solution.py:446
  373.2 47.2 %collective-permute-start.29 = (bf16[1,32,4096]{2,1,0:T(8,128)(2,1)}, bf16[1,32,4096]{2,1,0:T(8,128)(2,1)S(1)}, u32[]{:S(2)}, u32[]{:S(2)}) collective-permute-start(bf16[1,32,4096]{2,1,0:T(8,128)(2,1)} %get-tuple-element.321), channel_id=1, source_target_pairs={{0,1},{1,0},{2,3},{3,2},{4,5},{5,4},{6,7},{7,6},{8,9},{9,8},{10,11... | collective-permute-start | bytes 786440 | tf_op jit(solution)/shard_map/ppermute | solution.py:446
  373.2 47.2 %collective-permute-start.30 = (bf16[1,32,4096]{2,1,0:T(8,128)(2,1)}, bf16[1,32,4096]{2,1,0:T(8,128)(2,1)S(1)}, u32[]{:S(2)}, u32[]{:S(2)}) collective-permute-start(bf16[1,32,4096]{2,1,0:T(8,128)(2,1)} %get-tuple-element.322), channel_id=1, source_target_pairs={{0,2},{1,3},{2,0},{3,1},{4,6},{5,7},{6,4},{7,5},{8,10},{9,11},{10,... | collective-permute-start | bytes 786440 | tf_op jit(solution)/shard_map/ppermute | solution.py:446
  375.1 45.2 %collective-permute-start.31 = (bf16[1,32,4096]{2,1,0:T(8,128)(2,1)}, bf16[1,32,4096]{2,1,0:T(8,128)(2,1)}, u32[]{:S(2)}, u32[]{:S(2)}) collective-permute-start(bf16[1,32,4096]{2,1,0:T(8,128)(2,1)} %get-tuple-element.323), channel_id=1, source_target_pairs={{0,3},{1,2},{2,1},{3,0},{4,7},{5,6},{6,5},{7,4},{8,11},{9,10},{10,... | collective-permute-start | bytes 786440 | tf_op jit(solution)/shard_map/ppermute | solution.py:446
  393.6 26.7 %collective-permute-start.27 = (bf16[4,160,512]{2,1,0:T(8,128)(2,1)}, bf16[4,160,512]{2,1,0:T(8,128)(2,1)}, u32[]{:S(2)}, u32[]{:S(2)}) collective-permute-start(bf16[4,160,512]{2,1,0:T(8,128)(2,1)} %add_convert_fusion.6), channel_id=1, source_target_pairs={{0,16},{1,17},{2,18},{3,19},{4,12},{5,13},{6,14},{7,15},{8,24},{9,... | collective-permute-start | bytes 1966088 | tf_op jit(solution)/shard_map/ppermute | solution.py:446
  406.6 13.8 %collective-permute-start.28 = (bf16[8,112,512]{2,1,0:T(8,128)(2,1)}, bf16[8,112,512]{2,1,0:T(8,128)(2,1)}, u32[]{:S(2)}, u32[]{:S(2)}) collective-permute-start(bf16[8,112,512]{2,1,0:T(8,128)(2,1)} %add_convert_fusion.5), channel_id=1, source_target_pairs={{0,8},{1,9},{2,10},{3,11},{4,20},{5,21},{6,22},{7,23},{8,0},{9,1},... | collective-permute-start | bytes 2752520 | tf_op jit(solution)/shard_map/ppermute | solution.py:446
  425.1 19.0 %collective-permute-start.38 = (bf16[1,160,512]{2,1,0:T(8,128)(2,1)}, bf16[1,160,512]{2,1,0:T(8,128)(2,1)}, u32[]{:S(2)}, u32[]{:S(2)}) collective-permute-start(bf16[1,160,512]{2,1,0:T(8,128)(2,1)} %get-tuple-element.347), channel_id=1, source_target_pairs={{0,1},{1,0},{2,3},{3,2},{4,5},{5,4},{6,7},{7,6},{8,9},{9,8},{10,11... | collective-permute-start | bytes 491528 | tf_op jit(solution)/shard_map/ppermute | solution.py:446
  425.1 19.0 %collective-permute-start.39 = (bf16[1,160,512]{2,1,0:T(8,128)(2,1)}, bf16[1,160,512]{2,1,0:T(8,128)(2,1)}, u32[]{:S(2)}, u32[]{:S(2)}) collective-permute-start(bf16[1,160,512]{2,1,0:T(8,128)(2,1)} %get-tuple-element.348), channel_id=1, source_target_pairs={{0,2},{1,3},{2,0},{3,1},{4,6},{5,7},{6,4},{7,5},{8,10},{9,11},{10,... | collective-permute-start | bytes 491528 | tf_op jit(solution)/shard_map/ppermute | solution.py:446
  427.1 17.0 %collective-permute-start.40 = (bf16[1,160,512]{2,1,0:T(8,128)(2,1)}, bf16[1,160,512]{2,1,0:T(8,128)(2,1)}, u32[]{:S(2)}, u32[]{:S(2)}) collective-permute-start(bf16[1,160,512]{2,1,0:T(8,128)(2,1)} %get-tuple-element.349), channel_id=1, source_target_pairs={{0,3},{1,2},{2,1},{3,0},{4,7},{5,6},{6,5},{7,4},{8,11},{9,10},{10,... | collective-permute-start | bytes 491528 | tf_op jit(solution)/shard_map/ppermute | solution.py:446
  429.5 12.1 %collective-permute-start.32 = (bf16[4,112,512]{2,1,0:T(8,128)(2,1)}, bf16[4,112,512]{2,1,0:T(8,128)(2,1)}, u32[]{:S(2)}, u32[]{:S(2)}) collective-permute-start(bf16[4,112,512]{2,1,0:T(8,128)(2,1)} %add_convert_fusion.7), channel_id=1, source_target_pairs={{0,16},{1,17},{2,18},{3,19},{4,12},{5,13},{6,14},{7,15},{8,24},{9,... | collective-permute-start | bytes 1376264 | tf_op jit(solution)/shard_map/ppermute | solution.py:446
  458.7 10.2 %collective-permute-start.42 = (bf16[1,112,512]{2,1,0:T(8,128)(2,1)S(1)}, bf16[1,112,512]{2,1,0:T(8,128)(2,1)S(1)}, u32[]{:S(2)}, u32[]{:S(2)}) collective-permute-start(bf16[1,112,512]{2,1,0:T(8,128)(2,1)S(1)} %get-tuple-element.355), channel_id=1, source_target_pairs={{0,2},{1,3},{2,0},{3,1},{4,6},{5,7},{6,4},{7,5},{8,10},{9,11},{10,... | collective-permute-start | bytes 344072 | tf_op jit(solution)/shard_map/ppermute | solution.py:446
  (46 other events, 310.1 us)
Sparse Core Ops, SparseCore 0:
  12.3 156.2 all-gather.1

commit v3 on v2

v3 whole, which is shorter than its diff:
```python
import functools, math
import jax, jax.numpy as jnp
from jax import lax
from jax.sharding import PartitionSpec as P
from jax.experimental import pallas as pl
from jax.experimental.pallas import tpu as pltpu
HEADS=16
EPSILON = 1e-05
NEGATIVE = -1000000000.0
bf16=jnp.bfloat16; f32=jnp.float32
VMEM_LIMIT=60*1024*1024
HINT=pl.CostEstimate(flops=1000, bytes_accessed=1000, transcendentals=0)
def cp(n=1): return pltpu.CompilerParams(dimension_semantics=("arbitrary",)*n, vmem_limit_bytes=VMEM_LIMIT)
def dot(a,b): return lax.dot_general(a,b,(((1,),(0,)),((),())),preferred_element_type=f32)
def dot_nt(a,b): return lax.dot_general(a,b,(((1,),(1,)),((),())),preferred_element_type=f32)
def dot_tn(a,b): return lax.dot_general(a,b,(((0,),(0,)),((),())),preferred_element_type=f32)

GAIN1, SHIFT1, QBIAS, VBIAS, OBIAS, GAIN2, SHIFT2, DBIAS, UBIAS = range(9)

def row_of(ref, k):
    return ref[k:k + 1, :]

def norm_kernel(tokens_ref, out_ref):
    x = tokens_ref[...].astype(f32)
    center = x - jnp.mean(x, axis=-1, keepdims=True)
    spread = jnp.mean(center * center, axis=-1, keepdims=True)
    out_ref[...] = center * lax.rsqrt(spread + EPSILON)

def norm(tokens, tm=256):
    R, D = tokens.shape
    rows = pl.BlockSpec((tm, D), lambda i: (i, 0))
    return pl.pallas_call(
        norm_kernel, grid=(R // tm,), in_specs=[rows], out_specs=rows, out_shape=jax.ShapeDtypeStruct((R, D), f32),
        compiler_params=cp(), name="norm", cost_estimate=HINT,
    )(tokens)

def in_order(order_ref, pieces, whole_ref):
    n, rows, _ = pieces[0].shape
    for p, piece in enumerate(pieces):
        for i in range(n):
            whole_ref[pl.ds(pl.multiple_of(order_ref[p * n + i] * rows, rows), rows), :] = piece[i]

def project_kernel(order_ref, xhat_ref, *refs, count):
    pieces, sides = refs[:count], refs[count:2 * count]
    normed_ref, out_ref, weight_ref, vec_ref, side_ref, all_ref = refs[2 * count:]
    step = pl.program_id(0)
    @pl.when(step == 0)
    def _():
        in_order(order_ref, sides, side_ref)
        all_ref[...] = jnp.transpose(side_ref[...].astype(f32))
        vec_ref[...] = all_ref[:16, :]
        normed_ref[...] = (xhat_ref[...] * all_ref[GAIN1:GAIN1 + 1, :] + all_ref[SHIFT1:SHIFT1 + 1, :]).astype(bf16)
    in_order(order_ref, pieces, weight_ref)
    D = normed_ref.shape[1]
    tn = out_ref.shape[1]
    third = pl.num_programs(0) // 3
    at = pl.ds(pl.multiple_of(lax.rem(step, D // tn) * tn, tn), tn)
    bias = jnp.where(step < third, all_ref[QBIAS:QBIAS + 1, at], jnp.where(step < 2 * third, 0.0, all_ref[VBIAS:VBIAS + 1, at]))
    factor = jnp.where(step < third, 0.125, 1.0)
    out = dot(normed_ref[...], weight_ref[...]) + bias
    out_ref[...] = (out * factor).astype(bf16)

def project(order, xhat, pieces, tn=512):
    R, D = xhat.shape
    n, rows, width = pieces[0].shape
    N = 3 * D
    cols = pl.BlockSpec((R, tn), lambda j: (0, j))
    full = pl.BlockSpec((R, D), lambda j: (0, 0))
    return pl.pallas_call(
        functools.partial(project_kernel, count=len(pieces)), grid=(N // tn,),
        in_specs=[pl.BlockSpec(memory_space=pltpu.SMEM), full]
        + [pl.BlockSpec((n, rows, tn), lambda j: (0, 0, j))] * len(pieces)
        + [pl.BlockSpec((n, rows, 128), lambda j: (0, 0, width // 128 - 1))] * len(pieces),
        out_specs=[full, cols, pl.BlockSpec((D, tn), lambda j: (0, j)), pl.BlockSpec((16, D), lambda j: (0, 0))],
        out_shape=[jax.ShapeDtypeStruct((R, D), bf16), jax.ShapeDtypeStruct((R, N), bf16), jax.ShapeDtypeStruct((D, N), bf16),
                   jax.ShapeDtypeStruct((16, D), f32)],
        scratch_shapes=[pltpu.VMEM((D, 128), bf16), pltpu.VMEM((128, D), f32)],
        compiler_params=cp(), name="project", cost_estimate=HINT,
    )(order, xhat, *pieces, *pieces)

def key_bias(prefix, limit, lo, q0, bq, transposed, diagonal):
    shape = (bq, bq)
    kd = 0 if transposed else 1
    k = lo + lax.broadcasted_iota(jnp.int32, shape, kd)
    ok = k < limit
    if diagonal:
        q = q0 + lax.broadcasted_iota(jnp.int32, shape, 1 - kd)
        ok = ok & ((k < prefix) | (k <= q))
    return jnp.where(ok, 0.0, NEGATIVE)

def attend_kernel(prefix_ref, padding_ref, q_ref, k_ref, v_ref, out_ref, lse_ref, bias_ref, *, bq):
    L = q_ref.shape[0]
    step = pl.program_id(0)
    prefix = prefix_ref[0]
    limit = L - padding_ref[0]
    n = L // bq
    lane = lax.broadcasted_iota(jnp.int32, (1, 128), 1)
    @pl.when(step == 0)
    def _():
        for b in range(n):
            bias_ref[b] = key_bias(prefix, limit, b * bq, b * bq, bq, True, True)
    vT = jnp.transpose(v_ref[...])
    ones = jnp.ones((16, L), bf16)
    values = [jnp.concatenate([vT[64 * h:64 * h + 64], ones], axis=0) for h in range(2)]
    for b in range(n):
        start, stop = b * bq, (b + 1) * bq
        q = q_ref[start:stop, :]
        both = jnp.concatenate([jnp.where(lane < 64, q, 0), jnp.where(lane >= 64, q, 0)], axis=0).astype(bf16)
        s = []
        for kb in range(b + 1):
            t = dot_nt(k_ref[kb * bq:(kb + 1) * bq, :], both)
            if kb == b:
                t = t + jnp.concatenate([bias_ref[b], bias_ref[b]], axis=1)
            elif (kb + 1) * bq > L - 384:
                kk = kb * bq + lax.broadcasted_iota(jnp.int32, (bq, 1), 0)
                t = t + jnp.where(kk < limit, 0.0, NEGATIVE)
            s.append(t)
        m = functools.reduce(jnp.maximum, [jnp.max(t, axis=0, keepdims=True) for t in s])
        acc = [None, None]
        for kb in range(b + 1):
            e = jnp.exp(s[kb] - m).astype(bf16)
            for h in range(2):
                t = dot(values[h][:, kb * bq:(kb + 1) * bq], e[:, h * bq:(h + 1) * bq])
                acc[h] = t if acc[h] is None else acc[h] + t
        ctx = [a[:64] * (1.0 / a[64:65]) for a in acc]
        out_ref[start:stop, :] = jnp.transpose(jnp.concatenate(ctx, axis=0)).astype(bf16)
        for h in range(2):
            lse_ref[pl.ds(2 * step + h, 1), start:stop] = m[:, h * bq:(h + 1) * bq] + jnp.log(acc[h][64:65])

def attend(prefix, padding, qkv, bq=256):
    L = qkv.shape[0]
    D = qkv.shape[1] // 3
    n = D // 128
    smem = pl.BlockSpec(memory_space=pltpu.SMEM)
    col = lambda off: pl.BlockSpec((L, 128), lambda j: (0, j + off))
    return pl.pallas_call(
        functools.partial(attend_kernel, bq=bq), grid=(n,),
        in_specs=[smem, smem, col(0), col(n), col(2 * n)],
        out_specs=[col(0), pl.BlockSpec((2 * n, L), lambda j: (0, 0))],
        out_shape=[jax.ShapeDtypeStruct((L, D), bf16), jax.ShapeDtypeStruct((2 * n, L), f32)],
        scratch_shapes=[pltpu.VMEM((L // bq, bq, bq), f32)],
        compiler_params=cp(), name="attend",
        cost_estimate=HINT,
    )(prefix, padding, qkv, qkv, qkv)

def branch_kernel(order_ref, ctx_ref, tokens_ref, vec_ref, *refs):
    *pieces, resid_ref, normed_ref, weight_ref = refs
    @pl.when(pl.program_id(0) == 0)
    def _():
        in_order(order_ref, pieces, weight_ref)
    resid = tokens_ref[...].astype(f32) + (dot(ctx_ref[...], weight_ref[...]) + row_of(vec_ref, OBIAS))
    center = resid - jnp.mean(resid, axis=-1, keepdims=True)
    spread = jnp.mean(center * center, axis=-1, keepdims=True)
    normed = center * lax.rsqrt(spread + EPSILON) * row_of(vec_ref, GAIN2) + row_of(vec_ref, SHIFT2)
    resid_ref[...] = resid
    normed_ref[...] = normed.astype(bf16)

def branch(order, ctx, tokens, vecs, pieces, tm=256):
    R, D = ctx.shape
    n, high, _ = pieces[0].shape
    rows = pl.BlockSpec((tm, D), lambda i: (i, 0))
    return pl.pallas_call(
        branch_kernel, grid=(R // tm,),
        in_specs=[pl.BlockSpec(memory_space=pltpu.SMEM), rows, rows, pl.BlockSpec(vecs.shape, lambda i: (0, 0))]
        + [pl.BlockSpec((n, high, D), lambda i: (0, 0, 3))] * len(pieces),
        out_specs=[rows, rows, pl.BlockSpec((D, D), lambda i: (0, 0))],
        out_shape=[jax.ShapeDtypeStruct((R, D), f32), jax.ShapeDtypeStruct((R, D), bf16), jax.ShapeDtypeStruct((D, D), bf16)],
        compiler_params=cp(), name="branch", cost_estimate=HINT,
    )(order, ctx, tokens, vecs, *pieces)

def ffn_kernel(pos_ref, normed_ref, grad_ref, vec_ref, up_ref, down_ref, out_ref, dn_ref, keep1_ref, send1_ref, keep2_ref, send2_ref, biasg_ref,
               ups_ref, dns_ref, up_sem, dn_sem, *, shards, per, blocks):
    step = pl.program_id(0)
    last = pl.num_programs(0) - 1
    D = normed_ref.shape[1]
    tf = ups_ref.shape[3]
    half = shards // 2
    rows = D // shards
    each = blocks // 2
    slot = lax.rem(step, 2)
    block = lax.div(step, per)
    bslot = lax.rem(block, 2)
    groups = ((keep1_ref, send1_ref), (keep2_ref, send2_ref))

    def up_copies(slot, step, group):
        cols = pl.ds(pl.multiple_of(step * tf - group * each * D, tf), tf)
        return [pltpu.make_async_copy(ups_ref.at[slot, pl.ds(k * half, half)], groups[group][k].at[:, :, cols], up_sem.at[slot, k]) for k in range(2)]

    def down_copies(bslot, block, group):
        cols = pl.ds(pl.multiple_of((each + block - group * each) * D, D), D)
        return [pltpu.make_async_copy(dns_ref.at[bslot, pl.ds(k * half, half)], groups[group][k].at[:, :, cols], dn_sem.at[bslot, k]) for k in range(2)]

    def each_group(block, do):
        for group in range(2):
            pl.when((block >= group * each) & (block < (group + 1) * each))(functools.partial(do, group))

    def start_up(group):
        for c in up_copies(slot, step, group):
            c.start()

    def wait_up(slot, step):
        def do(group):
            for c in up_copies(slot, step, group):
                c.wait()
        each_group(lax.div(step, per), do)

    def start_down(group):
        for c in down_copies(bslot, block, group):
            c.start()

    def wait_down(bslot, block):
        def do(group):
            for c in down_copies(bslot, block, group):
                c.wait()
        each_group(block, do)

    @pl.when(step == 0)
    def _():
        out_ref[...] = jnp.zeros_like(out_ref)
        dn_ref[...] = jnp.zeros_like(dn_ref)

    @pl.when(step >= 2)
    def _():
        wait_up(slot, step - 2)

    @pl.when((step >= 2 * per) & (lax.rem(step, per) == 0))
    def _():
        wait_down(bslot, block - 2)

    n2 = normed_ref[...]
    go = grad_ref[...]
    up = up_ref[...]
    down = down_ref[...]
    bias = row_of(vec_ref, UBIAS)
    for k in range(1, blocks):
        bias = jnp.where(block == k, row_of(vec_ref, UBIAS + k), bias)
    u = dot(n2, up) + bias
    cdf = 0.5 * (1.0 + lax.erf(u * math.sqrt(0.5)))
    a = (u * cdf).astype(bf16)
    slope = cdf + u * (jnp.exp(-0.5 * u * u) * (1.0 / math.sqrt(2 * math.pi)))
    du = (dot_nt(go, down) * slope).astype(bf16)
    out_ref[...] += dot(a, down)
    dn_ref[...] += dot_nt(du, up)
    biasg_ref[...] = jnp.sum(du.astype(f32), axis=0, keepdims=True)
    upg = dot_tn(n2, du).astype(bf16)
    for i in range(shards):
        ups_ref[slot, pos_ref[i]] = upg[i * rows:(i + 1) * rows]
    downg = dot_tn(a, go).astype(bf16)
    here = tf // rows
    at = lax.rem(step, per) * here
    for i in range(here):
        dns_ref[bslot, pos_ref[at + i]] = downg[i * rows:(i + 1) * rows]
    each_group(block, start_up)

    @pl.when(lax.rem(step, per) == per - 1)
    def _():
        each_group(block, start_down)

    @pl.when(step == last)
    def _():
        for c in up_copies(1 - slot, step - 1, 1) + up_copies(slot, step, 1) + down_copies(1 - bslot, block - 1, 1) + down_copies(bslot, block, 1):
            c.wait()

def ffn(pos, normed, grad, vecs, wide, tf=512):
    R, D = normed.shape
    blocks = wide.shape[1] // D // 2
    F = blocks * D
    shards = pos.shape[0]
    rows = D // shards
    per = D // tf
    full = pl.BlockSpec((R, D), lambda j: (0, 0))
    hbm = pl.BlockSpec(memory_space=pl.ANY)
    part = jax.ShapeDtypeStruct((shards // 2, rows, F), bf16)
    return pl.pallas_call(
        functools.partial(ffn_kernel, shards=shards, per=per, blocks=blocks), grid=(F // tf,),
        in_specs=[pl.BlockSpec(memory_space=pltpu.SMEM), full, full, pl.BlockSpec((16, tf), lambda j: (0, lax.rem(j, per))),
                  pl.BlockSpec((D, tf), lambda j: (0, j)), pl.BlockSpec((tf, D), lambda j: (lax.rem(j, per), blocks + lax.div(j, per)))],
        out_specs=[full, full, hbm, hbm, hbm, hbm, pl.BlockSpec((1, tf), lambda j: (0, j))],
        out_shape=[jax.ShapeDtypeStruct((R, D), f32), jax.ShapeDtypeStruct((R, D), f32), part, part, part, part, jax.ShapeDtypeStruct((1, F), f32)],
        scratch_shapes=[pltpu.VMEM((2, shards, rows, tf), bf16), pltpu.VMEM((2, shards, rows, D), bf16),
                        pltpu.SemaphoreType.DMA((2, 2)), pltpu.SemaphoreType.DMA((2, 2))],
        compiler_params=cp(), name="ffn", cost_estimate=HINT,
    )(pos, normed, grad, vecs, wide, wide)

def middle_kernel(resid_ref, outacc_ref, dn_ref, go_ref, vec_ref, weight_ref,
                  out_ref, dres_ref, low_ref, dctx_ref, small_ref):
    i = pl.program_id(0)
    resid = resid_ref[...]
    out_ref[...] = (resid + outacc_ref[...] + row_of(vec_ref, DBIAS)).astype(bf16)
    center = resid - jnp.mean(resid, axis=-1, keepdims=True)
    spread = jnp.mean(center * center, axis=-1, keepdims=True)
    r = lax.rsqrt(spread + EPSILON)
    nhat = center * r
    dn = dn_ref[...]
    go = go_ref[...].astype(f32)
    e = dn * row_of(vec_ref, GAIN2)
    d_res = go + r * (e - jnp.mean(e, axis=-1, keepdims=True) - nhat * jnp.mean(e * nhat, axis=-1, keepdims=True))
    dres_ref[...] = d_res
    low = d_res.astype(bf16)
    low_ref[...] = low
    dctx_ref[...] = dot_nt(low, weight_ref[...]).astype(bf16)
    @pl.when(i == 0)
    def _():
        small_ref[...] = jnp.zeros_like(small_ref)
    small_ref[0:1, :] += jnp.sum(dn * nhat, axis=0, keepdims=True)
    small_ref[1:2, :] += jnp.sum(dn, axis=0, keepdims=True)
    small_ref[2:3, :] += jnp.sum(low.astype(f32), axis=0, keepdims=True)
    small_ref[3:4, :] += jnp.sum(go, axis=0, keepdims=True)

def middle(resid, outacc, dn, go, vecs, weight, tm=256):
    R, D = resid.shape
    rows = pl.BlockSpec((tm, D), lambda i: (i, 0))
    low = jax.ShapeDtypeStruct((R, D), bf16)
    return pl.pallas_call(
        middle_kernel, grid=(R // tm,),
        in_specs=[rows, rows, rows, rows, pl.BlockSpec(vecs.shape, lambda i: (0, 0)), pl.BlockSpec((D, D), lambda i: (0, 0))],
        out_specs=[rows, rows, rows, rows, pl.BlockSpec((8, D), lambda i: (0, 0))],
        out_shape=[low, jax.ShapeDtypeStruct((R, D), f32), low, low, jax.ShapeDtypeStruct((8, D), f32)],
        compiler_params=cp(), name="middle",
        cost_estimate=HINT,
    )(resid, outacc, dn, go, vecs, weight)

def attend_back_kernel(prefix_ref, padding_ref, q_ref, k_ref, v_ref, do_ref, o_ref, lse_ref, *refs, bq, first):
    dq_ref, dk_ref, dv_ref, small_ref, dka_ref, dva_ref, bias_ref = refs[-7:]
    L = q_ref.shape[0]
    step = pl.program_id(0) + first
    prefix = prefix_ref[0]
    limit = L - padding_ref[0]
    n = L // bq
    lane = lax.broadcasted_iota(jnp.int32, (1, 128), 1)
    @pl.when(pl.program_id(0) == 0)
    def _():
        for b in range(n):
            bias_ref[b] = key_bias(prefix, limit, b * bq, b * bq, bq, True, True)
    kT = jnp.transpose(k_ref[...])
    prod = do_ref[...].astype(f32) * o_ref[...].astype(f32)
    row = lax.broadcasted_iota(jnp.int32, (8, 128), 0)
    col = lax.broadcasted_iota(jnp.int32, (8, 128), 1)
    pick = jnp.where((col // 64) == row, 1.0, 0.0)
    delta = lax.dot_general(pick, prod, (((1,), (1,)), ((), ())), precision=lax.Precision.HIGHEST, preferred_element_type=f32)
    for b in range(n):
        start, stop = b * bq, (b + 1) * bq
        q = q_ref[start:stop, :]
        do = do_ref[start:stop, :]
        both = jnp.concatenate([jnp.where(lane < 64, q, 0), jnp.where(lane >= 64, q, 0)], axis=0).astype(bf16)
        dboth = jnp.concatenate([jnp.where(lane < 64, do, 0), jnp.where(lane >= 64, do, 0)], axis=0).astype(bf16)
        lse = jnp.concatenate([lse_ref[pl.ds(2 * step, 1), start:stop], lse_ref[pl.ds(2 * step + 1, 1), start:stop]], axis=1)
        inner = jnp.concatenate([delta[0:1, start:stop], delta[1:2, start:stop]], axis=1)
        dq = [None, None]
        for kb in range(b + 1):
            ks = slice(kb * bq, (kb + 1) * bq)
            s = dot_nt(k_ref[ks, :], both)
            if kb == b:
                s = s + jnp.concatenate([bias_ref[b], bias_ref[b]], axis=1)
            elif (kb + 1) * bq > L - 384:
                kk = kb * bq + lax.broadcasted_iota(jnp.int32, (bq, 1), 0)
                s = s + jnp.where(kk < limit, 0.0, NEGATIVE)
            p = jnp.exp(s - lse)
            ds = (p * (dot_nt(v_ref[ks, :], dboth) - inner)).astype(bf16)
            tv = dot(p.astype(bf16), dboth)
            tk = dot(ds, both)
            if kb == b:
                dva_ref[ks, :] = tv
                dka_ref[ks, :] = tk
            else:
                dva_ref[ks, :] += tv
                dka_ref[ks, :] += tk
            for h in range(2):
                t = dot(kT[64 * h:64 * h + 64, ks], ds[:, h * bq:(h + 1) * bq])
                dq[h] = t if dq[h] is None else dq[h] + t
        dq_ref[start:stop, :] = (jnp.transpose(jnp.concatenate(dq, axis=0)) * 0.125).astype(bf16)
    dk_ref[...] = dka_ref[...].astype(bf16)
    dv_ref[...] = dva_ref[...].astype(bf16)
    small_ref[0:1, :] = jnp.sum(dq_ref[...].astype(f32), axis=0, keepdims=True)
    small_ref[1:2, :] = jnp.sum(dv_ref[...].astype(f32), axis=0, keepdims=True)

def attend_back(prefix, padding, qkv, dctx, ctx, lse, first, count, width, earlier=(), bq=256):
    L = qkv.shape[0]
    D = dctx.shape[1]
    n = D // 128
    at = first % (width // 128)
    smem = pl.BlockSpec(memory_space=pltpu.SMEM)
    col = lambda off: pl.BlockSpec((L, 128), lambda j: (0, j + off))
    o = jax.ShapeDtypeStruct((L, width), bf16)
    return pl.pallas_call(
        functools.partial(attend_back_kernel, bq=bq, first=first), grid=(count,),
        in_specs=[smem, smem, col(first), col(n + first), col(2 * n + first), col(first), col(first), pl.BlockSpec((2 * n, L), lambda j: (0, 0))]
        + [pl.BlockSpec(memory_space=pl.ANY)] * len(earlier),
        out_specs=[col(at), col(at), col(at), pl.BlockSpec((8, 128), lambda j: (0, j + at))],
        out_shape=[o, o, o, jax.ShapeDtypeStruct((8, width), f32)],
        scratch_shapes=[pltpu.VMEM((L, 128), f32), pltpu.VMEM((L, 128), f32), pltpu.VMEM((L // bq, bq, bq), f32)],
        input_output_aliases={8 + i: i for i in range(len(earlier))},
        compiler_params=cp(), name="attend_back",
        cost_estimate=HINT,
    )(prefix, padding, qkv, qkv, qkv, dctx, ctx, lse, *earlier)

def weight_grad_kernel(pos_ref, *refs, sources, extra):
    left = refs[:max(sources) + 1]
    refs = refs[len(left):]
    right = refs[:len(sources)]
    refs = refs[len(right):]
    small_ref = refs[0] if extra else None
    keep_ref, send_ref, wide_ref = refs[1 if extra else 0:]
    shards = wide_ref.shape[0]
    half = shards // 2
    rows = left[0].shape[1] // shards
    for g, (source, d_ref) in enumerate(zip(sources, right)):
        value = dot_tn(left[source][...], d_ref[...]).astype(bf16)
        for i in range(shards):
            wide_ref[pos_ref[i], g * rows:(g + 1) * rows, :] = value[i * rows:(i + 1) * rows]
    if extra:
        for i in range(shards):
            wide_ref[pos_ref[i], len(sources) * rows:, :] = jnp.broadcast_to(small_ref[i:i + 1, :], (extra, small_ref.shape[1])).astype(bf16)
    keep_ref[...] = wide_ref[:half]
    send_ref[...] = wide_ref[half:]

def weight_grad(pos, left, right, sources, small=None, width=512, tn=256):
    R, D = left[0].shape
    shards = pos.shape[0]
    rows = D // shards
    extra = min(rows, 16) if small is not None else 0
    high = len(right) * rows + extra
    part = pl.BlockSpec((shards // 2, high, tn), lambda j: (0, 0, j))
    half = jax.ShapeDtypeStruct((shards // 2, high, width), bf16)
    more = [small] if extra else []
    cols = lambda first: pl.BlockSpec((R, tn), lambda j: (0, j + first))
    return pl.pallas_call(
        functools.partial(weight_grad_kernel, sources=sources, extra=extra), grid=(width // tn,),
        in_specs=[pl.BlockSpec(memory_space=pltpu.SMEM)] + [pl.BlockSpec((R, D), lambda j: (0, 0))] * len(left)
        + [cols(first) for _, first in right] + [pl.BlockSpec((shards, tn), lambda j: (0, j))] * len(more),
        out_specs=[part, part], out_shape=[half, half],
        scratch_shapes=[pltpu.VMEM((shards, high, tn), bf16)],
        compiler_params=cp(), name="weight_grad",
        cost_estimate=HINT,
    )(pos, *left, *[r for r, _ in right], *more)

def cotangent_kernel(*refs, count, chained):
    parts, w_ref, refs = refs[:count], refs[count], refs[count + 1:]
    step = pl.program_id(0)
    if chained:
        earlier_in, acc_ref, earlier_ref, sem = refs
        copy = pltpu.make_async_copy(earlier_in, earlier_ref, sem.at[0])
        @pl.when(step == 0)
        def _():
            copy.start()
    else:
        acc_ref, = refs
    for k, part in enumerate(parts):
        @pl.when(step == k)
        def _():
            term = dot_nt(part[...], w_ref[...])
            if k:
                term = term + acc_ref[...]
            if chained and k == count - 1:
                copy.wait()
                term = term + earlier_ref[...]
            acc_ref[...] = term

def cotangent(parts, w, number, earlier=None):
    R, width = parts[0].shape
    D = w.shape[0]
    per = D // width
    chained = earlier is not None
    return pl.pallas_call(
        functools.partial(cotangent_kernel, count=len(parts), chained=chained), grid=(len(parts),),
        in_specs=[pl.BlockSpec((R, width), lambda j: (0, 0))] * len(parts) + [pl.BlockSpec((D, width), lambda j: (0, j * per + number))]
        + [pl.BlockSpec(memory_space=pl.ANY)] * chained,
        out_specs=pl.BlockSpec((R, D), lambda j: (0, 0)), out_shape=jax.ShapeDtypeStruct((R, D), f32),
        scratch_shapes=[pltpu.VMEM((R, D), f32), pltpu.SemaphoreType.DMA((1,))] if chained else [],
        compiler_params=cp(), name="cotangent", cost_estimate=HINT,
    )(*parts, w, *([earlier] if chained else []))

def norm_back_kernel(dn_ref, xhat_ref, tokens_ref, dres_ref, vec_ref, out_ref, small_ref):
    dn = dn_ref[...]
    nhat = xhat_ref[...]
    x = tokens_ref[...].astype(f32)
    center = x - jnp.mean(x, axis=-1, keepdims=True)
    r = lax.rsqrt(jnp.mean(center * center, axis=-1, keepdims=True) + EPSILON)
    e = dn * row_of(vec_ref, GAIN1)
    d = dres_ref[...] + r * (e - jnp.mean(e, axis=-1, keepdims=True) - nhat * jnp.mean(e * nhat, axis=-1, keepdims=True))
    out_ref[...] = d.astype(bf16)
    @pl.when(pl.program_id(0) == 0)
    def _():
        small_ref[...] = jnp.zeros_like(small_ref)
    small_ref[0:1, :] += jnp.sum(dn * nhat, axis=0, keepdims=True)
    small_ref[1:2, :] += jnp.sum(dn, axis=0, keepdims=True)

def norm_back(dn, xhat, tokens, dres, vecs, tm=256):
    R, D = tokens.shape
    rows = pl.BlockSpec((tm, D), lambda i: (i, 0))
    return pl.pallas_call(
        norm_back_kernel, grid=(R // tm,),
        in_specs=[rows, rows, rows, rows, pl.BlockSpec(vecs.shape, lambda i: (0, 0))],
        out_specs=[rows, pl.BlockSpec((8, D), lambda i: (0, 0))],
        out_shape=[jax.ShapeDtypeStruct((R, D), bf16), jax.ShapeDtypeStruct((8, D), f32)],
        compiler_params=cp(), name="norm_back", cost_estimate=HINT,
    )(dn, xhat, tokens, dres, vecs)

def owned_kernel(*refs, counts, rows, blocks, wide):
    parts, at = [], 0
    for c in counts:
        parts.append(sum(r[0].astype(f32) for r in refs[at:at + c]))
        at += c
    up_ref, down_ref = refs[at:]
    half = blocks // len(counts)
    D = down_ref.shape[1]
    for h, part in enumerate(parts):
        for b in range(half):
            down_ref[(h * half + b) * rows:(h * half + b + 1) * rows, :] = part[:, (half + b) * D:(half + b + 1) * D]
    per = D // rows
    group = blocks * rows
    lane = lax.broadcasted_iota(jnp.int32, (rows, 128), 1)
    for tile in range(blocks * D // 128):
        value = None
        for k in range(128 // rows):
            unit = (tile * 128 + k * rows) // rows
            shard, b = unit // blocks, unit % blocks
            source = (b % half) * D + shard * rows
            piece = parts[b // half][:, source // 128 * 128:source // 128 * 128 + 128]
            shift = (k * rows - source % 128) % 128
            if shift:
                piece = pltpu.roll(piece, shift, 1)
            value = piece if value is None else jnp.where(lane >= k * rows, piece, value)
        up_ref[:, tile * 128:(tile + 1) * 128] = value

def owned(groups, D, blocks):
    _, rows, width = groups[0][0].shape
    terms = [t for g in groups for t in g]
    return pl.pallas_call(
        functools.partial(owned_kernel, counts=[len(g) for g in groups], rows=rows, blocks=blocks, wide=width), grid=(1,),
        in_specs=[pl.BlockSpec((1, rows, width), lambda i: (0, 0, 0))] * len(terms),
        out_specs=[pl.BlockSpec((rows, blocks * D), lambda i: (0, 0)), pl.BlockSpec((blocks * rows, D), lambda i: (0, 0))],
        out_shape=[jax.ShapeDtypeStruct((rows, blocks * D), f32), jax.ShapeDtypeStruct((blocks * rows, D), f32)],
        compiler_params=cp(), name="owned", cost_estimate=HINT,
    )(*terms)


class Plan:
    def __init__(self, dp, fsdp):
        self.total = dp * fsdp
        bits = self.total.bit_length() - 1
        low = fsdp.bit_length() - 1
        if fsdp == 4:
            self.core, z, rest = low, list(range(low)), list(range(low + 1, bits))
        else:
            self.core, z, rest = 0, list(range(1, low)), list(range(low, bits))
        a, b = rest[:len(rest) // 2], rest[len(rest) // 2:]
        self.stages = [(a, b), (b, a), (z, z)]
        self.third = len(z) == low

    def masks(self, stage, core):
        bits = self.stages[stage][core]
        return [sum(1 << b for k, b in enumerate(bits) if j >> k & 1) for j in range(1 << len(bits))]

    def pairs(self, stage, j):
        return [(i, i ^ self.masks(stage, i >> self.core & 1)[j]) for i in range(self.total)]

    def size(self, stage):
        return 1 << len(self.stages[stage][0])

    def places(self, me, fixed=False):
        shard = lax.iota(jnp.int32, self.total)
        rel = shard ^ me
        core = (shard >> self.core) & 1
        pos = (rel >> self.core) & 1
        for k, (a, b) in enumerate(self.stages):
            pick = lambda bits, v: sum((((v >> bit) & 1) << k) for k, bit in enumerate(bits))
            own = pick(a, shard) if fixed and k == 2 else jnp.where(core == 0, pick(a, rel), pick(b, rel))
            pos = (pos << len(a)) + own
        return pos

AXES = ("dp", "fsdp")

def swap_core(plan, x):
    return lax.ppermute(x, AXES, [(i, i ^ (1 << plan.core)) for i in range(plan.total)])

def exchange(plan, x, stage, j):
    return lax.ppermute(x, AXES, plan.pairs(stage, j))

class Gathering:
    def __init__(self, plan, shard):
        self.plan, self.shard = plan, shard
        self.arrays = [exchange(plan, shard, 2, j) for j in range(1, plan.size(2))]

    def spread(self):
        column = jnp.stack([self.shard] + self.arrays)
        self.near = [exchange(self.plan, column, 1, j) for j in range(1, self.plan.size(1))]
        self.far = [exchange(self.plan, column, 0, j) for j in range(1, self.plan.size(0))]
        self.arrays = [column] + self.near + self.far

    def spread_again(self):
        n = self.plan.size(1)
        near, far = self.arrays[:n], self.arrays[n:]
        rest = [[exchange(self.plan, p, 0, j + 1) for p in near[1:]] for j in range(len(far))]
        other = [swap_core(self.plan, p) for p in self.arrays]
        self.first, self.other, self.arrays = self.arrays, other, [p for row in rest for p in row]

    def finish(self):
        n = self.plan.size(1)
        sides = (self.first, self.arrays), (self.other, [swap_core(self.plan, p) for p in self.arrays])
        pieces = []
        for first, rest in sides:
            pieces += first[:n]
            for j in range(self.plan.size(0) - 1):
                pieces += [first[n + j]] + rest[j * (n - 1):(j + 1) * (n - 1)]
        return pieces

def step(x, after, *reductions):
    x, _ = tie(x, after, *reductions)
    reductions = [r for r in reductions if r.stage < 3]
    if reductions:
        for r in reductions:
            r.add()
        x, = tie(x, *reductions)
        for r in reductions:
            r.go()
    return x

class Reduction:
    def __init__(self, plan, keep, send, one=False):
        self.plan, self.stage, self.size, self.one = plan, 0, keep.shape[0], one and plan.third
        self.terms = [keep, swap_core(plan, send)]
        self.sent = []

    def add(self):
        n = self.plan.size(self.stage)
        part = self.size // n
        if self.one and self.stage == 2:
            self.sent = [sum(t[:n].astype(f32) for t in self.terms).astype(self.terms[0].dtype)]
            return
        self.sent = [sum(t[j * part:(j + 1) * part].astype(f32) for t in self.terms).astype(self.terms[0].dtype) for j in range(1, n)]

    def go(self):
        if self.one and self.stage == 2:
            self.terms = [lax.psum_scatter(self.sent[0], AXES[1], scatter_dimension=0, tiled=False)[None]]
        else:
            self.terms = self.terms + [exchange(self.plan, s, self.stage, j + 1) for j, s in enumerate(self.sent)]
        self.sent = []
        self.size //= self.plan.size(self.stage)
        self.stage += 1

    def finish(self):
        while self.stage < 3:
            self.add()
            self.go()
        return sum(t[0].astype(f32) for t in self.terms)

def tie(*trees):
    flat = []
    for t in trees:
        flat += t.terms + t.sent if isinstance(t, Reduction) else t.arrays if isinstance(t, Gathering) else [t]
    flat = list(lax.optimization_barrier(tuple(flat)))
    out = []
    for t in trees:
        if isinstance(t, Reduction):
            t.terms = [flat.pop(0) for _ in t.terms]
            t.sent = [flat.pop(0) for _ in t.sent]
        elif isinstance(t, Gathering):
            t.arrays = [flat.pop(0) for _ in t.arrays]
        else:
            out.append(flat.pop(0))
    return out

def body(plan, tokens, prefix_len, padding_len, first_gain, first_shift, inproj_weight, query_bias, value_bias,
         outproj_weight, outproj_bias, second_gain, second_shift, up_weight, up_bias, down_weight, down_bias, grad_out):
    total = plan.total
    R, D = tokens.shape
    F = up_weight.shape[1]
    rows = D // total
    blocks = F // D
    me = lax.axis_index(AXES)
    pos = plan.places(me)
    pos_one = plan.places(me, plan.third)
    shard = lax.iota(jnp.int32, total)
    order = jnp.sum(jnp.where(pos[None, :] == shard[:, None], shard[None, :], 0), axis=1)
    n = first_gain.shape[0]
    half = blocks // 2
    up_local = up_weight.reshape(rows, total, blocks, rows).transpose(0, 2, 1, 3).reshape(rows, F)
    down_local = [down_weight[b * rows:(b + 1) * rows] for b in range(blocks)]
    small = jnp.concatenate([first_gain, first_shift, query_bias, value_bias, outproj_bias, second_gain, second_shift, down_bias, up_bias])
    small = jnp.pad(small.reshape(8 + blocks, rows).T, ((0, 0), (0, 128 - 8 - blocks)))
    inward = Gathering(plan, jnp.concatenate([inproj_weight, outproj_weight, small], axis=1))
    wide = lax.all_gather(jnp.concatenate([up_local] + down_local, axis=1), AXES, axis=0, tiled=True)
    xhat = norm(tokens)
    xhat, = tie(xhat, inward)
    inward.spread()
    xhat, = tie(xhat, inward)
    inward.spread_again()
    xhat, *inward.other = tie(xhat, *inward.other, inward)
    inward = inward.finish()
    n1, qkv, w_in, vecs = project(order, xhat, inward)
    ctx, lse = attend(prefix_len, padding_len, qkv)
    resid, n2, w_out = branch(order, ctx, tokens, vecs, inward)
    cut = D // 2
    n_pairs = D // 128
    def back(first, x, earlier=()):
        return attend_back(prefix_len, padding_len, qkv, x, ctx, lse, first, n_pairs // 4, cut, earlier)
    acc, dn2, keep1, send1, keep2, send2, ubias_grad = ffn(pos_one, n2, grad_out, vecs, wide)
    g1 = Reduction(plan, keep1, send1, True)
    g2 = Reduction(plan, keep2, send2, True)
    out, dres, low, dctx, mid = middle(resid, acc, dn2, grad_out, vecs, w_out)
    dctx = step(dctx, dres, g1)
    d1 = back(0, dctx)
    dctx = step(dctx, d1[0], g2)
    d1 = back(n_pairs // 4, dctx, d1)
    n1a = step(n1, d1[0], g1)
    g3 = Reduction(plan, *weight_grad(pos, (n1a, ctx), ((d1[0], 0), (d1[1], 0), (d1[2], 0), (low, 0), (low, cut // 256)), (0, 0, 0, 1, 1), width=cut))
    dctx, _ = tie(dctx, g3.terms[0])
    d2 = back(n_pairs // 2, dctx)
    w_in = step(w_in, d2[0], g2, g1)
    part = cotangent(d1[:3], w_in, 0)
    dctx = step(dctx, part, g3)
    d2 = back(n_pairs * 3 // 4, dctx, d2)
    n1b = step(n1, d2[0], g2)
    per = lambda v: v.reshape(total, -1)
    att = jnp.concatenate([d1[3], d2[3]], axis=1)
    ubg = ubias_grad.reshape(blocks, total, rows).transpose(1, 0, 2).reshape(total, -1)
    early = jnp.concatenate([per(att[0]), per(att[1]), per(mid[2]), per(mid[0]), per(mid[1]), per(mid[3]), ubg], axis=1)
    early = jnp.pad(early, ((0, 0), (0, cut - early.shape[1])))
    g4 = Reduction(plan, *weight_grad(pos, (n1b,), ((d2[0], 0), (d2[1], 0), (d2[2], 0)), (0, 0, 0), early, width=cut))
    part = step(part, g4.terms[0], g3)
    part = cotangent(d2[:3], w_in, 1, part)
    part = step(part, part, g4, g3)
    tokens_grad, end = norm_back(part, xhat, tokens, dres, vecs)
    end = step(end, end, g4)
    end = jnp.concatenate([per(end[0]), per(end[1])], axis=1)
    end = jnp.sum(jnp.where((pos[:, None] == shard[None, :])[:, :, None], end[:, None, :], 0.0), axis=0)[:, None, :]
    late = Reduction(plan, end[:total // 2], end[total // 2:])
    out = step(out, out, late, g4)
    out = step(out, out, late, g1, g2)
    out = step(out, out, late, g4)
    late, in1, in2 = late.finish()[0], g3.finish(), g4.finish()
    up_grad, down_grad = owned([g1.terms, g2.terms], D, blocks)
    out_grad = jnp.concatenate([in1[3 * rows:4 * rows], in1[4 * rows:]], axis=1)
    in_grad = jnp.concatenate([g[k * rows:(k + 1) * rows] for k in range(3) for g in (in1, in2)], axis=1)
    early = in2[3 * rows]
    e = [early[i * n:(i + 1) * n] for i in range(6)]
    return (out, tokens_grad, late[:n], late[n:], in_grad, e[0], e[1], out_grad, e[2], e[3], e[4], up_grad, early[6 * n:6 * n + F // total], down_grad, e[5])

def solution(mesh):
    plan = Plan(mesh.shape["dp"], mesh.shape["fsdp"])
    rows, flat = P(AXES, None), P(AXES)
    ins = (rows, flat, flat, flat, flat, rows, flat, flat, rows, flat, flat, flat, rows, flat, rows, flat, rows)
    outs = (rows, rows, flat, flat, rows, flat, flat, rows, flat, flat, flat, rows, flat, rows, flat)
    return jax.shard_map(functools.partial(body, plan), mesh=mesh, in_specs=ins, out_specs=outs, check_vma=False)
```

time: 488 us -> 441 us (0.904)
  Pallas kernels: 236 us -> 217 us
  local copies, waits for them, and re-layouts: 25.8 us -> 10.4 us
    ppermute x10 -> x0, waiting for transfers between devices: 15.8 us -> none  [the longest x5 9.33 us: scatter_small(): lax.ppermute(jnp.where(low, upper, lower), AXES, [(i, i ^ stride) for i i...]
    pallas_call x1, Pallas kernels: 36 us -> 22.7 us  [attend(): pl.pallas_call(functools.partial(attend_kernel, bq=bq), grid=(n,), in_spe...]
    ppermute x10 -> x0, starting transfers between devices: 11.3 us -> none  [the longest x5 9.71 us: gather_small(): lax.ppermute(buf, AXES, [(i, i ^ stride) for i in range(plan.total)])]
    ppermute x26 -> x25, starting transfers between devices: 34.5 us -> 45.3 us  [exchange(): return lax.ppermute(x, AXES, plan.pairs(stage, j))]
    reshape x16 -> x5, local copies, waits for them, and re-layouts: 10.4 us -> 0.4 us  [the longest x3 0.22 us: body(): ubias_grad.reshape(blocks, total, rows).transpose(1, 0, 2)]
    ppermute x26 -> x25, waiting for transfers between devices: 81.4 us -> 89 us  [exchange(): return lax.ppermute(x, AXES, plan.pairs(stage, j))]
    all_gather x1, waiting for transfers between devices: 10.1 us -> 17.3 us  [body(): lax.all_gather(jnp.concatenate([up_local] + down_local, axis=1), AXES, ax...]
    pallas_call x4, Pallas kernels: 49.7 us -> 42.6 us  [attend_back(): pl.pallas_call(functools.partial(attend_back_kernel, bq=bq, first=first),...]
  transfers between devices with their start and end apart: 45 -> 37, of which waited for: 19 -> 16; matrix products, arithmetic and copies ran while one was open for 11% -> 10% of each run, Pallas kernels for 38% -> 35%
where the time goes in v3:
time: 441 us; the launch traced here: 437 us
  Pallas kernels  217 us (49%)
  waiting for transfers between devices  108 us (24%)
  starting transfers between devices  46.6 us (11%)
  other arithmetic  40 us (9%)
  between operations  15.9 us (4%)
  local copies, waits for them, and re-layouts  10.4 us (2%)
    ppermute x25, waiting for transfers between devices, exchange(): return lax.ppermute(x, AXES, plan.pairs(stage, j))  89 us
    pallas_call x1, Pallas kernels, ffn(): pl.pallas_call(functools.partial(ffn_kernel, shards=shards, per=per, bloc...  64.9 us
    ppermute x25, starting transfers between devices, exchange(): return lax.ppermute(x, AXES, plan.pairs(stage, j))  45.3 us
    pallas_call x4, Pallas kernels, attend_back(): pl.pallas_call(functools.partial(attend_back_kernel, bq=bq, first=first),...  42.6 us
    convert_element_type x9, other arithmetic, add(): sum((t[j * part:(j + 1) * part].astype(f32) for t in self.terms))  24.9 us
    pallas_call x1, Pallas kernels, attend(): pl.pallas_call(functools.partial(attend_kernel, bq=bq), grid=(n,), in_spe...  22.7 us
    pallas_call x2, Pallas kernels, weight_grad(): pl.pallas_call(functools.partial(weight_grad_kernel, sources=sources, ext...  19.3 us
    all_gather x1, waiting for transfers between devices, body(): lax.all_gather(jnp.concatenate([up_local] + down_local, axis=1), AXES, ax...  17.3 us
  transfers between devices with their start and end apart: 37, of which 16 were waited for; matrix products, arithmetic and copies ran while one was open for 10% of the time, Pallas kernels for 35%

profile of v3, /device:TPU:0, one launch (start us, length us, event | category | flops | bytes accessed | tf_op | source)
XLA Modules:
  0.0 437.2 jit_solution(10270564058926837408)
XLA Ops:
  11.8 3.1 collective-permute-start
  17.5 5.2 %norm.1.xhat_ref = f32[1024,1024]{1,0:T(8,128)} custom-call(bf16[1024,1024]{1,0:T(8,128)(2,1)} %tokens_ref.5), custom_call_target="tpu_custom_call" | custom-call | flops 1000 | bytes 1000 | tf_op jit(solution)/shard_map/norm/pallas_call | solution.py:32
  22.7 4.4 %collective-permute-done = bf16[32,4224]{1,0:T(8,128)(2,1)S(1)} collective-permute-done((bf16[32,4224]{1,0:T(8,128)(2,1)S(1)}, bf16[32,4224]{1,0:T(8,128)(2,1)S(1)}, u32[]{:S(2)}, u32[]{:S(2)}) %collective-permute-start) | collective-permute-done | bytes 270368 | tf_op jit(solution)/shard_map/ppermute | solution.py:578
  27.1 14.4 %collective-permute-done.1 = bf16[32,4224]{1,0:T(8,128)(2,1)S(1)} collective-permute-done((bf16[32,4224]{1,0:T(8,128)(2,1)S(1)}, bf16[32,4224]{1,0:T(8,128)(2,1)S(1)}, u32[]{:S(2)}, u32[]{:S(2)}) %collective-permute-start.1) | collective-permute-done | bytes 270368 | tf_op jit(solution)/shard_map/ppermute | solution.py:578
  44.8 29.3 %collective-permute-done.3.refs_1_.refs_9_ = bf16[4,32,4224]{2,1,0:T(8,128)(2,1)S(1)} collective-permute-done((bf16[4,32,4224]{2,1,0:T(8,128)(2,1)S(1)}, bf16[4,32,4224]{2,1,0:T(8,128)(2,1)S(1)}, u32[]{:S(2)}, u32[]{:S(2)}) %collective-permute-start.3) | collective-permute-done | bytes 1081376 | tf_op jit(solution)/shard_map/ppermute | solution.py:578
  79.4 12.7 %collective-permute-done.8.refs_3_.refs_11_ = bf16[4,32,4224]{2,1,0:T(8,128)(2,1)} collective-permute-done((bf16[4,32,4224]{2,1,0:T(8,128)(2,1)S(1)}, bf16[4,32,4224]{2,1,0:T(8,128)(2,1)}, u32[]{:S(2)}, u32[]{:S(2)}) %collective-permute-start.8) | collective-permute-done | bytes 1081376 | tf_op jit(solution)/shard_map/ppermute | solution.py:578
  95.9 13.9 %project.1 = (bf16[1024,1024]{1,0:T(8,128)(2,1)}, bf16[1024,3072]{1,0:T(8,128)(2,1)}, bf16[1024,3072]{1,0:T(8,128)(2,1)}, f32[16,1024]{1,0:T(8,128)}) custom-call(s32[32]{0:T(128)} %select_reduce_fusion.1.order_ref, f32[1024,1024]{1,0:T(8,128)} %norm.1.xhat_ref, bf16[4,32,4224]{2,1,0:T(8,128)(2,1)} %copy-done, bf16[4,32,4224]{2,1,0:T(8,128)(2,1)} %copy-done.1, ...), custom_call_target="tpu_custom_call" | custom-call | flops 1000 | bytes 1000 | tf_op jit(solution)/shard_map/project/pallas_call | solution.py:69
  109.8 22.7 %attend.1 = (bf16[1024,1024]{1,0:T(8,128)(2,1)}, f32[16,1024]{1,0:T(8,128)}) custom-call(s32[1]{0:T(128)S(6)} %copy.72.prefix_ref, s32[1]{0:T(128)S(6)} %copy.73.padding_ref, bf16[1024,3072]{1,0:T(8,128)(2,1)} %get-tuple-element.223.q_ref.k_ref.v_ref, bf16[1024,3072]{1,0:T(8,128)(2,1)} %get-tuple-element.223.q_ref.k_ref.v_ref, ...), custom_call_target="tpu_custom_call" | custom-call | flops 1000 | bytes 1000 | tf_op jit(solution)/shard_map/attend/pallas_call | solution.py:136
  132.5 7.9 %branch.1 = (f32[1024,1024]{1,0:T(8,128)}, bf16[1024,1024]{1,0:T(8,128)(2,1)}, bf16[1024,1024]{1,0:T(8,128)(2,1)}) custom-call(s32[32]{0:T(128)} %select_reduce_fusion.1.order_ref, bf16[1024,1024]{1,0:T(8,128)(2,1)} %get-tuple-element.224.ctx_ref.o_ref.refs_1_, bf16[1024,1024]{1,0:T(8,128)(2,1)} %tokens_ref.5, f32[16,1024]{1,0:T(8,128)} %get-tuple-element.225.vec_ref, ...), custom_call_target="tpu_custom_call" | custom-call | flops 1000 | bytes 1000 | tf_op jit(solution)/shard_map/branch/pallas_call | solution.py:162
  140.4 17.3 %all-gather.2.cloned.1.call-done.up_ref.down_ref = bf16[1024,8192]{1,0:T(8,128)(2,1)} async-done(((bf16[32,8192]{1,0:T(8,128)(2,1)}), bf16[1024,8192]{1,0:T(8,128)(2,1)}) %all-gather.2.cloned.1.call-update) | async-done | bytes 16777232 | tf_op jit(solution)/shard_map/all_gather | solution.py:683
  157.8 64.9 %ffn.1 = (f32[1024,1024]{1,0:T(8,128)}, f32[1024,1024]{1,0:T(8,128)}, bf16[16,32,4096]{2,1,0:T(8,128)(2,1)}, bf16[16,32,4096]{2,1,0:T(8,128)(2,1)}, bf16[16,32,4...) custom-call(s32[32]{0:T(128)} %fusion.11.pos_ref, ...), custom_call_target="tpu_custom_call" | custom-call | flops 1000 | bytes 1000 | tf_op jit(solution)/shard_map/ffn/pallas_call | solution.py:274
  223.2 12.6 %middle.1 = (bf16[1024,1024]{1,0:T(8,128)(2,1)}, f32[1024,1024]{1,0:T(8,128)}, bf16[1024,1024]{1,0:T(8,128)(2,1)}, bf16[1024,1024]{1,0:T(8,128)(2,1)}, f32[8,1024]{1,0:T(8,128)}) custom-call(f32[1024,1024]{1,0:T(8,128)} %get-tuple-element.226.resid_ref, f32[1024,1024]{1,0:T(8,128)} %get-tuple-element.228.outacc_ref, f32[1024,1024]{1,0:T(8,128)} %get-tuple-element.229.dn_ref, ...), custom_call_target="tpu_custom_call" | custom-call | flops 1000 | bytes 1000 | tf_op jit(solution)/shard_map/middle/pallas_call | solution.py:314
  235.9 4.3 add_convert_fusion.1
  241.6 10.6 %attend_back.4 = (bf16[1024,512]{1,0:T(8,128)(2,1)}, bf16[1024,512]{1,0:T(8,128)(2,1)}, bf16[1024,512]{1,0:T(8,128)(2,1)}, f32[8,512]{1,0:T(8,128)}) custom-call(s32[1]{0:T(128)S(6)} %copy.72.prefix_ref, s32[1]{0:T(128)S(6)} %copy.73.padding_ref, bf16[1024,3072]{1,0:T(8,128)(2,1)} %get-tuple-element.223.q_ref.k_ref.v_ref, ...), custom_call_target="tpu_custom_call" | custom-call | flops 1000 | bytes 1000 | tf_op jit(solution)/shard_map/attend_back/pallas_call | solution.py:385
  252.1 4.3 add_convert_fusion
  257.1 10.5 %attend_back.5 = (bf16[1024,512]{1,0:T(8,128)(2,1)}, bf16[1024,512]{1,0:T(8,128)(2,1)}, bf16[1024,512]{1,0:T(8,128)(2,1)}, f32[8,512]{1,0:T(8,128)}) custom-call(s32[1]{0:T(128)S(6)} %copy.72.prefix_ref, s32[1]{0:T(128)S(6)} %copy.73.padding_ref, ...), custom_call_target="tpu_custom_call", output_to_operand_aliasing={{0}: (8, {}), {1}: (9, {}), {2}: (10, {}), {3}: (11, {})} | custom-call | flops 1000 | bytes 1000 | tf_op jit(solution)/shard_map/attend_back/pallas_call | solution.py:385
  267.6 3.3 add_convert_fusion.6
  272.4 11.5 %weight_grad.2 = (bf16[16,160,512]{2,1,0:T(8,128)(2,1)}, bf16[16,160,512]{2,1,0:T(8,128)(2,1)}) custom-call(s32[32]{0:T(128)} %copy-done.19, bf16[1024,1024]{1,0:T(8,128)(2,1)} %get-tuple-element.304.refs_0_, bf16[1024,1024]{1,0:T(8,128)(2,1)} %get-tuple-element.224.ctx_ref.o_ref.refs_1_, bf16[1024,512]{1,0:T(8,128)(2,1)} %get-tuple-element.252.refs_2_.refs_0_, ...), custom_call_target="tpu_custom_call" | custom-call | flops 1000 | bytes 1000 | tf_op jit(solution)/shard_map/weight_grad/pallas_call | solution.py:427
  283.9 10.5 %attend_back.6 = (bf16[1024,512]{1,0:T(8,128)(2,1)}, bf16[1024,512]{1,0:T(8,128)(2,1)}, bf16[1024,512]{1,0:T(8,128)(2,1)}, f32[8,512]{1,0:T(8,128)}) custom-call(s32[1]{0:T(128)S(6)} %copy.72.prefix_ref, s32[1]{0:T(128)S(6)} %copy.73.padding_ref, bf16[1024,3072]{1,0:T(8,128)(2,1)} %get-tuple-element.223.q_ref.k_ref.v_ref, ...), custom_call_target="tpu_custom_call" | custom-call | flops 1000 | bytes 1000 | tf_op jit(solution)/shard_map/attend_back/pallas_call | solution.py:385
  294.5 5.6 %collective-permute-done.13 = bf16[8,32,4096]{2,1,0:T(8,128)(2,1)S(1)} collective-permute-done((bf16[8,32,4096]{2,1,0:T(8,128)(2,1)}, bf16[8,32,4096]{2,1,0:T(8,128)(2,1)S(1)}, u32[]{:S(2)}, u32[]{:S(2)}) %collective-permute-start.13) | collective-permute-done | bytes 2097184 | tf_op jit(solution)/shard_map/ppermute | solution.py:578
  300.1 5.9 %add_convert_fusion.4 = (bf16[4,32,4096]{2,1,0:T(8,128)(2,1)}, bf16[4,32,4096]{2,1,0:T(8,128)(2,1)}) fusion(bf16[4,32,4096]{2,1,0:T(8,128)(2,1)S(1)} %collective-permute-done.14, bf16[8,32,4096]{2,1,0:T(8,128)(2,1)} %collective-permute-done.12, bf16[16,32,4096]{2,1,0:T(8,128)(2,1)} %collective-permute-done.10, bf16[16,32,4096]{2,1,0:T(8,128)(2,1)} %get-tuple-element.279, ...), kind=kLoop, calls=%fused_computation.4 | loop fusion | flops 7340032 | bytes 9437184 | tf_op jit(solution)/shard_map/convert_element_type | solution.py:629
  309.3 8.3 %cotangent.2.refs_4_ = f32[1024,1024]{1,0:T(8,128)} custom-call(bf16[1024,512]{1,0:T(8,128)(2,1)} %get-tuple-element.252.refs_2_.refs_0_, bf16[1024,512]{1,0:T(8,128)(2,1)} %get-tuple-element.261.refs_3_.refs_1_, bf16[1024,512]{1,0:T(8,128)(2,1)} %get-tuple-element.262.refs_4_.refs_2_, bf16[1024,3072]{1,0:T(8,128)(2,1)} %get-tuple-element.283.refs_3_), custom_call_target="tpu_custom_call" | custom-call | flops 1000 | bytes 1000 | tf_op jit(solution)/shard_map/cotangent/pallas_call | solution.py:464
  317.7 2.7 add_convert_fusion.2
  320.4 11.0 %attend_back.7 = (bf16[1024,512]{1,0:T(8,128)(2,1)}, bf16[1024,512]{1,0:T(8,128)(2,1)}, bf16[1024,512]{1,0:T(8,128)(2,1)}, f32[8,512]{1,0:T(8,128)}) custom-call(s32[1]{0:T(128)S(6)} %copy.72.prefix_ref, s32[1]{0:T(128)S(6)} %copy.73.padding_ref, ...), custom_call_target="tpu_custom_call", output_to_operand_aliasing={{0}: (8, {}), {1}: (9, {}), {2}: (10, {}), {3}: (11, {})} | custom-call | flops 1000 | bytes 1000 | tf_op jit(solution)/shard_map/attend_back/pallas_call | solution.py:385
  332.1 3.8 add_convert_fusion.3
  336.9 7.8 %weight_grad.3 = (bf16[16,112,512]{2,1,0:T(8,128)(2,1)}, bf16[16,112,512]{2,1,0:T(8,128)(2,1)}) custom-call(s32[32]{0:T(128)} %copy-done.19, bf16[1024,1024]{1,0:T(8,128)(2,1)} %get-tuple-element.304.refs_0_, bf16[1024,512]{1,0:T(8,128)(2,1)} %get-tuple-element.292.refs_1_.refs_0_, bf16[1024,512]{1,0:T(8,128)(2,1)} %get-tuple-element.293.refs_2_.refs_1_, ...), custom_call_target="tpu_custom_call" | custom-call | flops 1000 | bytes 1000 | tf_op jit(solution)/shard_map/weight_grad/pallas_call | solution.py:427
  344.7 4.6 %collective-permute-done.17 = bf16[8,160,512]{2,1,0:T(8,128)(2,1)} collective-permute-done((bf16[8,160,512]{2,1,0:T(8,128)(2,1)}, bf16[8,160,512]{2,1,0:T(8,128)(2,1)}, u32[]{:S(2)}, u32[]{:S(2)}) %collective-permute-start.17) | collective-permute-done | bytes 1310752 | tf_op jit(solution)/shard_map/ppermute | solution.py:578
  352.2 8.8 %cotangent.3.dn_ref = f32[1024,1024]{1,0:T(8,128)} custom-call(bf16[1024,512]{1,0:T(8,128)(2,1)} %get-tuple-element.292.refs_1_.refs_0_, bf16[1024,512]{1,0:T(8,128)(2,1)} %get-tuple-element.293.refs_2_.refs_1_, bf16[1024,512]{1,0:T(8,128)(2,1)} %get-tuple-element.294.refs_3_.refs_2_, bf16[1024,3072]{1,0:T(8,128)(2,1)} %get-tuple-element.283.refs_3_, ...), custom_call_target="tpu_custom_call" | custom-call | flops 1000 | bytes 1000 | tf_op jit(solution)/shard_map/cotangent/pallas_call | solution.py:464
  368.2 3.2 collective-permute-start.32
  372.9 8.3 %norm_back.1 = (bf16[1024,1024]{1,0:T(8,128)(2,1)}, f32[8,1024]{1,0:T(8,128)}) custom-call(f32[1024,1024]{1,0:T(8,128)} %cotangent.3.dn_ref, f32[1024,1024]{1,0:T(8,128)} %norm.1.xhat_ref, bf16[1024,1024]{1,0:T(8,128)(2,1)} %tokens_ref.5, f32[1024,1024]{1,0:T(8,128)} %get-tuple-element.233.dres_ref, f32[16,1024]{1,0:T(8,128)} %get-tuple-element.225.vec_ref), custom_call_target="tpu_custom_call" | custom-call | flops 1000 | bytes 1000 | tf_op jit(solution)/shard_map/norm_back/pallas_call | solution.py:491
  389.1 6.0 %collective-permute-done.22 = bf16[4,112,512]{2,1,0:T(8,128)(2,1)S(1)} collective-permute-done((bf16[4,112,512]{2,1,0:T(8,128)(2,1)S(1)}, bf16[4,112,512]{2,1,0:T(8,128)(2,1)S(1)}, u32[]{:S(2)}, u32[]{:S(2)}) %collective-permute-start.22) | collective-permute-done | bytes 458784 | tf_op jit(solution)/shard_map/ppermute | solution.py:578
  396.7 14.0 %collective-permute-start.25 = (bf16[1,112,512]{2,1,0:T(8,128)(2,1)S(1)}, bf16[1,112,512]{2,1,0:T(8,128)(2,1)S(1)}, u32[]{:S(2)}, u32[]{:S(2)}) collective-permute-start(bf16[1,112,512]{2,1,0:T(8,128)(2,1)S(1)} %get-tuple-element.370), channel_id=1, source_target_pairs={{0,1},{1,0},{2,3},{3,2},{4,5},{5,4},{6,7},{7,6},{8,9},{9,8},{10,11... | collective-permute-start | bytes 344072 | tf_op jit(solution)/shard_map/ppermute | solution.py:578
  (189 shorter events, 67.7 us)
Async XLA Ops:
  7.2 150.6 %all-gather.2.cloned.1.call-start = ((), (), s32[]{:S(2)}) async-start(), calls=%async_computation.2 | async-start | bytes 17301504 | tf_op jit(solution)/shard_map/all_gather | solution.py:683
  11.3 403.1 %reduce-scatter.3.cloned.1.call-start = ((), (), s32[]{:S(2)}) async-start(), calls=%async_computation.3 | async-start | bytes 1310720 | tf_op jit(solution)/shard_map/reduce_scatter | solution.py:635
  11.8 15.3 %collective-permute-start = (bf16[32,4224]{1,0:T(8,128)(2,1)S(1)}, bf16[32,4224]{1,0:T(8,128)(2,1)S(1)}, u32[]{:S(2)}, u32[]{:S(2)}) collective-permute-start(bf16[32,4224]{1,0:T(8,128)(2,1)S(1)} %get-tuple-element.422), channel_id=1, source_target_pairs={{0,1},{1,0},{2,3},{3,2},{4,5},{5,4},{6,7},{7,6},{8,9},{9,8},{10,11... | collective-permute-start | bytes 811016 | tf_op jit(solution)/shard_map/ppermute | solution.py:578
  14.9 26.6 %collective-permute-start.1 = (bf16[32,4224]{1,0:T(8,128)(2,1)S(1)}, bf16[32,4224]{1,0:T(8,128)(2,1)S(1)}, u32[]{:S(2)}, u32[]{:S(2)}) collective-permute-start(bf16[32,4224]{1,0:T(8,128)(2,1)S(1)} %get-tuple-element.422), channel_id=1, source_target_pairs={{0,2},{1,3},{2,0},{3,1},{4,6},{5,7},{6,4},{7,5},{8,10},{9,11},{10,... | collective-permute-start | bytes 811016 | tf_op jit(solution)/shard_map/ppermute | solution.py:578
  17.5 24.0 %collective-permute-start.2 = (bf16[32,4224]{1,0:T(8,128)(2,1)S(1)}, bf16[32,4224]{1,0:T(8,128)(2,1)S(1)}, u32[]{:S(2)}, u32[]{:S(2)}) collective-permute-start(bf16[32,4224]{1,0:T(8,128)(2,1)S(1)} %get-tuple-element.422), channel_id=1, source_target_pairs={{0,3},{1,2},{2,1},{3,0},{4,7},{5,6},{6,5},{7,4},{8,11},{9,10},{10,... | collective-permute-start | bytes 811016 | tf_op jit(solution)/shard_map/ppermute | solution.py:578
  41.7 32.4 %collective-permute-start.3 = (bf16[4,32,4224]{2,1,0:T(8,128)(2,1)S(1)}, bf16[4,32,4224]{2,1,0:T(8,128)(2,1)S(1)}, u32[]{:S(2)}, u32[]{:S(2)}) collective-permute-start(bf16[4,32,4224]{2,1,0:T(8,128)(2,1)S(1)} %pad_maximum_fusion.refs_0_.refs_8_), channel_id=1, source_target_pairs={{0,16},{1,17},{2,18},{3,19},{4,12},{5,13},{6,14},{7,15},{8,24},{9,... | collective-permute-start | bytes 3244040 | tf_op jit(solution)/shard_map/ppermute | solution.py:578
  43.3 33.1 %collective-permute-start.4 = (bf16[4,32,4224]{2,1,0:T(8,128)(2,1)S(1)}, bf16[4,32,4224]{2,1,0:T(8,128)(2,1)S(1)}, u32[]{:S(2)}, u32[]{:S(2)}) collective-permute-start(bf16[4,32,4224]{2,1,0:T(8,128)(2,1)S(1)} %pad_maximum_fusion.refs_0_.refs_8_), channel_id=1, source_target_pairs={{0,8},{1,9},{2,10},{3,11},{4,20},{5,21},{6,22},{7,23},{8,0},{9,1},... | collective-permute-start | bytes 3244040 | tf_op jit(solution)/shard_map/ppermute | solution.py:578
  76.4 15.7 %collective-permute-start.8 = (bf16[4,32,4224]{2,1,0:T(8,128)(2,1)S(1)}, bf16[4,32,4224]{2,1,0:T(8,128)(2,1)}, u32[]{:S(2)}, u32[]{:S(2)}) collective-permute-start(bf16[4,32,4224]{2,1,0:T(8,128)(2,1)S(1)} %collective-permute-done.3.refs_1_.refs_9_), channel_id=1, source_target_pairs={{0,8},{1,9},{2,10},{3,11},{4,20},{5,21},{6,22},{7,23},{8,0},{9,1},... | collective-permute-start | bytes 3244040 | tf_op jit(solution)/shard_map/ppermute | solution.py:578
  78.8 13.2 %collective-permute-start.5 = (bf16[4,32,4224]{2,1,0:T(8,128)(2,1)S(1)}, bf16[4,32,4224]{2,1,0:T(8,128)(2,1)S(1)}, u32[]{:S(2)}, u32[]{:S(2)}) collective-permute-start(bf16[4,32,4224]{2,1,0:T(8,128)(2,1)S(1)} %pad_maximum_fusion.refs_0_.refs_8_), channel_id=1, source_target_pairs={{0,4},{1,5},{2,6},{3,7},{4,0},{5,1},{6,2},{7,3},{8,12},{9,13},{10,... | collective-permute-start | bytes 3244040 | tf_op jit(solution)/shard_map/ppermute | solution.py:575
  78.8 13.2 %collective-permute-start.7 = (bf16[4,32,4224]{2,1,0:T(8,128)(2,1)S(1)}, bf16[4,32,4224]{2,1,0:T(8,128)(2,1)S(1)}, u32[]{:S(2)}, u32[]{:S(2)}) collective-permute-start(bf16[4,32,4224]{2,1,0:T(8,128)(2,1)S(1)} %collective-permute-done.4.refs_2_.refs_10_), channel_id=1, source_target_pairs={{0,4},{1,5},{2,6},{3,7},{4,0},{5,1},{6,2},{7,3},{8,12},{9,13},{10,... | collective-permute-start | bytes 3244040 | tf_op jit(solution)/shard_map/ppermute | solution.py:575
  222.6 13.2 %collective-permute-start.10 = (bf16[16,32,4096]{2,1,0:T(8,128)(2,1)}, bf16[16,32,4096]{2,1,0:T(8,128)(2,1)}, u32[]{:S(2)}, u32[]{:S(2)}) collective-permute-start(bf16[16,32,4096]{2,1,0:T(8,128)(2,1)} %get-tuple-element.235), channel_id=1, source_target_pairs={{0,4},{1,5},{2,6},{3,7},{4,0},{5,1},{6,2},{7,3},{8,12},{9,13},{10,... | collective-permute-start | bytes 12582920 | tf_op jit(solution)/shard_map/ppermute | solution.py:575
  223.0 29.2 %collective-permute-start.11 = (bf16[16,32,4096]{2,1,0:T(8,128)(2,1)}, bf16[16,32,4096]{2,1,0:T(8,128)(2,1)}, u32[]{:S(2)}, u32[]{:S(2)}) collective-permute-start(bf16[16,32,4096]{2,1,0:T(8,128)(2,1)} %get-tuple-element.243), channel_id=1, source_target_pairs={{0,4},{1,5},{2,6},{3,7},{4,0},{5,1},{6,2},{7,3},{8,12},{9,13},{10,... | collective-permute-start | bytes 12582920 | tf_op jit(solution)/shard_map/ppermute | solution.py:575
  240.2 27.4 %collective-permute-start.12 = (bf16[8,32,4096]{2,1,0:T(8,128)(2,1)}, bf16[8,32,4096]{2,1,0:T(8,128)(2,1)}, u32[]{:S(2)}, u32[]{:S(2)}) collective-permute-start(bf16[8,32,4096]{2,1,0:T(8,128)(2,1)} %add_convert_fusion.1), channel_id=1, source_target_pairs={{0,8},{1,9},{2,10},{3,11},{4,20},{5,21},{6,22},{7,23},{8,0},{9,1},... | collective-permute-start | bytes 6291464 | tf_op jit(solution)/shard_map/ppermute | solution.py:578
  256.5 43.6 %collective-permute-start.13 = (bf16[8,32,4096]{2,1,0:T(8,128)(2,1)}, bf16[8,32,4096]{2,1,0:T(8,128)(2,1)S(1)}, u32[]{:S(2)}, u32[]{:S(2)}) collective-permute-start(bf16[8,32,4096]{2,1,0:T(8,128)(2,1)} %add_convert_fusion), channel_id=1, source_target_pairs={{0,8},{1,9},{2,10},{3,11},{4,20},{5,21},{6,22},{7,23},{8,0},{9,1},... | collective-permute-start | bytes 6291464 | tf_op jit(solution)/shard_map/ppermute | solution.py:578
  270.9 29.2 %collective-permute-start.14 = (bf16[4,32,4096]{2,1,0:T(8,128)(2,1)}, bf16[4,32,4096]{2,1,0:T(8,128)(2,1)S(1)}, u32[]{:S(2)}, u32[]{:S(2)}) collective-permute-start(bf16[4,32,4096]{2,1,0:T(8,128)(2,1)} %add_convert_fusion.6), channel_id=1, source_target_pairs={{0,16},{1,17},{2,18},{3,19},{4,12},{5,13},{6,14},{7,15},{8,24},{9,... | collective-permute-start | bytes 3145736 | tf_op jit(solution)/shard_map/ppermute | solution.py:578
  283.9 33.8 %collective-permute-start.15 = (bf16[16,160,512]{2,1,0:T(8,128)(2,1)}, bf16[16,160,512]{2,1,0:T(8,128)(2,1)}, u32[]{:S(2)}, u32[]{:S(2)}) collective-permute-start(bf16[16,160,512]{2,1,0:T(8,128)(2,1)} %get-tuple-element.284), channel_id=1, source_target_pairs={{0,4},{1,5},{2,6},{3,7},{4,0},{5,1},{6,2},{7,3},{8,12},{9,13},{10,... | collective-permute-start | bytes 7864328 | tf_op jit(solution)/shard_map/ppermute | solution.py:575
  306.0 25.4 %collective-permute-start.16 = (bf16[4,32,4096]{2,1,0:T(8,128)(2,1)}, bf16[4,32,4096]{2,1,0:T(8,128)(2,1)}, u32[]{:S(2)}, u32[]{:S(2)}) collective-permute-start(bf16[4,32,4096]{2,1,0:T(8,128)(2,1)} %get-tuple-element.298), channel_id=1, source_target_pairs={{0,16},{1,17},{2,18},{3,19},{4,12},{5,13},{6,14},{7,15},{8,24},{9,... | collective-permute-start | bytes 3145736 | tf_op jit(solution)/shard_map/ppermute | solution.py:578
  331.4 18.0 %collective-permute-start.17 = (bf16[8,160,512]{2,1,0:T(8,128)(2,1)}, bf16[8,160,512]{2,1,0:T(8,128)(2,1)}, u32[]{:S(2)}, u32[]{:S(2)}) collective-permute-start(bf16[8,160,512]{2,1,0:T(8,128)(2,1)} %add_convert_fusion.2), channel_id=1, source_target_pairs={{0,8},{1,9},{2,10},{3,11},{4,20},{5,21},{6,22},{7,23},{8,0},{9,1},... | collective-permute-start | bytes 3932168 | tf_op jit(solution)/shard_map/ppermute | solution.py:578
  344.6 16.4 %collective-permute-start.18 = (bf16[16,112,512]{2,1,0:T(8,128)(2,1)}, bf16[16,112,512]{2,1,0:T(8,128)(2,1)}, u32[]{:S(2)}, u32[]{:S(2)}) collective-permute-start(bf16[16,112,512]{2,1,0:T(8,128)(2,1)} %get-tuple-element.318), channel_id=1, source_target_pairs={{0,4},{1,5},{2,6},{3,7},{4,0},{5,1},{6,2},{7,3},{8,12},{9,13},{10,... | collective-permute-start | bytes 5505032 | tf_op jit(solution)/shard_map/ppermute | solution.py:575
  344.7 69.7 %reduce-scatter.5.cloned.1.call-start = ((), (), s32[]{:S(2)}) async-start(), calls=%async_computation.4 | async-start | bytes 1310720 | tf_op jit(solution)/shard_map/reduce_scatter | solution.py:635
  351.8 10.8 %collective-permute-start.19 = (bf16[4,160,512]{2,1,0:T(8,128)(2,1)}, bf16[4,160,512]{2,1,0:T(8,128)(2,1)S(1)}, u32[]{:S(2)}, u32[]{:S(2)}) collective-permute-start(bf16[4,160,512]{2,1,0:T(8,128)(2,1)} %add_convert_fusion.8), channel_id=1, source_target_pairs={{0,16},{1,17},{2,18},{3,19},{4,12},{5,13},{6,14},{7,15},{8,24},{9,... | collective-permute-start | bytes 1966088 | tf_op jit(solution)/shard_map/ppermute | solution.py:578
  367.5 17.5 %collective-permute-start.20 = (bf16[8,112,512]{2,1,0:T(8,128)(2,1)}, bf16[8,112,512]{2,1,0:T(8,128)(2,1)}, u32[]{:S(2)}, u32[]{:S(2)}) collective-permute-start(bf16[8,112,512]{2,1,0:T(8,128)(2,1)} %add_convert_fusion.7), channel_id=1, source_target_pairs={{0,8},{1,9},{2,10},{3,11},{4,20},{5,21},{6,22},{7,23},{8,0},{9,1},... | collective-permute-start | bytes 2752520 | tf_op jit(solution)/shard_map/ppermute | solution.py:578
  368.1 13.1 %collective-permute-start.31 = (bf16[1,160,512]{2,1,0:T(8,128)(2,1)}, bf16[1,160,512]{2,1,0:T(8,128)(2,1)S(1)}, u32[]{:S(2)}, u32[]{:S(2)}) collective-permute-start(bf16[1,160,512]{2,1,0:T(8,128)(2,1)} %get-tuple-element.391), channel_id=1, source_target_pairs={{0,1},{1,0},{2,3},{3,2},{4,5},{5,4},{6,7},{7,6},{8,9},{9,8},{10,11... | collective-permute-start | bytes 491528 | tf_op jit(solution)/shard_map/ppermute | solution.py:578
  368.2 15.6 %collective-permute-start.32 = (bf16[1,160,512]{2,1,0:T(8,128)(2,1)}, bf16[1,160,512]{2,1,0:T(8,128)(2,1)S(1)}, u32[]{:S(2)}, u32[]{:S(2)}) collective-permute-start(bf16[1,160,512]{2,1,0:T(8,128)(2,1)} %get-tuple-element.392), channel_id=1, source_target_pairs={{0,2},{1,3},{2,0},{3,1},{4,6},{5,7},{6,4},{7,5},{8,10},{9,11},{10,... | collective-permute-start | bytes 491528 | tf_op jit(solution)/shard_map/ppermute | solution.py:578
  371.5 12.3 %collective-permute-start.33 = (bf16[1,160,512]{2,1,0:T(8,128)(2,1)S(1)}, bf16[1,160,512]{2,1,0:T(8,128)(2,1)S(1)}, u32[]{:S(2)}, u32[]{:S(2)}) collective-permute-start(bf16[1,160,512]{2,1,0:T(8,128)(2,1)S(1)} %get-tuple-element.393), channel_id=1, source_target_pairs={{0,3},{1,2},{2,1},{3,0},{4,7},{5,6},{6,5},{7,4},{8,11},{9,10},{10,... | collective-permute-start | bytes 491528 | tf_op jit(solution)/shard_map/ppermute | solution.py:578
  386.5 8.6 %collective-permute-start.22 = (bf16[4,112,512]{2,1,0:T(8,128)(2,1)S(1)}, bf16[4,112,512]{2,1,0:T(8,128)(2,1)S(1)}, u32[]{:S(2)}, u32[]{:S(2)}) collective-permute-start(bf16[4,112,512]{2,1,0:T(8,128)(2,1)S(1)} %add_convert_fusion.9), channel_id=1, source_target_pairs={{0,16},{1,17},{2,18},{3,19},{4,12},{5,13},{6,14},{7,15},{8,24},{9,... | collective-permute-start | bytes 1376264 | tf_op jit(solution)/shard_map/ppermute | solution.py:578
  396.6 17.8 %collective-permute-start.23 = (f32[8,1,64]{2,0,1:T(8,128)S(1)}, f32[8,1,64]{2,0,1:T(8,128)S(1)}, u32[]{:S(2)}, u32[]{:S(2)}) collective-permute-start(f32[8,1,64]{2,0,1:T(8,128)S(1)} %slice_add_fusion), channel_id=1, source_target_pairs={{0,8},{1,9},{2,10},{3,11},{4,20},{5,21},{6,22},{7,23},{8,0},{9,1},... | collective-permute-start | bytes 6152 | tf_op jit(solution)/shard_map/ppermute | solution.py:578
  396.7 21.4 %collective-permute-start.25 = (bf16[1,112,512]{2,1,0:T(8,128)(2,1)S(1)}, bf16[1,112,512]{2,1,0:T(8,128)(2,1)S(1)}, u32[]{:S(2)}, u32[]{:S(2)}) collective-permute-start(bf16[1,112,512]{2,1,0:T(8,128)(2,1)S(1)} %get-tuple-element.370), channel_id=1, source_target_pairs={{0,1},{1,0},{2,3},{3,2},{4,5},{5,4},{6,7},{7,6},{8,9},{9,8},{10,11... | collective-permute-start | bytes 344072 | tf_op jit(solution)/shard_map/ppermute | solution.py:578
  410.7 7.4 %collective-permute-start.26 = (bf16[1,112,512]{2,1,0:T(8,128)(2,1)S(1)}, bf16[1,112,512]{2,1,0:T(8,128)(2,1)S(1)}, u32[]{:S(2)}, u32[]{:S(2)}) collective-permute-start(bf16[1,112,512]{2,1,0:T(8,128)(2,1)S(1)} %get-tuple-element.371), channel_id=1, source_target_pairs={{0,2},{1,3},{2,0},{3,1},{4,6},{5,7},{6,4},{7,5},{8,10},{9,11},{10,... | collective-permute-start | bytes 344072 | tf_op jit(solution)/shard_map/ppermute | solution.py:578
  413.0 6.7 %collective-permute-start.27 = (bf16[1,112,512]{2,1,0:T(8,128)(2,1)S(1)}, bf16[1,112,512]{2,1,0:T(8,128)(2,1)S(1)}, u32[]{:S(2)}, u32[]{:S(2)}) collective-permute-start(bf16[1,112,512]{2,1,0:T(8,128)(2,1)S(1)} %get-tuple-element.372), channel_id=1, source_target_pairs={{0,3},{1,2},{2,1},{3,0},{4,7},{5,6},{6,5},{7,4},{8,11},{9,10},{10,... | collective-permute-start | bytes 344072 | tf_op jit(solution)/shard_map/ppermute | solution.py:578
  421.6 5.0 %collective-permute-start.28 = (f32[1,1,64]{2,0,1:T(1,128)S(1)}, f32[1,1,64]{2,0,1:T(1,128)S(1)}, u32[]{:S(2)}, u32[]{:S(2)}) collective-permute-start(f32[1,1,64]{2,0,1:T(1,128)S(1)} %get-tuple-element.384), channel_id=1, source_target_pairs={{0,1},{1,0},{2,3},{3,2},{4,5},{5,4},{6,7},{7,6},{8,9},{9,8},{10,11... | collective-permute-start | bytes 776 | tf_op jit(solution)/shard_map/ppermute | solution.py:578
  424.6 5.3 %collective-permute-start.30 = (f32[1,1,64]{2,0,1:T(1,128)S(1)}, f32[1,1,64]{2,0,1:T(1,128)S(1)}, u32[]{:S(2)}, u32[]{:S(2)}) collective-permute-start(f32[1,1,64]{2,0,1:T(1,128)S(1)} %get-tuple-element.386), channel_id=1, source_target_pairs={{0,3},{1,2},{2,1},{3,0},{4,7},{5,6},{6,5},{7,4},{8,11},{9,10},{10,... | collective-permute-start | bytes 776 | tf_op jit(solution)/shard_map/ppermute | solution.py:578
  (35 other events, 241.6 us)
Sparse Core Ops, SparseCore 0:
  11.6 146.1 all-gather.1
  344.8 26.1 reduce-scatter.2
  373.4 27.9 reduce-scatter.4

commit v4 on v3

--- a/solution.py
+++ b/solution.py
@@ -22,16 +22,17 @@
 
 def norm_kernel(tokens_ref, out_ref):
     x = tokens_ref[...].astype(f32)
-    center = x - jnp.mean(x, axis=-1, keepdims=True)
-    spread = jnp.mean(center * center, axis=-1, keepdims=True)
-    out_ref[...] = center * lax.rsqrt(spread + EPSILON)
+    mean = jnp.mean(x, axis=-1, keepdims=True)
+    center = x - mean
+    r = lax.rsqrt(jnp.mean(center * center, axis=-1, keepdims=True) + EPSILON)
+    lane = lax.broadcasted_iota(jnp.int32, out_ref.shape, 1)
+    out_ref[...] = jnp.where(lane == 0, mean, r)
 
 def norm(tokens, tm=256):
     R, D = tokens.shape
-    rows = pl.BlockSpec((tm, D), lambda i: (i, 0))
     return pl.pallas_call(
-        norm_kernel, grid=(R // tm,), in_specs=[rows], out_specs=rows, out_shape=jax.ShapeDtypeStruct((R, D), f32),
-        compiler_params=cp(), name="norm", cost_estimate=HINT,
+        norm_kernel, grid=(R // tm,), in_specs=[pl.BlockSpec((tm, D), lambda i: (i, 0))], out_specs=pl.BlockSpec((tm, 128), lambda i: (i, 0)),
+        out_shape=jax.ShapeDtypeStruct((R, 128), f32), compiler_params=cp(), name="norm", cost_estimate=HINT,
     )(tokens)
 
 def in_order(order_ref, pieces, whole_ref):
@@ -40,16 +41,17 @@
         for i in range(n):
             whole_ref[pl.ds(pl.multiple_of(order_ref[p * n + i] * rows, rows), rows), :] = piece[i]
 
-def project_kernel(order_ref, xhat_ref, *refs, count):
+def project_kernel(order_ref, tokens_ref, stat_ref, *refs, count):
     pieces, sides = refs[:count], refs[count:2 * count]
-    normed_ref, out_ref, weight_ref, vec_ref, side_ref, all_ref = refs[2 * count:]
+    normed_ref, out_ref, vec_ref, weight_ref, side_ref, all_ref = refs[2 * count:]
     step = pl.program_id(0)
     @pl.when(step == 0)
     def _():
         in_order(order_ref, sides, side_ref)
         all_ref[...] = jnp.transpose(side_ref[...].astype(f32))
         vec_ref[...] = all_ref[:16, :]
-        normed_ref[...] = (xhat_ref[...] * all_ref[GAIN1:GAIN1 + 1, :] + all_ref[SHIFT1:SHIFT1 + 1, :]).astype(bf16)
+        xhat = (tokens_ref[...].astype(f32) - stat_ref[:, 0:1]) * stat_ref[:, 1:2]
+        normed_ref[...] = (xhat * all_ref[GAIN1:GAIN1 + 1, :] + all_ref[SHIFT1:SHIFT1 + 1, :]).astype(bf16)
     in_order(order_ref, pieces, weight_ref)
     D = normed_ref.shape[1]
     tn = out_ref.shape[1]
@@ -60,23 +62,21 @@
     out = dot(normed_ref[...], weight_ref[...]) + bias
     out_ref[...] = (out * factor).astype(bf16)
 
-def project(order, xhat, pieces, tn=512):
-    R, D = xhat.shape
+def project(order, tokens, stats, pieces, tn=512):
+    R, D = tokens.shape
     n, rows, width = pieces[0].shape
     N = 3 * D
-    cols = pl.BlockSpec((R, tn), lambda j: (0, j))
     full = pl.BlockSpec((R, D), lambda j: (0, 0))
     return pl.pallas_call(
         functools.partial(project_kernel, count=len(pieces)), grid=(N // tn,),
-        in_specs=[pl.BlockSpec(memory_space=pltpu.SMEM), full]
+        in_specs=[pl.BlockSpec(memory_space=pltpu.SMEM), full, pl.BlockSpec((R, 128), lambda j: (0, 0))]
         + [pl.BlockSpec((n, rows, tn), lambda j: (0, 0, j))] * len(pieces)
         + [pl.BlockSpec((n, rows, 128), lambda j: (0, 0, width // 128 - 1))] * len(pieces),
-        out_specs=[full, cols, pl.BlockSpec((D, tn), lambda j: (0, j)), pl.BlockSpec((16, D), lambda j: (0, 0))],
-        out_shape=[jax.ShapeDtypeStruct((R, D), bf16), jax.ShapeDtypeStruct((R, N), bf16), jax.ShapeDtypeStruct((D, N), bf16),
-                   jax.ShapeDtypeStruct((16, D), f32)],
-        scratch_shapes=[pltpu.VMEM((D, 128), bf16), pltpu.VMEM((128, D), f32)],
+        out_specs=[full, pl.BlockSpec((R, tn), lambda j: (0, j)), pl.BlockSpec((16, D), lambda j: (0, 0))],
+        out_shape=[jax.ShapeDtypeStruct((R, D), bf16), jax.ShapeDtypeStruct((R, N), bf16), jax.ShapeDtypeStruct((16, D), f32)],
+        scratch_shapes=[pltpu.VMEM((D, tn), bf16), pltpu.VMEM((D, 128), bf16), pltpu.VMEM((128, D), f32)],
         compiler_params=cp(), name="project", cost_estimate=HINT,
-    )(order, xhat, *pieces, *pieces)
+    )(order, tokens, stats, *pieces, *pieces)
 
 def key_bias(prefix, limit, lo, q0, bq, transposed, diagonal):
     shape = (bq, bq)
@@ -168,8 +168,9 @@
         compiler_params=cp(), name="branch", cost_estimate=HINT,
     )(order, ctx, tokens, vecs, *pieces)
 
-def ffn_kernel(pos_ref, normed_ref, grad_ref, vec_ref, up_ref, down_ref, out_ref, dn_ref, keep1_ref, send1_ref, keep2_ref, send2_ref, biasg_ref,
-               ups_ref, dns_ref, up_sem, dn_sem, *, shards, per, blocks):
+def ffn_kernel(pos_ref, normed_ref, grad_ref, vec_ref, rows_ref, up_ref, down_ref, resid_in, weight_in,
+               result_out, low_out, dctx_out, keep1_ref, send1_ref, keep2_ref, send2_ref, biasg_ref, small_ref,
+               out_ref, dn_ref, ups_ref, dns_ref, resid_ref, weight_ref, result_ref, low_ref, dctx_ref, up_sem, dn_sem, in_sem, out_sem, *, shards, per, blocks, tm):
     step = pl.program_id(0)
     last = pl.num_programs(0) - 1
     D = normed_ref.shape[1]
@@ -214,8 +215,12 @@
                 c.wait()
         each_group(block, do)
 
+    loads = [pltpu.make_async_copy(resid_in, resid_ref, in_sem.at[0]), pltpu.make_async_copy(weight_in, weight_ref, in_sem.at[1])]
+
     @pl.when(step == 0)
     def _():
+        for c in loads:
+            c.start()
         out_ref[...] = jnp.zeros_like(out_ref)
         dn_ref[...] = jnp.zeros_like(dn_ref)
 
@@ -258,10 +263,35 @@
 
     @pl.when(step == last)
     def _():
-        for c in up_copies(1 - slot, step - 1, 1) + up_copies(slot, step, 1) + down_copies(1 - bslot, block - 1, 1) + down_copies(bslot, block, 1):
+        for c in loads:
             c.wait()
-
-def ffn(pos, normed, grad, vecs, wide, tf=512):
+        small_ref[...] = jnp.zeros_like(small_ref)
+        stores = []
+        for i in range(resid_ref.shape[0] // tm):
+            at = slice(i * tm, (i + 1) * tm)
+            resid = resid_ref[at]
+            result_ref[at] = (resid + out_ref[at] + row_of(rows_ref, DBIAS)).astype(bf16)
+            center = resid - jnp.mean(resid, axis=-1, keepdims=True)
+            r = lax.rsqrt(jnp.mean(center * center, axis=-1, keepdims=True) + EPSILON)
+            nhat = center * r
+            dn = dn_ref[at]
+            go = grad_ref[at].astype(f32)
+            e = dn * row_of(rows_ref, GAIN2)
+            low = (go + r * (e - jnp.mean(e, axis=-1, keepdims=True) - nhat * jnp.mean(e * nhat, axis=-1, keepdims=True))).astype(bf16)
+            low_ref[at] = low
+            dctx_ref[at] = dot_nt(low, weight_ref[...]).astype(bf16)
+            small_ref[0:1, :] += jnp.sum(dn * nhat, axis=0, keepdims=True)
+            small_ref[1:2, :] += jnp.sum(dn, axis=0, keepdims=True)
+            small_ref[2:3, :] += jnp.sum(low.astype(f32), axis=0, keepdims=True)
+            small_ref[3:4, :] += jnp.sum(go, axis=0, keepdims=True)
+            for k, (here, there) in enumerate(((result_ref, result_out), (low_ref, low_out), (dctx_ref, dctx_out))):
+                c = pltpu.make_async_copy(here.at[pl.ds(i * tm, tm)], there.at[pl.ds(i * tm, tm)], out_sem.at[i, k])
+                c.start()
+                stores.append(c)
+        for c in stores + up_copies(1 - slot, step - 1, 1) + up_copies(slot, step, 1) + down_copies(1 - bslot, block - 1, 1) + down_copies(bslot, block, 1):
+            c.wait()
+
+def ffn(pos, normed, grad, vecs, wide, resid, weight, tf=512, tm=256):
     R, D = normed.shape
     blocks = wide.shape[1] // D // 2
     F = blocks * D
@@ -271,57 +301,21 @@
     full = pl.BlockSpec((R, D), lambda j: (0, 0))
     hbm = pl.BlockSpec(memory_space=pl.ANY)
     part = jax.ShapeDtypeStruct((shards // 2, rows, F), bf16)
-    return pl.pallas_call(
-        functools.partial(ffn_kernel, shards=shards, per=per, blocks=blocks), grid=(F // tf,),
-        in_specs=[pl.BlockSpec(memory_space=pltpu.SMEM), full, full, pl.BlockSpec((16, tf), lambda j: (0, lax.rem(j, per))),
-                  pl.BlockSpec((D, tf), lambda j: (0, j)), pl.BlockSpec((tf, D), lambda j: (lax.rem(j, per), blocks + lax.div(j, per)))],
-        out_specs=[full, full, hbm, hbm, hbm, hbm, pl.BlockSpec((1, tf), lambda j: (0, j))],
-        out_shape=[jax.ShapeDtypeStruct((R, D), f32), jax.ShapeDtypeStruct((R, D), f32), part, part, part, part, jax.ShapeDtypeStruct((1, F), f32)],
-        scratch_shapes=[pltpu.VMEM((2, shards, rows, tf), bf16), pltpu.VMEM((2, shards, rows, D), bf16),
-                        pltpu.SemaphoreType.DMA((2, 2)), pltpu.SemaphoreType.DMA((2, 2))],
-        compiler_params=cp(), name="ffn", cost_estimate=HINT,
-    )(pos, normed, grad, vecs, wide, wide)
-
-def middle_kernel(resid_ref, outacc_ref, dn_ref, go_ref, vec_ref, weight_ref,
-                  out_ref, dres_ref, low_ref, dctx_ref, small_ref):
-    i = pl.program_id(0)
-    resid = resid_ref[...]
-    out_ref[...] = (resid + outacc_ref[...] + row_of(vec_ref, DBIAS)).astype(bf16)
-    center = resid - jnp.mean(resid, axis=-1, keepdims=True)
-    spread = jnp.mean(center * center, axis=-1, keepdims=True)
-    r = lax.rsqrt(spread + EPSILON)
-    nhat = center * r
-    dn = dn_ref[...]
-    go = go_ref[...].astype(f32)
-    e = dn * row_of(vec_ref, GAIN2)
-    d_res = go + r * (e - jnp.mean(e, axis=-1, keepdims=True) - nhat * jnp.mean(e * nhat, axis=-1, keepdims=True))
-    dres_ref[...] = d_res
-    low = d_res.astype(bf16)
-    low_ref[...] = low
-    dctx_ref[...] = dot_nt(low, weight_ref[...]).astype(bf16)
-    @pl.when(i == 0)
-    def _():
-        small_ref[...] = jnp.zeros_like(small_ref)
-    small_ref[0:1, :] += jnp.sum(dn * nhat, axis=0, keepdims=True)
-    small_ref[1:2, :] += jnp.sum(dn, axis=0, keepdims=True)
-    small_ref[2:3, :] += jnp.sum(low.astype(f32), axis=0, keepdims=True)
-    small_ref[3:4, :] += jnp.sum(go, axis=0, keepdims=True)
-
-def middle(resid, outacc, dn, go, vecs, weight, tm=256):
-    R, D = resid.shape
-    rows = pl.BlockSpec((tm, D), lambda i: (i, 0))
     low = jax.ShapeDtypeStruct((R, D), bf16)
     return pl.pallas_call(
-        middle_kernel, grid=(R // tm,),
-        in_specs=[rows, rows, rows, rows, pl.BlockSpec(vecs.shape, lambda i: (0, 0)), pl.BlockSpec((D, D), lambda i: (0, 0))],
-        out_specs=[rows, rows, rows, rows, pl.BlockSpec((8, D), lambda i: (0, 0))],
-        out_shape=[low, jax.ShapeDtypeStruct((R, D), f32), low, low, jax.ShapeDtypeStruct((8, D), f32)],
-        compiler_params=cp(), name="middle",
-        cost_estimate=HINT,
-    )(resid, outacc, dn, go, vecs, weight)
+        functools.partial(ffn_kernel, shards=shards, per=per, blocks=blocks, tm=tm), grid=(F // tf,),
+        in_specs=[pl.BlockSpec(memory_space=pltpu.SMEM), full, full, pl.BlockSpec((16, tf), lambda j: (0, lax.rem(j, per))), pl.BlockSpec((16, D), lambda j: (0, 0)),
+                  pl.BlockSpec((D, tf), lambda j: (0, j)), pl.BlockSpec((tf, D), lambda j: (lax.rem(j, per), blocks + lax.div(j, per))), hbm, hbm],
+        out_specs=[hbm] * 7 + [pl.BlockSpec((1, tf), lambda j: (0, j)), pl.BlockSpec((8, D), lambda j: (0, 0))],
+        out_shape=[low, low, low, part, part, part, part, jax.ShapeDtypeStruct((1, F), f32), jax.ShapeDtypeStruct((8, D), f32)],
+        scratch_shapes=[pltpu.VMEM((R, D), f32), pltpu.VMEM((R, D), f32), pltpu.VMEM((2, shards, rows, tf), bf16), pltpu.VMEM((2, shards, rows, D), bf16),
+                        pltpu.VMEM((R, D), f32), pltpu.VMEM((D, D), bf16), pltpu.VMEM((R, D), bf16), pltpu.VMEM((R, D), bf16), pltpu.VMEM((R, D), bf16),
+                        pltpu.SemaphoreType.DMA((2, 2)), pltpu.SemaphoreType.DMA((2, 2)), pltpu.SemaphoreType.DMA((2,)), pltpu.SemaphoreType.DMA((R // tm, 3))],
+        compiler_params=cp(), name="ffn", cost_estimate=HINT,
+    )(pos, normed, grad, vecs, vecs, wide, wide, resid, weight)
 
 def attend_back_kernel(prefix_ref, padding_ref, q_ref, k_ref, v_ref, do_ref, o_ref, lse_ref, *refs, bq, first):
-    dq_ref, dk_ref, dv_ref, small_ref, dka_ref, dva_ref, bias_ref = refs[-7:]
+    d_ref, small_ref, dka_ref, dva_ref, bias_ref = refs[-5:]
     L = q_ref.shape[0]
     step = pl.program_id(0) + first
     prefix = prefix_ref[0]
@@ -368,11 +362,11 @@
             for h in range(2):
                 t = dot(kT[64 * h:64 * h + 64, ks], ds[:, h * bq:(h + 1) * bq])
                 dq[h] = t if dq[h] is None else dq[h] + t
-        dq_ref[start:stop, :] = (jnp.transpose(jnp.concatenate(dq, axis=0)) * 0.125).astype(bf16)
-    dk_ref[...] = dka_ref[...].astype(bf16)
-    dv_ref[...] = dva_ref[...].astype(bf16)
-    small_ref[0:1, :] = jnp.sum(dq_ref[...].astype(f32), axis=0, keepdims=True)
-    small_ref[1:2, :] = jnp.sum(dv_ref[...].astype(f32), axis=0, keepdims=True)
+        d_ref[0, start:stop, :] = (jnp.transpose(jnp.concatenate(dq, axis=0)) * 0.125).astype(bf16)
+    d_ref[1] = dka_ref[...].astype(bf16)
+    d_ref[2] = dva_ref[...].astype(bf16)
+    small_ref[0:1, :] = jnp.sum(d_ref[0].astype(f32), axis=0, keepdims=True)
+    small_ref[1:2, :] = jnp.sum(d_ref[2].astype(f32), axis=0, keepdims=True)
 
 def attend_back(prefix, padding, qkv, dctx, ctx, lse, first, count, width, earlier=(), bq=256):
     L = qkv.shape[0]
@@ -381,120 +375,189 @@
     at = first % (width // 128)
     smem = pl.BlockSpec(memory_space=pltpu.SMEM)
     col = lambda off: pl.BlockSpec((L, 128), lambda j: (0, j + off))
-    o = jax.ShapeDtypeStruct((L, width), bf16)
     return pl.pallas_call(
         functools.partial(attend_back_kernel, bq=bq, first=first), grid=(count,),
         in_specs=[smem, smem, col(first), col(n + first), col(2 * n + first), col(first), col(first), pl.BlockSpec((2 * n, L), lambda j: (0, 0))]
         + [pl.BlockSpec(memory_space=pl.ANY)] * len(earlier),
-        out_specs=[col(at), col(at), col(at), pl.BlockSpec((8, 128), lambda j: (0, j + at))],
-        out_shape=[o, o, o, jax.ShapeDtypeStruct((8, width), f32)],
+        out_specs=[pl.BlockSpec((3, L, 128), lambda j: (0, 0, j + at)), pl.BlockSpec((8, 128), lambda j: (0, j + at))],
+        out_shape=[jax.ShapeDtypeStruct((3, L, width), bf16), jax.ShapeDtypeStruct((8, width), f32)],
         scratch_shapes=[pltpu.VMEM((L, 128), f32), pltpu.VMEM((L, 128), f32), pltpu.VMEM((L // bq, bq, bq), f32)],
         input_output_aliases={8 + i: i for i in range(len(earlier))},
         compiler_params=cp(), name="attend_back",
         cost_estimate=HINT,
     )(prefix, padding, qkv, qkv, qkv, dctx, ctx, lse, *earlier)
 
-def weight_grad_kernel(pos_ref, *refs, sources, extra):
-    left = refs[:max(sources) + 1]
-    refs = refs[len(left):]
-    right = refs[:len(sources)]
-    refs = refs[len(right):]
-    small_ref = refs[0] if extra else None
-    keep_ref, send_ref, wide_ref = refs[1 if extra else 0:]
-    shards = wide_ref.shape[0]
+def weight_grad_kernel(pos_ref, left_ref, d_ref, *refs, each, other, extra):
+    refs = list(refs)
+    if other:
+        low_ref, second_in = refs[:2]
+        refs = refs[2:]
+    if extra:
+        small_ref = refs.pop(0)
+    keep_ref, send_ref, stage_ref, stage_sem = refs[:4]
+    refs = refs[4:]
+    if other:
+        second_ref, second_sem = refs[:2]
+        refs = refs[2:]
+    if extra:
+        extra_ref, extra_sem = refs
+    step = pl.program_id(0)
+    steps = 3 * each + other
+    _, shards, rows, tn = stage_ref.shape
     half = shards // 2
-    rows = left[0].shape[1] // shards
-    for g, (source, d_ref) in enumerate(zip(sources, right)):
-        value = dot_tn(left[source][...], d_ref[...]).astype(bf16)
+    slot = lax.rem(step, 2)
+
+    def copies(slot, step):
+        high = pl.ds(pl.multiple_of(lax.div(step, each) * rows, rows), rows)
+        cols = pl.ds(pl.multiple_of(lax.rem(step, each) * tn, tn), tn)
+        return [pltpu.make_async_copy(stage_ref.at[slot, pl.ds(k * half, half)], out.at[:, high, cols], stage_sem.at[slot, k]) for k, out in enumerate((keep_ref, send_ref))]
+
+    if extra:
+        behind = [pltpu.make_async_copy(extra_ref.at[pl.ds(k * half, half)], out.at[:, pl.ds(3 * rows, extra), :], extra_sem.at[k]) for k, out in enumerate((keep_ref, send_ref))]
+    if other:
+        second = pltpu.make_async_copy(second_in, second_ref, second_sem.at[0])
+
+    @pl.when(step == 0)
+    def _():
+        if other:
+            second.start()
+        if extra:
+            for i in range(shards):
+                extra_ref[pos_ref[i]] = jnp.broadcast_to(small_ref[i:i + 1, :], extra_ref.shape[1:]).astype(bf16)
+            for c in behind:
+                c.start()
+
+    @pl.when(step >= 2)
+    def _():
+        for c in copies(slot, step - 2):
+            c.wait()
+
+    def put(value):
         for i in range(shards):
-            wide_ref[pos_ref[i], g * rows:(g + 1) * rows, :] = value[i * rows:(i + 1) * rows]
-    if extra:
-        for i in range(shards):
-            wide_ref[pos_ref[i], len(sources) * rows:, :] = jnp.broadcast_to(small_ref[i:i + 1, :], (extra, small_ref.shape[1])).astype(bf16)
-    keep_ref[...] = wide_ref[:half]
-    send_ref[...] = wide_ref[half:]
-
-def weight_grad(pos, left, right, sources, small=None, width=512, tn=256):
-    R, D = left[0].shape
+            stage_ref[slot, pos_ref[i]] = value[i * rows:(i + 1) * rows].astype(bf16)
+
+    if other:
+        @pl.when(step == 3 * each)
+        def _():
+            second.wait()
+
+        @pl.when(step >= 3 * each)
+        def _():
+            put(dot_tn(second_ref[...], low_ref[...]))
+
+        @pl.when(step < 3 * each)
+        def _():
+            put(dot_tn(left_ref[...], d_ref[0]))
+    else:
+        put(dot_tn(left_ref[...], d_ref[0]))
+    for c in copies(slot, step):
+        c.start()
+
+    @pl.when(step == steps - 1)
+    def _():
+        for c in copies(1 - slot, step - 1) + copies(slot, step) + (behind if extra else []):
+            c.wait()
+
+def weight_grad(pos, left, d, second=None, low=None, small=None, tn=512):
+    R, D = left.shape
+    _, _, width = d.shape
     shards = pos.shape[0]
     rows = D // shards
+    each = width // tn
+    other = D // tn if second is not None else 0
     extra = min(rows, 16) if small is not None else 0
-    high = len(right) * rows + extra
-    part = pl.BlockSpec((shards // 2, high, tn), lambda j: (0, 0, j))
+    high = (3 * each + other) // each * rows + extra
     half = jax.ShapeDtypeStruct((shards // 2, high, width), bf16)
-    more = [small] if extra else []
-    cols = lambda first: pl.BlockSpec((R, tn), lambda j: (0, j + first))
+    hbm = pl.BlockSpec(memory_space=pl.ANY)
+    specs = [pl.BlockSpec(memory_space=pltpu.SMEM), pl.BlockSpec((R, D), lambda j: (0, 0)),
+             pl.BlockSpec((1, R, tn), lambda j: (jnp.minimum(lax.div(j, each), 2), 0, jnp.where(j < 3 * each, lax.rem(j, each), each - 1)))]
+    args = [pos, left, d]
+    scratch = [pltpu.VMEM((2, shards, rows, tn), bf16), pltpu.SemaphoreType.DMA((2, 2))]
+    if other:
+        specs = specs + [pl.BlockSpec((R, tn), lambda j: (0, jnp.maximum(j - 3 * each, 0))), hbm]
+        args = args + [low, second]
+        scratch = scratch + [pltpu.VMEM((R, D), bf16), pltpu.SemaphoreType.DMA((1,))]
+    if extra:
+        specs = specs + [pl.BlockSpec((shards, width), lambda j: (0, 0))]
+        args = args + [small]
+        scratch = scratch + [pltpu.VMEM((shards, extra, width), bf16), pltpu.SemaphoreType.DMA((2,))]
     return pl.pallas_call(
-        functools.partial(weight_grad_kernel, sources=sources, extra=extra), grid=(width // tn,),
-        in_specs=[pl.BlockSpec(memory_space=pltpu.SMEM)] + [pl.BlockSpec((R, D), lambda j: (0, 0))] * len(left)
-        + [cols(first) for _, first in right] + [pl.BlockSpec((shards, tn), lambda j: (0, j))] * len(more),
-        out_specs=[part, part], out_shape=[half, half],
-        scratch_shapes=[pltpu.VMEM((shards, high, tn), bf16)],
-        compiler_params=cp(), name="weight_grad",
-        cost_estimate=HINT,
-    )(pos, *left, *[r for r, _ in right], *more)
-
-def cotangent_kernel(*refs, count, chained):
-    parts, w_ref, refs = refs[:count], refs[count], refs[count + 1:]
+        functools.partial(weight_grad_kernel, each=each, other=other, extra=extra), grid=(3 * each + other,),
+        in_specs=specs, out_specs=[hbm, hbm], out_shape=[half, half], scratch_shapes=scratch,
+        compiler_params=cp(), name="weight_grad", cost_estimate=HINT,
+    )(*args)
+
+def cotangent_kernel(order_ref, d_ref, *refs, count, final, tm):
+    pieces, refs = refs[:count], refs[count:]
     step = pl.program_id(0)
-    if chained:
-        earlier_in, acc_ref, earlier_ref, sem = refs
-        copy = pltpu.make_async_copy(earlier_in, earlier_ref, sem.at[0])
+    if final:
+        stat_ref, vec_ref, earlier_in, tokens_in, low_in, out_ref, small_ref, weight_ref, acc_ref, earlier_ref, tokens_ref, low_ref, result_ref, in_sem, out_sem = refs
+        loads = [pltpu.make_async_copy(a, b, in_sem.at[k]) for k, (a, b) in enumerate(((earlier_in, earlier_ref), (tokens_in, tokens_ref), (low_in, low_ref)))]
         @pl.when(step == 0)
         def _():
-            copy.start()
+            for c in loads:
+                c.start()
     else:
-        acc_ref, = refs
-    for k, part in enumerate(parts):
-        @pl.when(step == k)
-        def _():
-            term = dot_nt(part[...], w_ref[...])
-            if k:
-                term = term + acc_ref[...]
-            if chained and k == count - 1:
-                copy.wait()
-                term = term + earlier_ref[...]
-            acc_ref[...] = term
-
-def cotangent(parts, w, number, earlier=None):
-    R, width = parts[0].shape
-    D = w.shape[0]
+        out_ref, weight_ref, acc_ref = refs
+    in_order(order_ref, pieces, weight_ref)
+    term = dot_nt(d_ref[0], weight_ref[...])
+    @pl.when(step == 0)
+    def _():
+        acc_ref[...] = term
+    @pl.when(step > 0)
+    def _():
+        acc_ref[...] += term
+
+    @pl.when(step == 2)
+    def _():
+        if not final:
+            out_ref[...] = acc_ref[...].astype(bf16)
+        else:
+            for c in loads:
+                c.wait()
+            small_ref[...] = jnp.zeros_like(small_ref)
+            gain = row_of(vec_ref, GAIN1)
+            stores = []
+            for i in range(acc_ref.shape[0] // tm):
+                at = slice(i * tm, (i + 1) * tm)
+                dn = acc_ref[at] + earlier_ref[at].astype(f32)
+                r = stat_ref[at, 1:2]
+                nhat = (tokens_ref[at].astype(f32) - stat_ref[at, 0:1]) * r
+                e = dn * gain
+                d = low_ref[at].astype(f32) + r * (e - jnp.mean(e, axis=-1, keepdims=True) - nhat * jnp.mean(e * nhat, axis=-1, keepdims=True))
+                result_ref[at] = d.astype(bf16)
+                small_ref[0:1, :] += jnp.sum(dn * nhat, axis=0, keepdims=True)
+                small_ref[1:2, :] += jnp.sum(dn, axis=0, keepdims=True)
+                c = pltpu.make_async_copy(result_ref.at[pl.ds(i * tm, tm)], out_ref.at[pl.ds(i * tm, tm)], out_sem.at[i])
+                c.start()
+                stores.append(c)
+            for c in stores:
+                c.wait()
+
+def cotangent(order, d, pieces, number, earlier=None, stats=None, vecs=None, tokens=None, low=None, tm=256):
+    _, R, width = d.shape
+    n, rows, _ = pieces[0].shape
+    D = rows * n * len(pieces)
     per = D // width
-    chained = earlier is not None
+    final = earlier is not None
+    hbm = pl.BlockSpec(memory_space=pl.ANY)
+    specs = [pl.BlockSpec(memory_space=pltpu.SMEM), pl.BlockSpec((1, R, width), lambda j: (j, 0, 0))]
+    specs = specs + [pl.BlockSpec((n, rows, width), lambda j: (0, 0, j * per + number))] * len(pieces)
+    scratch = [pltpu.VMEM((D, width), bf16), pltpu.VMEM((R, D), f32)]
+    result = jax.ShapeDtypeStruct((R, D), bf16)
+    more = ()
+    if final:
+        specs = specs + [pl.BlockSpec((R, 128), lambda j: (0, 0)), pl.BlockSpec(vecs.shape, lambda j: (0, 0)), hbm, hbm, hbm]
+        more = (stats, vecs, earlier, tokens, low)
+        outs, shapes = [hbm, pl.BlockSpec((8, D), lambda j: (0, 0))], [result, jax.ShapeDtypeStruct((8, D), f32)]
+        scratch = scratch + [pltpu.VMEM((R, D), bf16)] * 4 + [pltpu.SemaphoreType.DMA((3,)), pltpu.SemaphoreType.DMA((R // tm,))]
+    else:
+        outs, shapes = pl.BlockSpec((R, D), lambda j: (0, 0)), result
     return pl.pallas_call(
-        functools.partial(cotangent_kernel, count=len(parts), chained=chained), grid=(len(parts),),
-        in_specs=[pl.BlockSpec((R, width), lambda j: (0, 0))] * len(parts) + [pl.BlockSpec((D, width), lambda j: (0, j * per + number))]
-        + [pl.BlockSpec(memory_space=pl.ANY)] * chained,
-        out_specs=pl.BlockSpec((R, D), lambda j: (0, 0)), out_shape=jax.ShapeDtypeStruct((R, D), f32),
-        scratch_shapes=[pltpu.VMEM((R, D), f32), pltpu.SemaphoreType.DMA((1,))] if chained else [],
+        functools.partial(cotangent_kernel, count=len(pieces), final=final, tm=tm), grid=(3,),
+        in_specs=specs, out_specs=outs, out_shape=shapes, scratch_shapes=scratch,
         compiler_params=cp(), name="cotangent", cost_estimate=HINT,
-    )(*parts, w, *([earlier] if chained else []))
-
-def norm_back_kernel(dn_ref, xhat_ref, tokens_ref, dres_ref, vec_ref, out_ref, small_ref):
-    dn = dn_ref[...]
-    nhat = xhat_ref[...]
-    x = tokens_ref[...].astype(f32)
-    center = x - jnp.mean(x, axis=-1, keepdims=True)
-    r = lax.rsqrt(jnp.mean(center * center, axis=-1, keepdims=True) + EPSILON)
-    e = dn * row_of(vec_ref, GAIN1)
-    d = dres_ref[...] + r * (e - jnp.mean(e, axis=-1, keepdims=True) - nhat * jnp.mean(e * nhat, axis=-1, keepdims=True))
-    out_ref[...] = d.astype(bf16)
-    @pl.when(pl.program_id(0) == 0)
-    def _():
-        small_ref[...] = jnp.zeros_like(small_ref)
-    small_ref[0:1, :] += jnp.sum(dn * nhat, axis=0, keepdims=True)
-    small_ref[1:2, :] += jnp.sum(dn, axis=0, keepdims=True)
-
-def norm_back(dn, xhat, tokens, dres, vecs, tm=256):
-    R, D = tokens.shape
-    rows = pl.BlockSpec((tm, D), lambda i: (i, 0))
-    return pl.pallas_call(
-        norm_back_kernel, grid=(R // tm,),
-        in_specs=[rows, rows, rows, rows, pl.BlockSpec(vecs.shape, lambda i: (0, 0))],
-        out_specs=[rows, pl.BlockSpec((8, D), lambda i: (0, 0))],
-        out_shape=[jax.ShapeDtypeStruct((R, D), bf16), jax.ShapeDtypeStruct((8, D), f32)],
-        compiler_params=cp(), name="norm_back", cost_estimate=HINT,
-    )(dn, xhat, tokens, dres, vecs)
+    )(order, d, *pieces, *more)
 
 def owned_kernel(*refs, counts, rows, blocks, wide):
     parts, at = [], 0
@@ -681,61 +744,68 @@
     small = jnp.pad(small.reshape(8 + blocks, rows).T, ((0, 0), (0, 128 - 8 - blocks)))
     inward = Gathering(plan, jnp.concatenate([inproj_weight, outproj_weight, small], axis=1))
     wide = lax.all_gather(jnp.concatenate([up_local] + down_local, axis=1), AXES, axis=0, tiled=True)
-    xhat = norm(tokens)
-    xhat, = tie(xhat, inward)
+    stats = norm(tokens)
+    stats, = tie(stats, inward)
     inward.spread()
-    xhat, = tie(xhat, inward)
+    stats, = tie(stats, inward)
     inward.spread_again()
-    xhat, *inward.other = tie(xhat, *inward.other, inward)
+    stats, *inward.other = tie(stats, *inward.other, inward)
     inward = inward.finish()
-    n1, qkv, w_in, vecs = project(order, xhat, inward)
+    n1, qkv, vecs = project(order, tokens, stats, inward)
     ctx, lse = attend(prefix_len, padding_len, qkv)
     resid, n2, w_out = branch(order, ctx, tokens, vecs, inward)
     cut = D // 2
     n_pairs = D // 128
     def back(first, x, earlier=()):
         return attend_back(prefix_len, padding_len, qkv, x, ctx, lse, first, n_pairs // 4, cut, earlier)
-    acc, dn2, keep1, send1, keep2, send2, ubias_grad = ffn(pos_one, n2, grad_out, vecs, wide)
+    out, low, dctx, keep1, send1, keep2, send2, ubias_grad, mid = ffn(pos_one, n2, grad_out, vecs, wide, resid, w_out)
     g1 = Reduction(plan, keep1, send1, True)
     g2 = Reduction(plan, keep2, send2, True)
-    out, dres, low, dctx, mid = middle(resid, acc, dn2, grad_out, vecs, w_out)
-    dctx = step(dctx, dres, g1)
     d1 = back(0, dctx)
-    dctx = step(dctx, d1[0], g2)
+    dctx = step(dctx, d1[0], g1)
     d1 = back(n_pairs // 4, dctx, d1)
-    n1a = step(n1, d1[0], g1)
-    g3 = Reduction(plan, *weight_grad(pos, (n1a, ctx), ((d1[0], 0), (d1[1], 0), (d1[2], 0), (low, 0), (low, cut // 256)), (0, 0, 0, 1, 1), width=cut))
+    n1a = step(n1, d1[0], g2)
+    g3 = Reduction(plan, *weight_grad(pos, n1a, d1[0], ctx, low))
     dctx, _ = tie(dctx, g3.terms[0])
     d2 = back(n_pairs // 2, dctx)
-    w_in = step(w_in, d2[0], g2, g1)
-    part = cotangent(d1[:3], w_in, 0)
-    dctx = step(dctx, part, g3)
+    dctx = step(dctx, d2[0], g1)
     d2 = back(n_pairs * 3 // 4, dctx, d2)
-    n1b = step(n1, d2[0], g2)
+    n1b = step(n1, d2[0], g2, g1)
     per = lambda v: v.reshape(total, -1)
-    att = jnp.concatenate([d1[3], d2[3]], axis=1)
+    att = jnp.concatenate([d1[1], d2[1]], axis=1)
     ubg = ubias_grad.reshape(blocks, total, rows).transpose(1, 0, 2).reshape(total, -1)
     early = jnp.concatenate([per(att[0]), per(att[1]), per(mid[2]), per(mid[0]), per(mid[1]), per(mid[3]), ubg], axis=1)
     early = jnp.pad(early, ((0, 0), (0, cut - early.shape[1])))
-    g4 = Reduction(plan, *weight_grad(pos, (n1b,), ((d2[0], 0), (d2[1], 0), (d2[2], 0)), (0, 0, 0), early, width=cut))
-    part = step(part, g4.terms[0], g3)
-    part = cotangent(d2[:3], w_in, 1, part)
+    g4 = Reduction(plan, *weight_grad(pos, n1b, d2[0], small=early))
+    da = step(d1[0], g4.terms[0], g3, g2)
+    part = cotangent(order, da, inward, 0)
     part = step(part, part, g4, g3)
-    tokens_grad, end = norm_back(part, xhat, tokens, dres, vecs)
-    end = step(end, end, g4)
-    end = jnp.concatenate([per(end[0]), per(end[1])], axis=1)
-    end = jnp.sum(jnp.where((pos[:, None] == shard[None, :])[:, :, None], end[:, None, :], 0.0), axis=0)[:, None, :]
-    late = Reduction(plan, end[:total // 2], end[total // 2:])
-    out = step(out, out, late, g4)
-    out = step(out, out, late, g1, g2)
-    out = step(out, out, late, g4)
-    late, in1, in2 = late.finish()[0], g3.finish(), g4.finish()
+    tokens_grad, end = cotangent(order, d2[0], inward, 1, part, stats, vecs, tokens, low)
+    bits = [plan.core] + [bit for bit in range(total.bit_length() - 1) if bit != plan.core]
+    swap = lambda v, bit: lax.ppermute(v, AXES, [(i, i ^ (1 << bit)) for i in range(total)])
+    end = step(end[:2], end, g4)
+    other = swap(end, bits[0])
+    end = step(end, end, g3, g1)
+    end, other = tie(end, other, g4)
+    g4.add()
+    g4.go()
+    arriving = plan.size(2) - 1
+    for k, bit in enumerate(bits[1:]):
+        end = end + other
+        other = swap(end, bit)
+        if k < arriving:
+            at = k - arriving
+            other, g4.terms[at] = tie(other, g4.terms[at])
+        if k == 1:
+            other, = tie(other, g3)
+    late = lax.dynamic_slice_in_dim(end + other, me * n, n, axis=1)
+    in1, in2 = g3.finish(), g4.finish()
     up_grad, down_grad = owned([g1.terms, g2.terms], D, blocks)
     out_grad = jnp.concatenate([in1[3 * rows:4 * rows], in1[4 * rows:]], axis=1)
     in_grad = jnp.concatenate([g[k * rows:(k + 1) * rows] for k in range(3) for g in (in1, in2)], axis=1)
     early = in2[3 * rows]
     e = [early[i * n:(i + 1) * n] for i in range(6)]
-    return (out, tokens_grad, late[:n], late[n:], in_grad, e[0], e[1], out_grad, e[2], e[3], e[4], up_grad, early[6 * n:6 * n + F // total], down_grad, e[5])
+    return (out, tokens_grad, late[0], late[1], in_grad, e[0], e[1], out_grad, e[2], e[3], e[4], up_grad, early[6 * n:6 * n + F // total], down_grad, e[5])
 
 def solution(mesh):
     plan = Plan(mesh.shape["dp"], mesh.shape["fsdp"])

time: 441 us -> 426 us (0.966)
  Pallas kernels: 217 us -> 199 us
  starting transfers between devices: 46.6 us -> 36.8 us
  waiting for transfers between devices: 108 us -> 116 us
    pallas_call x7 -> x5, Pallas kernels: 62.6 us -> 42.5 us  [the longest x2 20.7 us: cotangent(): pl.pallas_call(functools.partial(cotangent_kernel, count=len(pieces), fin...]
    ppermute x25 -> x20, starting transfers between devices: 45.3 us -> 27.2 us  [exchange(): return lax.ppermute(x, AXES, plan.pairs(stage, j))]
    ppermute x0 -> x5, starting transfers between devices: none -> 7.84 us  [body(): lax.ppermute(v, AXES, [(i, i ^ 1 << bit) for i in range(total)])]
    ppermute x0 -> x5, waiting for transfers between devices: none -> 7.61 us  [body(): lax.ppermute(v, AXES, [(i, i ^ 1 << bit) for i in range(total)])]
    ppermute x25 -> x20, waiting for transfers between devices: 89 us -> 90.7 us  [exchange(): return lax.ppermute(x, AXES, plan.pairs(stage, j))]
  transfers between devices with their start and end apart: 37 -> 36, of which waited for: 16 -> 15; matrix products, arithmetic and copies ran while one was open for 10% -> 10% of each run, Pallas kernels for 35% -> 32%
where the time goes in v4:
time: 426 us; the launch traced here: 419 us
  Pallas kernels  199 us (47%)
  waiting for transfers between devices  116 us (27%)
  other arithmetic  40.5 us (10%)
  starting transfers between devices  36.8 us (9%)
  between operations  16.1 us (4%)
  local copies, waits for them, and re-layouts  10 us (2%)
    ppermute x20, waiting for transfers between devices, exchange(): return lax.ppermute(x, AXES, plan.pairs(stage, j))  90.7 us
    pallas_call x1, Pallas kernels, ffn(): pl.pallas_call(functools.partial(ffn_kernel, shards=shards, per=per, bloc...  67.3 us
    pallas_call x4, Pallas kernels, attend_back(): pl.pallas_call(functools.partial(attend_back_kernel, bq=bq, first=first),...  43.1 us
    ppermute x20, starting transfers between devices, exchange(): return lax.ppermute(x, AXES, plan.pairs(stage, j))  27.2 us
    convert_element_type x9, other arithmetic, add(): sum((t[j * part:(j + 1) * part].astype(f32) for t in self.terms))  25.1 us
    pallas_call x1, Pallas kernels, attend(): pl.pallas_call(functools.partial(attend_kernel, bq=bq), grid=(n,), in_spe...  22.7 us
    pallas_call x2, Pallas kernels, cotangent(): pl.pallas_call(functools.partial(cotangent_kernel, count=len(pieces), fin...  20.7 us
    pallas_call x2, Pallas kernels, weight_grad(): pl.pallas_call(functools.partial(weight_grad_kernel, each=each, other=oth...  17.8 us
  transfers between devices with their start and end apart: 36, of which 15 were waited for; matrix products, arithmetic and copies ran while one was open for 10% of the time, Pallas kernels for 32%

profile of v4, /device:TPU:0, one launch (start us, length us, event | category | flops | bytes accessed | tf_op | source)
XLA Modules:
  0.0 418.8 jit_solution(12681416403211414416)
XLA Ops:
  11.8 3.1 collective-permute-start
  17.5 4.1 norm.1.stat_ref.refs_8_
  21.6 5.6 %collective-permute-done = bf16[32,4224]{1,0:T(8,128)(2,1)S(1)} collective-permute-done((bf16[32,4224]{1,0:T(8,128)(2,1)S(1)}, bf16[32,4224]{1,0:T(8,128)(2,1)S(1)}, u32[]{:S(2)}, u32[]{:S(2)}) %collective-permute-start) | collective-permute-done | bytes 270368 | tf_op jit(solution)/shard_map/ppermute | solution.py:641
  27.1 14.4 %collective-permute-done.1 = bf16[32,4224]{1,0:T(8,128)(2,1)S(1)} collective-permute-done((bf16[32,4224]{1,0:T(8,128)(2,1)S(1)}, bf16[32,4224]{1,0:T(8,128)(2,1)S(1)}, u32[]{:S(2)}, u32[]{:S(2)}) %collective-permute-start.1) | collective-permute-done | bytes 270368 | tf_op jit(solution)/shard_map/ppermute | solution.py:641
  44.8 29.3 %collective-permute-done.3.refs_1_.refs_9_ = bf16[4,32,4224]{2,1,0:T(8,128)(2,1)S(1)} collective-permute-done((bf16[4,32,4224]{2,1,0:T(8,128)(2,1)S(1)}, bf16[4,32,4224]{2,1,0:T(8,128)(2,1)S(1)}, u32[]{:S(2)}, u32[]{:S(2)}) %collective-permute-start.3) | collective-permute-done | bytes 1081376 | tf_op jit(solution)/shard_map/ppermute | solution.py:641
  79.4 12.7 %collective-permute-done.8.refs_3_.refs_11_ = bf16[4,32,4224]{2,1,0:T(8,128)(2,1)} collective-permute-done((bf16[4,32,4224]{2,1,0:T(8,128)(2,1)S(1)}, bf16[4,32,4224]{2,1,0:T(8,128)(2,1)}, u32[]{:S(2)}, u32[]{:S(2)}) %collective-permute-start.8) | collective-permute-done | bytes 1081376 | tf_op jit(solution)/shard_map/ppermute | solution.py:641
  95.9 13.5 %project.1 = (bf16[1024,1024]{1,0:T(8,128)(2,1)}, bf16[1024,3072]{1,0:T(8,128)(2,1)}, f32[16,1024]{1,0:T(8,128)}) custom-call(s32[32]{0:T(128)} %select_reduce_fusion.order_ref, bf16[1024,1024]{1,0:T(8,128)(2,1)} %refs_11_.1, f32[1024,128]{1,0:T(8,128)} %norm.1.stat_ref.refs_8_, bf16[4,32,4224]{2,1,0:T(8,128)(2,1)} %copy-done, ...), custom_call_target="tpu_custom_call" | custom-call | flops 1000 | bytes 1000 | tf_op jit(solution)/shard_map/project/pallas_call | solution.py:70
  109.4 22.7 %attend.1 = (bf16[1024,1024]{1,0:T(8,128)(2,1)}, f32[16,1024]{1,0:T(8,128)}) custom-call(s32[1]{0:T(128)S(6)} %copy.62.prefix_ref, s32[1]{0:T(128)S(6)} %copy.63.padding_ref, bf16[1024,3072]{1,0:T(8,128)(2,1)} %get-tuple-element.181.q_ref.k_ref.v_ref, bf16[1024,3072]{1,0:T(8,128)(2,1)} %get-tuple-element.181.q_ref.k_ref.v_ref, ...), custom_call_target="tpu_custom_call" | custom-call | flops 1000 | bytes 1000 | tf_op jit(solution)/shard_map/attend/pallas_call | solution.py:136
  132.1 7.9 %branch.1 = (f32[1024,1024]{1,0:T(8,128)}, bf16[1024,1024]{1,0:T(8,128)(2,1)}, bf16[1024,1024]{1,0:T(8,128)(2,1)}) custom-call(s32[32]{0:T(128)} %select_reduce_fusion.order_ref, bf16[1024,1024]{1,0:T(8,128)(2,1)} %get-tuple-element.182.ctx_ref.o_ref.refs_1_, bf16[1024,1024]{1,0:T(8,128)(2,1)} %refs_11_.1, ...), custom_call_target="tpu_custom_call" | custom-call | flops 1000 | bytes 1000 | tf_op jit(solution)/shard_map/branch/pallas_call | solution.py:162
  140.0 17.8 %all-gather.2.cloned.1.call-done.up_ref.down_ref = bf16[1024,8192]{1,0:T(8,128)(2,1)} async-done(((bf16[32,8192]{1,0:T(8,128)(2,1)}), bf16[1024,8192]{1,0:T(8,128)(2,1)}) %all-gather.2.cloned.1.call-update) | async-done | bytes 16777232 | tf_op jit(solution)/shard_map/all_gather | solution.py:746
  157.8 67.3 %ffn.1 = (bf16[1024,1024]{1,0:T(8,128)(2,1)}, bf16[1024,1024]{1,0:T(8,128)(2,1)}, bf16[1024,1024]{1,0:T(8,128)(2,1)}, bf16[16,32,4096]{2,1,0:T(8,128)(2,1)}, bf1...) custom-call(s32[32]{0:T(128)} %fusion.11.pos_ref, ...), custom_call_target="tpu_custom_call" | custom-call | flops 1000 | bytes 1000 | tf_op jit(solution)/shard_map/ffn/pallas_call | solution.py:305
  225.7 10.8 %attend_back.4 = (bf16[3,1024,512]{2,1,0:T(8,128)(2,1)}, f32[8,512]{1,0:T(8,128)}) custom-call(s32[1]{0:T(128)S(6)} %copy.62.prefix_ref, s32[1]{0:T(128)S(6)} %copy.63.padding_ref, bf16[1024,3072]{1,0:T(8,128)(2,1)} %get-tuple-element.181.q_ref.k_ref.v_ref, bf16[1024,3072]{1,0:T(8,128)(2,1)} %get-tuple-element.181.q_ref.k_ref.v_ref, ...), custom_call_target="tpu_custom_call" | custom-call | flops 1000 | bytes 1000 | tf_op jit(solution)/shard_map/attend_back/pallas_call | solution.py:378
  236.5 3.0 add_convert_fusion.1
  240.9 10.7 %attend_back.5 = (bf16[3,1024,512]{2,1,0:T(8,128)(2,1)}, f32[8,512]{1,0:T(8,128)}) custom-call(s32[1]{0:T(128)S(6)} %copy.62.prefix_ref, s32[1]{0:T(128)S(6)} %copy.63.padding_ref, bf16[1024,3072]{1,0:T(8,128)(2,1)} %get-tuple-element.181.q_ref.k_ref.v_ref, ...), custom_call_target="tpu_custom_call", output_to_operand_aliasing={{0}: (8, {}), {1}: (9, {})} | custom-call | flops 1000 | bytes 1000 | tf_op jit(solution)/shard_map/attend_back/pallas_call | solution.py:378
  251.7 4.3 %add_convert_fusion = bf16[8,32,4096]{2,1,0:T(8,128)(2,1)} fusion(bf16[16,32,4096]{2,1,0:T(8,128)(2,1)} %collective-permute-done.11, bf16[16,32,4096]{2,1,0:T(8,128)(2,1)} %get-tuple-element.249), kind=kLoop, calls=%fused_computation | loop fusion | flops 4194304 | bytes 6291456 | tf_op jit(solution)/shard_map/convert_element_type | solution.py:694
  256.6 10.6 %weight_grad.2 = (bf16[16,160,512]{2,1,0:T(8,128)(2,1)}, bf16[16,160,512]{2,1,0:T(8,128)(2,1)}) custom-call(s32[32]{0:T(128)} %copy-done.17, bf16[1024,1024]{1,0:T(8,128)(2,1)} %get-tuple-element.235.left_ref, bf16[3,1024,512]{2,1,0:T(8,128)(2,1)} %get-tuple-element.253.d_ref, bf16[1024,1024]{1,0:T(8,128)(2,1)} %get-tuple-element.206.refs_0_.refs_12_, ...), custom_call_target="tpu_custom_call" | custom-call | flops 1000 | bytes 1000 | tf_op jit(solution)/shard_map/weight_grad/pallas_call | solution.py:484
  267.2 10.9 %attend_back.6 = (bf16[3,1024,512]{2,1,0:T(8,128)(2,1)}, f32[8,512]{1,0:T(8,128)}) custom-call(s32[1]{0:T(128)S(6)} %copy.62.prefix_ref, s32[1]{0:T(128)S(6)} %copy.63.padding_ref, bf16[1024,3072]{1,0:T(8,128)(2,1)} %get-tuple-element.181.q_ref.k_ref.v_ref, bf16[1024,3072]{1,0:T(8,128)(2,1)} %get-tuple-element.181.q_ref.k_ref.v_ref, ...), custom_call_target="tpu_custom_call" | custom-call | flops 1000 | bytes 1000 | tf_op jit(solution)/shard_map/attend_back/pallas_call | solution.py:378
  278.1 3.3 add_convert_fusion.6
  283.0 10.7 %attend_back.7 = (bf16[3,1024,512]{2,1,0:T(8,128)(2,1)}, f32[8,512]{1,0:T(8,128)}) custom-call(s32[1]{0:T(128)S(6)} %copy.62.prefix_ref, s32[1]{0:T(128)S(6)} %copy.63.padding_ref, bf16[1024,3072]{1,0:T(8,128)(2,1)} %get-tuple-element.181.q_ref.k_ref.v_ref, ...), custom_call_target="tpu_custom_call", output_to_operand_aliasing={{0}: (8, {}), {1}: (9, {})} | custom-call | flops 1000 | bytes 1000 | tf_op jit(solution)/shard_map/attend_back/pallas_call | solution.py:378
  293.6 5.0 %collective-permute-done.14 = bf16[4,32,4096]{2,1,0:T(8,128)(2,1)} collective-permute-done((bf16[4,32,4096]{2,1,0:T(8,128)(2,1)}, bf16[4,32,4096]{2,1,0:T(8,128)(2,1)}, u32[]{:S(2)}, u32[]{:S(2)}) %collective-permute-start.14) | collective-permute-done | bytes 1048608 | tf_op jit(solution)/shard_map/ppermute | solution.py:641
  298.7 5.8 %add_convert_fusion.4 = (bf16[4,32,4096]{2,1,0:T(8,128)(2,1)}, bf16[4,32,4096]{2,1,0:T(8,128)(2,1)}) fusion(bf16[4,32,4096]{2,1,0:T(8,128)(2,1)} %collective-permute-done.14, bf16[8,32,4096]{2,1,0:T(8,128)(2,1)} %collective-permute-done.12, bf16[16,32,4096]{2,1,0:T(8,128)(2,1)} %collective-permute-done.10, bf16[16,32,4096]{2,1,0:T(8,128)(2,1)} %get-tuple-element.231, ...), kind=kLoop, calls=%fused_computation.4 | loop fusion | flops 7340032 | bytes 9437184 | tf_op jit(solution)/shard_map/convert_element_type | solution.py:692
  308.7 7.2 %weight_grad.3 = (bf16[16,112,512]{2,1,0:T(8,128)(2,1)}, bf16[16,112,512]{2,1,0:T(8,128)(2,1)}) custom-call(s32[32]{0:T(128)} %copy-done.17, bf16[1024,1024]{1,0:T(8,128)(2,1)} %get-tuple-element.235.left_ref, bf16[3,1024,512]{2,1,0:T(8,128)(2,1)} %get-tuple-element.219.d_ref, f32[32,512]{1,0:T(8,128)} %pad.9.refs_0_), custom_call_target="tpu_custom_call" | custom-call | flops 1000 | bytes 1000 | tf_op jit(solution)/shard_map/weight_grad/pallas_call | solution.py:484
  316.5 3.1 collective-permute-done.16
  319.6 4.1 add_convert_fusion.3
  323.7 2.7 add_convert_fusion.2
  327.9 8.3 %cotangent.2.refs_10_ = bf16[1024,1024]{1,0:T(8,128)(2,1)} custom-call(s32[32]{0:T(128)} %select_reduce_fusion.order_ref, bf16[3,1024,512]{2,1,0:T(8,128)(2,1)} %get-tuple-element.253.d_ref, bf16[4,32,4224]{2,1,0:T(8,128)(2,1)} %copy-done, bf16[4,32,4224]{2,1,0:T(8,128)(2,1)} %copy-done.1, bf16[4,32,4224]{2,1,0:T(8,128)(2,1)} %copy-done.2, ...), custom_call_target="tpu_custom_call" | custom-call | flops 1000 | bytes 1000 | tf_op jit(solution)/shard_map/cotangent/pallas_call | solution.py:556
  336.2 8.2 %collective-permute-done.18 = bf16[8,160,512]{2,1,0:T(8,128)(2,1)} collective-permute-done((bf16[8,160,512]{2,1,0:T(8,128)(2,1)}, bf16[8,160,512]{2,1,0:T(8,128)(2,1)}, u32[]{:S(2)}, u32[]{:S(2)}) %collective-permute-start.18) | collective-permute-done | bytes 1310752 | tf_op jit(solution)/shard_map/ppermute | solution.py:641
  344.4 2.6 add_convert_fusion.7
  351.6 12.4 %cotangent.3 = (bf16[1024,1024]{1,0:T(8,128)(2,1)}, f32[8,1024]{1,0:T(8,128)}) custom-call(s32[32]{0:T(128)} %select_reduce_fusion.order_ref, bf16[3,1024,512]{2,1,0:T(8,128)(2,1)} %get-tuple-element.219.d_ref, bf16[4,32,4224]{2,1,0:T(8,128)(2,1)} %copy-done, bf16[4,32,4224]{2,1,0:T(8,128)(2,1)} %copy-done.1, bf16[4,32,4224]{2,1,0:T(8,128)(2,1)} %copy-done.2, ...), custom_call_target="tpu_custom_call" | custom-call | flops 1000 | bytes 1000 | tf_op jit(solution)/shard_map/cotangent/pallas_call | solution.py:556
  364.8 4.4 %collective-permute-done.19 = bf16[8,112,512]{2,1,0:T(8,128)(2,1)S(1)} collective-permute-done((bf16[8,112,512]{2,1,0:T(8,128)(2,1)}, bf16[8,112,512]{2,1,0:T(8,128)(2,1)S(1)}, u32[]{:S(2)}, u32[]{:S(2)}) %collective-permute-start.19) | collective-permute-done | bytes 917536 | tf_op jit(solution)/shard_map/ppermute | solution.py:641
  384.2 6.5 %collective-permute-done.23 = f32[2,1024]{1,0:T(2,128)S(1)} collective-permute-done((f32[2,1024]{1,0:T(2,128)S(1)}, f32[2,1024]{1,0:T(2,128)S(1)}, u32[]{:S(2)}, u32[]{:S(2)}) %collective-permute-start.23) | collective-permute-done | bytes 8224 | tf_op jit(solution)/shard_map/ppermute | solution.py:785
  395.9 2.8 collective-permute-done.26
  (174 shorter events, 67.0 us)
Async XLA Ops:
  7.2 150.6 %all-gather.2.cloned.1.call-start = ((), (), s32[]{:S(2)}) async-start(), calls=%async_computation.2 | async-start | bytes 17301504 | tf_op jit(solution)/shard_map/all_gather | solution.py:746
  11.3 360.5 %reduce-scatter.3.cloned.1.call-start = ((), (), s32[]{:S(2)}) async-start(), calls=%async_computation.3 | async-start | bytes 1310720 | tf_op jit(solution)/shard_map/reduce_scatter | solution.py:698
  11.8 15.3 %collective-permute-start = (bf16[32,4224]{1,0:T(8,128)(2,1)S(1)}, bf16[32,4224]{1,0:T(8,128)(2,1)S(1)}, u32[]{:S(2)}, u32[]{:S(2)}) collective-permute-start(bf16[32,4224]{1,0:T(8,128)(2,1)S(1)} %get-tuple-element.336), channel_id=1, source_target_pairs={{0,1},{1,0},{2,3},{3,2},{4,5},{5,4},{6,7},{7,6},{8,9},{9,8},{10,11... | collective-permute-start | bytes 811016 | tf_op jit(solution)/shard_map/ppermute | solution.py:641
  14.9 26.6 %collective-permute-start.1 = (bf16[32,4224]{1,0:T(8,128)(2,1)S(1)}, bf16[32,4224]{1,0:T(8,128)(2,1)S(1)}, u32[]{:S(2)}, u32[]{:S(2)}) collective-permute-start(bf16[32,4224]{1,0:T(8,128)(2,1)S(1)} %get-tuple-element.336), channel_id=1, source_target_pairs={{0,2},{1,3},{2,0},{3,1},{4,6},{5,7},{6,4},{7,5},{8,10},{9,11},{10,... | collective-permute-start | bytes 811016 | tf_op jit(solution)/shard_map/ppermute | solution.py:641
  17.5 24.0 %collective-permute-start.2 = (bf16[32,4224]{1,0:T(8,128)(2,1)S(1)}, bf16[32,4224]{1,0:T(8,128)(2,1)S(1)}, u32[]{:S(2)}, u32[]{:S(2)}) collective-permute-start(bf16[32,4224]{1,0:T(8,128)(2,1)S(1)} %get-tuple-element.336), channel_id=1, source_target_pairs={{0,3},{1,2},{2,1},{3,0},{4,7},{5,6},{6,5},{7,4},{8,11},{9,10},{10,... | collective-permute-start | bytes 811016 | tf_op jit(solution)/shard_map/ppermute | solution.py:641
  41.7 32.4 %collective-permute-start.3 = (bf16[4,32,4224]{2,1,0:T(8,128)(2,1)S(1)}, bf16[4,32,4224]{2,1,0:T(8,128)(2,1)S(1)}, u32[]{:S(2)}, u32[]{:S(2)}) collective-permute-start(bf16[4,32,4224]{2,1,0:T(8,128)(2,1)S(1)} %pad_maximum_fusion.refs_0_.refs_8_), channel_id=1, source_target_pairs={{0,16},{1,17},{2,18},{3,19},{4,12},{5,13},{6,14},{7,15},{8,24},{9,... | collective-permute-start | bytes 3244040 | tf_op jit(solution)/shard_map/ppermute | solution.py:641
  43.3 33.1 %collective-permute-start.4 = (bf16[4,32,4224]{2,1,0:T(8,128)(2,1)S(1)}, bf16[4,32,4224]{2,1,0:T(8,128)(2,1)S(1)}, u32[]{:S(2)}, u32[]{:S(2)}) collective-permute-start(bf16[4,32,4224]{2,1,0:T(8,128)(2,1)S(1)} %pad_maximum_fusion.refs_0_.refs_8_), channel_id=1, source_target_pairs={{0,8},{1,9},{2,10},{3,11},{4,20},{5,21},{6,22},{7,23},{8,0},{9,1},... | collective-permute-start | bytes 3244040 | tf_op jit(solution)/shard_map/ppermute | solution.py:641
  76.4 15.7 %collective-permute-start.8 = (bf16[4,32,4224]{2,1,0:T(8,128)(2,1)S(1)}, bf16[4,32,4224]{2,1,0:T(8,128)(2,1)}, u32[]{:S(2)}, u32[]{:S(2)}) collective-permute-start(bf16[4,32,4224]{2,1,0:T(8,128)(2,1)S(1)} %collective-permute-done.3.refs_1_.refs_9_), channel_id=1, source_target_pairs={{0,8},{1,9},{2,10},{3,11},{4,20},{5,21},{6,22},{7,23},{8,0},{9,1},... | collective-permute-start | bytes 3244040 | tf_op jit(solution)/shard_map/ppermute | solution.py:641
  78.8 13.2 %collective-permute-start.5 = (bf16[4,32,4224]{2,1,0:T(8,128)(2,1)S(1)}, bf16[4,32,4224]{2,1,0:T(8,128)(2,1)S(1)}, u32[]{:S(2)}, u32[]{:S(2)}) collective-permute-start(bf16[4,32,4224]{2,1,0:T(8,128)(2,1)S(1)} %pad_maximum_fusion.refs_0_.refs_8_), channel_id=1, source_target_pairs={{0,4},{1,5},{2,6},{3,7},{4,0},{5,1},{6,2},{7,3},{8,12},{9,13},{10,... | collective-permute-start | bytes 3244040 | tf_op jit(solution)/shard_map/ppermute | solution.py:638
  78.8 13.2 %collective-permute-start.7 = (bf16[4,32,4224]{2,1,0:T(8,128)(2,1)S(1)}, bf16[4,32,4224]{2,1,0:T(8,128)(2,1)S(1)}, u32[]{:S(2)}, u32[]{:S(2)}) collective-permute-start(bf16[4,32,4224]{2,1,0:T(8,128)(2,1)S(1)} %collective-permute-done.4.refs_2_.refs_10_), channel_id=1, source_target_pairs={{0,4},{1,5},{2,6},{3,7},{4,0},{5,1},{6,2},{7,3},{8,12},{9,13},{10,... | collective-permute-start | bytes 3244040 | tf_op jit(solution)/shard_map/ppermute | solution.py:638
  225.1 11.4 %collective-permute-start.10 = (bf16[16,32,4096]{2,1,0:T(8,128)(2,1)}, bf16[16,32,4096]{2,1,0:T(8,128)(2,1)}, u32[]{:S(2)}, u32[]{:S(2)}) collective-permute-start(bf16[16,32,4096]{2,1,0:T(8,128)(2,1)} %get-tuple-element.192), channel_id=1, source_target_pairs={{0,4},{1,5},{2,6},{3,7},{4,0},{5,1},{6,2},{7,3},{8,12},{9,13},{10,... | collective-permute-start | bytes 12582920 | tf_op jit(solution)/shard_map/ppermute | solution.py:638
  225.4 26.3 %collective-permute-start.11 = (bf16[16,32,4096]{2,1,0:T(8,128)(2,1)}, bf16[16,32,4096]{2,1,0:T(8,128)(2,1)}, u32[]{:S(2)}, u32[]{:S(2)}) collective-permute-start(bf16[16,32,4096]{2,1,0:T(8,128)(2,1)} %get-tuple-element.201), channel_id=1, source_target_pairs={{0,4},{1,5},{2,6},{3,7},{4,0},{5,1},{6,2},{7,3},{8,12},{9,13},{10,... | collective-permute-start | bytes 12582920 | tf_op jit(solution)/shard_map/ppermute | solution.py:638
  239.5 38.6 %collective-permute-start.12 = (bf16[8,32,4096]{2,1,0:T(8,128)(2,1)S(1)}, bf16[8,32,4096]{2,1,0:T(8,128)(2,1)}, u32[]{:S(2)}, u32[]{:S(2)}) collective-permute-start(bf16[8,32,4096]{2,1,0:T(8,128)(2,1)S(1)} %add_convert_fusion.1), channel_id=1, source_target_pairs={{0,8},{1,9},{2,10},{3,11},{4,20},{5,21},{6,22},{7,23},{8,0},{9,1},... | collective-permute-start | bytes 6291464 | tf_op jit(solution)/shard_map/ppermute | solution.py:641
  256.0 37.7 %collective-permute-start.13 = (bf16[8,32,4096]{2,1,0:T(8,128)(2,1)}, bf16[8,32,4096]{2,1,0:T(8,128)(2,1)}, u32[]{:S(2)}, u32[]{:S(2)}) collective-permute-start(bf16[8,32,4096]{2,1,0:T(8,128)(2,1)} %add_convert_fusion), channel_id=1, source_target_pairs={{0,8},{1,9},{2,10},{3,11},{4,20},{5,21},{6,22},{7,23},{8,0},{9,1},... | collective-permute-start | bytes 6291464 | tf_op jit(solution)/shard_map/ppermute | solution.py:641
  281.5 17.2 %collective-permute-start.14 = (bf16[4,32,4096]{2,1,0:T(8,128)(2,1)}, bf16[4,32,4096]{2,1,0:T(8,128)(2,1)}, u32[]{:S(2)}, u32[]{:S(2)}) collective-permute-start(bf16[4,32,4096]{2,1,0:T(8,128)(2,1)} %add_convert_fusion.6), channel_id=1, source_target_pairs={{0,16},{1,17},{2,18},{3,19},{4,12},{5,13},{6,14},{7,15},{8,24},{9,... | collective-permute-start | bytes 3145736 | tf_op jit(solution)/shard_map/ppermute | solution.py:641
  283.0 33.5 %collective-permute-start.15 = (bf16[16,160,512]{2,1,0:T(8,128)(2,1)}, bf16[16,160,512]{2,1,0:T(8,128)(2,1)S(1)}, u32[]{:S(2)}, u32[]{:S(2)}) collective-permute-start(bf16[16,160,512]{2,1,0:T(8,128)(2,1)} %get-tuple-element.241), channel_id=1, source_target_pairs={{0,4},{1,5},{2,6},{3,7},{4,0},{5,1},{6,2},{7,3},{8,12},{9,13},{10,... | collective-permute-start | bytes 7864328 | tf_op jit(solution)/shard_map/ppermute | solution.py:638
  304.5 15.1 %collective-permute-start.16 = (bf16[4,32,4096]{2,1,0:T(8,128)(2,1)}, bf16[4,32,4096]{2,1,0:T(8,128)(2,1)}, u32[]{:S(2)}, u32[]{:S(2)}) collective-permute-start(bf16[4,32,4096]{2,1,0:T(8,128)(2,1)} %get-tuple-element.245), channel_id=1, source_target_pairs={{0,16},{1,17},{2,18},{3,19},{4,12},{5,13},{6,14},{7,15},{8,24},{9,... | collective-permute-start | bytes 3145736 | tf_op jit(solution)/shard_map/ppermute | solution.py:641
  315.9 20.3 %collective-permute-start.17 = (bf16[16,112,512]{2,1,0:T(8,128)(2,1)}, bf16[16,112,512]{2,1,0:T(8,128)(2,1)}, u32[]{:S(2)}, u32[]{:S(2)}) collective-permute-start(bf16[16,112,512]{2,1,0:T(8,128)(2,1)} %get-tuple-element.254), channel_id=1, source_target_pairs={{0,4},{1,5},{2,6},{3,7},{4,0},{5,1},{6,2},{7,3},{8,12},{9,13},{10,... | collective-permute-start | bytes 5505032 | tf_op jit(solution)/shard_map/ppermute | solution.py:638
  316.2 77.6 %reduce-scatter.5.cloned.1.call-start = ((), (), s32[]{:S(2)}) async-start(), calls=%async_computation.4 | async-start | bytes 1310720 | tf_op jit(solution)/shard_map/reduce_scatter | solution.py:698
  326.5 17.9 %collective-permute-start.18 = (bf16[8,160,512]{2,1,0:T(8,128)(2,1)}, bf16[8,160,512]{2,1,0:T(8,128)(2,1)}, u32[]{:S(2)}, u32[]{:S(2)}) collective-permute-start(bf16[8,160,512]{2,1,0:T(8,128)(2,1)} %add_convert_fusion.2), channel_id=1, source_target_pairs={{0,8},{1,9},{2,10},{3,11},{4,20},{5,21},{6,22},{7,23},{8,0},{9,1},... | collective-permute-start | bytes 3932168 | tf_op jit(solution)/shard_map/ppermute | solution.py:641
  349.4 19.7 %collective-permute-start.19 = (bf16[8,112,512]{2,1,0:T(8,128)(2,1)}, bf16[8,112,512]{2,1,0:T(8,128)(2,1)S(1)}, u32[]{:S(2)}, u32[]{:S(2)}) collective-permute-start(bf16[8,112,512]{2,1,0:T(8,128)(2,1)} %add_convert_fusion.7), channel_id=1, source_target_pairs={{0,8},{1,9},{2,10},{3,11},{4,20},{5,21},{6,22},{7,23},{8,0},{9,1},... | collective-permute-start | bytes 2752520 | tf_op jit(solution)/shard_map/ppermute | solution.py:641
  350.9 20.9 %collective-permute-start.20 = (bf16[4,160,512]{2,1,0:T(8,128)(2,1)}, bf16[4,160,512]{2,1,0:T(8,128)(2,1)}, u32[]{:S(2)}, u32[]{:S(2)}) collective-permute-start(bf16[4,160,512]{2,1,0:T(8,128)(2,1)} %add_convert_fusion.8), channel_id=1, source_target_pairs={{0,16},{1,17},{2,18},{3,19},{4,12},{5,13},{6,14},{7,15},{8,24},{9,... | collective-permute-start | bytes 1966088 | tf_op jit(solution)/shard_map/ppermute | solution.py:641
  371.3 8.8 %collective-permute-start.22 = (bf16[4,112,512]{2,1,0:T(8,128)(2,1)}, bf16[4,112,512]{2,1,0:T(8,128)(2,1)}, u32[]{:S(2)}, u32[]{:S(2)}) collective-permute-start(bf16[4,112,512]{2,1,0:T(8,128)(2,1)} %add_convert_fusion.9), channel_id=1, source_target_pairs={{0,16},{1,17},{2,18},{3,19},{4,12},{5,13},{6,14},{7,15},{8,24},{9,... | collective-permute-start | bytes 1376264 | tf_op jit(solution)/shard_map/ppermute | solution.py:641
  371.8 6.8 %collective-permute-start.21 = (f32[2,1024]{1,0:T(2,128)S(1)}, f32[2,1024]{1,0:T(2,128)S(1)}, u32[]{:S(2)}, u32[]{:S(2)}) collective-permute-start(f32[2,1024]{1,0:T(2,128)S(1)} %slice.320), channel_id=1, source_target_pairs={{0,4},{1,5},{2,6},{3,7},{4,0},{5,1},{6,2},{7,3},{8,12},{9,13},{10,... | collective-permute-start | bytes 24584 | tf_op jit(solution)/shard_map/ppermute | solution.py:785
  374.2 25.9 %collective-permute-start.27 = (bf16[1,160,512]{2,1,0:T(8,128)(2,1)}, bf16[1,160,512]{2,1,0:T(8,128)(2,1)}, u32[]{:S(2)}, u32[]{:S(2)}) collective-permute-start(bf16[1,160,512]{2,1,0:T(8,128)(2,1)} %get-tuple-element.302), channel_id=1, source_target_pairs={{0,1},{1,0},{2,3},{3,2},{4,5},{5,4},{6,7},{7,6},{8,9},{9,8},{10,11... | collective-permute-start | bytes 491528 | tf_op jit(solution)/shard_map/ppermute | solution.py:641
  374.2 25.9 %collective-permute-start.28 = (bf16[1,160,512]{2,1,0:T(8,128)(2,1)}, bf16[1,160,512]{2,1,0:T(8,128)(2,1)}, u32[]{:S(2)}, u32[]{:S(2)}) collective-permute-start(bf16[1,160,512]{2,1,0:T(8,128)(2,1)} %get-tuple-element.303), channel_id=1, source_target_pairs={{0,2},{1,3},{2,0},{3,1},{4,6},{5,7},{6,4},{7,5},{8,10},{9,11},{10,... | collective-permute-start | bytes 491528 | tf_op jit(solution)/shard_map/ppermute | solution.py:641
  376.1 24.1 %collective-permute-start.29 = (bf16[1,160,512]{2,1,0:T(8,128)(2,1)}, bf16[1,160,512]{2,1,0:T(8,128)(2,1)}, u32[]{:S(2)}, u32[]{:S(2)}) collective-permute-start(bf16[1,160,512]{2,1,0:T(8,128)(2,1)} %get-tuple-element.304), channel_id=1, source_target_pairs={{0,3},{1,2},{2,1},{3,0},{4,7},{5,6},{6,5},{7,4},{8,11},{9,10},{10,... | collective-permute-start | bytes 491528 | tf_op jit(solution)/shard_map/ppermute | solution.py:641
  382.2 9.5 %collective-permute-start.24 = (bf16[1,112,512]{2,1,0:T(8,128)(2,1)S(1)}, bf16[1,112,512]{2,1,0:T(8,128)(2,1)}, u32[]{:S(2)}, u32[]{:S(2)}) collective-permute-start(bf16[1,112,512]{2,1,0:T(8,128)(2,1)S(1)} %get-tuple-element.332), channel_id=1, source_target_pairs={{0,1},{1,0},{2,3},{3,2},{4,5},{5,4},{6,7},{7,6},{8,9},{9,8},{10,11... | collective-permute-start | bytes 344072 | tf_op jit(solution)/shard_map/ppermute | solution.py:641
  382.2 8.5 %collective-permute-start.23 = (f32[2,1024]{1,0:T(2,128)S(1)}, f32[2,1024]{1,0:T(2,128)S(1)}, u32[]{:S(2)}, u32[]{:S(2)}) collective-permute-start(f32[2,1024]{1,0:T(2,128)S(1)} %add.250), channel_id=1, source_target_pairs={{0,1},{1,0},{2,3},{3,2},{4,5},{5,4},{6,7},{7,6},{8,9},{9,8},{10,11... | collective-permute-start | bytes 24584 | tf_op jit(solution)/shard_map/ppermute | solution.py:785
  390.7 8.1 %collective-permute-start.26 = (bf16[1,112,512]{2,1,0:T(8,128)(2,1)}, bf16[1,112,512]{2,1,0:T(8,128)(2,1)}, u32[]{:S(2)}, u32[]{:S(2)}) collective-permute-start(bf16[1,112,512]{2,1,0:T(8,128)(2,1)} %get-tuple-element.331), channel_id=1, source_target_pairs={{0,2},{1,3},{2,0},{3,1},{4,6},{5,7},{6,4},{7,5},{8,10},{9,11},{10,... | collective-permute-start | bytes 344072 | tf_op jit(solution)/shard_map/ppermute | solution.py:641
  391.7 8.5 %collective-permute-start.25 = (f32[2,1024]{1,0:T(2,128)S(1)}, f32[2,1024]{1,0:T(2,128)S(1)}, u32[]{:S(2)}, u32[]{:S(2)}) collective-permute-start(f32[2,1024]{1,0:T(2,128)S(1)} %add.254), channel_id=1, source_target_pairs={{0,2},{1,3},{2,0},{3,1},{4,6},{5,7},{6,4},{7,5},{8,10},{9,11},{10,... | collective-permute-start | bytes 24584 | tf_op jit(solution)/shard_map/ppermute | solution.py:785
  398.8 6.8 %collective-permute-start.31 = (bf16[1,112,512]{2,1,0:T(8,128)(2,1)}, bf16[1,112,512]{2,1,0:T(8,128)(2,1)S(1)}, u32[]{:S(2)}, u32[]{:S(2)}) collective-permute-start(bf16[1,112,512]{2,1,0:T(8,128)(2,1)} %get-tuple-element.330), channel_id=1, source_target_pairs={{0,3},{1,2},{2,1},{3,0},{4,7},{5,6},{6,5},{7,4},{8,11},{9,10},{10,... | collective-permute-start | bytes 344072 | tf_op jit(solution)/shard_map/ppermute | solution.py:641
  (31 other events, 216.5 us)
Sparse Core Ops, SparseCore 0:
  11.6 146.1 all-gather.1
  316.3 25.3 reduce-scatter.2
  344.1 25.7 reduce-scatter.4

commit v5 on v4

--- a/solution.py
+++ b/solution.py
@@ -779,7 +779,7 @@
     g4 = Reduction(plan, *weight_grad(pos, n1b, d2[0], small=early))
     da = step(d1[0], g4.terms[0], g3, g2)
     part = cotangent(order, da, inward, 0)
-    part = step(part, part, g4, g3)
+    part = step(part, part, g4)
     tokens_grad, end = cotangent(order, d2[0], inward, 1, part, stats, vecs, tokens, low)
     bits = [plan.core] + [bit for bit in range(total.bit_length() - 1) if bit != plan.core]
     swap = lambda v, bit: lax.ppermute(v, AXES, [(i, i ^ (1 << bit)) for i in range(total)])
@@ -796,8 +796,8 @@
         if k < arriving:
             at = k - arriving
             other, g4.terms[at] = tie(other, g4.terms[at])
-        if k == 1:
-            other, = tie(other, g3)
+        if k == 0:
+            other = step(other, other, g3)
     late = lax.dynamic_slice_in_dim(end + other, me * n, n, axis=1)
     in1, in2 = g3.finish(), g4.finish()
     up_grad, down_grad = owned([g1.terms, g2.terms], D, blocks)

time: 426 us -> 414 us (0.972)
  waiting for transfers between devices: 116 us -> 106 us
    ppermute x20, waiting for transfers between devices: 90.7 us -> 82.2 us  [exchange(): return lax.ppermute(x, AXES, plan.pairs(stage, j))]
  transfers between devices with their start and end apart: 36 -> 36, of which waited for: 15 -> 16; matrix products, arithmetic and copies ran while one was open for 10% -> 10% of each run, Pallas kernels for 32% -> 32%
where the time goes in v5:
time: 414 us; the launch traced here: 407 us
  Pallas kernels  199 us (48%)
  waiting for transfers between devices  106 us (26%)
  other arithmetic  39.7 us (10%)
  starting transfers between devices  35 us (8%)
  between operations  16.1 us (4%)
  local copies, waits for them, and re-layouts  11 us (3%)
    ppermute x20, waiting for transfers between devices, exchange(): return lax.ppermute(x, AXES, plan.pairs(stage, j))  82.2 us
    pallas_call x1, Pallas kernels, ffn(): pl.pallas_call(functools.partial(ffn_kernel, shards=shards, per=per, bloc...  67.3 us
    pallas_call x4, Pallas kernels, attend_back(): pl.pallas_call(functools.partial(attend_back_kernel, bq=bq, first=first),...  43.2 us
    ppermute x20, starting transfers between devices, exchange(): return lax.ppermute(x, AXES, plan.pairs(stage, j))  27.2 us
    convert_element_type x9, other arithmetic, add(): sum((t[j * part:(j + 1) * part].astype(f32) for t in self.terms))  25.6 us
    pallas_call x1, Pallas kernels, attend(): pl.pallas_call(functools.partial(attend_kernel, bq=bq), grid=(n,), in_spe...  22.6 us
    pallas_call x2, Pallas kernels, cotangent(): pl.pallas_call(functools.partial(cotangent_kernel, count=len(pieces), fin...  20.7 us
    pallas_call x2, Pallas kernels, weight_grad(): pl.pallas_call(functools.partial(weight_grad_kernel, each=each, other=oth...  17.9 us
  transfers between devices with their start and end apart: 36, of which 16 were waited for; matrix products, arithmetic and copies ran while one was open for 10% of the time, Pallas kernels for 32%

profile of v5, /device:TPU:0, one launch (start us, length us, event | category | flops | bytes accessed | tf_op | source)
XLA Modules:
  0.0 407.0 jit_solution(11873969209586544807)
XLA Ops:
  11.8 3.1 collective-permute-start
  14.9 2.6 collective-permute-start.1
  17.5 4.1 norm.1.stat_ref.refs_8_
  21.6 5.6 %collective-permute-done = bf16[32,4224]{1,0:T(8,128)(2,1)S(1)} collective-permute-done((bf16[32,4224]{1,0:T(8,128)(2,1)S(1)}, bf16[32,4224]{1,0:T(8,128)(2,1)S(1)}, u32[]{:S(2)}, u32[]{:S(2)}) %collective-permute-start) | collective-permute-done | bytes 270368 | tf_op jit(solution)/shard_map/ppermute | solution.py:641
  27.1 14.4 %collective-permute-done.1 = bf16[32,4224]{1,0:T(8,128)(2,1)S(1)} collective-permute-done((bf16[32,4224]{1,0:T(8,128)(2,1)S(1)}, bf16[32,4224]{1,0:T(8,128)(2,1)S(1)}, u32[]{:S(2)}, u32[]{:S(2)}) %collective-permute-start.1) | collective-permute-done | bytes 270368 | tf_op jit(solution)/shard_map/ppermute | solution.py:641
  44.8 29.3 %collective-permute-done.3.refs_1_.refs_9_ = bf16[4,32,4224]{2,1,0:T(8,128)(2,1)S(1)} collective-permute-done((bf16[4,32,4224]{2,1,0:T(8,128)(2,1)S(1)}, bf16[4,32,4224]{2,1,0:T(8,128)(2,1)S(1)}, u32[]{:S(2)}, u32[]{:S(2)}) %collective-permute-start.3) | collective-permute-done | bytes 1081376 | tf_op jit(solution)/shard_map/ppermute | solution.py:641
  76.4 2.5 collective-permute-start.8
  79.4 12.7 %collective-permute-done.8.refs_3_.refs_11_ = bf16[4,32,4224]{2,1,0:T(8,128)(2,1)} collective-permute-done((bf16[4,32,4224]{2,1,0:T(8,128)(2,1)S(1)}, bf16[4,32,4224]{2,1,0:T(8,128)(2,1)}, u32[]{:S(2)}, u32[]{:S(2)}) %collective-permute-start.8) | collective-permute-done | bytes 1081376 | tf_op jit(solution)/shard_map/ppermute | solution.py:641
  95.9 13.5 %project.1 = (bf16[1024,1024]{1,0:T(8,128)(2,1)}, bf16[1024,3072]{1,0:T(8,128)(2,1)}, f32[16,1024]{1,0:T(8,128)}) custom-call(s32[32]{0:T(128)} %select_reduce_fusion.order_ref, bf16[1024,1024]{1,0:T(8,128)(2,1)} %refs_11_.1, f32[1024,128]{1,0:T(8,128)} %norm.1.stat_ref.refs_8_, bf16[4,32,4224]{2,1,0:T(8,128)(2,1)} %copy-done, ...), custom_call_target="tpu_custom_call" | custom-call | flops 1000 | bytes 1000 | tf_op jit(solution)/shard_map/project/pallas_call | solution.py:70
  109.4 22.6 %attend.1 = (bf16[1024,1024]{1,0:T(8,128)(2,1)}, f32[16,1024]{1,0:T(8,128)}) custom-call(s32[1]{0:T(128)S(6)} %copy.62.prefix_ref, s32[1]{0:T(128)S(6)} %copy.63.padding_ref, bf16[1024,3072]{1,0:T(8,128)(2,1)} %get-tuple-element.175.q_ref.k_ref.v_ref, bf16[1024,3072]{1,0:T(8,128)(2,1)} %get-tuple-element.175.q_ref.k_ref.v_ref, ...), custom_call_target="tpu_custom_call" | custom-call | flops 1000 | bytes 1000 | tf_op jit(solution)/shard_map/attend/pallas_call | solution.py:136
  132.1 8.0 %branch.1 = (f32[1024,1024]{1,0:T(8,128)}, bf16[1024,1024]{1,0:T(8,128)(2,1)}, bf16[1024,1024]{1,0:T(8,128)(2,1)}) custom-call(s32[32]{0:T(128)} %select_reduce_fusion.order_ref, bf16[1024,1024]{1,0:T(8,128)(2,1)} %get-tuple-element.176.ctx_ref.o_ref.refs_1_, bf16[1024,1024]{1,0:T(8,128)(2,1)} %refs_11_.1, ...), custom_call_target="tpu_custom_call" | custom-call | flops 1000 | bytes 1000 | tf_op jit(solution)/shard_map/branch/pallas_call | solution.py:162
  140.0 17.7 %all-gather.2.cloned.1.call-done.up_ref.down_ref = bf16[1024,8192]{1,0:T(8,128)(2,1)} async-done(((bf16[32,8192]{1,0:T(8,128)(2,1)}), bf16[1024,8192]{1,0:T(8,128)(2,1)}) %all-gather.2.cloned.1.call-update) | async-done | bytes 16777232 | tf_op jit(solution)/shard_map/all_gather | solution.py:746
  157.8 67.3 %ffn.1 = (bf16[1024,1024]{1,0:T(8,128)(2,1)}, bf16[1024,1024]{1,0:T(8,128)(2,1)}, bf16[1024,1024]{1,0:T(8,128)(2,1)}, bf16[16,32,4096]{2,1,0:T(8,128)(2,1)}, bf1...) custom-call(s32[32]{0:T(128)} %fusion.11.pos_ref, ...), custom_call_target="tpu_custom_call" | custom-call | flops 1000 | bytes 1000 | tf_op jit(solution)/shard_map/ffn/pallas_call | solution.py:305
  225.7 10.8 %attend_back.4 = (bf16[3,1024,512]{2,1,0:T(8,128)(2,1)}, f32[8,512]{1,0:T(8,128)}) custom-call(s32[1]{0:T(128)S(6)} %copy.62.prefix_ref, s32[1]{0:T(128)S(6)} %copy.63.padding_ref, bf16[1024,3072]{1,0:T(8,128)(2,1)} %get-tuple-element.175.q_ref.k_ref.v_ref, bf16[1024,3072]{1,0:T(8,128)(2,1)} %get-tuple-element.175.q_ref.k_ref.v_ref, ...), custom_call_target="tpu_custom_call" | custom-call | flops 1000 | bytes 1000 | tf_op jit(solution)/shard_map/attend_back/pallas_call | solution.py:378
  236.5 4.4 %add_convert_fusion.1 = bf16[8,32,4096]{2,1,0:T(8,128)(2,1)} fusion(bf16[16,32,4096]{2,1,0:T(8,128)(2,1)} %collective-permute-done.10, bf16[16,32,4096]{2,1,0:T(8,128)(2,1)} %get-tuple-element.225), kind=kLoop, calls=%fused_computation.1 | loop fusion | flops 4194304 | bytes 6291456 | tf_op jit(solution)/shard_map/convert_element_type | solution.py:694
  242.3 10.8 %attend_back.5 = (bf16[3,1024,512]{2,1,0:T(8,128)(2,1)}, f32[8,512]{1,0:T(8,128)}) custom-call(s32[1]{0:T(128)S(6)} %copy.62.prefix_ref, s32[1]{0:T(128)S(6)} %copy.63.padding_ref, bf16[1024,3072]{1,0:T(8,128)(2,1)} %get-tuple-element.175.q_ref.k_ref.v_ref, ...), custom_call_target="tpu_custom_call", output_to_operand_aliasing={{0}: (8, {}), {1}: (9, {})} | custom-call | flops 1000 | bytes 1000 | tf_op jit(solution)/shard_map/attend_back/pallas_call | solution.py:378
  253.0 4.4 %add_convert_fusion = bf16[8,32,4096]{2,1,0:T(8,128)(2,1)} fusion(bf16[16,32,4096]{2,1,0:T(8,128)(2,1)} %collective-permute-done.11, bf16[16,32,4096]{2,1,0:T(8,128)(2,1)} %get-tuple-element.243), kind=kLoop, calls=%fused_computation | loop fusion | flops 4194304 | bytes 6291456 | tf_op jit(solution)/shard_map/convert_element_type | solution.py:694
  258.0 10.5 %weight_grad.2 = (bf16[16,160,512]{2,1,0:T(8,128)(2,1)}, bf16[16,160,512]{2,1,0:T(8,128)(2,1)}) custom-call(s32[32]{0:T(128)} %copy-done.21, bf16[1024,1024]{1,0:T(8,128)(2,1)} %get-tuple-element.229.left_ref, bf16[3,1024,512]{2,1,0:T(8,128)(2,1)} %get-tuple-element.247.d_ref, bf16[1024,1024]{1,0:T(8,128)(2,1)} %get-tuple-element.200.refs_0_.refs_12_, ...), custom_call_target="tpu_custom_call" | custom-call | flops 1000 | bytes 1000 | tf_op jit(solution)/shard_map/weight_grad/pallas_call | solution.py:484
  268.6 10.9 %attend_back.6 = (bf16[3,1024,512]{2,1,0:T(8,128)(2,1)}, f32[8,512]{1,0:T(8,128)}) custom-call(s32[1]{0:T(128)S(6)} %copy.62.prefix_ref, s32[1]{0:T(128)S(6)} %copy.63.padding_ref, bf16[1024,3072]{1,0:T(8,128)(2,1)} %get-tuple-element.175.q_ref.k_ref.v_ref, bf16[1024,3072]{1,0:T(8,128)(2,1)} %get-tuple-element.175.q_ref.k_ref.v_ref, ...), custom_call_target="tpu_custom_call" | custom-call | flops 1000 | bytes 1000 | tf_op jit(solution)/shard_map/attend_back/pallas_call | solution.py:378
  279.5 3.3 add_convert_fusion.6
  284.3 10.7 %attend_back.7 = (bf16[3,1024,512]{2,1,0:T(8,128)(2,1)}, f32[8,512]{1,0:T(8,128)}) custom-call(s32[1]{0:T(128)S(6)} %copy.62.prefix_ref, s32[1]{0:T(128)S(6)} %copy.63.padding_ref, bf16[1024,3072]{1,0:T(8,128)(2,1)} %get-tuple-element.175.q_ref.k_ref.v_ref, ...), custom_call_target="tpu_custom_call", output_to_operand_aliasing={{0}: (8, {}), {1}: (9, {})} | custom-call | flops 1000 | bytes 1000 | tf_op jit(solution)/shard_map/attend_back/pallas_call | solution.py:378
  295.0 5.1 %collective-permute-done.14 = bf16[4,32,4096]{2,1,0:T(8,128)(2,1)S(1)} collective-permute-done((bf16[4,32,4096]{2,1,0:T(8,128)(2,1)}, bf16[4,32,4096]{2,1,0:T(8,128)(2,1)S(1)}, u32[]{:S(2)}, u32[]{:S(2)}) %collective-permute-start.14) | collective-permute-done | bytes 1048608 | tf_op jit(solution)/shard_map/ppermute | solution.py:641
  300.1 5.2 %add_convert_fusion.4 = (bf16[4,32,4096]{2,1,0:T(8,128)(2,1)}, bf16[4,32,4096]{2,1,0:T(8,128)(2,1)}) fusion(bf16[4,32,4096]{2,1,0:T(8,128)(2,1)S(1)} %collective-permute-done.14, bf16[8,32,4096]{2,1,0:T(8,128)(2,1)} %collective-permute-done.12, bf16[16,32,4096]{2,1,0:T(8,128)(2,1)} %collective-permute-done.10, bf16[16,32,4096]{2,1,0:T(8,128)(2,1)} %get-tuple-element.225, ...), kind=kLoop, calls=%fused_computation.4 | loop fusion | flops 7340032 | bytes 9437184 | tf_op jit(solution)/shard_map/convert_element_type | solution.py:692
  309.6 7.4 %weight_grad.3 = (bf16[16,112,512]{2,1,0:T(8,128)(2,1)}, bf16[16,112,512]{2,1,0:T(8,128)(2,1)}) custom-call(s32[32]{0:T(128)} %copy-done.21, bf16[1024,1024]{1,0:T(8,128)(2,1)} %get-tuple-element.229.left_ref, bf16[3,1024,512]{2,1,0:T(8,128)(2,1)} %get-tuple-element.213.d_ref, f32[32,512]{1,0:T(8,128)} %pad.9.refs_0_), custom_call_target="tpu_custom_call" | custom-call | flops 1000 | bytes 1000 | tf_op jit(solution)/shard_map/weight_grad/pallas_call | solution.py:484
  317.5 2.9 collective-permute-done.16
  320.4 2.8 add_convert_fusion.2
  323.3 3.5 add_convert_fusion.3
  328.1 8.2 %cotangent.2.refs_10_ = bf16[1024,1024]{1,0:T(8,128)(2,1)} custom-call(s32[32]{0:T(128)} %select_reduce_fusion.order_ref, bf16[3,1024,512]{2,1,0:T(8,128)(2,1)} %get-tuple-element.247.d_ref, bf16[4,32,4224]{2,1,0:T(8,128)(2,1)} %copy-done, bf16[4,32,4224]{2,1,0:T(8,128)(2,1)} %copy-done.1, bf16[4,32,4224]{2,1,0:T(8,128)(2,1)} %copy-done.2, ...), custom_call_target="tpu_custom_call" | custom-call | flops 1000 | bytes 1000 | tf_op jit(solution)/shard_map/cotangent/pallas_call | solution.py:556
  336.4 2.6 add_convert_fusion.7
  339.7 12.4 %cotangent.3 = (bf16[1024,1024]{1,0:T(8,128)(2,1)}, f32[8,1024]{1,0:T(8,128)}) custom-call(s32[32]{0:T(128)} %select_reduce_fusion.order_ref, bf16[3,1024,512]{2,1,0:T(8,128)(2,1)} %get-tuple-element.213.d_ref, bf16[4,32,4224]{2,1,0:T(8,128)(2,1)} %copy-done, bf16[4,32,4224]{2,1,0:T(8,128)(2,1)} %copy-done.1, bf16[4,32,4224]{2,1,0:T(8,128)(2,1)} %copy-done.2, ...), custom_call_target="tpu_custom_call" | custom-call | flops 1000 | bytes 1000 | tf_op jit(solution)/shard_map/cotangent/pallas_call | solution.py:556
  361.4 3.9 collective-permute-done.21
  395.2 2.8 collective-permute-done.31
  (182 shorter events, 64.9 us)
Async XLA Ops:
  7.2 150.6 %all-gather.2.cloned.1.call-start = ((), (), s32[]{:S(2)}) async-start(), calls=%async_computation.2 | async-start | bytes 17301504 | tf_op jit(solution)/shard_map/all_gather | solution.py:746
  11.3 345.2 %reduce-scatter.3.cloned.1.call-start = ((), (), s32[]{:S(2)}) async-start(), calls=%async_computation.3 | async-start | bytes 1310720 | tf_op jit(solution)/shard_map/reduce_scatter | solution.py:698
  11.8 15.3 %collective-permute-start = (bf16[32,4224]{1,0:T(8,128)(2,1)S(1)}, bf16[32,4224]{1,0:T(8,128)(2,1)S(1)}, u32[]{:S(2)}, u32[]{:S(2)}) collective-permute-start(bf16[32,4224]{1,0:T(8,128)(2,1)S(1)} %get-tuple-element.324), channel_id=1, source_target_pairs={{0,1},{1,0},{2,3},{3,2},{4,5},{5,4},{6,7},{7,6},{8,9},{9,8},{10,11... | collective-permute-start | bytes 811016 | tf_op jit(solution)/shard_map/ppermute | solution.py:641
  14.9 26.6 %collective-permute-start.1 = (bf16[32,4224]{1,0:T(8,128)(2,1)S(1)}, bf16[32,4224]{1,0:T(8,128)(2,1)S(1)}, u32[]{:S(2)}, u32[]{:S(2)}) collective-permute-start(bf16[32,4224]{1,0:T(8,128)(2,1)S(1)} %get-tuple-element.324), channel_id=1, source_target_pairs={{0,2},{1,3},{2,0},{3,1},{4,6},{5,7},{6,4},{7,5},{8,10},{9,11},{10,... | collective-permute-start | bytes 811016 | tf_op jit(solution)/shard_map/ppermute | solution.py:641
  17.5 24.0 %collective-permute-start.2 = (bf16[32,4224]{1,0:T(8,128)(2,1)S(1)}, bf16[32,4224]{1,0:T(8,128)(2,1)S(1)}, u32[]{:S(2)}, u32[]{:S(2)}) collective-permute-start(bf16[32,4224]{1,0:T(8,128)(2,1)S(1)} %get-tuple-element.324), channel_id=1, source_target_pairs={{0,3},{1,2},{2,1},{3,0},{4,7},{5,6},{6,5},{7,4},{8,11},{9,10},{10,... | collective-permute-start | bytes 811016 | tf_op jit(solution)/shard_map/ppermute | solution.py:641
  41.7 32.4 %collective-permute-start.3 = (bf16[4,32,4224]{2,1,0:T(8,128)(2,1)S(1)}, bf16[4,32,4224]{2,1,0:T(8,128)(2,1)S(1)}, u32[]{:S(2)}, u32[]{:S(2)}) collective-permute-start(bf16[4,32,4224]{2,1,0:T(8,128)(2,1)S(1)} %pad_maximum_fusion.refs_0_.refs_8_), channel_id=1, source_target_pairs={{0,16},{1,17},{2,18},{3,19},{4,12},{5,13},{6,14},{7,15},{8,24},{9,... | collective-permute-start | bytes 3244040 | tf_op jit(solution)/shard_map/ppermute | solution.py:641
  43.3 33.1 %collective-permute-start.4 = (bf16[4,32,4224]{2,1,0:T(8,128)(2,1)S(1)}, bf16[4,32,4224]{2,1,0:T(8,128)(2,1)S(1)}, u32[]{:S(2)}, u32[]{:S(2)}) collective-permute-start(bf16[4,32,4224]{2,1,0:T(8,128)(2,1)S(1)} %pad_maximum_fusion.refs_0_.refs_8_), channel_id=1, source_target_pairs={{0,8},{1,9},{2,10},{3,11},{4,20},{5,21},{6,22},{7,23},{8,0},{9,1},... | collective-permute-start | bytes 3244040 | tf_op jit(solution)/shard_map/ppermute | solution.py:641
  76.4 15.7 %collective-permute-start.8 = (bf16[4,32,4224]{2,1,0:T(8,128)(2,1)S(1)}, bf16[4,32,4224]{2,1,0:T(8,128)(2,1)}, u32[]{:S(2)}, u32[]{:S(2)}) collective-permute-start(bf16[4,32,4224]{2,1,0:T(8,128)(2,1)S(1)} %collective-permute-done.3.refs_1_.refs_9_), channel_id=1, source_target_pairs={{0,8},{1,9},{2,10},{3,11},{4,20},{5,21},{6,22},{7,23},{8,0},{9,1},... | collective-permute-start | bytes 3244040 | tf_op jit(solution)/shard_map/ppermute | solution.py:641
  78.8 13.2 %collective-permute-start.5 = (bf16[4,32,4224]{2,1,0:T(8,128)(2,1)S(1)}, bf16[4,32,4224]{2,1,0:T(8,128)(2,1)S(1)}, u32[]{:S(2)}, u32[]{:S(2)}) collective-permute-start(bf16[4,32,4224]{2,1,0:T(8,128)(2,1)S(1)} %pad_maximum_fusion.refs_0_.refs_8_), channel_id=1, source_target_pairs={{0,4},{1,5},{2,6},{3,7},{4,0},{5,1},{6,2},{7,3},{8,12},{9,13},{10,... | collective-permute-start | bytes 3244040 | tf_op jit(solution)/shard_map/ppermute | solution.py:638
  78.8 13.2 %collective-permute-start.7 = (bf16[4,32,4224]{2,1,0:T(8,128)(2,1)S(1)}, bf16[4,32,4224]{2,1,0:T(8,128)(2,1)S(1)}, u32[]{:S(2)}, u32[]{:S(2)}) collective-permute-start(bf16[4,32,4224]{2,1,0:T(8,128)(2,1)S(1)} %collective-permute-done.4.refs_2_.refs_10_), channel_id=1, source_target_pairs={{0,4},{1,5},{2,6},{3,7},{4,0},{5,1},{6,2},{7,3},{8,12},{9,13},{10,... | collective-permute-start | bytes 3244040 | tf_op jit(solution)/shard_map/ppermute | solution.py:638
  225.1 11.4 %collective-permute-start.10 = (bf16[16,32,4096]{2,1,0:T(8,128)(2,1)}, bf16[16,32,4096]{2,1,0:T(8,128)(2,1)}, u32[]{:S(2)}, u32[]{:S(2)}) collective-permute-start(bf16[16,32,4096]{2,1,0:T(8,128)(2,1)} %get-tuple-element.186), channel_id=1, source_target_pairs={{0,4},{1,5},{2,6},{3,7},{4,0},{5,1},{6,2},{7,3},{8,12},{9,13},{10,... | collective-permute-start | bytes 12582920 | tf_op jit(solution)/shard_map/ppermute | solution.py:638
  225.4 27.6 %collective-permute-start.11 = (bf16[16,32,4096]{2,1,0:T(8,128)(2,1)}, bf16[16,32,4096]{2,1,0:T(8,128)(2,1)}, u32[]{:S(2)}, u32[]{:S(2)}) collective-permute-start(bf16[16,32,4096]{2,1,0:T(8,128)(2,1)} %get-tuple-element.195), channel_id=1, source_target_pairs={{0,4},{1,5},{2,6},{3,7},{4,0},{5,1},{6,2},{7,3},{8,12},{9,13},{10,... | collective-permute-start | bytes 12582920 | tf_op jit(solution)/shard_map/ppermute | solution.py:638
  240.9 38.6 %collective-permute-start.12 = (bf16[8,32,4096]{2,1,0:T(8,128)(2,1)}, bf16[8,32,4096]{2,1,0:T(8,128)(2,1)}, u32[]{:S(2)}, u32[]{:S(2)}) collective-permute-start(bf16[8,32,4096]{2,1,0:T(8,128)(2,1)} %add_convert_fusion.1), channel_id=1, source_target_pairs={{0,8},{1,9},{2,10},{3,11},{4,20},{5,21},{6,22},{7,23},{8,0},{9,1},... | collective-permute-start | bytes 6291464 | tf_op jit(solution)/shard_map/ppermute | solution.py:641
  257.4 37.6 %collective-permute-start.13 = (bf16[8,32,4096]{2,1,0:T(8,128)(2,1)}, bf16[8,32,4096]{2,1,0:T(8,128)(2,1)S(1)}, u32[]{:S(2)}, u32[]{:S(2)}) collective-permute-start(bf16[8,32,4096]{2,1,0:T(8,128)(2,1)} %add_convert_fusion), channel_id=1, source_target_pairs={{0,8},{1,9},{2,10},{3,11},{4,20},{5,21},{6,22},{7,23},{8,0},{9,1},... | collective-permute-start | bytes 6291464 | tf_op jit(solution)/shard_map/ppermute | solution.py:641
  282.8 17.3 %collective-permute-start.14 = (bf16[4,32,4096]{2,1,0:T(8,128)(2,1)}, bf16[4,32,4096]{2,1,0:T(8,128)(2,1)S(1)}, u32[]{:S(2)}, u32[]{:S(2)}) collective-permute-start(bf16[4,32,4096]{2,1,0:T(8,128)(2,1)} %add_convert_fusion.6), channel_id=1, source_target_pairs={{0,16},{1,17},{2,18},{3,19},{4,12},{5,13},{6,14},{7,15},{8,24},{9,... | collective-permute-start | bytes 3145736 | tf_op jit(solution)/shard_map/ppermute | solution.py:641
  284.3 33.2 %collective-permute-start.15 = (bf16[16,160,512]{2,1,0:T(8,128)(2,1)}, bf16[16,160,512]{2,1,0:T(8,128)(2,1)}, u32[]{:S(2)}, u32[]{:S(2)}) collective-permute-start(bf16[16,160,512]{2,1,0:T(8,128)(2,1)} %get-tuple-element.235), channel_id=1, source_target_pairs={{0,4},{1,5},{2,6},{3,7},{4,0},{5,1},{6,2},{7,3},{8,12},{9,13},{10,... | collective-permute-start | bytes 7864328 | tf_op jit(solution)/shard_map/ppermute | solution.py:638
  305.3 15.1 %collective-permute-start.16 = (bf16[4,32,4096]{2,1,0:T(8,128)(2,1)}, bf16[4,32,4096]{2,1,0:T(8,128)(2,1)}, u32[]{:S(2)}, u32[]{:S(2)}) collective-permute-start(bf16[4,32,4096]{2,1,0:T(8,128)(2,1)} %get-tuple-element.239), channel_id=1, source_target_pairs={{0,16},{1,17},{2,18},{3,19},{4,12},{5,13},{6,14},{7,15},{8,24},{9,... | collective-permute-start | bytes 3145736 | tf_op jit(solution)/shard_map/ppermute | solution.py:641
  316.9 19.4 %collective-permute-start.17 = (bf16[16,112,512]{2,1,0:T(8,128)(2,1)}, bf16[16,112,512]{2,1,0:T(8,128)(2,1)}, u32[]{:S(2)}, u32[]{:S(2)}) collective-permute-start(bf16[16,112,512]{2,1,0:T(8,128)(2,1)} %get-tuple-element.248), channel_id=1, source_target_pairs={{0,4},{1,5},{2,6},{3,7},{4,0},{5,1},{6,2},{7,3},{8,12},{9,13},{10,... | collective-permute-start | bytes 5505032 | tf_op jit(solution)/shard_map/ppermute | solution.py:638
  317.2 65.2 %reduce-scatter.5.cloned.1.call-start = ((), (), s32[]{:S(2)}) async-start(), calls=%async_computation.4 | async-start | bytes 1310720 | tf_op jit(solution)/shard_map/reduce_scatter | solution.py:698
  326.8 29.8 %collective-permute-start.19 = (bf16[8,160,512]{2,1,0:T(8,128)(2,1)}, bf16[8,160,512]{2,1,0:T(8,128)(2,1)}, u32[]{:S(2)}, u32[]{:S(2)}) collective-permute-start(bf16[8,160,512]{2,1,0:T(8,128)(2,1)} %add_convert_fusion.2), channel_id=1, source_target_pairs={{0,8},{1,9},{2,10},{3,11},{4,20},{5,21},{6,22},{7,23},{8,0},{9,1},... | collective-permute-start | bytes 3932168 | tf_op jit(solution)/shard_map/ppermute | solution.py:641
  339.0 15.4 %collective-permute-start.18 = (bf16[8,112,512]{2,1,0:T(8,128)(2,1)}, bf16[8,112,512]{2,1,0:T(8,128)(2,1)S(1)}, u32[]{:S(2)}, u32[]{:S(2)}) collective-permute-start(bf16[8,112,512]{2,1,0:T(8,128)(2,1)} %add_convert_fusion.7), channel_id=1, source_target_pairs={{0,8},{1,9},{2,10},{3,11},{4,20},{5,21},{6,22},{7,23},{8,0},{9,1},... | collective-permute-start | bytes 2752520 | tf_op jit(solution)/shard_map/ppermute | solution.py:641
  356.5 8.7 %collective-permute-start.21 = (bf16[4,112,512]{2,1,0:T(8,128)(2,1)}, bf16[4,112,512]{2,1,0:T(8,128)(2,1)S(1)}, u32[]{:S(2)}, u32[]{:S(2)}) collective-permute-start(bf16[4,112,512]{2,1,0:T(8,128)(2,1)} %add_convert_fusion.9), channel_id=1, source_target_pairs={{0,16},{1,17},{2,18},{3,19},{4,12},{5,13},{6,14},{7,15},{8,24},{9,... | collective-permute-start | bytes 1376264 | tf_op jit(solution)/shard_map/ppermute | solution.py:641
  359.6 13.5 %collective-permute-start.24 = (bf16[4,160,512]{2,1,0:T(8,128)(2,1)S(1)}, bf16[4,160,512]{2,1,0:T(8,128)(2,1)S(1)}, u32[]{:S(2)}, u32[]{:S(2)}) collective-permute-start(bf16[4,160,512]{2,1,0:T(8,128)(2,1)S(1)} %add_convert_fusion.8), channel_id=1, source_target_pairs={{0,16},{1,17},{2,18},{3,19},{4,12},{5,13},{6,14},{7,15},{8,24},{9,... | collective-permute-start | bytes 1966088 | tf_op jit(solution)/shard_map/ppermute | solution.py:641
  367.4 5.7 %collective-permute-start.23 = (bf16[1,112,512]{2,1,0:T(8,128)(2,1)S(1)}, bf16[1,112,512]{2,1,0:T(8,128)(2,1)S(1)}, u32[]{:S(2)}, u32[]{:S(2)}) collective-permute-start(bf16[1,112,512]{2,1,0:T(8,128)(2,1)S(1)} %get-tuple-element.320), channel_id=1, source_target_pairs={{0,1},{1,0},{2,3},{3,2},{4,5},{5,4},{6,7},{7,6},{8,9},{9,8},{10,11... | collective-permute-start | bytes 344072 | tf_op jit(solution)/shard_map/ppermute | solution.py:641
  367.4 5.7 %collective-permute-start.22 = (f32[2,1024]{1,0:T(2,128)S(1)}, f32[2,1024]{1,0:T(2,128)S(1)}, u32[]{:S(2)}, u32[]{:S(2)}) collective-permute-start(f32[2,1024]{1,0:T(2,128)S(1)} %add.241), channel_id=1, source_target_pairs={{0,1},{1,0},{2,3},{3,2},{4,5},{5,4},{6,7},{7,6},{8,9},{9,8},{10,11... | collective-permute-start | bytes 24584 | tf_op jit(solution)/shard_map/ppermute | solution.py:785
  369.4 10.1 %collective-permute-start.26 = (bf16[1,112,512]{2,1,0:T(8,128)(2,1)S(1)}, bf16[1,112,512]{2,1,0:T(8,128)(2,1)}, u32[]{:S(2)}, u32[]{:S(2)}) collective-permute-start(bf16[1,112,512]{2,1,0:T(8,128)(2,1)S(1)} %get-tuple-element.319), channel_id=1, source_target_pairs={{0,2},{1,3},{2,0},{3,1},{4,6},{5,7},{6,4},{7,5},{8,10},{9,11},{10,... | collective-permute-start | bytes 344072 | tf_op jit(solution)/shard_map/ppermute | solution.py:641
  370.2 18.8 %collective-permute-start.28 = (bf16[1,112,512]{2,1,0:T(8,128)(2,1)}, bf16[1,112,512]{2,1,0:T(8,128)(2,1)}, u32[]{:S(2)}, u32[]{:S(2)}) collective-permute-start(bf16[1,112,512]{2,1,0:T(8,128)(2,1)} %get-tuple-element.318), channel_id=1, source_target_pairs={{0,3},{1,2},{2,1},{3,0},{4,7},{5,6},{6,5},{7,4},{8,11},{9,10},{10,... | collective-permute-start | bytes 344072 | tf_op jit(solution)/shard_map/ppermute | solution.py:641
  376.3 4.6 %collective-permute-start.25 = (f32[2,1024]{1,0:T(2,128)S(1)}, f32[2,1024]{1,0:T(2,128)S(1)}, u32[]{:S(2)}, u32[]{:S(2)}) collective-permute-start(f32[2,1024]{1,0:T(2,128)S(1)} %add.254), channel_id=1, source_target_pairs={{0,2},{1,3},{2,0},{3,1},{4,6},{5,7},{6,4},{7,5},{8,10},{9,11},{10,... | collective-permute-start | bytes 24584 | tf_op jit(solution)/shard_map/ppermute | solution.py:785
  380.9 8.0 %collective-permute-start.27 = (f32[2,1024]{1,0:T(2,128)S(1)}, f32[2,1024]{1,0:T(2,128)S(1)}, u32[]{:S(2)}, u32[]{:S(2)}) collective-permute-start(f32[2,1024]{1,0:T(2,128)S(1)} %add.258), channel_id=1, source_target_pairs={{0,8},{1,9},{2,10},{3,11},{4,12},{5,13},{6,14},{7,15},{8,0},{9,1},... | collective-permute-start | bytes 24584 | tf_op jit(solution)/shard_map/ppermute | solution.py:785
  384.6 10.6 %collective-permute-start.30 = (bf16[1,160,512]{2,1,0:T(8,128)(2,1)}, bf16[1,160,512]{2,1,0:T(8,128)(2,1)S(1)}, u32[]{:S(2)}, u32[]{:S(2)}) collective-permute-start(bf16[1,160,512]{2,1,0:T(8,128)(2,1)} %get-tuple-element.299), channel_id=1, source_target_pairs={{0,1},{1,0},{2,3},{3,2},{4,5},{5,4},{6,7},{7,6},{8,9},{9,8},{10,11... | collective-permute-start | bytes 491528 | tf_op jit(solution)/shard_map/ppermute | solution.py:641
  384.9 13.0 %collective-permute-start.31 = (bf16[1,160,512]{2,1,0:T(8,128)(2,1)}, bf16[1,160,512]{2,1,0:T(8,128)(2,1)S(1)}, u32[]{:S(2)}, u32[]{:S(2)}) collective-permute-start(bf16[1,160,512]{2,1,0:T(8,128)(2,1)} %get-tuple-element.300), channel_id=1, source_target_pairs={{0,2},{1,3},{2,0},{3,1},{4,6},{5,7},{6,4},{7,5},{8,10},{9,11},{10,... | collective-permute-start | bytes 491528 | tf_op jit(solution)/shard_map/ppermute | solution.py:641
  387.0 10.9 %collective-permute-start.32 = (bf16[1,160,512]{2,1,0:T(8,128)(2,1)}, bf16[1,160,512]{2,1,0:T(8,128)(2,1)S(1)}, u32[]{:S(2)}, u32[]{:S(2)}) collective-permute-start(bf16[1,160,512]{2,1,0:T(8,128)(2,1)} %get-tuple-element.301), channel_id=1, source_target_pairs={{0,3},{1,2},{2,1},{3,0},{4,7},{5,6},{6,5},{7,4},{8,11},{9,10},{10,... | collective-permute-start | bytes 491528 | tf_op jit(solution)/shard_map/ppermute | solution.py:641
  (35 other events, 242.2 us)
Sparse Core Ops, SparseCore 0:
  11.6 146.1 all-gather.1
  317.3 25.4 reduce-scatter.2
  345.2 26.3 reduce-scatter.4

commit v6 on v5

--- a/solution.py
+++ b/solution.py
@@ -266,29 +266,39 @@
         for c in loads:
             c.wait()
         small_ref[...] = jnp.zeros_like(small_ref)
-        stores = []
-        for i in range(resid_ref.shape[0] // tm):
-            at = slice(i * tm, (i + 1) * tm)
-            resid = resid_ref[at]
-            result_ref[at] = (resid + out_ref[at] + row_of(rows_ref, DBIAS)).astype(bf16)
+        pairs = ((result_ref, result_out), (low_ref, low_out), (dctx_ref, dctx_out))
+
+        def stores(i):
+            at = pl.ds(pl.multiple_of(i * tm, tm), tm)
+            return [pltpu.make_async_copy(here.at[at], there.at[at], out_sem.at[i, k]) for k, (here, there) in enumerate(pairs)]
+
+        def tile(i, carry):
+            at = pl.ds(pl.multiple_of(i * tm, tm), tm)
+            resid = resid_ref[at, :]
+            result_ref[at, :] = (resid + out_ref[at, :] + row_of(rows_ref, DBIAS)).astype(bf16)
             center = resid - jnp.mean(resid, axis=-1, keepdims=True)
             r = lax.rsqrt(jnp.mean(center * center, axis=-1, keepdims=True) + EPSILON)
             nhat = center * r
-            dn = dn_ref[at]
-            go = grad_ref[at].astype(f32)
+            dn = dn_ref[at, :]
+            go = grad_ref[at, :].astype(f32)
             e = dn * row_of(rows_ref, GAIN2)
             low = (go + r * (e - jnp.mean(e, axis=-1, keepdims=True) - nhat * jnp.mean(e * nhat, axis=-1, keepdims=True))).astype(bf16)
-            low_ref[at] = low
-            dctx_ref[at] = dot_nt(low, weight_ref[...]).astype(bf16)
+            low_ref[at, :] = low
+            dctx_ref[at, :] = dot_nt(low, weight_ref[...]).astype(bf16)
             small_ref[0:1, :] += jnp.sum(dn * nhat, axis=0, keepdims=True)
             small_ref[1:2, :] += jnp.sum(dn, axis=0, keepdims=True)
             small_ref[2:3, :] += jnp.sum(low.astype(f32), axis=0, keepdims=True)
             small_ref[3:4, :] += jnp.sum(go, axis=0, keepdims=True)
-            for k, (here, there) in enumerate(((result_ref, result_out), (low_ref, low_out), (dctx_ref, dctx_out))):
-                c = pltpu.make_async_copy(here.at[pl.ds(i * tm, tm)], there.at[pl.ds(i * tm, tm)], out_sem.at[i, k])
+            for c in stores(i):
                 c.start()
-                stores.append(c)
-        for c in stores + up_copies(1 - slot, step - 1, 1) + up_copies(slot, step, 1) + down_copies(1 - bslot, block - 1, 1) + down_copies(bslot, block, 1):
+            return carry
+
+        tiles = resid_ref.shape[0] // tm
+        lax.fori_loop(0, tiles, tile, 0)
+        for i in range(tiles):
+            for c in stores(i):
+                c.wait()
+        for c in up_copies(1 - slot, step - 1, 1) + up_copies(slot, step, 1) + down_copies(1 - bslot, block - 1, 1) + down_copies(bslot, block, 1):
             c.wait()
 
 def ffn(pos, normed, grad, vecs, wide, resid, weight, tf=512, tm=256):
@@ -517,22 +527,27 @@
                 c.wait()
             small_ref[...] = jnp.zeros_like(small_ref)
             gain = row_of(vec_ref, GAIN1)
-            stores = []
-            for i in range(acc_ref.shape[0] // tm):
-                at = slice(i * tm, (i + 1) * tm)
-                dn = acc_ref[at] + earlier_ref[at].astype(f32)
+            def store(i):
+                at = pl.ds(pl.multiple_of(i * tm, tm), tm)
+                return pltpu.make_async_copy(result_ref.at[at], out_ref.at[at], out_sem.at[i])
+
+            def tile(i, carry):
+                at = pl.ds(pl.multiple_of(i * tm, tm), tm)
+                dn = acc_ref[at, :] + earlier_ref[at, :].astype(f32)
                 r = stat_ref[at, 1:2]
-                nhat = (tokens_ref[at].astype(f32) - stat_ref[at, 0:1]) * r
+                nhat = (tokens_ref[at, :].astype(f32) - stat_ref[at, 0:1]) * r
                 e = dn * gain
-                d = low_ref[at].astype(f32) + r * (e - jnp.mean(e, axis=-1, keepdims=True) - nhat * jnp.mean(e * nhat, axis=-1, keepdims=True))
-                result_ref[at] = d.astype(bf16)
+                d = low_ref[at, :].astype(f32) + r * (e - jnp.mean(e, axis=-1, keepdims=True) - nhat * jnp.mean(e * nhat, axis=-1, keepdims=True))
+                result_ref[at, :] = d.astype(bf16)
                 small_ref[0:1, :] += jnp.sum(dn * nhat, axis=0, keepdims=True)
                 small_ref[1:2, :] += jnp.sum(dn, axis=0, keepdims=True)
-                c = pltpu.make_async_copy(result_ref.at[pl.ds(i * tm, tm)], out_ref.at[pl.ds(i * tm, tm)], out_sem.at[i])
-                c.start()
-                stores.append(c)
-            for c in stores:
-                c.wait()
+                store(i).start()
+                return carry
+
+            tiles = acc_ref.shape[0] // tm
+            lax.fori_loop(0, tiles, tile, 0)
+            for i in range(tiles):
+                store(i).wait()
 
 def cotangent(order, d, pieces, number, earlier=None, stats=None, vecs=None, tokens=None, low=None, tm=256):
     _, R, width = d.shape

time: 414 us -> 415 us (level)
  transfers between devices with their start and end apart: 36 -> 36, of which waited for: 16 -> 16; matrix products, arithmetic and copies ran while one was open for 10% -> 10% of each run, Pallas kernels for 32% -> 33%
where the time goes in v6:
time: 415 us; the launch traced here: 407 us
  Pallas kernels  200 us (48%)
  waiting for transfers between devices  106 us (26%)
  other arithmetic  39.7 us (10%)
  starting transfers between devices  34.7 us (8%)
  between operations  16.1 us (4%)
  local copies, waits for them, and re-layouts  11 us (3%)
    ppermute x20, waiting for transfers between devices, exchange(): return lax.ppermute(x, AXES, plan.pairs(stage, j))  82 us
    pallas_call x1, Pallas kernels, ffn(): pl.pallas_call(functools.partial(ffn_kernel, shards=shards, per=per, bloc...  67.7 us
    pallas_call x4, Pallas kernels, attend_back(): pl.pallas_call(functools.partial(attend_back_kernel, bq=bq, first=first),...  43.2 us
    ppermute x20, starting transfers between devices, exchange(): return lax.ppermute(x, AXES, plan.pairs(stage, j))  27.2 us
    convert_element_type x9, other arithmetic, add(): sum((t[j * part:(j + 1) * part].astype(f32) for t in self.terms))  25.6 us
    pallas_call x1, Pallas kernels, attend(): pl.pallas_call(functools.partial(attend_kernel, bq=bq), grid=(n,), in_spe...  22.6 us
    pallas_call x2, Pallas kernels, cotangent(): pl.pallas_call(functools.partial(cotangent_kernel, count=len(pieces), fin...  21 us
    pallas_call x2, Pallas kernels, weight_grad(): pl.pallas_call(functools.partial(weight_grad_kernel, each=each, other=oth...  17.9 us
  transfers between devices with their start and end apart: 36, of which 16 were waited for; matrix products, arithmetic and copies ran while one was open for 10% of the time, Pallas kernels for 33%

profile of v6, /device:TPU:0, one launch (start us, length us, event | category | flops | bytes accessed | tf_op | source)
XLA Modules:
  0.0 407.3 jit_solution(13110357095255388690)
XLA Ops:
  11.8 3.1 collective-permute-start
  14.9 2.6 collective-permute-start.1
  17.5 4.1 norm.1.stat_ref.refs_8_
  21.6 5.6 %collective-permute-done = bf16[32,4224]{1,0:T(8,128)(2,1)S(1)} collective-permute-done((bf16[32,4224]{1,0:T(8,128)(2,1)S(1)}, bf16[32,4224]{1,0:T(8,128)(2,1)S(1)}, u32[]{:S(2)}, u32[]{:S(2)}) %collective-permute-start) | collective-permute-done | bytes 270368 | tf_op jit(solution)/shard_map/ppermute | solution.py:656
  27.1 14.4 %collective-permute-done.1 = bf16[32,4224]{1,0:T(8,128)(2,1)S(1)} collective-permute-done((bf16[32,4224]{1,0:T(8,128)(2,1)S(1)}, bf16[32,4224]{1,0:T(8,128)(2,1)S(1)}, u32[]{:S(2)}, u32[]{:S(2)}) %collective-permute-start.1) | collective-permute-done | bytes 270368 | tf_op jit(solution)/shard_map/ppermute | solution.py:656
  44.8 29.3 %collective-permute-done.3.refs_1_.refs_9_ = bf16[4,32,4224]{2,1,0:T(8,128)(2,1)S(1)} collective-permute-done((bf16[4,32,4224]{2,1,0:T(8,128)(2,1)S(1)}, bf16[4,32,4224]{2,1,0:T(8,128)(2,1)S(1)}, u32[]{:S(2)}, u32[]{:S(2)}) %collective-permute-start.3) | collective-permute-done | bytes 1081376 | tf_op jit(solution)/shard_map/ppermute | solution.py:656
  76.4 2.5 collective-permute-start.8
  79.4 12.7 %collective-permute-done.8.refs_3_.refs_11_ = bf16[4,32,4224]{2,1,0:T(8,128)(2,1)} collective-permute-done((bf16[4,32,4224]{2,1,0:T(8,128)(2,1)S(1)}, bf16[4,32,4224]{2,1,0:T(8,128)(2,1)}, u32[]{:S(2)}, u32[]{:S(2)}) %collective-permute-start.8) | collective-permute-done | bytes 1081376 | tf_op jit(solution)/shard_map/ppermute | solution.py:656
  95.9 13.5 %project.1 = (bf16[1024,1024]{1,0:T(8,128)(2,1)}, bf16[1024,3072]{1,0:T(8,128)(2,1)}, f32[16,1024]{1,0:T(8,128)}) custom-call(s32[32]{0:T(128)} %select_reduce_fusion.order_ref, bf16[1024,1024]{1,0:T(8,128)(2,1)} %refs_11_.1, f32[1024,128]{1,0:T(8,128)} %norm.1.stat_ref.refs_8_, bf16[4,32,4224]{2,1,0:T(8,128)(2,1)} %copy-done, ...), custom_call_target="tpu_custom_call" | custom-call | flops 1000 | bytes 1000 | tf_op jit(solution)/shard_map/project/pallas_call | solution.py:70
  109.4 22.6 %attend.1 = (bf16[1024,1024]{1,0:T(8,128)(2,1)}, f32[16,1024]{1,0:T(8,128)}) custom-call(s32[1]{0:T(128)S(6)} %copy.62.prefix_ref, s32[1]{0:T(128)S(6)} %copy.63.padding_ref, bf16[1024,3072]{1,0:T(8,128)(2,1)} %get-tuple-element.175.q_ref.k_ref.v_ref, bf16[1024,3072]{1,0:T(8,128)(2,1)} %get-tuple-element.175.q_ref.k_ref.v_ref, ...), custom_call_target="tpu_custom_call" | custom-call | flops 1000 | bytes 1000 | tf_op jit(solution)/shard_map/attend/pallas_call | solution.py:136
  132.1 8.0 %branch.1 = (f32[1024,1024]{1,0:T(8,128)}, bf16[1024,1024]{1,0:T(8,128)(2,1)}, bf16[1024,1024]{1,0:T(8,128)(2,1)}) custom-call(s32[32]{0:T(128)} %select_reduce_fusion.order_ref, bf16[1024,1024]{1,0:T(8,128)(2,1)} %get-tuple-element.176.ctx_ref.o_ref.refs_1_, bf16[1024,1024]{1,0:T(8,128)(2,1)} %refs_11_.1, ...), custom_call_target="tpu_custom_call" | custom-call | flops 1000 | bytes 1000 | tf_op jit(solution)/shard_map/branch/pallas_call | solution.py:162
  140.0 17.7 %all-gather.2.cloned.1.call-done.up_ref.down_ref = bf16[1024,8192]{1,0:T(8,128)(2,1)} async-done(((bf16[32,8192]{1,0:T(8,128)(2,1)}), bf16[1024,8192]{1,0:T(8,128)(2,1)}) %all-gather.2.cloned.1.call-update) | async-done | bytes 16777232 | tf_op jit(solution)/shard_map/all_gather | solution.py:761
  157.8 67.7 %ffn.1 = (bf16[1024,1024]{1,0:T(8,128)(2,1)}, bf16[1024,1024]{1,0:T(8,128)(2,1)}, bf16[1024,1024]{1,0:T(8,128)(2,1)}, bf16[16,32,4096]{2,1,0:T(8,128)(2,1)}, bf1...) custom-call(s32[32]{0:T(128)} %fusion.11.pos_ref, ...), custom_call_target="tpu_custom_call" | custom-call | flops 1000 | bytes 1000 | tf_op jit(solution)/shard_map/ffn/pallas_call | solution.py:315
  226.1 10.7 %attend_back.4 = (bf16[3,1024,512]{2,1,0:T(8,128)(2,1)}, f32[8,512]{1,0:T(8,128)}) custom-call(s32[1]{0:T(128)S(6)} %copy.62.prefix_ref, s32[1]{0:T(128)S(6)} %copy.63.padding_ref, bf16[1024,3072]{1,0:T(8,128)(2,1)} %get-tuple-element.175.q_ref.k_ref.v_ref, bf16[1024,3072]{1,0:T(8,128)(2,1)} %get-tuple-element.175.q_ref.k_ref.v_ref, ...), custom_call_target="tpu_custom_call" | custom-call | flops 1000 | bytes 1000 | tf_op jit(solution)/shard_map/attend_back/pallas_call | solution.py:388
  236.7 4.4 %add_convert_fusion.1 = bf16[8,32,4096]{2,1,0:T(8,128)(2,1)} fusion(bf16[16,32,4096]{2,1,0:T(8,128)(2,1)} %collective-permute-done.10, bf16[16,32,4096]{2,1,0:T(8,128)(2,1)} %get-tuple-element.225), kind=kLoop, calls=%fused_computation.1 | loop fusion | flops 4194304 | bytes 6291456 | tf_op jit(solution)/shard_map/convert_element_type | solution.py:709
  242.5 10.9 %attend_back.5 = (bf16[3,1024,512]{2,1,0:T(8,128)(2,1)}, f32[8,512]{1,0:T(8,128)}) custom-call(s32[1]{0:T(128)S(6)} %copy.62.prefix_ref, s32[1]{0:T(128)S(6)} %copy.63.padding_ref, bf16[1024,3072]{1,0:T(8,128)(2,1)} %get-tuple-element.175.q_ref.k_ref.v_ref, ...), custom_call_target="tpu_custom_call", output_to_operand_aliasing={{0}: (8, {}), {1}: (9, {})} | custom-call | flops 1000 | bytes 1000 | tf_op jit(solution)/shard_map/attend_back/pallas_call | solution.py:388
  253.4 4.4 %add_convert_fusion = bf16[8,32,4096]{2,1,0:T(8,128)(2,1)} fusion(bf16[16,32,4096]{2,1,0:T(8,128)(2,1)} %collective-permute-done.11, bf16[16,32,4096]{2,1,0:T(8,128)(2,1)} %get-tuple-element.243), kind=kLoop, calls=%fused_computation | loop fusion | flops 4194304 | bytes 6291456 | tf_op jit(solution)/shard_map/convert_element_type | solution.py:709
  258.4 10.5 %weight_grad.2 = (bf16[16,160,512]{2,1,0:T(8,128)(2,1)}, bf16[16,160,512]{2,1,0:T(8,128)(2,1)}) custom-call(s32[32]{0:T(128)} %copy-done.21, bf16[1024,1024]{1,0:T(8,128)(2,1)} %get-tuple-element.229.left_ref, bf16[3,1024,512]{2,1,0:T(8,128)(2,1)} %get-tuple-element.247.d_ref, bf16[1024,1024]{1,0:T(8,128)(2,1)} %get-tuple-element.200.refs_0_.refs_12_, ...), custom_call_target="tpu_custom_call" | custom-call | flops 1000 | bytes 1000 | tf_op jit(solution)/shard_map/weight_grad/pallas_call | solution.py:494
  269.0 10.7 %attend_back.6 = (bf16[3,1024,512]{2,1,0:T(8,128)(2,1)}, f32[8,512]{1,0:T(8,128)}) custom-call(s32[1]{0:T(128)S(6)} %copy.62.prefix_ref, s32[1]{0:T(128)S(6)} %copy.63.padding_ref, bf16[1024,3072]{1,0:T(8,128)(2,1)} %get-tuple-element.175.q_ref.k_ref.v_ref, bf16[1024,3072]{1,0:T(8,128)(2,1)} %get-tuple-element.175.q_ref.k_ref.v_ref, ...), custom_call_target="tpu_custom_call" | custom-call | flops 1000 | bytes 1000 | tf_op jit(solution)/shard_map/attend_back/pallas_call | solution.py:388
  279.7 3.3 add_convert_fusion.6
  284.5 10.9 %attend_back.7 = (bf16[3,1024,512]{2,1,0:T(8,128)(2,1)}, f32[8,512]{1,0:T(8,128)}) custom-call(s32[1]{0:T(128)S(6)} %copy.62.prefix_ref, s32[1]{0:T(128)S(6)} %copy.63.padding_ref, bf16[1024,3072]{1,0:T(8,128)(2,1)} %get-tuple-element.175.q_ref.k_ref.v_ref, ...), custom_call_target="tpu_custom_call", output_to_operand_aliasing={{0}: (8, {}), {1}: (9, {})} | custom-call | flops 1000 | bytes 1000 | tf_op jit(solution)/shard_map/attend_back/pallas_call | solution.py:388
  295.4 4.9 %collective-permute-done.14 = bf16[4,32,4096]{2,1,0:T(8,128)(2,1)S(1)} collective-permute-done((bf16[4,32,4096]{2,1,0:T(8,128)(2,1)}, bf16[4,32,4096]{2,1,0:T(8,128)(2,1)S(1)}, u32[]{:S(2)}, u32[]{:S(2)}) %collective-permute-start.14) | collective-permute-done | bytes 1048608 | tf_op jit(solution)/shard_map/ppermute | solution.py:656
  300.3 5.2 %add_convert_fusion.4 = (bf16[4,32,4096]{2,1,0:T(8,128)(2,1)}, bf16[4,32,4096]{2,1,0:T(8,128)(2,1)}) fusion(bf16[4,32,4096]{2,1,0:T(8,128)(2,1)S(1)} %collective-permute-done.14, bf16[8,32,4096]{2,1,0:T(8,128)(2,1)} %collective-permute-done.12, bf16[16,32,4096]{2,1,0:T(8,128)(2,1)} %collective-permute-done.10, bf16[16,32,4096]{2,1,0:T(8,128)(2,1)} %get-tuple-element.225, ...), kind=kLoop, calls=%fused_computation.4 | loop fusion | flops 7340032 | bytes 9437184 | tf_op jit(solution)/shard_map/convert_element_type | solution.py:707
  309.8 7.4 %weight_grad.3 = (bf16[16,112,512]{2,1,0:T(8,128)(2,1)}, bf16[16,112,512]{2,1,0:T(8,128)(2,1)}) custom-call(s32[32]{0:T(128)} %copy-done.21, bf16[1024,1024]{1,0:T(8,128)(2,1)} %get-tuple-element.229.left_ref, bf16[3,1024,512]{2,1,0:T(8,128)(2,1)} %get-tuple-element.213.d_ref, f32[32,512]{1,0:T(8,128)} %pad.9.refs_0_), custom_call_target="tpu_custom_call" | custom-call | flops 1000 | bytes 1000 | tf_op jit(solution)/shard_map/weight_grad/pallas_call | solution.py:494
  317.5 3.2 collective-permute-done.16
  320.7 2.8 add_convert_fusion.2
  323.5 3.5 add_convert_fusion.3
  328.4 8.5 %cotangent.2.refs_10_ = bf16[1024,1024]{1,0:T(8,128)(2,1)} custom-call(s32[32]{0:T(128)} %select_reduce_fusion.order_ref, bf16[3,1024,512]{2,1,0:T(8,128)(2,1)} %get-tuple-element.247.d_ref, bf16[4,32,4224]{2,1,0:T(8,128)(2,1)} %copy-done, bf16[4,32,4224]{2,1,0:T(8,128)(2,1)} %copy-done.1, bf16[4,32,4224]{2,1,0:T(8,128)(2,1)} %copy-done.2, ...), custom_call_target="tpu_custom_call" | custom-call | flops 1000 | bytes 1000 | tf_op jit(solution)/shard_map/cotangent/pallas_call | solution.py:571
  336.9 2.6 add_convert_fusion.7
  340.2 12.5 %cotangent.3 = (bf16[1024,1024]{1,0:T(8,128)(2,1)}, f32[8,1024]{1,0:T(8,128)}) custom-call(s32[32]{0:T(128)} %select_reduce_fusion.order_ref, bf16[3,1024,512]{2,1,0:T(8,128)(2,1)} %get-tuple-element.213.d_ref, bf16[4,32,4224]{2,1,0:T(8,128)(2,1)} %copy-done, bf16[4,32,4224]{2,1,0:T(8,128)(2,1)} %copy-done.1, bf16[4,32,4224]{2,1,0:T(8,128)(2,1)} %copy-done.2, ...), custom_call_target="tpu_custom_call" | custom-call | flops 1000 | bytes 1000 | tf_op jit(solution)/shard_map/cotangent/pallas_call | solution.py:571
  361.6 3.9 collective-permute-done.21
  395.4 2.8 collective-permute-done.31
  (182 shorter events, 64.4 us)
Async XLA Ops:
  7.2 150.6 %all-gather.2.cloned.1.call-start = ((), (), s32[]{:S(2)}) async-start(), calls=%async_computation.2 | async-start | bytes 17301504 | tf_op jit(solution)/shard_map/all_gather | solution.py:761
  11.3 345.4 %reduce-scatter.3.cloned.1.call-start = ((), (), s32[]{:S(2)}) async-start(), calls=%async_computation.3 | async-start | bytes 1310720 | tf_op jit(solution)/shard_map/reduce_scatter | solution.py:713
  11.8 15.3 %collective-permute-start = (bf16[32,4224]{1,0:T(8,128)(2,1)S(1)}, bf16[32,4224]{1,0:T(8,128)(2,1)S(1)}, u32[]{:S(2)}, u32[]{:S(2)}) collective-permute-start(bf16[32,4224]{1,0:T(8,128)(2,1)S(1)} %get-tuple-element.324), channel_id=1, source_target_pairs={{0,1},{1,0},{2,3},{3,2},{4,5},{5,4},{6,7},{7,6},{8,9},{9,8},{10,11... | collective-permute-start | bytes 811016 | tf_op jit(solution)/shard_map/ppermute | solution.py:656
  14.9 26.6 %collective-permute-start.1 = (bf16[32,4224]{1,0:T(8,128)(2,1)S(1)}, bf16[32,4224]{1,0:T(8,128)(2,1)S(1)}, u32[]{:S(2)}, u32[]{:S(2)}) collective-permute-start(bf16[32,4224]{1,0:T(8,128)(2,1)S(1)} %get-tuple-element.324), channel_id=1, source_target_pairs={{0,2},{1,3},{2,0},{3,1},{4,6},{5,7},{6,4},{7,5},{8,10},{9,11},{10,... | collective-permute-start | bytes 811016 | tf_op jit(solution)/shard_map/ppermute | solution.py:656
  17.5 24.0 %collective-permute-start.2 = (bf16[32,4224]{1,0:T(8,128)(2,1)S(1)}, bf16[32,4224]{1,0:T(8,128)(2,1)S(1)}, u32[]{:S(2)}, u32[]{:S(2)}) collective-permute-start(bf16[32,4224]{1,0:T(8,128)(2,1)S(1)} %get-tuple-element.324), channel_id=1, source_target_pairs={{0,3},{1,2},{2,1},{3,0},{4,7},{5,6},{6,5},{7,4},{8,11},{9,10},{10,... | collective-permute-start | bytes 811016 | tf_op jit(solution)/shard_map/ppermute | solution.py:656
  41.7 32.4 %collective-permute-start.3 = (bf16[4,32,4224]{2,1,0:T(8,128)(2,1)S(1)}, bf16[4,32,4224]{2,1,0:T(8,128)(2,1)S(1)}, u32[]{:S(2)}, u32[]{:S(2)}) collective-permute-start(bf16[4,32,4224]{2,1,0:T(8,128)(2,1)S(1)} %pad_maximum_fusion.refs_0_.refs_8_), channel_id=1, source_target_pairs={{0,16},{1,17},{2,18},{3,19},{4,12},{5,13},{6,14},{7,15},{8,24},{9,... | collective-permute-start | bytes 3244040 | tf_op jit(solution)/shard_map/ppermute | solution.py:656
  43.3 33.1 %collective-permute-start.4 = (bf16[4,32,4224]{2,1,0:T(8,128)(2,1)S(1)}, bf16[4,32,4224]{2,1,0:T(8,128)(2,1)S(1)}, u32[]{:S(2)}, u32[]{:S(2)}) collective-permute-start(bf16[4,32,4224]{2,1,0:T(8,128)(2,1)S(1)} %pad_maximum_fusion.refs_0_.refs_8_), channel_id=1, source_target_pairs={{0,8},{1,9},{2,10},{3,11},{4,20},{5,21},{6,22},{7,23},{8,0},{9,1},... | collective-permute-start | bytes 3244040 | tf_op jit(solution)/shard_map/ppermute | solution.py:656
  76.4 15.7 %collective-permute-start.8 = (bf16[4,32,4224]{2,1,0:T(8,128)(2,1)S(1)}, bf16[4,32,4224]{2,1,0:T(8,128)(2,1)}, u32[]{:S(2)}, u32[]{:S(2)}) collective-permute-start(bf16[4,32,4224]{2,1,0:T(8,128)(2,1)S(1)} %collective-permute-done.3.refs_1_.refs_9_), channel_id=1, source_target_pairs={{0,8},{1,9},{2,10},{3,11},{4,20},{5,21},{6,22},{7,23},{8,0},{9,1},... | collective-permute-start | bytes 3244040 | tf_op jit(solution)/shard_map/ppermute | solution.py:656
  78.8 13.2 %collective-permute-start.5 = (bf16[4,32,4224]{2,1,0:T(8,128)(2,1)S(1)}, bf16[4,32,4224]{2,1,0:T(8,128)(2,1)S(1)}, u32[]{:S(2)}, u32[]{:S(2)}) collective-permute-start(bf16[4,32,4224]{2,1,0:T(8,128)(2,1)S(1)} %pad_maximum_fusion.refs_0_.refs_8_), channel_id=1, source_target_pairs={{0,4},{1,5},{2,6},{3,7},{4,0},{5,1},{6,2},{7,3},{8,12},{9,13},{10,... | collective-permute-start | bytes 3244040 | tf_op jit(solution)/shard_map/ppermute | solution.py:653
  78.8 13.2 %collective-permute-start.7 = (bf16[4,32,4224]{2,1,0:T(8,128)(2,1)S(1)}, bf16[4,32,4224]{2,1,0:T(8,128)(2,1)S(1)}, u32[]{:S(2)}, u32[]{:S(2)}) collective-permute-start(bf16[4,32,4224]{2,1,0:T(8,128)(2,1)S(1)} %collective-permute-done.4.refs_2_.refs_10_), channel_id=1, source_target_pairs={{0,4},{1,5},{2,6},{3,7},{4,0},{5,1},{6,2},{7,3},{8,12},{9,13},{10,... | collective-permute-start | bytes 3244040 | tf_op jit(solution)/shard_map/ppermute | solution.py:653
  225.5 11.2 %collective-permute-start.10 = (bf16[16,32,4096]{2,1,0:T(8,128)(2,1)}, bf16[16,32,4096]{2,1,0:T(8,128)(2,1)}, u32[]{:S(2)}, u32[]{:S(2)}) collective-permute-start(bf16[16,32,4096]{2,1,0:T(8,128)(2,1)} %get-tuple-element.186), channel_id=1, source_target_pairs={{0,4},{1,5},{2,6},{3,7},{4,0},{5,1},{6,2},{7,3},{8,12},{9,13},{10,... | collective-permute-start | bytes 12582920 | tf_op jit(solution)/shard_map/ppermute | solution.py:653
  225.8 27.6 %collective-permute-start.11 = (bf16[16,32,4096]{2,1,0:T(8,128)(2,1)}, bf16[16,32,4096]{2,1,0:T(8,128)(2,1)}, u32[]{:S(2)}, u32[]{:S(2)}) collective-permute-start(bf16[16,32,4096]{2,1,0:T(8,128)(2,1)} %get-tuple-element.195), channel_id=1, source_target_pairs={{0,4},{1,5},{2,6},{3,7},{4,0},{5,1},{6,2},{7,3},{8,12},{9,13},{10,... | collective-permute-start | bytes 12582920 | tf_op jit(solution)/shard_map/ppermute | solution.py:653
  241.1 38.6 %collective-permute-start.12 = (bf16[8,32,4096]{2,1,0:T(8,128)(2,1)}, bf16[8,32,4096]{2,1,0:T(8,128)(2,1)}, u32[]{:S(2)}, u32[]{:S(2)}) collective-permute-start(bf16[8,32,4096]{2,1,0:T(8,128)(2,1)} %add_convert_fusion.1), channel_id=1, source_target_pairs={{0,8},{1,9},{2,10},{3,11},{4,20},{5,21},{6,22},{7,23},{8,0},{9,1},... | collective-permute-start | bytes 6291464 | tf_op jit(solution)/shard_map/ppermute | solution.py:656
  257.8 37.6 %collective-permute-start.13 = (bf16[8,32,4096]{2,1,0:T(8,128)(2,1)}, bf16[8,32,4096]{2,1,0:T(8,128)(2,1)S(1)}, u32[]{:S(2)}, u32[]{:S(2)}) collective-permute-start(bf16[8,32,4096]{2,1,0:T(8,128)(2,1)} %add_convert_fusion), channel_id=1, source_target_pairs={{0,8},{1,9},{2,10},{3,11},{4,20},{5,21},{6,22},{7,23},{8,0},{9,1},... | collective-permute-start | bytes 6291464 | tf_op jit(solution)/shard_map/ppermute | solution.py:656
  283.0 17.3 %collective-permute-start.14 = (bf16[4,32,4096]{2,1,0:T(8,128)(2,1)}, bf16[4,32,4096]{2,1,0:T(8,128)(2,1)S(1)}, u32[]{:S(2)}, u32[]{:S(2)}) collective-permute-start(bf16[4,32,4096]{2,1,0:T(8,128)(2,1)} %add_convert_fusion.6), channel_id=1, source_target_pairs={{0,16},{1,17},{2,18},{3,19},{4,12},{5,13},{6,14},{7,15},{8,24},{9,... | collective-permute-start | bytes 3145736 | tf_op jit(solution)/shard_map/ppermute | solution.py:656
  284.5 33.0 %collective-permute-start.15 = (bf16[16,160,512]{2,1,0:T(8,128)(2,1)}, bf16[16,160,512]{2,1,0:T(8,128)(2,1)}, u32[]{:S(2)}, u32[]{:S(2)}) collective-permute-start(bf16[16,160,512]{2,1,0:T(8,128)(2,1)} %get-tuple-element.235), channel_id=1, source_target_pairs={{0,4},{1,5},{2,6},{3,7},{4,0},{5,1},{6,2},{7,3},{8,12},{9,13},{10,... | collective-permute-start | bytes 7864328 | tf_op jit(solution)/shard_map/ppermute | solution.py:653
  305.6 15.1 %collective-permute-start.16 = (bf16[4,32,4096]{2,1,0:T(8,128)(2,1)}, bf16[4,32,4096]{2,1,0:T(8,128)(2,1)}, u32[]{:S(2)}, u32[]{:S(2)}) collective-permute-start(bf16[4,32,4096]{2,1,0:T(8,128)(2,1)} %get-tuple-element.239), channel_id=1, source_target_pairs={{0,16},{1,17},{2,18},{3,19},{4,12},{5,13},{6,14},{7,15},{8,24},{9,... | collective-permute-start | bytes 3145736 | tf_op jit(solution)/shard_map/ppermute | solution.py:656
  317.2 19.7 %collective-permute-start.17 = (bf16[16,112,512]{2,1,0:T(8,128)(2,1)}, bf16[16,112,512]{2,1,0:T(8,128)(2,1)}, u32[]{:S(2)}, u32[]{:S(2)}) collective-permute-start(bf16[16,112,512]{2,1,0:T(8,128)(2,1)} %get-tuple-element.248), channel_id=1, source_target_pairs={{0,4},{1,5},{2,6},{3,7},{4,0},{5,1},{6,2},{7,3},{8,12},{9,13},{10,... | collective-permute-start | bytes 5505032 | tf_op jit(solution)/shard_map/ppermute | solution.py:653
  317.4 65.2 %reduce-scatter.5.cloned.1.call-start = ((), (), s32[]{:S(2)}) async-start(), calls=%async_computation.4 | async-start | bytes 1310720 | tf_op jit(solution)/shard_map/reduce_scatter | solution.py:713
  327.0 29.8 %collective-permute-start.19 = (bf16[8,160,512]{2,1,0:T(8,128)(2,1)}, bf16[8,160,512]{2,1,0:T(8,128)(2,1)}, u32[]{:S(2)}, u32[]{:S(2)}) collective-permute-start(bf16[8,160,512]{2,1,0:T(8,128)(2,1)} %add_convert_fusion.2), channel_id=1, source_target_pairs={{0,8},{1,9},{2,10},{3,11},{4,20},{5,21},{6,22},{7,23},{8,0},{9,1},... | collective-permute-start | bytes 3932168 | tf_op jit(solution)/shard_map/ppermute | solution.py:656
  339.5 15.2 %collective-permute-start.18 = (bf16[8,112,512]{2,1,0:T(8,128)(2,1)}, bf16[8,112,512]{2,1,0:T(8,128)(2,1)S(1)}, u32[]{:S(2)}, u32[]{:S(2)}) collective-permute-start(bf16[8,112,512]{2,1,0:T(8,128)(2,1)} %add_convert_fusion.7), channel_id=1, source_target_pairs={{0,8},{1,9},{2,10},{3,11},{4,20},{5,21},{6,22},{7,23},{8,0},{9,1},... | collective-permute-start | bytes 2752520 | tf_op jit(solution)/shard_map/ppermute | solution.py:656
  356.8 8.7 %collective-permute-start.21 = (bf16[4,112,512]{2,1,0:T(8,128)(2,1)}, bf16[4,112,512]{2,1,0:T(8,128)(2,1)S(1)}, u32[]{:S(2)}, u32[]{:S(2)}) collective-permute-start(bf16[4,112,512]{2,1,0:T(8,128)(2,1)} %add_convert_fusion.9), channel_id=1, source_target_pairs={{0,16},{1,17},{2,18},{3,19},{4,12},{5,13},{6,14},{7,15},{8,24},{9,... | collective-permute-start | bytes 1376264 | tf_op jit(solution)/shard_map/ppermute | solution.py:656
  359.8 13.5 %collective-permute-start.24 = (bf16[4,160,512]{2,1,0:T(8,128)(2,1)S(1)}, bf16[4,160,512]{2,1,0:T(8,128)(2,1)S(1)}, u32[]{:S(2)}, u32[]{:S(2)}) collective-permute-start(bf16[4,160,512]{2,1,0:T(8,128)(2,1)S(1)} %add_convert_fusion.8), channel_id=1, source_target_pairs={{0,16},{1,17},{2,18},{3,19},{4,12},{5,13},{6,14},{7,15},{8,24},{9,... | collective-permute-start | bytes 1966088 | tf_op jit(solution)/shard_map/ppermute | solution.py:656
  367.6 5.7 %collective-permute-start.23 = (bf16[1,112,512]{2,1,0:T(8,128)(2,1)S(1)}, bf16[1,112,512]{2,1,0:T(8,128)(2,1)S(1)}, u32[]{:S(2)}, u32[]{:S(2)}) collective-permute-start(bf16[1,112,512]{2,1,0:T(8,128)(2,1)S(1)} %get-tuple-element.320), channel_id=1, source_target_pairs={{0,1},{1,0},{2,3},{3,2},{4,5},{5,4},{6,7},{7,6},{8,9},{9,8},{10,11... | collective-permute-start | bytes 344072 | tf_op jit(solution)/shard_map/ppermute | solution.py:656
  367.6 5.7 %collective-permute-start.22 = (f32[2,1024]{1,0:T(2,128)S(1)}, f32[2,1024]{1,0:T(2,128)S(1)}, u32[]{:S(2)}, u32[]{:S(2)}) collective-permute-start(f32[2,1024]{1,0:T(2,128)S(1)} %add.241), channel_id=1, source_target_pairs={{0,1},{1,0},{2,3},{3,2},{4,5},{5,4},{6,7},{7,6},{8,9},{9,8},{10,11... | collective-permute-start | bytes 24584 | tf_op jit(solution)/shard_map/ppermute | solution.py:800
  369.7 10.1 %collective-permute-start.26 = (bf16[1,112,512]{2,1,0:T(8,128)(2,1)S(1)}, bf16[1,112,512]{2,1,0:T(8,128)(2,1)}, u32[]{:S(2)}, u32[]{:S(2)}) collective-permute-start(bf16[1,112,512]{2,1,0:T(8,128)(2,1)S(1)} %get-tuple-element.319), channel_id=1, source_target_pairs={{0,2},{1,3},{2,0},{3,1},{4,6},{5,7},{6,4},{7,5},{8,10},{9,11},{10,... | collective-permute-start | bytes 344072 | tf_op jit(solution)/shard_map/ppermute | solution.py:656
  370.4 18.8 %collective-permute-start.28 = (bf16[1,112,512]{2,1,0:T(8,128)(2,1)}, bf16[1,112,512]{2,1,0:T(8,128)(2,1)}, u32[]{:S(2)}, u32[]{:S(2)}) collective-permute-start(bf16[1,112,512]{2,1,0:T(8,128)(2,1)} %get-tuple-element.318), channel_id=1, source_target_pairs={{0,3},{1,2},{2,1},{3,0},{4,7},{5,6},{6,5},{7,4},{8,11},{9,10},{10,... | collective-permute-start | bytes 344072 | tf_op jit(solution)/shard_map/ppermute | solution.py:656
  376.5 4.6 %collective-permute-start.25 = (f32[2,1024]{1,0:T(2,128)S(1)}, f32[2,1024]{1,0:T(2,128)S(1)}, u32[]{:S(2)}, u32[]{:S(2)}) collective-permute-start(f32[2,1024]{1,0:T(2,128)S(1)} %add.254), channel_id=1, source_target_pairs={{0,2},{1,3},{2,0},{3,1},{4,6},{5,7},{6,4},{7,5},{8,10},{9,11},{10,... | collective-permute-start | bytes 24584 | tf_op jit(solution)/shard_map/ppermute | solution.py:800
  381.2 8.0 %collective-permute-start.27 = (f32[2,1024]{1,0:T(2,128)S(1)}, f32[2,1024]{1,0:T(2,128)S(1)}, u32[]{:S(2)}, u32[]{:S(2)}) collective-permute-start(f32[2,1024]{1,0:T(2,128)S(1)} %add.258), channel_id=1, source_target_pairs={{0,8},{1,9},{2,10},{3,11},{4,12},{5,13},{6,14},{7,15},{8,0},{9,1},... | collective-permute-start | bytes 24584 | tf_op jit(solution)/shard_map/ppermute | solution.py:800
  384.8 10.6 %collective-permute-start.30 = (bf16[1,160,512]{2,1,0:T(8,128)(2,1)}, bf16[1,160,512]{2,1,0:T(8,128)(2,1)S(1)}, u32[]{:S(2)}, u32[]{:S(2)}) collective-permute-start(bf16[1,160,512]{2,1,0:T(8,128)(2,1)} %get-tuple-element.299), channel_id=1, source_target_pairs={{0,1},{1,0},{2,3},{3,2},{4,5},{5,4},{6,7},{7,6},{8,9},{9,8},{10,11... | collective-permute-start | bytes 491528 | tf_op jit(solution)/shard_map/ppermute | solution.py:656
  385.1 13.0 %collective-permute-start.31 = (bf16[1,160,512]{2,1,0:T(8,128)(2,1)}, bf16[1,160,512]{2,1,0:T(8,128)(2,1)S(1)}, u32[]{:S(2)}, u32[]{:S(2)}) collective-permute-start(bf16[1,160,512]{2,1,0:T(8,128)(2,1)} %get-tuple-element.300), channel_id=1, source_target_pairs={{0,2},{1,3},{2,0},{3,1},{4,6},{5,7},{6,4},{7,5},{8,10},{9,11},{10,... | collective-permute-start | bytes 491528 | tf_op jit(solution)/shard_map/ppermute | solution.py:656
  387.3 10.9 %collective-permute-start.32 = (bf16[1,160,512]{2,1,0:T(8,128)(2,1)}, bf16[1,160,512]{2,1,0:T(8,128)(2,1)S(1)}, u32[]{:S(2)}, u32[]{:S(2)}) collective-permute-start(bf16[1,160,512]{2,1,0:T(8,128)(2,1)} %get-tuple-element.301), channel_id=1, source_target_pairs={{0,3},{1,2},{2,1},{3,0},{4,7},{5,6},{6,5},{7,4},{8,11},{9,10},{10,... | collective-permute-start | bytes 491528 | tf_op jit(solution)/shard_map/ppermute | solution.py:656
  (35 other events, 242.3 us)
Sparse Core Ops, SparseCore 0:
  11.6 146.1 all-gather.1
  317.5 25.4 reduce-scatter.2
  345.4 26.3 reduce-scatter.4

commit v7 on v6

--- a/solution.py
+++ b/solution.py
@@ -794,13 +794,13 @@
     g4 = Reduction(plan, *weight_grad(pos, n1b, d2[0], small=early))
     da = step(d1[0], g4.terms[0], g3, g2)
     part = cotangent(order, da, inward, 0)
-    part = step(part, part, g4)
+    part = step(part, part, g4, g1)
     tokens_grad, end = cotangent(order, d2[0], inward, 1, part, stats, vecs, tokens, low)
     bits = [plan.core] + [bit for bit in range(total.bit_length() - 1) if bit != plan.core]
     swap = lambda v, bit: lax.ppermute(v, AXES, [(i, i ^ (1 << bit)) for i in range(total)])
     end = step(end[:2], end, g4)
     other = swap(end, bits[0])
-    end = step(end, end, g3, g1)
+    end = step(end, end, g3)
     end, other = tie(end, other, g4)
     g4.add()
     g4.go()
@@ -812,7 +812,7 @@
             at = k - arriving
             other, g4.terms[at] = tie(other, g4.terms[at])
         if k == 0:
-            other = step(other, other, g3)
+            other = step(other, other, g3, g2)
     late = lax.dynamic_slice_in_dim(end + other, me * n, n, axis=1)
     in1, in2 = g3.finish(), g4.finish()
     up_grad, down_grad = owned([g1.terms, g2.terms], D, blocks)

time: 415 us -> 413 us (level)
  transfers between devices with their start and end apart: 36 -> 36, of which waited for: 16 -> 16; matrix products, arithmetic and copies ran while one was open for 10% -> 11% of each run, Pallas kernels for 33% -> 33%
where the time goes in v7:
time: 413 us; the launch traced here: 405 us
  Pallas kernels  200 us (48%)
  waiting for transfers between devices  106 us (26%)
  other arithmetic  39.8 us (10%)
  starting transfers between devices  32.6 us (8%)
  between operations  15.9 us (4%)
  local copies, waits for them, and re-layouts  10.8 us (3%)
    ppermute x20, waiting for transfers between devices, exchange(): return lax.ppermute(x, AXES, plan.pairs(stage, j))  79.9 us
    pallas_call x1, Pallas kernels, ffn(): pl.pallas_call(functools.partial(ffn_kernel, shards=shards, per=per, bloc...  67.4 us
    pallas_call x4, Pallas kernels, attend_back(): pl.pallas_call(functools.partial(attend_back_kernel, bq=bq, first=first),...  43.4 us
    ppermute x20, starting transfers between devices, exchange(): return lax.ppermute(x, AXES, plan.pairs(stage, j))  27.2 us
    convert_element_type x9, other arithmetic, add(): sum((t[j * part:(j + 1) * part].astype(f32) for t in self.terms))  25.6 us
    pallas_call x1, Pallas kernels, attend(): pl.pallas_call(functools.partial(attend_kernel, bq=bq), grid=(n,), in_spe...  22.7 us
    pallas_call x2, Pallas kernels, cotangent(): pl.pallas_call(functools.partial(cotangent_kernel, count=len(pieces), fin...  20.9 us
    pallas_call x2, Pallas kernels, weight_grad(): pl.pallas_call(functools.partial(weight_grad_kernel, each=each, other=oth...  17.9 us
  transfers between devices with their start and end apart: 36, of which 16 were waited for; matrix products, arithmetic and copies ran while one was open for 11% of the time, Pallas kernels for 33%

profile of v7, /device:TPU:0, one launch (start us, length us, event | category | flops | bytes accessed | tf_op | source)
XLA Modules:
  0.0 405.2 jit_solution(4289515898080533880)
XLA Ops:
  11.8 3.1 collective-permute-start
  14.9 2.6 collective-permute-start.1
  17.5 4.1 %norm.1.stat_ref.refs_8_ = f32[1024,128]{1,0:T(8,128)} custom-call(bf16[1024,1024]{1,0:T(8,128)(2,1)} %refs_11_.1), custom_call_target="tpu_custom_call" | custom-call | flops 1000 | bytes 1000 | tf_op jit(solution)/shard_map/norm/pallas_call | solution.py:33
  21.6 5.6 %collective-permute-done = bf16[32,4224]{1,0:T(8,128)(2,1)S(1)} collective-permute-done((bf16[32,4224]{1,0:T(8,128)(2,1)S(1)}, bf16[32,4224]{1,0:T(8,128)(2,1)S(1)}, u32[]{:S(2)}, u32[]{:S(2)}) %collective-permute-start) | collective-permute-done | bytes 270368 | tf_op jit(solution)/shard_map/ppermute | solution.py:656
  27.1 14.4 %collective-permute-done.1 = bf16[32,4224]{1,0:T(8,128)(2,1)S(1)} collective-permute-done((bf16[32,4224]{1,0:T(8,128)(2,1)S(1)}, bf16[32,4224]{1,0:T(8,128)(2,1)S(1)}, u32[]{:S(2)}, u32[]{:S(2)}) %collective-permute-start.1) | collective-permute-done | bytes 270368 | tf_op jit(solution)/shard_map/ppermute | solution.py:656
  44.8 29.3 %collective-permute-done.3.refs_1_.refs_9_ = bf16[4,32,4224]{2,1,0:T(8,128)(2,1)S(1)} collective-permute-done((bf16[4,32,4224]{2,1,0:T(8,128)(2,1)S(1)}, bf16[4,32,4224]{2,1,0:T(8,128)(2,1)S(1)}, u32[]{:S(2)}, u32[]{:S(2)}) %collective-permute-start.3) | collective-permute-done | bytes 1081376 | tf_op jit(solution)/shard_map/ppermute | solution.py:656
  79.4 12.7 %collective-permute-done.8.refs_3_.refs_11_ = bf16[4,32,4224]{2,1,0:T(8,128)(2,1)} collective-permute-done((bf16[4,32,4224]{2,1,0:T(8,128)(2,1)S(1)}, bf16[4,32,4224]{2,1,0:T(8,128)(2,1)}, u32[]{:S(2)}, u32[]{:S(2)}) %collective-permute-start.8) | collective-permute-done | bytes 1081376 | tf_op jit(solution)/shard_map/ppermute | solution.py:656
  95.9 13.5 %project.1 = (bf16[1024,1024]{1,0:T(8,128)(2,1)}, bf16[1024,3072]{1,0:T(8,128)(2,1)}, f32[16,1024]{1,0:T(8,128)}) custom-call(s32[32]{0:T(128)} %select_reduce_fusion.order_ref, bf16[1024,1024]{1,0:T(8,128)(2,1)} %refs_11_.1, f32[1024,128]{1,0:T(8,128)} %norm.1.stat_ref.refs_8_, bf16[4,32,4224]{2,1,0:T(8,128)(2,1)} %copy-done, ...), custom_call_target="tpu_custom_call" | custom-call | flops 1000 | bytes 1000 | tf_op jit(solution)/shard_map/project/pallas_call | solution.py:70
  109.4 22.7 %attend.1 = (bf16[1024,1024]{1,0:T(8,128)(2,1)}, f32[16,1024]{1,0:T(8,128)}) custom-call(s32[1]{0:T(128)S(6)} %copy.62.prefix_ref, s32[1]{0:T(128)S(6)} %copy.63.padding_ref, bf16[1024,3072]{1,0:T(8,128)(2,1)} %get-tuple-element.176.q_ref.k_ref.v_ref, bf16[1024,3072]{1,0:T(8,128)(2,1)} %get-tuple-element.176.q_ref.k_ref.v_ref, ...), custom_call_target="tpu_custom_call" | custom-call | flops 1000 | bytes 1000 | tf_op jit(solution)/shard_map/attend/pallas_call | solution.py:136
  132.0 8.0 %branch.1 = (f32[1024,1024]{1,0:T(8,128)}, bf16[1024,1024]{1,0:T(8,128)(2,1)}, bf16[1024,1024]{1,0:T(8,128)(2,1)}) custom-call(s32[32]{0:T(128)} %select_reduce_fusion.order_ref, bf16[1024,1024]{1,0:T(8,128)(2,1)} %get-tuple-element.177.ctx_ref.o_ref.refs_1_, bf16[1024,1024]{1,0:T(8,128)(2,1)} %refs_11_.1, ...), custom_call_target="tpu_custom_call" | custom-call | flops 1000 | bytes 1000 | tf_op jit(solution)/shard_map/branch/pallas_call | solution.py:162
  140.0 17.7 %all-gather.2.cloned.1.call-done.up_ref.down_ref = bf16[1024,8192]{1,0:T(8,128)(2,1)} async-done(((bf16[32,8192]{1,0:T(8,128)(2,1)}), bf16[1024,8192]{1,0:T(8,128)(2,1)}) %all-gather.2.cloned.1.call-update) | async-done | bytes 16777232 | tf_op jit(solution)/shard_map/all_gather | solution.py:761
  157.8 67.4 %ffn.1 = (bf16[1024,1024]{1,0:T(8,128)(2,1)}, bf16[1024,1024]{1,0:T(8,128)(2,1)}, bf16[1024,1024]{1,0:T(8,128)(2,1)}, bf16[16,32,4096]{2,1,0:T(8,128)(2,1)}, bf1...) custom-call(s32[32]{0:T(128)} %fusion.11.pos_ref, ...), custom_call_target="tpu_custom_call" | custom-call | flops 1000 | bytes 1000 | tf_op jit(solution)/shard_map/ffn/pallas_call | solution.py:315
  225.8 10.7 %attend_back.4 = (bf16[3,1024,512]{2,1,0:T(8,128)(2,1)}, f32[8,512]{1,0:T(8,128)}) custom-call(s32[1]{0:T(128)S(6)} %copy.62.prefix_ref, s32[1]{0:T(128)S(6)} %copy.63.padding_ref, bf16[1024,3072]{1,0:T(8,128)(2,1)} %get-tuple-element.176.q_ref.k_ref.v_ref, bf16[1024,3072]{1,0:T(8,128)(2,1)} %get-tuple-element.176.q_ref.k_ref.v_ref, ...), custom_call_target="tpu_custom_call" | custom-call | flops 1000 | bytes 1000 | tf_op jit(solution)/shard_map/attend_back/pallas_call | solution.py:388
  236.4 4.4 %add_convert_fusion.1 = bf16[8,32,4096]{2,1,0:T(8,128)(2,1)} fusion(bf16[16,32,4096]{2,1,0:T(8,128)(2,1)} %collective-permute-done.10, bf16[16,32,4096]{2,1,0:T(8,128)(2,1)} %get-tuple-element.226), kind=kLoop, calls=%fused_computation.1 | loop fusion | flops 4194304 | bytes 6291456 | tf_op jit(solution)/shard_map/convert_element_type | solution.py:709
  242.2 11.1 %attend_back.5 = (bf16[3,1024,512]{2,1,0:T(8,128)(2,1)}, f32[8,512]{1,0:T(8,128)}) custom-call(s32[1]{0:T(128)S(6)} %copy.62.prefix_ref, s32[1]{0:T(128)S(6)} %copy.63.padding_ref, bf16[1024,3072]{1,0:T(8,128)(2,1)} %get-tuple-element.176.q_ref.k_ref.v_ref, ...), custom_call_target="tpu_custom_call", output_to_operand_aliasing={{0}: (8, {}), {1}: (9, {})} | custom-call | flops 1000 | bytes 1000 | tf_op jit(solution)/shard_map/attend_back/pallas_call | solution.py:388
  253.4 4.4 %add_convert_fusion = bf16[8,32,4096]{2,1,0:T(8,128)(2,1)} fusion(bf16[16,32,4096]{2,1,0:T(8,128)(2,1)} %collective-permute-done.11, bf16[16,32,4096]{2,1,0:T(8,128)(2,1)} %get-tuple-element.244), kind=kLoop, calls=%fused_computation | loop fusion | flops 4194304 | bytes 6291456 | tf_op jit(solution)/shard_map/convert_element_type | solution.py:709
  258.4 10.5 %weight_grad.2 = (bf16[16,160,512]{2,1,0:T(8,128)(2,1)}, bf16[16,160,512]{2,1,0:T(8,128)(2,1)}) custom-call(s32[32]{0:T(128)} %copy-done.19, bf16[1024,1024]{1,0:T(8,128)(2,1)} %get-tuple-element.230.left_ref, bf16[3,1024,512]{2,1,0:T(8,128)(2,1)} %get-tuple-element.248.d_ref, bf16[1024,1024]{1,0:T(8,128)(2,1)} %get-tuple-element.201.refs_0_.refs_12_, ...), custom_call_target="tpu_custom_call" | custom-call | flops 1000 | bytes 1000 | tf_op jit(solution)/shard_map/weight_grad/pallas_call | solution.py:494
  268.9 10.8 %attend_back.6 = (bf16[3,1024,512]{2,1,0:T(8,128)(2,1)}, f32[8,512]{1,0:T(8,128)}) custom-call(s32[1]{0:T(128)S(6)} %copy.62.prefix_ref, s32[1]{0:T(128)S(6)} %copy.63.padding_ref, bf16[1024,3072]{1,0:T(8,128)(2,1)} %get-tuple-element.176.q_ref.k_ref.v_ref, bf16[1024,3072]{1,0:T(8,128)(2,1)} %get-tuple-element.176.q_ref.k_ref.v_ref, ...), custom_call_target="tpu_custom_call" | custom-call | flops 1000 | bytes 1000 | tf_op jit(solution)/shard_map/attend_back/pallas_call | solution.py:388
  279.6 3.3 add_convert_fusion.6
  284.4 10.9 %attend_back.7 = (bf16[3,1024,512]{2,1,0:T(8,128)(2,1)}, f32[8,512]{1,0:T(8,128)}) custom-call(s32[1]{0:T(128)S(6)} %copy.62.prefix_ref, s32[1]{0:T(128)S(6)} %copy.63.padding_ref, bf16[1024,3072]{1,0:T(8,128)(2,1)} %get-tuple-element.176.q_ref.k_ref.v_ref, ...), custom_call_target="tpu_custom_call", output_to_operand_aliasing={{0}: (8, {}), {1}: (9, {})} | custom-call | flops 1000 | bytes 1000 | tf_op jit(solution)/shard_map/attend_back/pallas_call | solution.py:388
  295.3 4.7 %collective-permute-done.14 = bf16[4,32,4096]{2,1,0:T(8,128)(2,1)S(1)} collective-permute-done((bf16[4,32,4096]{2,1,0:T(8,128)(2,1)}, bf16[4,32,4096]{2,1,0:T(8,128)(2,1)S(1)}, u32[]{:S(2)}, u32[]{:S(2)}) %collective-permute-start.14) | collective-permute-done | bytes 1048608 | tf_op jit(solution)/shard_map/ppermute | solution.py:656
  300.0 5.2 %add_convert_fusion.4 = (bf16[4,32,4096]{2,1,0:T(8,128)(2,1)}, bf16[4,32,4096]{2,1,0:T(8,128)(2,1)}) fusion(bf16[4,32,4096]{2,1,0:T(8,128)(2,1)S(1)} %collective-permute-done.14, bf16[8,32,4096]{2,1,0:T(8,128)(2,1)} %collective-permute-done.12, bf16[16,32,4096]{2,1,0:T(8,128)(2,1)} %collective-permute-done.10, bf16[16,32,4096]{2,1,0:T(8,128)(2,1)} %get-tuple-element.226, ...), kind=kLoop, calls=%fused_computation.4 | loop fusion | flops 7340032 | bytes 9437184 | tf_op jit(solution)/shard_map/convert_element_type | solution.py:707
  309.6 7.4 %weight_grad.3 = (bf16[16,112,512]{2,1,0:T(8,128)(2,1)}, bf16[16,112,512]{2,1,0:T(8,128)(2,1)}) custom-call(s32[32]{0:T(128)} %copy-done.19, bf16[1024,1024]{1,0:T(8,128)(2,1)} %get-tuple-element.230.left_ref, bf16[3,1024,512]{2,1,0:T(8,128)(2,1)} %get-tuple-element.214.d_ref, f32[32,512]{1,0:T(8,128)} %pad.9.refs_0_), custom_call_target="tpu_custom_call" | custom-call | flops 1000 | bytes 1000 | tf_op jit(solution)/shard_map/weight_grad/pallas_call | solution.py:494
  317.2 3.1 collective-permute-done.16
  320.4 2.8 add_convert_fusion.2
  323.1 3.6 add_convert_fusion.3
  328.1 8.2 %cotangent.2.refs_10_ = bf16[1024,1024]{1,0:T(8,128)(2,1)} custom-call(s32[32]{0:T(128)} %select_reduce_fusion.order_ref, bf16[3,1024,512]{2,1,0:T(8,128)(2,1)} %get-tuple-element.248.d_ref, bf16[4,32,4224]{2,1,0:T(8,128)(2,1)} %copy-done, bf16[4,32,4224]{2,1,0:T(8,128)(2,1)} %copy-done.1, bf16[4,32,4224]{2,1,0:T(8,128)(2,1)} %copy-done.2, ...), custom_call_target="tpu_custom_call" | custom-call | flops 1000 | bytes 1000 | tf_op jit(solution)/shard_map/cotangent/pallas_call | solution.py:571
  336.4 2.6 add_convert_fusion.7
  339.7 12.7 %cotangent.3 = (bf16[1024,1024]{1,0:T(8,128)(2,1)}, f32[8,1024]{1,0:T(8,128)}) custom-call(s32[32]{0:T(128)} %select_reduce_fusion.order_ref, bf16[3,1024,512]{2,1,0:T(8,128)(2,1)} %get-tuple-element.214.d_ref, bf16[4,32,4224]{2,1,0:T(8,128)(2,1)} %copy-done, bf16[4,32,4224]{2,1,0:T(8,128)(2,1)} %copy-done.1, bf16[4,32,4224]{2,1,0:T(8,128)(2,1)} %copy-done.2, ...), custom_call_target="tpu_custom_call" | custom-call | flops 1000 | bytes 1000 | tf_op jit(solution)/shard_map/cotangent/pallas_call | solution.py:571
  361.4 2.9 collective-permute-done.21
  384.2 2.7 collective-permute-start.32
  392.0 2.7 collective-permute-done.29
  (178 shorter events, 63.8 us)
Async XLA Ops:
  7.2 150.6 %all-gather.2.cloned.1.call-start = ((), (), s32[]{:S(2)}) async-start(), calls=%async_computation.2 | async-start | bytes 17301504 | tf_op jit(solution)/shard_map/all_gather | solution.py:761
  11.3 325.1 %reduce-scatter.3.cloned.1.call-start = ((), (), s32[]{:S(2)}) async-start(), calls=%async_computation.3 | async-start | bytes 1310720 | tf_op jit(solution)/shard_map/reduce_scatter | solution.py:713
  11.8 15.3 %collective-permute-start = (bf16[32,4224]{1,0:T(8,128)(2,1)S(1)}, bf16[32,4224]{1,0:T(8,128)(2,1)S(1)}, u32[]{:S(2)}, u32[]{:S(2)}) collective-permute-start(bf16[32,4224]{1,0:T(8,128)(2,1)S(1)} %get-tuple-element.326), channel_id=1, source_target_pairs={{0,1},{1,0},{2,3},{3,2},{4,5},{5,4},{6,7},{7,6},{8,9},{9,8},{10,11... | collective-permute-start | bytes 811016 | tf_op jit(solution)/shard_map/ppermute | solution.py:656
  14.9 26.6 %collective-permute-start.1 = (bf16[32,4224]{1,0:T(8,128)(2,1)S(1)}, bf16[32,4224]{1,0:T(8,128)(2,1)S(1)}, u32[]{:S(2)}, u32[]{:S(2)}) collective-permute-start(bf16[32,4224]{1,0:T(8,128)(2,1)S(1)} %get-tuple-element.326), channel_id=1, source_target_pairs={{0,2},{1,3},{2,0},{3,1},{4,6},{5,7},{6,4},{7,5},{8,10},{9,11},{10,... | collective-permute-start | bytes 811016 | tf_op jit(solution)/shard_map/ppermute | solution.py:656
  17.5 24.0 %collective-permute-start.2 = (bf16[32,4224]{1,0:T(8,128)(2,1)S(1)}, bf16[32,4224]{1,0:T(8,128)(2,1)S(1)}, u32[]{:S(2)}, u32[]{:S(2)}) collective-permute-start(bf16[32,4224]{1,0:T(8,128)(2,1)S(1)} %get-tuple-element.326), channel_id=1, source_target_pairs={{0,3},{1,2},{2,1},{3,0},{4,7},{5,6},{6,5},{7,4},{8,11},{9,10},{10,... | collective-permute-start | bytes 811016 | tf_op jit(solution)/shard_map/ppermute | solution.py:656
  41.7 32.4 %collective-permute-start.3 = (bf16[4,32,4224]{2,1,0:T(8,128)(2,1)S(1)}, bf16[4,32,4224]{2,1,0:T(8,128)(2,1)S(1)}, u32[]{:S(2)}, u32[]{:S(2)}) collective-permute-start(bf16[4,32,4224]{2,1,0:T(8,128)(2,1)S(1)} %pad_maximum_fusion.refs_0_.refs_8_), channel_id=1, source_target_pairs={{0,16},{1,17},{2,18},{3,19},{4,12},{5,13},{6,14},{7,15},{8,24},{9,... | collective-permute-start | bytes 3244040 | tf_op jit(solution)/shard_map/ppermute | solution.py:656
  43.3 33.1 %collective-permute-start.4 = (bf16[4,32,4224]{2,1,0:T(8,128)(2,1)S(1)}, bf16[4,32,4224]{2,1,0:T(8,128)(2,1)S(1)}, u32[]{:S(2)}, u32[]{:S(2)}) collective-permute-start(bf16[4,32,4224]{2,1,0:T(8,128)(2,1)S(1)} %pad_maximum_fusion.refs_0_.refs_8_), channel_id=1, source_target_pairs={{0,8},{1,9},{2,10},{3,11},{4,20},{5,21},{6,22},{7,23},{8,0},{9,1},... | collective-permute-start | bytes 3244040 | tf_op jit(solution)/shard_map/ppermute | solution.py:656
  76.4 15.7 %collective-permute-start.8 = (bf16[4,32,4224]{2,1,0:T(8,128)(2,1)S(1)}, bf16[4,32,4224]{2,1,0:T(8,128)(2,1)}, u32[]{:S(2)}, u32[]{:S(2)}) collective-permute-start(bf16[4,32,4224]{2,1,0:T(8,128)(2,1)S(1)} %collective-permute-done.3.refs_1_.refs_9_), channel_id=1, source_target_pairs={{0,8},{1,9},{2,10},{3,11},{4,20},{5,21},{6,22},{7,23},{8,0},{9,1},... | collective-permute-start | bytes 3244040 | tf_op jit(solution)/shard_map/ppermute | solution.py:656
  78.8 13.2 %collective-permute-start.5 = (bf16[4,32,4224]{2,1,0:T(8,128)(2,1)S(1)}, bf16[4,32,4224]{2,1,0:T(8,128)(2,1)S(1)}, u32[]{:S(2)}, u32[]{:S(2)}) collective-permute-start(bf16[4,32,4224]{2,1,0:T(8,128)(2,1)S(1)} %pad_maximum_fusion.refs_0_.refs_8_), channel_id=1, source_target_pairs={{0,4},{1,5},{2,6},{3,7},{4,0},{5,1},{6,2},{7,3},{8,12},{9,13},{10,... | collective-permute-start | bytes 3244040 | tf_op jit(solution)/shard_map/ppermute | solution.py:653
  78.8 13.2 %collective-permute-start.7 = (bf16[4,32,4224]{2,1,0:T(8,128)(2,1)S(1)}, bf16[4,32,4224]{2,1,0:T(8,128)(2,1)S(1)}, u32[]{:S(2)}, u32[]{:S(2)}) collective-permute-start(bf16[4,32,4224]{2,1,0:T(8,128)(2,1)S(1)} %collective-permute-done.4.refs_2_.refs_10_), channel_id=1, source_target_pairs={{0,4},{1,5},{2,6},{3,7},{4,0},{5,1},{6,2},{7,3},{8,12},{9,13},{10,... | collective-permute-start | bytes 3244040 | tf_op jit(solution)/shard_map/ppermute | solution.py:653
  225.2 11.2 %collective-permute-start.10 = (bf16[16,32,4096]{2,1,0:T(8,128)(2,1)}, bf16[16,32,4096]{2,1,0:T(8,128)(2,1)}, u32[]{:S(2)}, u32[]{:S(2)}) collective-permute-start(bf16[16,32,4096]{2,1,0:T(8,128)(2,1)} %get-tuple-element.187), channel_id=1, source_target_pairs={{0,4},{1,5},{2,6},{3,7},{4,0},{5,1},{6,2},{7,3},{8,12},{9,13},{10,... | collective-permute-start | bytes 12582920 | tf_op jit(solution)/shard_map/ppermute | solution.py:653
  225.5 27.8 %collective-permute-start.11 = (bf16[16,32,4096]{2,1,0:T(8,128)(2,1)}, bf16[16,32,4096]{2,1,0:T(8,128)(2,1)}, u32[]{:S(2)}, u32[]{:S(2)}) collective-permute-start(bf16[16,32,4096]{2,1,0:T(8,128)(2,1)} %get-tuple-element.196), channel_id=1, source_target_pairs={{0,4},{1,5},{2,6},{3,7},{4,0},{5,1},{6,2},{7,3},{8,12},{9,13},{10,... | collective-permute-start | bytes 12582920 | tf_op jit(solution)/shard_map/ppermute | solution.py:653
  240.8 38.8 %collective-permute-start.12 = (bf16[8,32,4096]{2,1,0:T(8,128)(2,1)}, bf16[8,32,4096]{2,1,0:T(8,128)(2,1)}, u32[]{:S(2)}, u32[]{:S(2)}) collective-permute-start(bf16[8,32,4096]{2,1,0:T(8,128)(2,1)} %add_convert_fusion.1), channel_id=1, source_target_pairs={{0,8},{1,9},{2,10},{3,11},{4,20},{5,21},{6,22},{7,23},{8,0},{9,1},... | collective-permute-start | bytes 6291464 | tf_op jit(solution)/shard_map/ppermute | solution.py:656
  257.7 37.6 %collective-permute-start.13 = (bf16[8,32,4096]{2,1,0:T(8,128)(2,1)}, bf16[8,32,4096]{2,1,0:T(8,128)(2,1)S(1)}, u32[]{:S(2)}, u32[]{:S(2)}) collective-permute-start(bf16[8,32,4096]{2,1,0:T(8,128)(2,1)} %add_convert_fusion), channel_id=1, source_target_pairs={{0,8},{1,9},{2,10},{3,11},{4,20},{5,21},{6,22},{7,23},{8,0},{9,1},... | collective-permute-start | bytes 6291464 | tf_op jit(solution)/shard_map/ppermute | solution.py:656
  282.9 17.1 %collective-permute-start.14 = (bf16[4,32,4096]{2,1,0:T(8,128)(2,1)}, bf16[4,32,4096]{2,1,0:T(8,128)(2,1)S(1)}, u32[]{:S(2)}, u32[]{:S(2)}) collective-permute-start(bf16[4,32,4096]{2,1,0:T(8,128)(2,1)} %add_convert_fusion.6), channel_id=1, source_target_pairs={{0,16},{1,17},{2,18},{3,19},{4,12},{5,13},{6,14},{7,15},{8,24},{9,... | collective-permute-start | bytes 3145736 | tf_op jit(solution)/shard_map/ppermute | solution.py:656
  284.4 32.8 %collective-permute-start.15 = (bf16[16,160,512]{2,1,0:T(8,128)(2,1)}, bf16[16,160,512]{2,1,0:T(8,128)(2,1)}, u32[]{:S(2)}, u32[]{:S(2)}) collective-permute-start(bf16[16,160,512]{2,1,0:T(8,128)(2,1)} %get-tuple-element.236), channel_id=1, source_target_pairs={{0,4},{1,5},{2,6},{3,7},{4,0},{5,1},{6,2},{7,3},{8,12},{9,13},{10,... | collective-permute-start | bytes 7864328 | tf_op jit(solution)/shard_map/ppermute | solution.py:653
  305.2 15.1 %collective-permute-start.16 = (bf16[4,32,4096]{2,1,0:T(8,128)(2,1)}, bf16[4,32,4096]{2,1,0:T(8,128)(2,1)}, u32[]{:S(2)}, u32[]{:S(2)}) collective-permute-start(bf16[4,32,4096]{2,1,0:T(8,128)(2,1)} %get-tuple-element.240), channel_id=1, source_target_pairs={{0,16},{1,17},{2,18},{3,19},{4,12},{5,13},{6,14},{7,15},{8,24},{9,... | collective-permute-start | bytes 3145736 | tf_op jit(solution)/shard_map/ppermute | solution.py:656
  308.6 65.5 %reduce-scatter.5.cloned.1.call-start = ((), (), s32[]{:S(2)}) async-start(), calls=%async_computation.4 | async-start | bytes 1310720 | tf_op jit(solution)/shard_map/reduce_scatter | solution.py:713
  317.0 19.4 %collective-permute-start.17 = (bf16[16,112,512]{2,1,0:T(8,128)(2,1)}, bf16[16,112,512]{2,1,0:T(8,128)(2,1)}, u32[]{:S(2)}, u32[]{:S(2)}) collective-permute-start(bf16[16,112,512]{2,1,0:T(8,128)(2,1)} %get-tuple-element.249), channel_id=1, source_target_pairs={{0,4},{1,5},{2,6},{3,7},{4,0},{5,1},{6,2},{7,3},{8,12},{9,13},{10,... | collective-permute-start | bytes 5505032 | tf_op jit(solution)/shard_map/ppermute | solution.py:653
  326.7 29.0 %collective-permute-start.19 = (bf16[8,160,512]{2,1,0:T(8,128)(2,1)}, bf16[8,160,512]{2,1,0:T(8,128)(2,1)}, u32[]{:S(2)}, u32[]{:S(2)}) collective-permute-start(bf16[8,160,512]{2,1,0:T(8,128)(2,1)} %add_convert_fusion.2), channel_id=1, source_target_pairs={{0,8},{1,9},{2,10},{3,11},{4,20},{5,21},{6,22},{7,23},{8,0},{9,1},... | collective-permute-start | bytes 3932168 | tf_op jit(solution)/shard_map/ppermute | solution.py:656
  339.1 15.3 %collective-permute-start.18 = (bf16[8,112,512]{2,1,0:T(8,128)(2,1)}, bf16[8,112,512]{2,1,0:T(8,128)(2,1)S(1)}, u32[]{:S(2)}, u32[]{:S(2)}) collective-permute-start(bf16[8,112,512]{2,1,0:T(8,128)(2,1)} %add_convert_fusion.7), channel_id=1, source_target_pairs={{0,8},{1,9},{2,10},{3,11},{4,20},{5,21},{6,22},{7,23},{8,0},{9,1},... | collective-permute-start | bytes 2752520 | tf_op jit(solution)/shard_map/ppermute | solution.py:656
  355.7 8.5 %collective-permute-start.21 = (bf16[4,112,512]{2,1,0:T(8,128)(2,1)S(1)}, bf16[4,112,512]{2,1,0:T(8,128)(2,1)S(1)}, u32[]{:S(2)}, u32[]{:S(2)}) collective-permute-start(bf16[4,112,512]{2,1,0:T(8,128)(2,1)S(1)} %add_convert_fusion.9), channel_id=1, source_target_pairs={{0,16},{1,17},{2,18},{3,19},{4,12},{5,13},{6,14},{7,15},{8,24},{9,... | collective-permute-start | bytes 1376264 | tf_op jit(solution)/shard_map/ppermute | solution.py:656
  359.7 14.3 %collective-permute-start.24 = (bf16[4,160,512]{2,1,0:T(8,128)(2,1)}, bf16[4,160,512]{2,1,0:T(8,128)(2,1)}, u32[]{:S(2)}, u32[]{:S(2)}) collective-permute-start(bf16[4,160,512]{2,1,0:T(8,128)(2,1)} %add_convert_fusion.8), channel_id=1, source_target_pairs={{0,16},{1,17},{2,18},{3,19},{4,12},{5,13},{6,14},{7,15},{8,24},{9,... | collective-permute-start | bytes 1966088 | tf_op jit(solution)/shard_map/ppermute | solution.py:656
  367.1 7.0 %collective-permute-start.23 = (bf16[1,112,512]{2,1,0:T(8,128)(2,1)S(1)}, bf16[1,112,512]{2,1,0:T(8,128)(2,1)}, u32[]{:S(2)}, u32[]{:S(2)}) collective-permute-start(bf16[1,112,512]{2,1,0:T(8,128)(2,1)S(1)} %get-tuple-element.322), channel_id=1, source_target_pairs={{0,1},{1,0},{2,3},{3,2},{4,5},{5,4},{6,7},{7,6},{8,9},{9,8},{10,11... | collective-permute-start | bytes 344072 | tf_op jit(solution)/shard_map/ppermute | solution.py:656
  367.1 6.9 %collective-permute-start.22 = (f32[2,1024]{1,0:T(2,128)S(1)}, f32[2,1024]{1,0:T(2,128)S(1)}, u32[]{:S(2)}, u32[]{:S(2)}) collective-permute-start(f32[2,1024]{1,0:T(2,128)S(1)} %add.241), channel_id=1, source_target_pairs={{0,1},{1,0},{2,3},{3,2},{4,5},{5,4},{6,7},{7,6},{8,9},{9,8},{10,11... | collective-permute-start | bytes 24584 | tf_op jit(solution)/shard_map/ppermute | solution.py:800
  369.1 10.0 %collective-permute-start.26 = (bf16[1,112,512]{2,1,0:T(8,128)(2,1)}, bf16[1,112,512]{2,1,0:T(8,128)(2,1)}, u32[]{:S(2)}, u32[]{:S(2)}) collective-permute-start(bf16[1,112,512]{2,1,0:T(8,128)(2,1)} %get-tuple-element.321), channel_id=1, source_target_pairs={{0,2},{1,3},{2,0},{3,1},{4,6},{5,7},{6,4},{7,5},{8,10},{9,11},{10,... | collective-permute-start | bytes 344072 | tf_op jit(solution)/shard_map/ppermute | solution.py:656
  369.9 19.2 %collective-permute-start.28 = (bf16[1,112,512]{2,1,0:T(8,128)(2,1)}, bf16[1,112,512]{2,1,0:T(8,128)(2,1)}, u32[]{:S(2)}, u32[]{:S(2)}) collective-permute-start(bf16[1,112,512]{2,1,0:T(8,128)(2,1)} %get-tuple-element.320), channel_id=1, source_target_pairs={{0,3},{1,2},{2,1},{3,0},{4,7},{5,6},{6,5},{7,4},{8,11},{9,10},{10,... | collective-permute-start | bytes 344072 | tf_op jit(solution)/shard_map/ppermute | solution.py:656
  376.5 4.6 %collective-permute-start.25 = (f32[2,1024]{1,0:T(2,128)S(1)}, f32[2,1024]{1,0:T(2,128)S(1)}, u32[]{:S(2)}, u32[]{:S(2)}) collective-permute-start(f32[2,1024]{1,0:T(2,128)S(1)} %add.254), channel_id=1, source_target_pairs={{0,2},{1,3},{2,0},{3,1},{4,6},{5,7},{6,4},{7,5},{8,10},{9,11},{10,... | collective-permute-start | bytes 24584 | tf_op jit(solution)/shard_map/ppermute | solution.py:800
  381.1 8.0 %collective-permute-start.27 = (f32[2,1024]{1,0:T(2,128)S(1)}, f32[2,1024]{1,0:T(2,128)S(1)}, u32[]{:S(2)}, u32[]{:S(2)}) collective-permute-start(f32[2,1024]{1,0:T(2,128)S(1)} %add.258), channel_id=1, source_target_pairs={{0,8},{1,9},{2,10},{3,11},{4,12},{5,13},{6,14},{7,15},{8,0},{9,1},... | collective-permute-start | bytes 24584 | tf_op jit(solution)/shard_map/ppermute | solution.py:800
  382.4 12.9 %collective-permute-start.30 = (bf16[1,160,512]{2,1,0:T(8,128)(2,1)}, bf16[1,160,512]{2,1,0:T(8,128)(2,1)S(1)}, u32[]{:S(2)}, u32[]{:S(2)}) collective-permute-start(bf16[1,160,512]{2,1,0:T(8,128)(2,1)} %get-tuple-element.301), channel_id=1, source_target_pairs={{0,1},{1,0},{2,3},{3,2},{4,5},{5,4},{6,7},{7,6},{8,9},{9,8},{10,11... | collective-permute-start | bytes 491528 | tf_op jit(solution)/shard_map/ppermute | solution.py:656
  382.5 13.9 %collective-permute-start.31 = (bf16[1,160,512]{2,1,0:T(8,128)(2,1)}, bf16[1,160,512]{2,1,0:T(8,128)(2,1)S(1)}, u32[]{:S(2)}, u32[]{:S(2)}) collective-permute-start(bf16[1,160,512]{2,1,0:T(8,128)(2,1)} %get-tuple-element.302), channel_id=1, source_target_pairs={{0,2},{1,3},{2,0},{3,1},{4,6},{5,7},{6,4},{7,5},{8,10},{9,11},{10,... | collective-permute-start | bytes 491528 | tf_op jit(solution)/shard_map/ppermute | solution.py:656
  384.2 12.2 %collective-permute-start.32 = (bf16[1,160,512]{2,1,0:T(8,128)(2,1)}, bf16[1,160,512]{2,1,0:T(8,128)(2,1)S(1)}, u32[]{:S(2)}, u32[]{:S(2)}) collective-permute-start(bf16[1,160,512]{2,1,0:T(8,128)(2,1)} %get-tuple-element.303), channel_id=1, source_target_pairs={{0,3},{1,2},{2,1},{3,0},{4,7},{5,6},{6,5},{7,4},{8,11},{9,10},{10,... | collective-permute-start | bytes 491528 | tf_op jit(solution)/shard_map/ppermute | solution.py:656
  (33 other events, 227.7 us)
Sparse Core Ops, SparseCore 0:
  11.6 146.1 all-gather.1
  308.7 25.2 reduce-scatter.2
  339.8 26.1 reduce-scatter.4

commit v8 on v7

--- a/solution.py
+++ b/solution.py
@@ -564,7 +564,7 @@
     if final:
         specs = specs + [pl.BlockSpec((R, 128), lambda j: (0, 0)), pl.BlockSpec(vecs.shape, lambda j: (0, 0)), hbm, hbm, hbm]
         more = (stats, vecs, earlier, tokens, low)
-        outs, shapes = [hbm, pl.BlockSpec((8, D), lambda j: (0, 0))], [result, jax.ShapeDtypeStruct((8, D), f32)]
+        outs, shapes = [hbm, pl.BlockSpec((2, D), lambda j: (0, 0))], [result, jax.ShapeDtypeStruct((2, D), f32)]
         scratch = scratch + [pltpu.VMEM((R, D), bf16)] * 4 + [pltpu.SemaphoreType.DMA((3,)), pltpu.SemaphoreType.DMA((R // tm,))]
     else:
         outs, shapes = pl.BlockSpec((R, D), lambda j: (0, 0)), result
@@ -798,7 +798,7 @@
     tokens_grad, end = cotangent(order, d2[0], inward, 1, part, stats, vecs, tokens, low)
     bits = [plan.core] + [bit for bit in range(total.bit_length() - 1) if bit != plan.core]
     swap = lambda v, bit: lax.ppermute(v, AXES, [(i, i ^ (1 << bit)) for i in range(total)])
-    end = step(end[:2], end, g4)
+    end = step(end, end, g4)
     other = swap(end, bits[0])
     end = step(end, end, g3)
     end, other = tie(end, other, g4)

time: 413 us -> 413 us (level)
  transfers between devices with their start and end apart: 36 -> 36, of which waited for: 16 -> 16; matrix products, arithmetic and copies ran while one was open for 11% -> 10% of each run, Pallas kernels for 33% -> 33%
where the time goes in v8:
time: 413 us; the launch traced here: 405 us
  Pallas kernels  200 us (48%)
  waiting for transfers between devices  107 us (26%)
  other arithmetic  39.8 us (10%)
  starting transfers between devices  32.6 us (8%)
  between operations  15.9 us (4%)
  local copies, waits for them, and re-layouts  10.1 us (2%)
    ppermute x20, waiting for transfers between devices, exchange(): return lax.ppermute(x, AXES, plan.pairs(stage, j))  80.7 us
    pallas_call x1, Pallas kernels, ffn(): pl.pallas_call(functools.partial(ffn_kernel, shards=shards, per=per, bloc...  67.4 us
    pallas_call x4, Pallas kernels, attend_back(): pl.pallas_call(functools.partial(attend_back_kernel, bq=bq, first=first),...  43.4 us
    ppermute x20, starting transfers between devices, exchange(): return lax.ppermute(x, AXES, plan.pairs(stage, j))  27.2 us
    convert_element_type x9, other arithmetic, add(): sum((t[j * part:(j + 1) * part].astype(f32) for t in self.terms))  25.7 us
    pallas_call x1, Pallas kernels, attend(): pl.pallas_call(functools.partial(attend_kernel, bq=bq), grid=(n,), in_spe...  22.6 us
    pallas_call x2, Pallas kernels, cotangent(): pl.pallas_call(functools.partial(cotangent_kernel, count=len(pieces), fin...  20.9 us
    pallas_call x2, Pallas kernels, weight_grad(): pl.pallas_call(functools.partial(weight_grad_kernel, each=each, other=oth...  17.8 us
  transfers between devices with their start and end apart: 36, of which 16 were waited for; matrix products, arithmetic and copies ran while one was open for 10% of the time, Pallas kernels for 33%

profile of v8, /device:TPU:0, one launch (start us, length us, event | category | flops | bytes accessed | tf_op | source)
XLA Modules:
  0.0 405.2 jit_solution(2908047401227064624)
XLA Ops:
  11.8 3.1 collective-permute-start
  14.9 2.6 collective-permute-start.1
  17.5 4.1 %norm.1.stat_ref.refs_8_ = f32[1024,128]{1,0:T(8,128)} custom-call(bf16[1024,1024]{1,0:T(8,128)(2,1)} %refs_11_.1), custom_call_target="tpu_custom_call" | custom-call | flops 1000 | bytes 1000 | tf_op jit(solution)/shard_map/norm/pallas_call | solution.py:33
  21.6 5.6 %collective-permute-done = bf16[32,4224]{1,0:T(8,128)(2,1)S(1)} collective-permute-done((bf16[32,4224]{1,0:T(8,128)(2,1)S(1)}, bf16[32,4224]{1,0:T(8,128)(2,1)S(1)}, u32[]{:S(2)}, u32[]{:S(2)}) %collective-permute-start) | collective-permute-done | bytes 270368 | tf_op jit(solution)/shard_map/ppermute | solution.py:656
  27.1 14.4 %collective-permute-done.1 = bf16[32,4224]{1,0:T(8,128)(2,1)S(1)} collective-permute-done((bf16[32,4224]{1,0:T(8,128)(2,1)S(1)}, bf16[32,4224]{1,0:T(8,128)(2,1)S(1)}, u32[]{:S(2)}, u32[]{:S(2)}) %collective-permute-start.1) | collective-permute-done | bytes 270368 | tf_op jit(solution)/shard_map/ppermute | solution.py:656
  44.8 29.3 %collective-permute-done.3.refs_1_.refs_9_ = bf16[4,32,4224]{2,1,0:T(8,128)(2,1)S(1)} collective-permute-done((bf16[4,32,4224]{2,1,0:T(8,128)(2,1)S(1)}, bf16[4,32,4224]{2,1,0:T(8,128)(2,1)S(1)}, u32[]{:S(2)}, u32[]{:S(2)}) %collective-permute-start.3) | collective-permute-done | bytes 1081376 | tf_op jit(solution)/shard_map/ppermute | solution.py:656
  79.4 12.7 %collective-permute-done.8.refs_3_.refs_11_ = bf16[4,32,4224]{2,1,0:T(8,128)(2,1)} collective-permute-done((bf16[4,32,4224]{2,1,0:T(8,128)(2,1)S(1)}, bf16[4,32,4224]{2,1,0:T(8,128)(2,1)}, u32[]{:S(2)}, u32[]{:S(2)}) %collective-permute-start.8) | collective-permute-done | bytes 1081376 | tf_op jit(solution)/shard_map/ppermute | solution.py:656
  95.9 13.5 %project.1 = (bf16[1024,1024]{1,0:T(8,128)(2,1)}, bf16[1024,3072]{1,0:T(8,128)(2,1)}, f32[16,1024]{1,0:T(8,128)}) custom-call(s32[32]{0:T(128)} %select_reduce_fusion.order_ref, bf16[1024,1024]{1,0:T(8,128)(2,1)} %refs_11_.1, f32[1024,128]{1,0:T(8,128)} %norm.1.stat_ref.refs_8_, bf16[4,32,4224]{2,1,0:T(8,128)(2,1)} %copy-done, ...), custom_call_target="tpu_custom_call" | custom-call | flops 1000 | bytes 1000 | tf_op jit(solution)/shard_map/project/pallas_call | solution.py:70
  109.4 22.6 %attend.1 = (bf16[1024,1024]{1,0:T(8,128)(2,1)}, f32[16,1024]{1,0:T(8,128)}) custom-call(s32[1]{0:T(128)S(6)} %copy.62.prefix_ref, s32[1]{0:T(128)S(6)} %copy.63.padding_ref, bf16[1024,3072]{1,0:T(8,128)(2,1)} %get-tuple-element.176.q_ref.k_ref.v_ref, bf16[1024,3072]{1,0:T(8,128)(2,1)} %get-tuple-element.176.q_ref.k_ref.v_ref, ...), custom_call_target="tpu_custom_call" | custom-call | flops 1000 | bytes 1000 | tf_op jit(solution)/shard_map/attend/pallas_call | solution.py:136
  132.1 8.0 %branch.1 = (f32[1024,1024]{1,0:T(8,128)}, bf16[1024,1024]{1,0:T(8,128)(2,1)}, bf16[1024,1024]{1,0:T(8,128)(2,1)}) custom-call(s32[32]{0:T(128)} %select_reduce_fusion.order_ref, bf16[1024,1024]{1,0:T(8,128)(2,1)} %get-tuple-element.177.ctx_ref.o_ref.refs_1_, bf16[1024,1024]{1,0:T(8,128)(2,1)} %refs_11_.1, ...), custom_call_target="tpu_custom_call" | custom-call | flops 1000 | bytes 1000 | tf_op jit(solution)/shard_map/branch/pallas_call | solution.py:162
  140.1 17.7 %all-gather.2.cloned.1.call-done.up_ref.down_ref = bf16[1024,8192]{1,0:T(8,128)(2,1)} async-done(((bf16[32,8192]{1,0:T(8,128)(2,1)}), bf16[1024,8192]{1,0:T(8,128)(2,1)}) %all-gather.2.cloned.1.call-update) | async-done | bytes 16777232 | tf_op jit(solution)/shard_map/all_gather | solution.py:761
  157.8 67.4 %ffn.1 = (bf16[1024,1024]{1,0:T(8,128)(2,1)}, bf16[1024,1024]{1,0:T(8,128)(2,1)}, bf16[1024,1024]{1,0:T(8,128)(2,1)}, bf16[16,32,4096]{2,1,0:T(8,128)(2,1)}, bf1...) custom-call(s32[32]{0:T(128)} %fusion.11.pos_ref, ...), custom_call_target="tpu_custom_call" | custom-call | flops 1000 | bytes 1000 | tf_op jit(solution)/shard_map/ffn/pallas_call | solution.py:315
  225.8 10.7 %attend_back.4 = (bf16[3,1024,512]{2,1,0:T(8,128)(2,1)}, f32[8,512]{1,0:T(8,128)}) custom-call(s32[1]{0:T(128)S(6)} %copy.62.prefix_ref, s32[1]{0:T(128)S(6)} %copy.63.padding_ref, bf16[1024,3072]{1,0:T(8,128)(2,1)} %get-tuple-element.176.q_ref.k_ref.v_ref, bf16[1024,3072]{1,0:T(8,128)(2,1)} %get-tuple-element.176.q_ref.k_ref.v_ref, ...), custom_call_target="tpu_custom_call" | custom-call | flops 1000 | bytes 1000 | tf_op jit(solution)/shard_map/attend_back/pallas_call | solution.py:388
  236.4 4.4 %add_convert_fusion.1 = bf16[8,32,4096]{2,1,0:T(8,128)(2,1)} fusion(bf16[16,32,4096]{2,1,0:T(8,128)(2,1)} %collective-permute-done.10, bf16[16,32,4096]{2,1,0:T(8,128)(2,1)} %get-tuple-element.226), kind=kLoop, calls=%fused_computation.1 | loop fusion | flops 4194304 | bytes 6291456 | tf_op jit(solution)/shard_map/convert_element_type | solution.py:709
  242.2 11.1 %attend_back.5 = (bf16[3,1024,512]{2,1,0:T(8,128)(2,1)}, f32[8,512]{1,0:T(8,128)}) custom-call(s32[1]{0:T(128)S(6)} %copy.62.prefix_ref, s32[1]{0:T(128)S(6)} %copy.63.padding_ref, bf16[1024,3072]{1,0:T(8,128)(2,1)} %get-tuple-element.176.q_ref.k_ref.v_ref, ...), custom_call_target="tpu_custom_call", output_to_operand_aliasing={{0}: (8, {}), {1}: (9, {})} | custom-call | flops 1000 | bytes 1000 | tf_op jit(solution)/shard_map/attend_back/pallas_call | solution.py:388
  253.3 4.4 %add_convert_fusion = bf16[8,32,4096]{2,1,0:T(8,128)(2,1)} fusion(bf16[16,32,4096]{2,1,0:T(8,128)(2,1)} %collective-permute-done.11, bf16[16,32,4096]{2,1,0:T(8,128)(2,1)} %get-tuple-element.244), kind=kLoop, calls=%fused_computation | loop fusion | flops 4194304 | bytes 6291456 | tf_op jit(solution)/shard_map/convert_element_type | solution.py:709
  258.3 10.5 %weight_grad.2 = (bf16[16,160,512]{2,1,0:T(8,128)(2,1)}, bf16[16,160,512]{2,1,0:T(8,128)(2,1)}) custom-call(s32[32]{0:T(128)} %copy-done.20, bf16[1024,1024]{1,0:T(8,128)(2,1)} %get-tuple-element.230.left_ref, bf16[3,1024,512]{2,1,0:T(8,128)(2,1)} %get-tuple-element.248.d_ref, bf16[1024,1024]{1,0:T(8,128)(2,1)} %get-tuple-element.201.refs_0_.refs_12_, ...), custom_call_target="tpu_custom_call" | custom-call | flops 1000 | bytes 1000 | tf_op jit(solution)/shard_map/weight_grad/pallas_call | solution.py:494
  268.8 10.7 %attend_back.6 = (bf16[3,1024,512]{2,1,0:T(8,128)(2,1)}, f32[8,512]{1,0:T(8,128)}) custom-call(s32[1]{0:T(128)S(6)} %copy.62.prefix_ref, s32[1]{0:T(128)S(6)} %copy.63.padding_ref, bf16[1024,3072]{1,0:T(8,128)(2,1)} %get-tuple-element.176.q_ref.k_ref.v_ref, bf16[1024,3072]{1,0:T(8,128)(2,1)} %get-tuple-element.176.q_ref.k_ref.v_ref, ...), custom_call_target="tpu_custom_call" | custom-call | flops 1000 | bytes 1000 | tf_op jit(solution)/shard_map/attend_back/pallas_call | solution.py:388
  279.6 3.3 add_convert_fusion.6
  284.4 10.9 %attend_back.7 = (bf16[3,1024,512]{2,1,0:T(8,128)(2,1)}, f32[8,512]{1,0:T(8,128)}) custom-call(s32[1]{0:T(128)S(6)} %copy.62.prefix_ref, s32[1]{0:T(128)S(6)} %copy.63.padding_ref, bf16[1024,3072]{1,0:T(8,128)(2,1)} %get-tuple-element.176.q_ref.k_ref.v_ref, ...), custom_call_target="tpu_custom_call", output_to_operand_aliasing={{0}: (8, {}), {1}: (9, {})} | custom-call | flops 1000 | bytes 1000 | tf_op jit(solution)/shard_map/attend_back/pallas_call | solution.py:388
  295.3 4.8 %collective-permute-done.14 = bf16[4,32,4096]{2,1,0:T(8,128)(2,1)S(1)} collective-permute-done((bf16[4,32,4096]{2,1,0:T(8,128)(2,1)}, bf16[4,32,4096]{2,1,0:T(8,128)(2,1)S(1)}, u32[]{:S(2)}, u32[]{:S(2)}) %collective-permute-start.14) | collective-permute-done | bytes 1048608 | tf_op jit(solution)/shard_map/ppermute | solution.py:656
  300.0 5.2 %add_convert_fusion.4 = (bf16[4,32,4096]{2,1,0:T(8,128)(2,1)}, bf16[4,32,4096]{2,1,0:T(8,128)(2,1)}) fusion(bf16[4,32,4096]{2,1,0:T(8,128)(2,1)S(1)} %collective-permute-done.14, bf16[8,32,4096]{2,1,0:T(8,128)(2,1)} %collective-permute-done.12, bf16[16,32,4096]{2,1,0:T(8,128)(2,1)} %collective-permute-done.10, bf16[16,32,4096]{2,1,0:T(8,128)(2,1)} %get-tuple-element.226, ...), kind=kLoop, calls=%fused_computation.4 | loop fusion | flops 7340032 | bytes 9437184 | tf_op jit(solution)/shard_map/convert_element_type | solution.py:707
  309.6 7.4 %weight_grad.3 = (bf16[16,112,512]{2,1,0:T(8,128)(2,1)}, bf16[16,112,512]{2,1,0:T(8,128)(2,1)}) custom-call(s32[32]{0:T(128)} %copy-done.20, bf16[1024,1024]{1,0:T(8,128)(2,1)} %get-tuple-element.230.left_ref, bf16[3,1024,512]{2,1,0:T(8,128)(2,1)} %get-tuple-element.214.d_ref, f32[32,512]{1,0:T(8,128)} %pad.9.refs_0_), custom_call_target="tpu_custom_call" | custom-call | flops 1000 | bytes 1000 | tf_op jit(solution)/shard_map/weight_grad/pallas_call | solution.py:494
  317.2 3.2 collective-permute-done.16
  320.4 2.8 add_convert_fusion.2
  323.1 3.6 add_convert_fusion.3
  328.1 8.2 %cotangent.2.refs_10_ = bf16[1024,1024]{1,0:T(8,128)(2,1)} custom-call(s32[32]{0:T(128)} %select_reduce_fusion.order_ref, bf16[3,1024,512]{2,1,0:T(8,128)(2,1)} %get-tuple-element.248.d_ref, bf16[4,32,4224]{2,1,0:T(8,128)(2,1)} %copy-done, bf16[4,32,4224]{2,1,0:T(8,128)(2,1)} %copy-done.1, bf16[4,32,4224]{2,1,0:T(8,128)(2,1)} %copy-done.2, ...), custom_call_target="tpu_custom_call" | custom-call | flops 1000 | bytes 1000 | tf_op jit(solution)/shard_map/cotangent/pallas_call | solution.py:571
  336.4 2.7 add_convert_fusion.7
  339.7 12.6 %cotangent.3 = (bf16[1024,1024]{1,0:T(8,128)(2,1)}, f32[2,1024]{1,0:T(2,128)}) custom-call(s32[32]{0:T(128)} %select_reduce_fusion.order_ref, bf16[3,1024,512]{2,1,0:T(8,128)(2,1)} %get-tuple-element.214.d_ref, bf16[4,32,4224]{2,1,0:T(8,128)(2,1)} %copy-done, bf16[4,32,4224]{2,1,0:T(8,128)(2,1)} %copy-done.1, bf16[4,32,4224]{2,1,0:T(8,128)(2,1)} %copy-done.2, ...), custom_call_target="tpu_custom_call" | custom-call | flops 1000 | bytes 1000 | tf_op jit(solution)/shard_map/cotangent/pallas_call | solution.py:571
  361.4 2.9 collective-permute-done.21
  384.2 2.7 collective-permute-start.32
  392.0 2.7 collective-permute-done.29
  (179 shorter events, 63.9 us)
Async XLA Ops:
  7.2 150.6 %all-gather.2.cloned.1.call-start = ((), (), s32[]{:S(2)}) async-start(), calls=%async_computation.2 | async-start | bytes 17301504 | tf_op jit(solution)/shard_map/all_gather | solution.py:761
  11.3 325.0 %reduce-scatter.3.cloned.1.call-start = ((), (), s32[]{:S(2)}) async-start(), calls=%async_computation.3 | async-start | bytes 1310720 | tf_op jit(solution)/shard_map/reduce_scatter | solution.py:713
  11.8 15.3 %collective-permute-start = (bf16[32,4224]{1,0:T(8,128)(2,1)S(1)}, bf16[32,4224]{1,0:T(8,128)(2,1)S(1)}, u32[]{:S(2)}, u32[]{:S(2)}) collective-permute-start(bf16[32,4224]{1,0:T(8,128)(2,1)S(1)} %get-tuple-element.326), channel_id=1, source_target_pairs={{0,1},{1,0},{2,3},{3,2},{4,5},{5,4},{6,7},{7,6},{8,9},{9,8},{10,11... | collective-permute-start | bytes 811016 | tf_op jit(solution)/shard_map/ppermute | solution.py:656
  14.9 26.6 %collective-permute-start.1 = (bf16[32,4224]{1,0:T(8,128)(2,1)S(1)}, bf16[32,4224]{1,0:T(8,128)(2,1)S(1)}, u32[]{:S(2)}, u32[]{:S(2)}) collective-permute-start(bf16[32,4224]{1,0:T(8,128)(2,1)S(1)} %get-tuple-element.326), channel_id=1, source_target_pairs={{0,2},{1,3},{2,0},{3,1},{4,6},{5,7},{6,4},{7,5},{8,10},{9,11},{10,... | collective-permute-start | bytes 811016 | tf_op jit(solution)/shard_map/ppermute | solution.py:656
  17.5 24.0 %collective-permute-start.2 = (bf16[32,4224]{1,0:T(8,128)(2,1)S(1)}, bf16[32,4224]{1,0:T(8,128)(2,1)S(1)}, u32[]{:S(2)}, u32[]{:S(2)}) collective-permute-start(bf16[32,4224]{1,0:T(8,128)(2,1)S(1)} %get-tuple-element.326), channel_id=1, source_target_pairs={{0,3},{1,2},{2,1},{3,0},{4,7},{5,6},{6,5},{7,4},{8,11},{9,10},{10,... | collective-permute-start | bytes 811016 | tf_op jit(solution)/shard_map/ppermute | solution.py:656
  41.7 32.4 %collective-permute-start.3 = (bf16[4,32,4224]{2,1,0:T(8,128)(2,1)S(1)}, bf16[4,32,4224]{2,1,0:T(8,128)(2,1)S(1)}, u32[]{:S(2)}, u32[]{:S(2)}) collective-permute-start(bf16[4,32,4224]{2,1,0:T(8,128)(2,1)S(1)} %pad_maximum_fusion.refs_0_.refs_8_), channel_id=1, source_target_pairs={{0,16},{1,17},{2,18},{3,19},{4,12},{5,13},{6,14},{7,15},{8,24},{9,... | collective-permute-start | bytes 3244040 | tf_op jit(solution)/shard_map/ppermute | solution.py:656
  43.3 33.1 %collective-permute-start.4 = (bf16[4,32,4224]{2,1,0:T(8,128)(2,1)S(1)}, bf16[4,32,4224]{2,1,0:T(8,128)(2,1)S(1)}, u32[]{:S(2)}, u32[]{:S(2)}) collective-permute-start(bf16[4,32,4224]{2,1,0:T(8,128)(2,1)S(1)} %pad_maximum_fusion.refs_0_.refs_8_), channel_id=1, source_target_pairs={{0,8},{1,9},{2,10},{3,11},{4,20},{5,21},{6,22},{7,23},{8,0},{9,1},... | collective-permute-start | bytes 3244040 | tf_op jit(solution)/shard_map/ppermute | solution.py:656
  76.4 15.7 %collective-permute-start.8 = (bf16[4,32,4224]{2,1,0:T(8,128)(2,1)S(1)}, bf16[4,32,4224]{2,1,0:T(8,128)(2,1)}, u32[]{:S(2)}, u32[]{:S(2)}) collective-permute-start(bf16[4,32,4224]{2,1,0:T(8,128)(2,1)S(1)} %collective-permute-done.3.refs_1_.refs_9_), channel_id=1, source_target_pairs={{0,8},{1,9},{2,10},{3,11},{4,20},{5,21},{6,22},{7,23},{8,0},{9,1},... | collective-permute-start | bytes 3244040 | tf_op jit(solution)/shard_map/ppermute | solution.py:656
  78.8 13.2 %collective-permute-start.5 = (bf16[4,32,4224]{2,1,0:T(8,128)(2,1)S(1)}, bf16[4,32,4224]{2,1,0:T(8,128)(2,1)S(1)}, u32[]{:S(2)}, u32[]{:S(2)}) collective-permute-start(bf16[4,32,4224]{2,1,0:T(8,128)(2,1)S(1)} %pad_maximum_fusion.refs_0_.refs_8_), channel_id=1, source_target_pairs={{0,4},{1,5},{2,6},{3,7},{4,0},{5,1},{6,2},{7,3},{8,12},{9,13},{10,... | collective-permute-start | bytes 3244040 | tf_op jit(solution)/shard_map/ppermute | solution.py:653
  78.8 13.2 %collective-permute-start.7 = (bf16[4,32,4224]{2,1,0:T(8,128)(2,1)S(1)}, bf16[4,32,4224]{2,1,0:T(8,128)(2,1)S(1)}, u32[]{:S(2)}, u32[]{:S(2)}) collective-permute-start(bf16[4,32,4224]{2,1,0:T(8,128)(2,1)S(1)} %collective-permute-done.4.refs_2_.refs_10_), channel_id=1, source_target_pairs={{0,4},{1,5},{2,6},{3,7},{4,0},{5,1},{6,2},{7,3},{8,12},{9,13},{10,... | collective-permute-start | bytes 3244040 | tf_op jit(solution)/shard_map/ppermute | solution.py:653
  225.2 11.2 %collective-permute-start.10 = (bf16[16,32,4096]{2,1,0:T(8,128)(2,1)}, bf16[16,32,4096]{2,1,0:T(8,128)(2,1)}, u32[]{:S(2)}, u32[]{:S(2)}) collective-permute-start(bf16[16,32,4096]{2,1,0:T(8,128)(2,1)} %get-tuple-element.187), channel_id=1, source_target_pairs={{0,4},{1,5},{2,6},{3,7},{4,0},{5,1},{6,2},{7,3},{8,12},{9,13},{10,... | collective-permute-start | bytes 12582920 | tf_op jit(solution)/shard_map/ppermute | solution.py:653
  225.5 27.8 %collective-permute-start.11 = (bf16[16,32,4096]{2,1,0:T(8,128)(2,1)}, bf16[16,32,4096]{2,1,0:T(8,128)(2,1)}, u32[]{:S(2)}, u32[]{:S(2)}) collective-permute-start(bf16[16,32,4096]{2,1,0:T(8,128)(2,1)} %get-tuple-element.196), channel_id=1, source_target_pairs={{0,4},{1,5},{2,6},{3,7},{4,0},{5,1},{6,2},{7,3},{8,12},{9,13},{10,... | collective-permute-start | bytes 12582920 | tf_op jit(solution)/shard_map/ppermute | solution.py:653
  240.8 38.8 %collective-permute-start.12 = (bf16[8,32,4096]{2,1,0:T(8,128)(2,1)}, bf16[8,32,4096]{2,1,0:T(8,128)(2,1)}, u32[]{:S(2)}, u32[]{:S(2)}) collective-permute-start(bf16[8,32,4096]{2,1,0:T(8,128)(2,1)} %add_convert_fusion.1), channel_id=1, source_target_pairs={{0,8},{1,9},{2,10},{3,11},{4,20},{5,21},{6,22},{7,23},{8,0},{9,1},... | collective-permute-start | bytes 6291464 | tf_op jit(solution)/shard_map/ppermute | solution.py:656
  257.7 37.5 %collective-permute-start.13 = (bf16[8,32,4096]{2,1,0:T(8,128)(2,1)}, bf16[8,32,4096]{2,1,0:T(8,128)(2,1)S(1)}, u32[]{:S(2)}, u32[]{:S(2)}) collective-permute-start(bf16[8,32,4096]{2,1,0:T(8,128)(2,1)} %add_convert_fusion), channel_id=1, source_target_pairs={{0,8},{1,9},{2,10},{3,11},{4,20},{5,21},{6,22},{7,23},{8,0},{9,1},... | collective-permute-start | bytes 6291464 | tf_op jit(solution)/shard_map/ppermute | solution.py:656
  282.9 17.2 %collective-permute-start.14 = (bf16[4,32,4096]{2,1,0:T(8,128)(2,1)}, bf16[4,32,4096]{2,1,0:T(8,128)(2,1)S(1)}, u32[]{:S(2)}, u32[]{:S(2)}) collective-permute-start(bf16[4,32,4096]{2,1,0:T(8,128)(2,1)} %add_convert_fusion.6), channel_id=1, source_target_pairs={{0,16},{1,17},{2,18},{3,19},{4,12},{5,13},{6,14},{7,15},{8,24},{9,... | collective-permute-start | bytes 3145736 | tf_op jit(solution)/shard_map/ppermute | solution.py:656
  284.4 32.8 %collective-permute-start.15 = (bf16[16,160,512]{2,1,0:T(8,128)(2,1)}, bf16[16,160,512]{2,1,0:T(8,128)(2,1)}, u32[]{:S(2)}, u32[]{:S(2)}) collective-permute-start(bf16[16,160,512]{2,1,0:T(8,128)(2,1)} %get-tuple-element.236), channel_id=1, source_target_pairs={{0,4},{1,5},{2,6},{3,7},{4,0},{5,1},{6,2},{7,3},{8,12},{9,13},{10,... | collective-permute-start | bytes 7864328 | tf_op jit(solution)/shard_map/ppermute | solution.py:653
  305.3 15.1 %collective-permute-start.16 = (bf16[4,32,4096]{2,1,0:T(8,128)(2,1)}, bf16[4,32,4096]{2,1,0:T(8,128)(2,1)}, u32[]{:S(2)}, u32[]{:S(2)}) collective-permute-start(bf16[4,32,4096]{2,1,0:T(8,128)(2,1)} %get-tuple-element.240), channel_id=1, source_target_pairs={{0,16},{1,17},{2,18},{3,19},{4,12},{5,13},{6,14},{7,15},{8,24},{9,... | collective-permute-start | bytes 3145736 | tf_op jit(solution)/shard_map/ppermute | solution.py:656
  308.6 65.5 %reduce-scatter.5.cloned.1.call-start = ((), (), s32[]{:S(2)}) async-start(), calls=%async_computation.4 | async-start | bytes 1310720 | tf_op jit(solution)/shard_map/reduce_scatter | solution.py:713
  317.0 19.4 %collective-permute-start.17 = (bf16[16,112,512]{2,1,0:T(8,128)(2,1)}, bf16[16,112,512]{2,1,0:T(8,128)(2,1)}, u32[]{:S(2)}, u32[]{:S(2)}) collective-permute-start(bf16[16,112,512]{2,1,0:T(8,128)(2,1)} %get-tuple-element.249), channel_id=1, source_target_pairs={{0,4},{1,5},{2,6},{3,7},{4,0},{5,1},{6,2},{7,3},{8,12},{9,13},{10,... | collective-permute-start | bytes 5505032 | tf_op jit(solution)/shard_map/ppermute | solution.py:653
  326.7 29.0 %collective-permute-start.19 = (bf16[8,160,512]{2,1,0:T(8,128)(2,1)}, bf16[8,160,512]{2,1,0:T(8,128)(2,1)}, u32[]{:S(2)}, u32[]{:S(2)}) collective-permute-start(bf16[8,160,512]{2,1,0:T(8,128)(2,1)} %add_convert_fusion.2), channel_id=1, source_target_pairs={{0,8},{1,9},{2,10},{3,11},{4,20},{5,21},{6,22},{7,23},{8,0},{9,1},... | collective-permute-start | bytes 3932168 | tf_op jit(solution)/shard_map/ppermute | solution.py:656
  339.0 15.3 %collective-permute-start.18 = (bf16[8,112,512]{2,1,0:T(8,128)(2,1)}, bf16[8,112,512]{2,1,0:T(8,128)(2,1)S(1)}, u32[]{:S(2)}, u32[]{:S(2)}) collective-permute-start(bf16[8,112,512]{2,1,0:T(8,128)(2,1)} %add_convert_fusion.7), channel_id=1, source_target_pairs={{0,8},{1,9},{2,10},{3,11},{4,20},{5,21},{6,22},{7,23},{8,0},{9,1},... | collective-permute-start | bytes 2752520 | tf_op jit(solution)/shard_map/ppermute | solution.py:656
  355.7 8.5 %collective-permute-start.21 = (bf16[4,112,512]{2,1,0:T(8,128)(2,1)S(1)}, bf16[4,112,512]{2,1,0:T(8,128)(2,1)S(1)}, u32[]{:S(2)}, u32[]{:S(2)}) collective-permute-start(bf16[4,112,512]{2,1,0:T(8,128)(2,1)S(1)} %add_convert_fusion.9), channel_id=1, source_target_pairs={{0,16},{1,17},{2,18},{3,19},{4,12},{5,13},{6,14},{7,15},{8,24},{9,... | collective-permute-start | bytes 1376264 | tf_op jit(solution)/shard_map/ppermute | solution.py:656
  359.7 14.4 %collective-permute-start.24 = (bf16[4,160,512]{2,1,0:T(8,128)(2,1)}, bf16[4,160,512]{2,1,0:T(8,128)(2,1)}, u32[]{:S(2)}, u32[]{:S(2)}) collective-permute-start(bf16[4,160,512]{2,1,0:T(8,128)(2,1)} %add_convert_fusion.8), channel_id=1, source_target_pairs={{0,16},{1,17},{2,18},{3,19},{4,12},{5,13},{6,14},{7,15},{8,24},{9,... | collective-permute-start | bytes 1966088 | tf_op jit(solution)/shard_map/ppermute | solution.py:656
  367.1 7.0 %collective-permute-start.23 = (bf16[1,112,512]{2,1,0:T(8,128)(2,1)S(1)}, bf16[1,112,512]{2,1,0:T(8,128)(2,1)}, u32[]{:S(2)}, u32[]{:S(2)}) collective-permute-start(bf16[1,112,512]{2,1,0:T(8,128)(2,1)S(1)} %get-tuple-element.322), channel_id=1, source_target_pairs={{0,1},{1,0},{2,3},{3,2},{4,5},{5,4},{6,7},{7,6},{8,9},{9,8},{10,11... | collective-permute-start | bytes 344072 | tf_op jit(solution)/shard_map/ppermute | solution.py:656
  367.1 7.0 %collective-permute-start.22 = (f32[2,1024]{1,0:T(2,128)S(1)}, f32[2,1024]{1,0:T(2,128)S(1)}, u32[]{:S(2)}, u32[]{:S(2)}) collective-permute-start(f32[2,1024]{1,0:T(2,128)S(1)} %add.241), channel_id=1, source_target_pairs={{0,1},{1,0},{2,3},{3,2},{4,5},{5,4},{6,7},{7,6},{8,9},{9,8},{10,11... | collective-permute-start | bytes 24584 | tf_op jit(solution)/shard_map/ppermute | solution.py:800
  369.1 10.0 %collective-permute-start.26 = (bf16[1,112,512]{2,1,0:T(8,128)(2,1)}, bf16[1,112,512]{2,1,0:T(8,128)(2,1)}, u32[]{:S(2)}, u32[]{:S(2)}) collective-permute-start(bf16[1,112,512]{2,1,0:T(8,128)(2,1)} %get-tuple-element.321), channel_id=1, source_target_pairs={{0,2},{1,3},{2,0},{3,1},{4,6},{5,7},{6,4},{7,5},{8,10},{9,11},{10,... | collective-permute-start | bytes 344072 | tf_op jit(solution)/shard_map/ppermute | solution.py:656
  369.9 19.2 %collective-permute-start.28 = (bf16[1,112,512]{2,1,0:T(8,128)(2,1)}, bf16[1,112,512]{2,1,0:T(8,128)(2,1)}, u32[]{:S(2)}, u32[]{:S(2)}) collective-permute-start(bf16[1,112,512]{2,1,0:T(8,128)(2,1)} %get-tuple-element.320), channel_id=1, source_target_pairs={{0,3},{1,2},{2,1},{3,0},{4,7},{5,6},{6,5},{7,4},{8,11},{9,10},{10,... | collective-permute-start | bytes 344072 | tf_op jit(solution)/shard_map/ppermute | solution.py:656
  376.5 4.6 %collective-permute-start.25 = (f32[2,1024]{1,0:T(2,128)S(1)}, f32[2,1024]{1,0:T(2,128)S(1)}, u32[]{:S(2)}, u32[]{:S(2)}) collective-permute-start(f32[2,1024]{1,0:T(2,128)S(1)} %add.254), channel_id=1, source_target_pairs={{0,2},{1,3},{2,0},{3,1},{4,6},{5,7},{6,4},{7,5},{8,10},{9,11},{10,... | collective-permute-start | bytes 24584 | tf_op jit(solution)/shard_map/ppermute | solution.py:800
  381.1 8.0 %collective-permute-start.27 = (f32[2,1024]{1,0:T(2,128)S(1)}, f32[2,1024]{1,0:T(2,128)S(1)}, u32[]{:S(2)}, u32[]{:S(2)}) collective-permute-start(f32[2,1024]{1,0:T(2,128)S(1)} %add.258), channel_id=1, source_target_pairs={{0,8},{1,9},{2,10},{3,11},{4,12},{5,13},{6,14},{7,15},{8,0},{9,1},... | collective-permute-start | bytes 24584 | tf_op jit(solution)/shard_map/ppermute | solution.py:800
  382.5 12.9 %collective-permute-start.30 = (bf16[1,160,512]{2,1,0:T(8,128)(2,1)}, bf16[1,160,512]{2,1,0:T(8,128)(2,1)S(1)}, u32[]{:S(2)}, u32[]{:S(2)}) collective-permute-start(bf16[1,160,512]{2,1,0:T(8,128)(2,1)} %get-tuple-element.301), channel_id=1, source_target_pairs={{0,1},{1,0},{2,3},{3,2},{4,5},{5,4},{6,7},{7,6},{8,9},{9,8},{10,11... | collective-permute-start | bytes 491528 | tf_op jit(solution)/shard_map/ppermute | solution.py:656
  382.5 13.9 %collective-permute-start.31 = (bf16[1,160,512]{2,1,0:T(8,128)(2,1)}, bf16[1,160,512]{2,1,0:T(8,128)(2,1)S(1)}, u32[]{:S(2)}, u32[]{:S(2)}) collective-permute-start(bf16[1,160,512]{2,1,0:T(8,128)(2,1)} %get-tuple-element.302), channel_id=1, source_target_pairs={{0,2},{1,3},{2,0},{3,1},{4,6},{5,7},{6,4},{7,5},{8,10},{9,11},{10,... | collective-permute-start | bytes 491528 | tf_op jit(solution)/shard_map/ppermute | solution.py:656
  384.2 12.2 %collective-permute-start.32 = (bf16[1,160,512]{2,1,0:T(8,128)(2,1)}, bf16[1,160,512]{2,1,0:T(8,128)(2,1)S(1)}, u32[]{:S(2)}, u32[]{:S(2)}) collective-permute-start(bf16[1,160,512]{2,1,0:T(8,128)(2,1)} %get-tuple-element.303), channel_id=1, source_target_pairs={{0,3},{1,2},{2,1},{3,0},{4,7},{5,6},{6,5},{7,4},{8,11},{9,10},{10,... | collective-permute-start | bytes 491528 | tf_op jit(solution)/shard_map/ppermute | solution.py:656
  (34 other events, 233.8 us)
Sparse Core Ops, SparseCore 0:
  11.6 146.1 all-gather.1
  308.7 25.2 reduce-scatter.2
  339.8 26.1 reduce-scatter.4
